TPU v7x, 256 devices: a whole 4x4x8 slice. The times are simulated.
256 devices in a mesh: tm: 4 (over x_hi, core), row: 64 (over y, z, x_lo).
Axes of the slice: x: 4 (x_hi: 2, x_lo: 2; x = x_hi * 2 + x_lo), y: 4, z: 8, core: 2. Of those that a mesh axis runs over, the one named last changes fastest.
Arguments:
- event_counts: int32 [4, 4096, 4096], P('tm', 'row'), may hold values from 0 to 8
- latent_mean: float32 [4, 4096, 4096], P('tm', 'row'), may hold values from -3 to 3
- latent_var: float32 [4, 4096, 4096], P('tm', 'row'), may hold values from 0.05 to 0.6
- eigen_basis: bfloat16 [4096, 4096], P('row', 'tm'), may hold values from -0.09375 to 0.09375
- spectrum: float32 [4096], replicated, may hold values from 0.2 to 2
- correlation: float32 [1], replicated, may hold values from 0.3 to 0.9
- whitened: float32 [4, 64, 16, 4, 4096], P(None, 'row', None, None, 'tm'), may hold values from -6 to 6
Outputs:
- gradient: float32 [4, 64, 16, 4, 4096], P(None, 'row', None, None, 'tm')
All inputs are finite; a program needn't handle non-finite values.
Results may differ from a plain program's by a relative error of at most 0.0045.
Values may be sent and summed in bfloat16 or wider, within the bound.
No kernel may reach another device: no remote copies, remote signals or barrier semaphores. Data moves between devices by JAX's collectives and lax.ppermute only.
A program may use at most 64 MiB of HBM per device.

v0:
```python
import math

import jax
import jax.numpy as jnp
from jax import lax
from jax.sharding import Mesh
from jax.sharding import PartitionSpec as P

ROW = ("row_0", "row_1", "row_2")


HERMITE_NODES = (
    -2.0201828704560856,
    -0.9585724646138185,
    0.0,
    0.9585724646138185,
    2.0201828704560856,
)
HERMITE_WEIGHTS = (
    0.019953242059045913,
    0.3936193231522412,
    0.9453087204829419,
    0.3936193231522412,
    0.019953242059045913,
)


def sent_to_all(array, axis):
    size = lax.axis_size(axis)
    return lax.all_to_all(
        jnp.broadcast_to(array[None], (size, *array.shape)), axis, 0, 0, tiled=True
    )


def laid_out(tiles, dim):
    tiles = jnp.moveaxis(tiles, 0, dim)
    dims = tiles.shape
    return tiles.reshape(*dims[:dim], dims[dim] * dims[dim + 1], *dims[dim + 2 :])


def gathered_copies(array, axis, dim):
    tiles = sent_to_all(array, axis)
    return laid_out(tiles, dim)


def stacked_from(array, axes, sequence):
    tiles = array
    for k in sequence:
        tiles = lax.all_gather(tiles, axes[k])
    done = sequence[::-1]
    back = [done.index(k) for k in range(len(axes))]
    tiles = tiles.transpose(*back, *range(len(axes), tiles.ndim))
    return tiles.reshape(-1, *array.shape)


def gathered_by_axis(array, axes, sequence, dim):
    return laid_out(stacked_from(array, axes, sequence), dim)


def moments(event_counts, latent_mean, latent_var):
    spread = jnp.sqrt(2.0 * latent_var)
    normal = 1.0 / math.sqrt(math.pi)
    points = [latent_mean + spread * abscissa for abscissa in HERMITE_NODES]
    rate_points = [jnp.exp(value) for value in points]
    mean_rate = sum(
        (weight * normal * value for weight, value in zip(HERMITE_WEIGHTS, rate_points))
    )
    covariance = sum(
        (
            weight * normal * (node_value - latent_mean) * (value - mean_rate)
            for weight, node_value, value in zip(HERMITE_WEIGHTS, points, rate_points)
        )
    )
    rate_var = sum(
        (
            weight * normal * (value - mean_rate) * (value - mean_rate)
            for weight, value in zip(HERMITE_WEIGHTS, rate_points)
        )
    )
    slope_gain = covariance / latent_var
    noise_var = rate_var - slope_gain * covariance + mean_rate
    return slope_gain * (event_counts.astype(latent_mean.dtype) - mean_rate) / noise_var


def time_factor(correlation, total):
    later = jnp.arange(total)[:, None]
    earlier = jnp.arange(total)[None, :]
    distance = jnp.maximum(later - earlier, 0).astype(correlation.dtype)
    lower = jnp.where(later >= earlier, jnp.power(correlation, distance), jnp.zeros_like(distance))
    column_scale = jnp.where(
        earlier == 0,
        jnp.ones_like(distance),
        jnp.sqrt(1.0 - correlation * correlation) * jnp.ones_like(distance),
    )
    return lower * column_scale


def local(event_counts, latent_mean, latent_var, eigen_basis, spectrum, correlation, whitened):
    time_count = lax.axis_size("tm")
    row_devices = lax.axis_size(ROW)
    pseudo = moments(event_counts, latent_mean, latent_var).astype(jnp.bfloat16)
    slices = gathered_copies(pseudo, "tm", 0)
    total, row_count, width = slices.shape
    factor = time_factor(correlation[0], total)
    flat = slices.reshape(total, row_count * width).astype(jnp.float32)
    mixed_field = (
        jnp.dot(factor.T, flat, precision=lax.Precision.HIGHEST)
        .reshape(total, row_count, width)
        .astype(jnp.bfloat16)
    )
    band_width = eigen_basis.shape[1]
    gathered = gathered_by_axis(eigen_basis, ROW, (2, 0, 1), 0)
    partial_y = jnp.einsum("akj,jq->qak", mixed_field, gathered, preferred_element_type=jnp.float32)
    partial_y = partial_y.astype(jnp.bfloat16)
    mode_columns = lax.all_to_all(partial_y, ROW, split_axis=0, concat_axis=2, tiled=True)
    band_rows = gathered_copies(mode_columns, "tm", 0)
    group_size = band_rows.shape[0]
    mode_values = jnp.einsum("qak,kp->qap", band_rows, gathered, preferred_element_type=jnp.float32)
    block_modes = group_size // time_count
    scale_x = lax.dynamic_slice_in_dim(spectrum, lax.axis_index("tm") * band_width, band_width, 0)
    scale_y = lax.dynamic_slice_in_dim(
        spectrum.reshape(time_count, row_devices, block_modes), lax.axis_index(ROW), 1, 1
    ).reshape(group_size)
    scaled = jnp.sqrt(scale_y)[:, None, None] * jnp.sqrt(scale_x)[None, None, :] * mode_values
    gradient = scaled - whitened.reshape(group_size, total, band_width)
    return gradient.reshape(time_count, 1, block_modes, total, band_width)


def solution(mesh):
    finer = Mesh(mesh.devices.reshape(mesh.shape["tm"], 4, 8, 2), ("tm", "row_0", "row_1", "row_2"))
    placed = (
        P("tm", ROW, None),
        P("tm", ROW, None),
        P("tm", ROW, None),
        P(ROW, "tm"),
        P(),
        P(),
        P(None, ROW, None, None, "tm"),
    )
    return jax.shard_map(
        local,
        mesh=finer,
        in_specs=placed,
        out_specs=P(None, ROW, None, None, "tm"),
        check_vma=False,
    )
```

profile of v0, /device:TPU:32, one launch (start us, length us, event | category | flops | bytes accessed | tf_op | source)
XLA Modules:
  0.0 230.5 jit_solution(4145253441493333681)
XLA Ops:
  6.5 0.0 all-gather.6.cloned.1.call-start
  6.5 7.6 %all-gather = bf16[128,1024]{1,0:T(8,128)(2,1)} all-gather(bf16[64,1024]{1,0:T(8,128)(2,1)} %param.10), channel_id=2, replica_groups=mesh['tm'=4,'row_0'=4,'row_1'=8,'row_2'=2] {'row_2'}, dimensions={0}, use_global_device_ids=true | all-gather | bytes 393216 | tf_op jit(solution)/shard_map/all_gather | solution.py:49
  14.2 0.0 all-gather.6.cloned.1.call-update
  14.2 0.0 all-gather.8.cloned.1.call-start
  14.2 29.0 %all-gather.6.cloned.1.call-done = bf16[8,64,1024]{2,1,0:T(8,128)(2,1)} async-done(((bf16[2,64,1024]{2,1,0:T(8,128)(2,1)}), bf16[8,64,1024]{2,1,0:T(8,128)(2,1)}) %all-gather.6.cloned.1.call-update) | async-done | bytes 1048592 | tf_op jit(solution)/shard_map/all_gather | solution.py:49
  43.2 0.0 all-gather.8.cloned.1.call-update
  43.2 4.1 %fusion.17 = bf16[64,4096]{1,0:T(8,128)(2,1)S(1)} fusion(s32[1,64,4096]{2,1,0:T(8,128)S(1)} %copy-done, f32[1,64,4096]{2,1,0:T(8,128)} %param.9, f32[1,64,4096]{2,1,0:T(8,128)} %param.8), kind=kLoop, calls=%fused_computation.20 | loop fusion | flops 17563648 | bytes 3670016 | tf_op jit(solution)/shard_map/broadcast_in_dim | solution.py:31
  47.4 1.6 broadcast_in_dim.30
  49.0 4.2 %all-to-all-start = ((bf16[4,1,64,4096]{3,2,1,0:T(8,128)(2,1)}), bf16[4,1,64,4096]{3,2,1,0:T(8,128)(2,1)S(1)}, u32[]{:S(2)}, u32[]{:S(2)}) async-start(bf16[4,1,64,4096]{3,2,1,0:T(8,128)(2,1)} %broadcast_in_dim.30), calls=%async_computation | async-start | bytes 4194304 | tf_op jit(solution)/shard_map/all_to_all | solution.py:30
  54.0 26.5 %all-to-all-done = bf16[4,1,64,4096]{3,2,1,0:T(8,128)(2,1)S(1)} async-done(((bf16[4,1,64,4096]{3,2,1,0:T(8,128)(2,1)}), bf16[4,1,64,4096]{3,2,1,0:T(8,128)(2,1)S(1)}, u32[]{:S(2)}, u32[]{:S(2)}) %all-to-all-start) | async-done | bytes 2097184 | tf_op jit(solution)/shard_map/all_to_all | solution.py:30
  80.5 5.3 %convolution_convert_fusion = bf16[4,64,4096]{2,0,1:T(4,128)(2,1)} fusion(f32[4]{0:T(128)S(1)} %compare_select_fusion, f32[]{:T(128)} %bitcast.38, bf16[1,4,64,4096]{3,2,1,0:T(8,128)(2,1)S(1)} %bitcast.45), kind=kOutput, calls=%fused_computation | convolution fusion | flops 51380320 | bytes 4194324 | tf_op jit(solution)/shard_map/dot_general | solution.py:107
  85.7 52.0 %all-gather.8.cloned.1.call-done = bf16[32,2,64,1024]{3,2,1,0:T(8,128)(2,1)} async-done(((bf16[4,2,64,1024]{3,2,1,0:T(8,128)(2,1)}), bf16[32,2,64,1024]{3,2,1,0:T(8,128)(2,1)}) %all-gather.8.cloned.1.call-update) | async-done | bytes 8388624 | tf_op jit(solution)/shard_map/all_gather | solution.py:49
  137.7 8.6 %copy.15 = bf16[4,8,2,64,1024]{4,3,2,1,0:T(8,128)(2,1)} copy(bf16[4,8,2,64,1024]{4,3,2,0,1:T(8,128)(2,1)} %bitcast.43) | data formatting | bytes 16777216 | tf_op jit(solution)/shard_map/transpose | solution.py:52
  146.3 6.5 %fusion.6 = bf16[1024,4,64]{0,2,1:T(8,128)(2,1)S(1)} fusion(bf16[4096,1024,1]{1,0,2:T(8,128)(2,1)} %bitcast.41, bf16[4,64,4096]{2,0,1:T(4,128)(2,1)S(1)} %copy-done.4), kind=kOutput, calls=%fused_computation.11 | convolution fusion | flops 2147745792 | bytes 11010048 | tf_op jit(solution)/shard_map/akj,jq->qak/dot_general | solution.py:113
  152.8 0.7 copy.17
  153.5 0.7 reshape.76
  154.2 27.1 %all_to_all.25 = bf16[64,2,2048]{2,1,0:T(2,128)(2,1)S(1)} all-to-all(bf16[64,2,2048]{2,1,0:T(2,128)(2,1)S(1)} %reshape.76), channel_id=1, replica_groups=mesh['tm'=4,'row_0'=4,'row_1'=8,'row_2'=2] {'row_0','row_1','row_2'}, dimensions={0} | all-to-all | bytes 1048576 | tf_op jit(solution)/shard_map/all_to_all | solution.py:115
  181.3 0.7 reshape.77
  182.0 0.1 copy.18
  182.1 0.3 copy.19
  182.4 0.8 broadcast_in_dim.31
  183.2 1.6 broadcast_in_dim.32
  184.8 4.1 %all-to-all-start.2 = ((bf16[4,16,4,4096]{3,1,2,0:T(8,128)(2,1)}), bf16[4,16,4,4096]{3,1,2,0:T(8,128)(2,1)S(1)}, u32[]{:S(2)}, u32[]{:S(2)}) async-start(bf16[4,16,4,4096]{3,1,2,0:T(8,128)(2,1)} %broadcast_in_dim.32), calls=%async_computation.2 | async-start | bytes 4194304 | tf_op jit(solution)/shard_map/all_to_all | solution.py:30
  188.9 0.1 reshape.60
  189.0 0.1 sqrt.20
  189.1 1.6 copy.21
  190.7 0.1 broadcast_multiply_fusion
  190.8 0.0 copy-start.2
  190.8 25.3 %all-to-all-done.2 = bf16[4,16,4,4096]{3,1,2,0:T(8,128)(2,1)S(1)} async-done(((bf16[4,16,4,4096]{3,1,2,0:T(8,128)(2,1)}), bf16[4,16,4,4096]{3,1,2,0:T(8,128)(2,1)S(1)}, u32[]{:S(2)}, u32[]{:S(2)}) %all-to-all-start.2) | async-done | bytes 2097184 | tf_op jit(solution)/shard_map/all_to_all | solution.py:30
  216.1 0.1 copy.20
  216.2 5.8 %fusion.2 = f32[64,4,1024]{2,0,1:T(8,128)S(1)} fusion(f32[64,4,1024]{2,0,1:T(8,128)S(1)} %bitcast.48, bf16[64,4,4096]{2,0,1:T(8,128)(2,1)S(1)} %bitcast.46, bf16[4096,1024,1]{1,0,2:T(8,128)(2,1)} %bitcast.42, f32[64,1024]{1,0:T(8,128)S(1)} %broadcast_multiply_fusion), kind=kOutput, calls=%fused_computation.9 | convolution fusion | flops 2148007936 | bytes 12845056 | tf_op jit(solution)/shard_map/qak,kp->qap/dot_general | solution.py:118
  222.0 1.6 copy.22
  (12 shorter events, 0.1 us)
Async XLA Ops:
  6.5 36.7 %copy-start = (s32[1,64,4096]{2,1,0:T(8,128)S(1)}, s32[1,64,4096]{2,1,0:T(8,128)}, u32[]{:S(2)}) copy-start(s32[1,64,4096]{2,1,0:T(8,128)} %param.7) | copy-start | bytes 3145732
  6.5 36.7 %all-gather.6.cloned.1.call-start = ((), (), s32[]{:S(2)}) async-start(), calls=%async_computation.3 | async-start | bytes 1310720 | tf_op jit(solution)/shard_map/all_gather | solution.py:49
  14.2 123.5 %all-gather.8.cloned.1.call-start = ((), (), s32[]{:S(2)}) async-start(), calls=%async_computation.4 | async-start | bytes 9437184 | tf_op jit(solution)/shard_map/all_gather | solution.py:49
  49.0 31.5 %all-to-all-start = ((bf16[4,1,64,4096]{3,2,1,0:T(8,128)(2,1)}), bf16[4,1,64,4096]{3,2,1,0:T(8,128)(2,1)S(1)}, u32[]{:S(2)}, u32[]{:S(2)}) async-start(bf16[4,1,64,4096]{3,2,1,0:T(8,128)(2,1)} %broadcast_in_dim.30), calls=%async_computation | async-start | bytes 4194304 | tf_op jit(solution)/shard_map/all_to_all | solution.py:30
  137.7 8.6 %copy-start.4 = (bf16[4,64,4096]{2,0,1:T(4,128)(2,1)S(1)}, bf16[4,64,4096]{2,0,1:T(4,128)(2,1)}, u32[]{:S(2)}) copy-start(bf16[4,64,4096]{2,0,1:T(4,128)(2,1)} %convolution_convert_fusion) | copy-start | bytes 6291460
  184.8 4.1 %copy-start.3 = (f32[4096]{0:T(1024)S(1)}, f32[4096]{0:T(1024)}, u32[]{:S(2)}) copy-start(f32[4096]{0:T(1024)} %param.11) | copy-start | bytes 49156
  184.8 4.3 %copy-start.1 = (f32[4,1,16,4,1024]{4,3,2,1,0:T(4,128)S(1)}, f32[4,1,16,4,1024]{4,3,2,1,0:T(4,128)}, u32[]{:S(2)}) copy-start(f32[4,1,16,4,1024]{4,3,2,1,0:T(4,128)} %param.13) | copy-start | bytes 3145732
  184.8 31.3 %all-to-all-start.2 = ((bf16[4,16,4,4096]{3,1,2,0:T(8,128)(2,1)}), bf16[4,16,4,4096]{3,1,2,0:T(8,128)(2,1)S(1)}, u32[]{:S(2)}, u32[]{:S(2)}) async-start(bf16[4,16,4,4096]{3,1,2,0:T(8,128)(2,1)} %broadcast_in_dim.32), calls=%async_computation.2 | async-start | bytes 4194304 | tf_op jit(solution)/shard_map/all_to_all | solution.py:30
  190.8 25.4 %copy-start.2 = (f32[4,1,16,4,1024]{4,2,0,3,1:T(8,128)S(1)}, f32[4,1,16,4,1024]{4,2,0,3,1:T(8,128)}, u32[]{:S(2)}) copy-start(f32[4,1,16,4,1024]{4,2,0,3,1:T(8,128)} %copy.21) | copy-start | bytes 3145732
Sparse Core Ops, SparseCore 0:
  14.3 28.8 all-gather.5
  45.0 92.6 all-gather.7
where the time goes:
time: 233 us; the launch traced here: 231 us
  waiting for transfers between devices  133 us (57%)
  blocking collectives  34.7 us (15%)
  local copies, waits for them, and re-layouts  18.7 us (8%)
  matrix products  17.5 us (8%)
  between operations  14.2 us (6%)
  starting transfers between devices  8.37 us (4%)
  other arithmetic  4.24 us (2%)
    all_gather x2, waiting for transfers between devices, stacked_from(): tiles = lax.all_gather(tiles, axes[k])  81 us
    all_to_all x2, waiting for transfers between devices, sent_to_all(): lax.all_to_all(jnp.broadcast_to(array[None], (size, *array.shape)), axis,...  51.8 us
    all_to_all x1, blocking collectives, local(): lax.all_to_all(partial_y, ROW, split_axis=0, concat_axis=2, tiled=True)  27.1 us
    transpose x1, local copies, waits for them, and re-layouts, stacked_from(): tiles = tiles.transpose(*back, *range(len(axes), tiles.ndim))  8.57 us
    all_to_all x2, starting transfers between devices, sent_to_all(): lax.all_to_all(jnp.broadcast_to(array[None], (size, *array.shape)), axis,...  8.33 us
    all_gather x1, blocking collectives, stacked_from(): tiles = lax.all_gather(tiles, axes[k])  7.63 us
    dot_general x1, matrix products, local(): jnp.einsum('akj,jq->qak', mixed_field, gathered, preferred_element_type=j...  6.5 us
    dot_general x1, matrix products, local(): jnp.einsum('qak,kp->qap', band_rows, gathered, preferred_element_type=jnp...  5.79 us
  transfers between devices with their start and end apart: 4, of which 4 were waited for; matrix products, arithmetic and copies ran while one was open for 6% of the time, Pallas kernels for 0%

commit v1 on v0

v1 whole, which is shorter than its diff:
```python
import math

import jax
import jax.numpy as jnp
from jax import lax
from jax.experimental import pallas as pl
from jax.experimental.pallas import tpu as pltpu
from jax.sharding import Mesh
from jax.sharding import PartitionSpec as P

TM = ("hi", "core")
ROW = ("y", "z", "lo")
RING = ("hi", "lo")

HERMITE_NODES = (
    -2.0201828704560856,
    -0.9585724646138185,
    0.0,
    0.9585724646138185,
    2.0201828704560856,
)
HERMITE_WEIGHTS = (
    0.019953242059045913,
    0.3936193231522412,
    0.9453087204829419,
    0.3936193231522412,
    0.019953242059045913,
)
VMEM = pl.BlockSpec(memory_space=pltpu.VMEM)
SMEM = pl.BlockSpec(memory_space=pltpu.SMEM)


def moments(event_counts, latent_mean, latent_var):
    spread = jnp.sqrt(2.0 * latent_var)
    normal = 1.0 / math.sqrt(math.pi)
    points = [latent_mean + spread * abscissa for abscissa in HERMITE_NODES]
    rate_points = [jnp.exp(value) for value in points]
    mean_rate = sum(
        (weight * normal * value for weight, value in zip(HERMITE_WEIGHTS, rate_points))
    )
    covariance = sum(
        (
            weight * normal * (node_value - latent_mean) * (value - mean_rate)
            for weight, node_value, value in zip(HERMITE_WEIGHTS, points, rate_points)
        )
    )
    rate_var = sum(
        (
            weight * normal * (value - mean_rate) * (value - mean_rate)
            for weight, value in zip(HERMITE_WEIGHTS, rate_points)
        )
    )
    slope_gain = covariance / latent_var
    noise_var = rate_var - slope_gain * covariance + mean_rate
    return slope_gain * (event_counts.astype(latent_mean.dtype) - mean_rate) / noise_var


def time_factor(correlation, total):
    later = jnp.arange(total)[:, None]
    earlier = jnp.arange(total)[None, :]
    distance = jnp.maximum(later - earlier, 0).astype(correlation.dtype)
    lower = jnp.where(later >= earlier, jnp.power(correlation, distance), jnp.zeros_like(distance))
    column_scale = jnp.where(
        earlier == 0,
        jnp.ones_like(distance),
        jnp.sqrt(1.0 - correlation * correlation) * jnp.ones_like(distance),
    )
    return lower * column_scale


def shifted(array, axis, step):
    size = lax.axis_size(axis)
    return lax.ppermute(array, axis, [(k, (k + step) % size) for k in range(size)])


def copies_along(array, axis):
    size = lax.axis_size(axis)
    return lax.all_to_all(
        jnp.broadcast_to(array[None], (size, *array.shape)), axis, 0, 0, tiled=True
    )


def split_kernel(basis_ref, halves_ref):
    source = lax.broadcasted_iota(jnp.int32, (256, 128), 0)
    target = lax.broadcasted_iota(jnp.int32, (256, 128), 1)
    for half in range(2):
        chosen = (source == (target // 8) * 16 + half * 8 + target % 8).astype(jnp.bfloat16)
        for block in range(basis_ref.shape[1] // 256):
            moved = jnp.dot(
                basis_ref[:, block * 256 : block * 256 + 256],
                chosen,
                preferred_element_type=jnp.float32,
            )
            halves_ref[half, :, block * 128 : block * 128 + 128] = moved.astype(jnp.bfloat16)


def split_columns(basis):
    rows, columns = basis.shape
    return pl.pallas_call(
        split_kernel,
        out_shape=jax.ShapeDtypeStruct((2, rows, columns // 2), basis.dtype),
        in_specs=[VMEM],
        out_specs=VMEM,
        name="split_columns",
    )(basis)


def first_kernel(
    mix_ref, place_ref, a0, a1, a2, a3, b0, b1, b2, b3, zy_ref, yz_ref, out_ref, acc_ref, tmp_ref
):
    blocks = (a0, a1, a2, a3, b0, b1, b2, b3)
    rows = a0.shape[0]
    ny, nz = yz_ref.shape[:2]
    depth = a0.shape[1] // ny
    half = zy_ref.shape[-1]
    for y in range(ny):
        field = jnp.concatenate([ref[:, y * depth : (y + 1) * depth] for ref in blocks], axis=0)
        for part in range(2):
            pieces = [zy_ref[z, y] if part == 0 else yz_ref[y, z] for z in range(nz)]
            product = jnp.dot(
                field, jnp.concatenate(pieces, axis=0), preferred_element_type=jnp.float32
            )
            span = slice(part * half, part * half + half)
            if y == 0:
                acc_ref[:, span] = product
            else:
                acc_ref[:, span] += product
    place = place_ref[0]
    for a in range(4):
        for group in range(2):
            mixed = sum(
                mix_ref[group * 4 + t, a]
                * acc_ref[(group * 4 + t) * rows : (group * 4 + t + 1) * rows, :]
                for t in range(4)
            )
            at = place if group == 0 else 1 - place
            tmp_ref[pl.ds(pl.multiple_of(at * rows, rows), rows), :] = mixed
        out_ref[:, a * 2 * rows : (a + 1) * 2 * rows] = tmp_ref[...].T.astype(jnp.bfloat16)


def first_product(mix, place, fields, zy, yz):
    rows, depth = fields[0].shape
    width = zy.shape[-1] + yz.shape[-1]
    return pl.pallas_call(
        first_kernel,
        out_shape=jax.ShapeDtypeStruct((width, 8 * rows), jnp.bfloat16),
        in_specs=[SMEM, SMEM] + [VMEM] * 10,
        out_specs=VMEM,
        scratch_shapes=[
            pltpu.VMEM((8 * rows, width), jnp.float32),
            pltpu.VMEM((2 * rows, width), jnp.float32),
        ],
        cost_estimate=pl.CostEstimate(
            flops=2 * 8 * rows * depth * width, bytes_accessed=8 << 20, transcendentals=0
        ),
        name="first_product",
    )(mix, place, *fields, zy, yz)


def last_kernel(
    place_ref, t0, t1, t2, t3, zy_ref, yz_ref, rest_ref, sx_ref, sy_ref, white_ref, out_ref, acc_ref
):
    fields = (t0, t1, t2, t3)
    ny, nz = yz_ref.shape[:2]
    times, rows, total = t0.shape
    depth = total // ny
    half = zy_ref.shape[-1]
    for y in range(ny):
        field = jnp.concatenate(
            [ref[a, :, y * depth : (y + 1) * depth] for a in range(times) for ref in fields], axis=0
        )
        for part in range(3):
            pieces = [
                (zy_ref[z, y], yz_ref[y, z], rest_ref[z, y])[part] for z in range(nz)
            ]
            product = jnp.dot(
                field, jnp.concatenate(pieces, axis=0), preferred_element_type=jnp.float32
            )
            span = slice(part * half, part * half + product.shape[-1])
            if y == 0:
                acc_ref[:, span] = product
            else:
                acc_ref[:, span] += product
    lo, time = place_ref[0], place_ref[1]
    source = lax.broadcasted_iota(jnp.int32, (256, 256), 0)
    target = lax.broadcasted_iota(jnp.int32, (256, 256), 1)
    within = lax.rem(source, 128)
    which = jnp.where(source < 128, lo, 1 - lo)
    chosen = (target == (within // 8) * 16 + which * 8 + lax.rem(within, 8)).astype(jnp.float32)
    width = out_ref.shape[-1]
    for block in range(width // 256):
        pair = jnp.concatenate(
            [
                acc_ref[:, block * 128 : block * 128 + 128],
                acc_ref[:, width // 2 + block * 128 : width // 2 + block * 128 + 128],
            ],
            axis=1,
        )
        natural = jnp.dot(pair, chosen, precision=lax.Precision.HIGHEST)
        span = slice(block * 256, block * 256 + 256)
        for a in range(times):
            for b in range(4):
                first = (a * 4 + b) * rows
                own = pl.ds(pl.multiple_of(lax.bitwise_xor(time, b) * rows, rows), rows)
                scale = sy_ref[b * rows : (b + 1) * rows, :1] * sx_ref[:, span]
                out_ref[own, a, span] = (
                    scale * natural[first : first + rows] - white_ref[own, a, span]
                )


def last_product(place, fields, zy, yz, rest, sx, sy, white):
    times, rows, total = fields[0].shape
    width = white.shape[-1]
    return pl.pallas_call(
        last_kernel,
        out_shape=jax.ShapeDtypeStruct(white.shape, jnp.float32),
        in_specs=[SMEM] + [VMEM] * 10,
        out_specs=VMEM,
        scratch_shapes=[pltpu.VMEM((4 * times * rows, width), jnp.float32)],
        cost_estimate=pl.CostEstimate(
            flops=2 * 4 * times * rows * total * width, bytes_accessed=12 << 20, transcendentals=0
        ),
        name="last_product",
    )(place, *fields, zy, yz, rest, sx, sy, white)


def local(event_counts, latent_mean, latent_var, eigen_basis, spectrum, correlation, whitened):
    hi, core = lax.axis_index("hi"), lax.axis_index("core")
    y, z, lo = (lax.axis_index(axis) for axis in ROW)
    time = hi * 2 + core
    ny, nz = lax.axis_size("y"), lax.axis_size("z")

    halves = split_columns(eigen_basis)
    other = shifted(halves, "lo", 1)
    stacked = jnp.where(lo == 0, jnp.stack([halves, other]), jnp.stack([other, halves]))
    mine = jnp.where(lo == 0, stacked[:, 0], stacked[:, 1])
    rest = jnp.where(lo == 0, stacked[:, 1], stacked[:, 0])
    mine = mine.reshape(-1, mine.shape[-1])
    rest = rest.reshape(-1, rest.shape[-1])
    quarter = mine.shape[-1] // 2

    yz = copies_along(lax.all_gather(mine[:, quarter:], "z"), "y")
    zy = lax.all_gather(copies_along(mine[:, :quarter], "y"), "z")
    rest_y = copies_along(rest, "y")
    rest_y, zy = lax.optimization_barrier((rest_y, zy))
    rest = lax.all_gather(rest_y, "z")

    pseudo = moments(event_counts, latent_mean, latent_var).astype(jnp.bfloat16)[0]
    around = [pseudo] + [shifted(pseudo, RING, step) for step in (2, 1, 3)]
    own, far, before, after = [(block, shifted(block, "core", 1)) for block in around]
    fields = (*own, *far, *before, *after)
    flips = jnp.array([0, 1, 2, 3], jnp.int32)
    before_flip, after_flip = 2 * (1 - lo), 2 * lo
    crossed = jnp.stack([before_flip, before_flip + 1, after_flip, after_flip + 1])
    slices = lax.bitwise_xor(time, jnp.concatenate([flips, crossed]))
    factor = time_factor(correlation[0], 4)
    mix = jnp.take(factor, slices, axis=0)
    place = jnp.stack([lo, time]).astype(jnp.int32)
    partial_y = first_product(mix, place, fields, zy, yz)

    modes, width = partial_y.shape
    row_devices = lax.axis_size(ROW)
    sent = partial_y.reshape(row_devices, modes // row_devices, width)
    got = lax.all_to_all(sent, ROW, 0, 0, tiled=True)
    got = got.reshape(ny * nz, 2, modes // row_devices, 4, width // 4)
    got = got.transpose(3, 1, 2, 0, 4).reshape(4, 2 * (modes // row_devices), -1)
    across = shifted(got, "hi", 1)
    bands = (got, shifted(got, "core", 1), across, shifted(across, "core", 1))

    root = jnp.sqrt(spectrum)
    sx = lax.dynamic_slice_in_dim(root, time * 1024, 1024, 0)[None]
    row = (y * nz + z) * 2 + lo
    by_row = lax.dynamic_slice_in_dim(root.reshape(4, row_devices, -1), row, 1, 1)[:, 0]
    sy = jnp.take(by_row, lax.bitwise_xor(time, flips), axis=0).reshape(-1, 1)
    sy = jnp.broadcast_to(sy, (sy.shape[0], 128))
    white = whitened.reshape(-1, *whitened.shape[3:])
    gradient = last_product(place, bands, zy, yz, rest, sx, sy, white)
    return gradient.reshape(whitened.shape)


def solution(mesh):
    finer = Mesh(mesh.devices.reshape(2, 2, 4, 8, 2), ("hi", "core", "y", "z", "lo"))
    placed = (
        P(TM, ROW, None),
        P(TM, ROW, None),
        P(TM, ROW, None),
        P(ROW, TM),
        P(),
        P(),
        P(None, ROW, None, None, TM),
    )
    return jax.shard_map(
        local,
        mesh=finer,
        in_specs=placed,
        out_specs=P(None, ROW, None, None, TM),
        check_vma=False,
    )
```

time: 233 us -> 194 us (0.83)
  waiting for transfers between devices: 133 us -> 55.4 us
  blocking collectives: 34.7 us -> 75 us
  Pallas kernels: 0 us -> 18.2 us
  matrix products: 17.5 us -> 0 us
  local copies, waits for them, and re-layouts: 18.7 us -> 7.32 us
  starting transfers between devices: 8.37 us -> 15.3 us
  other arithmetic: 4.24 us -> 6.74 us
    all_to_all x2 -> x1, waiting for transfers between devices: 51.8 us -> 0.01 us  [copies_along(): lax.all_to_all(jnp.broadcast_to(array[None], (size, *array.shape)), axis,...]
    all_gather x2, waiting for transfers between devices: 81 us -> 30.5 us  [the longest x1 30.5 us: local(): zy = lax.all_gather(copies_along(mine[:, :quarter], 'y'), 'z')]
    ppermute x0 -> x11, waiting for transfers between devices: none -> 25 us  [shifted(): lax.ppermute(array, axis, [(k, (k + step) % size) for k in range(size)])]
    all_to_all x1 -> x3, blocking collectives: 27.1 us -> 49.4 us  [the longest x1 27.2 us: local(): got = lax.all_to_all(sent, ROW, 0, 0, tiled=True)]
    pallas_call x0 -> x3, Pallas kernels: none -> 18.2 us  [the longest x1 9.31 us: last_product(): pl.pallas_call(last_kernel, out_shape=jax.ShapeDtypeStruct(white.shape, j...]
    all_gather x1, blocking collectives: 7.63 us -> 25.6 us  [local(): yz = copies_along(lax.all_gather(mine[:, quarter:], 'z'), 'y')]
    dot_general x3 -> x0, matrix products: 17.5 us -> none  [the longest x1 6.5 us: local(): jnp.einsum('akj,jq->qak', mixed_field, gathered, preferred_element_type=j...]
    ppermute x0 -> x11, starting transfers between devices: none -> 10.9 us  [shifted(): lax.ppermute(array, axis, [(k, (k + step) % size) for k in range(size)])]
  transfers between devices with their start and end apart: 4 -> 14, of which waited for: 4 -> 8; matrix products, arithmetic and copies ran while one was open for 6% -> 5% of each run, Pallas kernels for 0% -> 4%
where the time goes in v1:
time: 194 us; the launch traced here: 192 us
  blocking collectives  75 us (39%)
  waiting for transfers between devices  55.4 us (29%)
  Pallas kernels  18.2 us (9%)
  starting transfers between devices  15.3 us (8%)
  between operations  14.3 us (7%)
  local copies, waits for them, and re-layouts  7.32 us (4%)
  other arithmetic  6.74 us (3%)
    all_gather x1, waiting for transfers between devices, local(): zy = lax.all_gather(copies_along(mine[:, :quarter], 'y'), 'z')  30.5 us
    all_to_all x1, blocking collectives, local(): got = lax.all_to_all(sent, ROW, 0, 0, tiled=True)  27.2 us
    all_gather x1, blocking collectives, local(): yz = copies_along(lax.all_gather(mine[:, quarter:], 'z'), 'y')  25.6 us
    ppermute x11, waiting for transfers between devices, shifted(): lax.ppermute(array, axis, [(k, (k + step) % size) for k in range(size)])  25 us
    all_to_all x2, blocking collectives, copies_along(): lax.all_to_all(jnp.broadcast_to(array[None], (size, *array.shape)), axis,...  22.2 us
    ppermute x11, starting transfers between devices, shifted(): lax.ppermute(array, axis, [(k, (k + step) % size) for k in range(size)])  10.9 us
    pallas_call x1, Pallas kernels, last_product(): pl.pallas_call(last_kernel, out_shape=jax.ShapeDtypeStruct(white.shape, j...  9.31 us
    pallas_call x1, Pallas kernels, first_product(): pl.pallas_call(first_kernel, out_shape=jax.ShapeDtypeStruct((width, 8 * r...  7.12 us
  transfers between devices with their start and end apart: 14, of which 8 were waited for; matrix products, arithmetic and copies ran while one was open for 5% of the time, Pallas kernels for 4%

profile of v1, /device:TPU:32, one launch (start us, length us, event | category | flops | bytes accessed | tf_op | source)
XLA Modules:
  0.0 192.3 jit_solution(4423702927351171610)
XLA Ops:
  6.5 1.8 split_columns.1
  8.3 1.5 collective-permute-start.7
  9.8 4.0 %collective-permute-done.7 = bf16[2,64,512]{2,1,0:T(8,128)(2,1)S(1)} collective-permute-done((bf16[2,64,512]{2,1,0:T(8,128)(2,1)}, bf16[2,64,512]{2,1,0:T(8,128)(2,1)S(1)}, u32[]{:S(2)}, u32[]{:S(2)}) %collective-permute-start.7) | collective-permute-done | bytes 131104 | tf_op jit(solution)/shard_map/ppermute | solution.py:73
  13.8 1.0 maximum_select_fusion
  14.9 11.0 %all_to_all.20 = bf16[4,128,256]{2,1,0:T(8,128)(2,1)} all-to-all(bf16[4,128,256]{2,1,0:T(8,128)(2,1)S(1)} %broadcast_in_dim.61), channel_id=1, replica_groups=mesh['hi'=2,'core'=2,'y'=4,'z'=8,'lo'=2] {'y'}, dimensions={0} | all-to-all | bytes 524288 | tf_op jit(solution)/shard_map/all_to_all | solution.py:78
  26.0 11.2 %all_to_all.21 = bf16[4,128,512]{2,1,0:T(8,128)(2,1)} all-to-all(bf16[4,128,512]{2,1,0:T(8,128)(2,1)S(1)} %broadcast_in_dim.60), channel_id=1, replica_groups=mesh['hi'=2,'core'=2,'y'=4,'z'=8,'lo'=2] {'y'}, dimensions={0} | all-to-all | bytes 1048576 | tf_op jit(solution)/shard_map/all_to_all | solution.py:78
  37.2 30.5 %all-gather.6.cloned.1.call-done = bf16[32,128,256]{2,1,0:T(8,128)(2,1)} async-done(((bf16[4,128,256]{2,1,0:T(8,128)(2,1)}), bf16[32,128,256]{2,1,0:T(8,128)(2,1)}) %all-gather.6.cloned.1.call-update) | async-done | bytes 2097168 | tf_op jit(solution)/shard_map/all_gather | solution.py:243
  67.7 25.6 %all-gather.1 = bf16[1024,256]{1,0:T(8,128)(2,1)S(1)} all-gather(bf16[128,256]{1,0:T(8,128)(2,1)S(1)} %get-tuple-element.11), channel_id=3, replica_groups=mesh['hi'=2,'core'=2,'y'=4,'z'=8,'lo'=2] {'z'}, dimensions={0}, use_global_device_ids=true | all-gather | bytes 589824 | tf_op jit(solution)/shard_map/all_gather | solution.py:242
  93.3 1.6 broadcast_in_dim.62
  94.9 4.4 %all-to-all-start.2 = ((bf16[4,8,128,256]{3,2,1,0:T(8,128)(2,1)}), bf16[4,8,128,256]{3,2,1,0:T(8,128)(2,1)S(1)}, u32[]{:S(2)}, u32[]{:S(2)}) async-start(bf16[4,8,128,256]{3,2,1,0:T(8,128)(2,1)} %broadcast_in_dim.62), calls=%async_computation.2 | async-start | bytes 4194304 | tf_op jit(solution)/shard_map/all_to_all | solution.py:78
  99.3 4.3 %fusion.8.a0 = bf16[64,4096]{1,0:T(8,128)(2,1)S(1)} fusion(s32[1,64,4096]{2,1,0:T(8,128)} %param.8, f32[1,64,4096]{2,1,0:T(8,128)} %param.10, f32[1,64,4096]{2,1,0:T(8,128)} %param.9), kind=kLoop, calls=%fused_computation.16 | loop fusion | flops 17563648 | bytes 3670016 | tf_op jit(solution)/shard_map/squeeze | solution.py:248
  103.6 3.1 %collective-permute-start.1 = (bf16[64,4096]{1,0:T(8,128)(2,1)S(1)}, bf16[64,4096]{1,0:T(8,128)(2,1)S(1)}, u32[]{:S(2)}, u32[]{:S(2)}) collective-permute-start(bf16[64,4096]{1,0:T(8,128)(2,1)S(1)} %fusion.8.a0), channel_id=1, source_target_pairs={{0,128},{1,129},{128,0},{129,1},{2,130},{3,131},{130,2},{131,3},{4... | collective-permute-start | bytes 1572872 | tf_op jit(solution)/shard_map/ppermute | solution.py:73
  106.7 0.6 collective-permute-start.3
  107.3 2.7 %collective-permute-start.5 = (bf16[64,4096]{1,0:T(8,128)(2,1)S(1)}, bf16[64,4096]{1,0:T(8,128)(2,1)}, u32[]{:S(2)}, u32[]{:S(2)}) collective-permute-start(bf16[64,4096]{1,0:T(8,128)(2,1)S(1)} %fusion.8.a0), channel_id=1, source_target_pairs={{0,129},{1,0},{128,1},{129,128},{2,131},{3,2},{130,3},{131,130},{4... | collective-permute-start | bytes 1572872 | tf_op jit(solution)/shard_map/ppermute | solution.py:73
  110.8 0.6 gather_fusion
  111.4 3.1 %collective-permute-done.1.a2 = bf16[64,4096]{1,0:T(8,128)(2,1)S(1)} collective-permute-done((bf16[64,4096]{1,0:T(8,128)(2,1)S(1)}, bf16[64,4096]{1,0:T(8,128)(2,1)S(1)}, u32[]{:S(2)}, u32[]{:S(2)}) %collective-permute-start.1) | collective-permute-done | bytes 524320 | tf_op jit(solution)/shard_map/ppermute | solution.py:73
  114.5 5.6 %collective-permute-done.3.b0 = bf16[64,4096]{1,0:T(8,128)(2,1)} collective-permute-done((bf16[64,4096]{1,0:T(8,128)(2,1)S(1)}, bf16[64,4096]{1,0:T(8,128)(2,1)}, u32[]{:S(2)}, u32[]{:S(2)}) %collective-permute-start.3) | collective-permute-done | bytes 524320 | tf_op jit(solution)/shard_map/ppermute | solution.py:73
  120.2 0.5 collective-permute-start.6
  120.6 0.6 pad_add_fusion.place_ref
  121.2 0.7 broadcast_select_fusion.2.mix_ref
  121.9 0.5 collective-permute-done.4.b1
  122.7 0.8 copy-done.8
  123.6 1.4 copy-done
  125.0 7.1 %first_product.1 = bf16[512,512]{1,0:T(8,128)(2,1)} custom-call(f32[8,4]{1,0:T(8,128)} %broadcast_select_fusion.2.mix_ref, s32[2]{0:T(128)} %pad_add_fusion.place_ref, bf16[64,4096]{1,0:T(8,128)(2,1)} %copy-done.1, bf16[64,4096]{1,0:T(8,128)(2,1)} %collective-permute-done.a1, bf16[64,4096]{1,0:T(8,128)(2,1)} %copy-done.3, bf16[64,4096]{1,0:T(8,128)(2,1)} %copy-done.7, ...), custom_call_target="tpu_custom_call" | custom-call | flops 2147483648 | bytes 8388608 | tf_op jit(solution)/shard_map/first_product/pallas_call | solution.py:144
  132.1 27.2 %all_to_all.22 = bf16[64,8,512]{2,1,0:T(8,128)(2,1)S(1)} all-to-all(bf16[64,8,512]{2,1,0:T(8,128)(2,1)} %bitcast.44), channel_id=1, replica_groups=mesh['hi'=2,'core'=2,'y'=4,'z'=8,'lo'=2] {'y','z','lo'}, dimensions={0} | all-to-all | bytes 1048576 | tf_op jit(solution)/shard_map/all_to_all | solution.py:264
  159.4 2.5 %collective-permute-start.9 = (bf16[4,16,4096]{2,1,0:T(8,128)(2,1)S(1)}, bf16[4,16,4096]{2,1,0:T(8,128)(2,1)S(1)}, u32[]{:S(2)}, u32[]{:S(2)}) collective-permute-start(bf16[4,16,4096]{2,1,0:T(8,128)(2,1)S(1)} %bitcast.41), channel_id=1, source_target_pairs={{0,128},{128,0},{1,129},{129,1},{2,130},{130,2},{3,131},{131,3},{4... | collective-permute-start | bytes 1572872 | tf_op jit(solution)/shard_map/ppermute | solution.py:73
  162.1 11.2 %collective-permute-done.9.t2 = bf16[4,16,4096]{2,1,0:T(8,128)(2,1)S(1)} collective-permute-done((bf16[4,16,4096]{2,1,0:T(8,128)(2,1)S(1)}, bf16[4,16,4096]{2,1,0:T(8,128)(2,1)S(1)}, u32[]{:S(2)}, u32[]{:S(2)}) %collective-permute-start.9) | collective-permute-done | bytes 524320 | tf_op jit(solution)/shard_map/ppermute | solution.py:73
  173.4 0.6 gather_fusion.1
  174.1 0.6 dynamic_slice.6
  174.7 0.6 collective-permute-done.10.t3
  175.3 0.8 broadcast_in_dim.67.sy_ref
  176.1 9.3 %last_product.1 = f32[64,4,1024]{2,1,0:T(4,128)} custom-call(s32[2]{0:T(128)} %pad_add_fusion.place_ref, bf16[4,16,4096]{2,1,0:T(8,128)(2,1)} %bitcast.43, bf16[4,16,4096]{2,1,0:T(8,128)(2,1)} %copy-done.5, bf16[4,16,4096]{2,1,0:T(8,128)(2,1)} %copy-done.4, bf16[4,16,4096]{2,1,0:T(8,128)(2,1)} %copy-done.6, bf16[8,4,128,256]{3,2,1,0:T(8,128)(2,1)} %bitcast.39, ...), custom_call_target="tpu_custom_call" | custom-call | flops 2147483648 | bytes 12582912 | tf_op jit(solution)/shard_map/last_product/pallas_call | solution.py:214
  (56 shorter events, 1.4 us)
Async XLA Ops:
  6.5 61.1 %all-gather.6.cloned.1.call-start = ((), (), s32[]{:S(2)}) async-start(), calls=%async_computation.4 | async-start | bytes 2359296 | tf_op jit(solution)/shard_map/all_gather | solution.py:243
  8.3 5.4 %collective-permute-start.7 = (bf16[2,64,512]{2,1,0:T(8,128)(2,1)}, bf16[2,64,512]{2,1,0:T(8,128)(2,1)S(1)}, u32[]{:S(2)}, u32[]{:S(2)}) collective-permute-start(bf16[2,64,512]{2,1,0:T(8,128)(2,1)} %split_columns.1), channel_id=1, source_target_pairs={{0,1},{1,0},{2,3},{3,2},{4,5},{5,4},{6,7},{7,6},{8,9},{9,8},{10,11... | collective-permute-start | bytes 393224 | tf_op jit(solution)/shard_map/ppermute | solution.py:73
  25.9 149.3 %all-gather.8.cloned.1.call-start = ((), (), s32[]{:S(2)}) async-start(), calls=%async_computation.5 | async-start | bytes 4718592 | tf_op jit(solution)/shard_map/all_gather | solution.py:246
  94.9 28.6 %all-to-all-start.2 = ((bf16[4,8,128,256]{3,2,1,0:T(8,128)(2,1)}), bf16[4,8,128,256]{3,2,1,0:T(8,128)(2,1)S(1)}, u32[]{:S(2)}, u32[]{:S(2)}) async-start(bf16[4,8,128,256]{3,2,1,0:T(8,128)(2,1)} %broadcast_in_dim.62), calls=%async_computation.2 | async-start | bytes 4194304 | tf_op jit(solution)/shard_map/all_to_all | solution.py:78
  103.6 20.0 %copy-start.1 = (bf16[64,4096]{1,0:T(8,128)(2,1)}, bf16[64,4096]{1,0:T(8,128)(2,1)S(1)}, u32[]{:S(2)}) copy-start(bf16[64,4096]{1,0:T(8,128)(2,1)S(1)} %fusion.8.a0) | copy-start | bytes 1572868
  103.6 10.9 %collective-permute-start.1 = (bf16[64,4096]{1,0:T(8,128)(2,1)S(1)}, bf16[64,4096]{1,0:T(8,128)(2,1)S(1)}, u32[]{:S(2)}, u32[]{:S(2)}) collective-permute-start(bf16[64,4096]{1,0:T(8,128)(2,1)S(1)} %fusion.8.a0), channel_id=1, source_target_pairs={{0,128},{1,129},{128,0},{129,1},{2,130},{3,131},{130,2},{131,3},{4... | collective-permute-start | bytes 1572872 | tf_op jit(solution)/shard_map/ppermute | solution.py:73
  106.7 13.4 %collective-permute-start.3 = (bf16[64,4096]{1,0:T(8,128)(2,1)S(1)}, bf16[64,4096]{1,0:T(8,128)(2,1)}, u32[]{:S(2)}, u32[]{:S(2)}) collective-permute-start(bf16[64,4096]{1,0:T(8,128)(2,1)S(1)} %fusion.8.a0), channel_id=1, source_target_pairs={{0,1},{1,128},{128,129},{129,0},{2,3},{3,130},{130,131},{131,2},{4... | collective-permute-start | bytes 1572872 | tf_op jit(solution)/shard_map/ppermute | solution.py:73
  107.3 12.9 %collective-permute-start.5 = (bf16[64,4096]{1,0:T(8,128)(2,1)S(1)}, bf16[64,4096]{1,0:T(8,128)(2,1)}, u32[]{:S(2)}, u32[]{:S(2)}) collective-permute-start(bf16[64,4096]{1,0:T(8,128)(2,1)S(1)} %fusion.8.a0), channel_id=1, source_target_pairs={{0,129},{1,0},{128,1},{129,128},{2,131},{3,2},{130,3},{131,130},{4... | collective-permute-start | bytes 1572872 | tf_op jit(solution)/shard_map/ppermute | solution.py:73
  109.9 12.0 %collective-permute-start = (bf16[64,4096]{1,0:T(8,128)(2,1)S(1)}, bf16[64,4096]{1,0:T(8,128)(2,1)}, u32[]{:S(2)}, u32[]{:S(2)}) collective-permute-start(bf16[64,4096]{1,0:T(8,128)(2,1)S(1)} %fusion.8.a0), channel_id=1, source_target_pairs={{0,64},{64,0},{1,65},{65,1},{2,66},{66,2},{3,67},{67,3},{4,68},{68... | collective-permute-start | bytes 1572872 | tf_op jit(solution)/shard_map/ppermute | solution.py:73
  114.5 9.1 %copy-start.3 = (bf16[64,4096]{1,0:T(8,128)(2,1)}, bf16[64,4096]{1,0:T(8,128)(2,1)S(1)}, u32[]{:S(2)}) copy-start(bf16[64,4096]{1,0:T(8,128)(2,1)S(1)} %collective-permute-done.1.a2) | copy-start | bytes 1572868
  114.5 7.4 %collective-permute-start.2 = (bf16[64,4096]{1,0:T(8,128)(2,1)S(1)}, bf16[64,4096]{1,0:T(8,128)(2,1)S(1)}, u32[]{:S(2)}, u32[]{:S(2)}) collective-permute-start(bf16[64,4096]{1,0:T(8,128)(2,1)S(1)} %collective-permute-done.1.a2), channel_id=1, source_target_pairs={{0,64},{64,0},{1,65},{65,1},{2,66},{66,2},{3,67},{67,3},{4,68},{68... | collective-permute-start | bytes 1572872 | tf_op jit(solution)/shard_map/ppermute | solution.py:73
  120.1 2.3 %collective-permute-start.4 = (bf16[64,4096]{1,0:T(8,128)(2,1)}, bf16[64,4096]{1,0:T(8,128)(2,1)S(1)}, u32[]{:S(2)}, u32[]{:S(2)}) collective-permute-start(bf16[64,4096]{1,0:T(8,128)(2,1)} %collective-permute-done.3.b0), channel_id=1, source_target_pairs={{0,64},{64,0},{1,65},{65,1},{2,66},{66,2},{3,67},{67,3},{4,68},{68... | collective-permute-start | bytes 1572872 | tf_op jit(solution)/shard_map/ppermute | solution.py:73
  120.2 3.4 %collective-permute-start.6 = (bf16[64,4096]{1,0:T(8,128)(2,1)}, bf16[64,4096]{1,0:T(8,128)(2,1)}, u32[]{:S(2)}, u32[]{:S(2)}) collective-permute-start(bf16[64,4096]{1,0:T(8,128)(2,1)} %collective-permute-done.5.b2), channel_id=1, source_target_pairs={{0,64},{64,0},{1,65},{65,1},{2,66},{66,2},{3,67},{67,3},{4,68},{68... | collective-permute-start | bytes 1572872 | tf_op jit(solution)/shard_map/ppermute | solution.py:73
  121.9 0.8 copy-start.7
  122.7 0.8 copy-start.8
  123.6 1.4 copy-start
  132.1 29.8 %copy-start.9 = (f32[4096]{0:T(1024)S(1)}, f32[4096]{0:T(1024)}, u32[]{:S(2)}) copy-start(f32[4096]{0:T(1024)} %param.12) | copy-start | bytes 49156
  159.3 16.7 %copy-start.2 = (bf16[4,2,8,32,128]{4,2,3,1,0:T(8,128)(2,1)}, bf16[4,2,8,32,128]{4,2,3,1,0:T(8,128)(2,1)S(1)}, u32[]{:S(2)}) copy-start(bf16[4,2,8,32,128]{4,2,3,1,0:T(8,128)(2,1)S(1)} %copy.15) | copy-start | bytes 1572868
  159.4 14.0 %collective-permute-start.9 = (bf16[4,16,4096]{2,1,0:T(8,128)(2,1)S(1)}, bf16[4,16,4096]{2,1,0:T(8,128)(2,1)S(1)}, u32[]{:S(2)}, u32[]{:S(2)}) collective-permute-start(bf16[4,16,4096]{2,1,0:T(8,128)(2,1)S(1)} %bitcast.41), channel_id=1, source_target_pairs={{0,128},{128,0},{1,129},{129,1},{2,130},{130,2},{3,131},{131,3},{4... | collective-permute-start | bytes 1572872 | tf_op jit(solution)/shard_map/ppermute | solution.py:73
  162.0 12.7 %collective-permute-start.8 = (bf16[4,16,4096]{2,1,0:T(8,128)(2,1)S(1)}, bf16[4,16,4096]{2,1,0:T(8,128)(2,1)S(1)}, u32[]{:S(2)}, u32[]{:S(2)}) collective-permute-start(bf16[4,16,4096]{2,1,0:T(8,128)(2,1)S(1)} %bitcast.42), channel_id=1, source_target_pairs={{0,64},{64,0},{1,65},{65,1},{2,66},{66,2},{3,67},{67,3},{4,68},{68... | collective-permute-start | bytes 1572872 | tf_op jit(solution)/shard_map/ppermute | solution.py:73
  173.4 2.7 %copy-start.4 = (bf16[4,16,4096]{2,1,0:T(8,128)(2,1)}, bf16[4,16,4096]{2,1,0:T(8,128)(2,1)S(1)}, u32[]{:S(2)}) copy-start(bf16[4,16,4096]{2,1,0:T(8,128)(2,1)S(1)} %collective-permute-done.9.t2) | copy-start | bytes 1572868
  173.4 1.9 collective-permute-start.10
  174.7 1.4 copy-start.5
  175.3 0.8 copy-start.6
Sparse Core Ops, SparseCore 0:
  26.1 41.5 all-gather.5
  69.5 53.3 all-gather.7

commit v2 on v1

--- a/solution.py
+++ b/solution.py
@@ -73,36 +73,40 @@
     return lax.ppermute(array, axis, [(k, (k + step) % size) for k in range(size)])
 
 
-def copies_along(array, axis):
-    size = lax.axis_size(axis)
-    return lax.all_to_all(
-        jnp.broadcast_to(array[None], (size, *array.shape)), axis, 0, 0, tiled=True
-    )
-
-
-def split_kernel(basis_ref, halves_ref):
+def split_kernel(first_ref, basis_ref, halves_ref):
     source = lax.broadcasted_iota(jnp.int32, (256, 128), 0)
     target = lax.broadcasted_iota(jnp.int32, (256, 128), 1)
-    for half in range(2):
-        chosen = (source == (target // 8) * 16 + half * 8 + target % 8).astype(jnp.bfloat16)
+    for place in range(2):
+        half = first_ref[0] if place == 0 else 1 - first_ref[0]
+        match = source == (target // 8) * 16 + half * 8 + lax.rem(target, 8)
+        chosen = match.astype(jnp.float32).astype(jnp.bfloat16)
         for block in range(basis_ref.shape[1] // 256):
             moved = jnp.dot(
                 basis_ref[:, block * 256 : block * 256 + 256],
                 chosen,
                 preferred_element_type=jnp.float32,
-            )
-            halves_ref[half, :, block * 128 : block * 128 + 128] = moved.astype(jnp.bfloat16)
-
-
-def split_columns(basis):
+            ).astype(jnp.bfloat16)
+            for copy in range(halves_ref.shape[0]):
+                halves_ref[copy, place, :, block * 128 : block * 128 + 128] = moved
+
+
+def split_columns(first, basis, copies):
     rows, columns = basis.shape
     return pl.pallas_call(
         split_kernel,
-        out_shape=jax.ShapeDtypeStruct((2, rows, columns // 2), basis.dtype),
-        in_specs=[VMEM],
+        out_shape=jax.ShapeDtypeStruct((copies, 2, rows, columns // 2), basis.dtype),
+        in_specs=[SMEM, VMEM],
         out_specs=VMEM,
         name="split_columns",
-    )(basis)
+    )(first, basis)
+
+
+def depth_of(ref, y):
+    if len(ref.shape) == 4:
+        pieces = [ref[z, y] for z in range(ref.shape[0])]
+    else:
+        pieces = [ref[y, lo, z] for z in range(ref.shape[2]) for lo in range(2)]
+    return jnp.concatenate(pieces, axis=0)
 
 
 def first_kernel(
@@ -110,16 +114,14 @@
 ):
     blocks = (a0, a1, a2, a3, b0, b1, b2, b3)
     rows = a0.shape[0]
-    ny, nz = yz_ref.shape[:2]
+    ny, nz = yz_ref.shape[0], yz_ref.shape[2]
     depth = a0.shape[1] // ny
     half = zy_ref.shape[-1]
     for y in range(ny):
         field = jnp.concatenate([ref[:, y * depth : (y + 1) * depth] for ref in blocks], axis=0)
         for part in range(2):
-            pieces = [zy_ref[z, y] if part == 0 else yz_ref[y, z] for z in range(nz)]
-            product = jnp.dot(
-                field, jnp.concatenate(pieces, axis=0), preferred_element_type=jnp.float32
-            )
+            basis = depth_of((zy_ref, yz_ref)[part], y)
+            product = jnp.dot(field, basis, preferred_element_type=jnp.float32)
             span = slice(part * half, part * half + half)
             if y == 0:
                 acc_ref[:, span] = product
@@ -158,25 +160,20 @@
 
 
 def last_kernel(
-    place_ref, t0, t1, t2, t3, zy_ref, yz_ref, rest_ref, sx_ref, sy_ref, white_ref, out_ref, acc_ref
+    place_ref, t0, t1, t2, t3, zy0, yz0, zy1, yz1, sx_ref, sy_ref, white_ref, out_ref, acc_ref
 ):
     fields = (t0, t1, t2, t3)
-    ny, nz = yz_ref.shape[:2]
+    ny, nz = yz0.shape[0], yz0.shape[2]
     times, rows, total = t0.shape
     depth = total // ny
-    half = zy_ref.shape[-1]
+    half = zy0.shape[-1]
     for y in range(ny):
         field = jnp.concatenate(
             [ref[a, :, y * depth : (y + 1) * depth] for a in range(times) for ref in fields], axis=0
         )
-        for part in range(3):
-            pieces = [
-                (zy_ref[z, y], yz_ref[y, z], rest_ref[z, y])[part] for z in range(nz)
-            ]
-            product = jnp.dot(
-                field, jnp.concatenate(pieces, axis=0), preferred_element_type=jnp.float32
-            )
-            span = slice(part * half, part * half + product.shape[-1])
+        for part, ref in enumerate((zy0, yz0, zy1, yz1)):
+            product = jnp.dot(field, depth_of(ref, y), preferred_element_type=jnp.float32)
+            span = slice(part * half, part * half + half)
             if y == 0:
                 acc_ref[:, span] = product
             else:
@@ -208,20 +205,20 @@
                 )
 
 
-def last_product(place, fields, zy, yz, rest, sx, sy, white):
+def last_product(place, fields, basis, sx, sy, white):
     times, rows, total = fields[0].shape
     width = white.shape[-1]
     return pl.pallas_call(
         last_kernel,
         out_shape=jax.ShapeDtypeStruct(white.shape, jnp.float32),
-        in_specs=[SMEM] + [VMEM] * 10,
+        in_specs=[SMEM] + [VMEM] * 11,
         out_specs=VMEM,
         scratch_shapes=[pltpu.VMEM((4 * times * rows, width), jnp.float32)],
         cost_estimate=pl.CostEstimate(
             flops=2 * 4 * times * rows * total * width, bytes_accessed=12 << 20, transcendentals=0
         ),
         name="last_product",
-    )(place, *fields, zy, yz, rest, sx, sy, white)
+    )(place, *fields, *basis, sx, sy, white)
 
 
 def local(event_counts, latent_mean, latent_var, eigen_basis, spectrum, correlation, whitened):
@@ -230,23 +227,25 @@
     time = hi * 2 + core
     ny, nz = lax.axis_size("y"), lax.axis_size("z")
 
-    halves = split_columns(eigen_basis)
-    other = shifted(halves, "lo", 1)
-    stacked = jnp.where(lo == 0, jnp.stack([halves, other]), jnp.stack([other, halves]))
-    mine = jnp.where(lo == 0, stacked[:, 0], stacked[:, 1])
-    rest = jnp.where(lo == 0, stacked[:, 1], stacked[:, 0])
-    mine = mine.reshape(-1, mine.shape[-1])
-    rest = rest.reshape(-1, rest.shape[-1])
-    quarter = mine.shape[-1] // 2
-
-    yz = copies_along(lax.all_gather(mine[:, quarter:], "z"), "y")
-    zy = lax.all_gather(copies_along(mine[:, :quarter], "y"), "z")
-    rest_y = copies_along(rest, "y")
-    rest_y, zy = lax.optimization_barrier((rest_y, zy))
-    rest = lax.all_gather(rest_y, "z")
-
+    rows, columns = eigen_basis.shape
+    part = columns // 4
+    raw = lax.all_gather(eigen_basis, "z").reshape(nz * rows, columns)
+    left = jnp.broadcast_to(eigen_basis[None, :, : 2 * part], (2 * ny, rows, 2 * part))
+    left = lax.all_to_all(left, ("y", "lo"), 0, 0, tiled=True).reshape(-1, 2 * part)
     pseudo = moments(event_counts, latent_mean, latent_var).astype(jnp.bfloat16)[0]
+    left, pseudo = lax.optimization_barrier((left, pseudo))
+    first = lo[None].astype(jnp.int32)
+    left = split_columns(first, left, 1).reshape(2, ny, 2 * rows, part)
+    left, raw = lax.optimization_barrier((left, raw))
+    right = split_columns(jnp.zeros((1,), jnp.int32), raw[:, 2 * part :], ny)
+    yz = lax.all_to_all(right.reshape(2 * ny, nz * rows, part), ("y", "lo"), 0, 0, tiled=True)
+    yz = yz.reshape(ny, 2, nz, rows, part)
+    zy = lax.all_gather(left[0], "z")
     around = [pseudo] + [shifted(pseudo, RING, step) for step in (2, 1, 3)]
+    left_rest, zy, around = lax.optimization_barrier((left[1], zy, around))
+    zy_rest = lax.all_gather(left_rest, "z")
+    yz_rest = shifted(yz, "lo", 1)
+
     own, far, before, after = [(block, shifted(block, "core", 1)) for block in around]
     fields = (*own, *far, *before, *after)
     flips = jnp.array([0, 1, 2, 3], jnp.int32)
@@ -274,7 +273,7 @@
     sy = jnp.take(by_row, lax.bitwise_xor(time, flips), axis=0).reshape(-1, 1)
     sy = jnp.broadcast_to(sy, (sy.shape[0], 128))
     white = whitened.reshape(-1, *whitened.shape[3:])
-    gradient = last_product(place, bands, zy, yz, rest, sx, sy, white)
+    gradient = last_product(place, bands, (zy, yz, zy_rest, yz_rest), sx, sy, white)
     return gradient.reshape(whitened.shape)
 
 

time: 194 us -> 201 us (1.036)
  blocking collectives: 75 us -> 0 us
  waiting for transfers between devices: 55.4 us -> 118 us
  starting transfers between devices: 15.3 us -> 29 us
  Pallas kernels: 18.2 us -> 21.5 us
  local copies, waits for them, and re-layouts: 7.32 us -> 10.5 us
    all_to_all x3 -> x0, blocking collectives: 49.4 us -> none  [the longest x1 27.2 us: local(): got = lax.all_to_all(sent, ROW, 0, 0, tiled=True)]
    all_to_all x1 -> x3, waiting for transfers between devices: 0.01 us -> 29.7 us  [the longest x1 21.3 us: local(): got = lax.all_to_all(sent, ROW, 0, 0, tiled=True)]
    ppermute x11, waiting for transfers between devices: 25 us -> 52.7 us  [shifted(): lax.ppermute(array, axis, [(k, (k + step) % size) for k in range(size)])]
    all_gather x1 -> x0, blocking collectives: 25.6 us -> none  [local(): yz = copies_along(lax.all_gather(mine[:, quarter:], 'z'), 'y')]
    all_to_all x1 -> x3, starting transfers between devices: 4.36 us -> 17.1 us  [the longest x1 7.42 us: local(): got = lax.all_to_all(sent, ROW, 0, 0, tiled=True)]
    slice x1 -> x3, local copies, waits for them, and re-layouts: 0.01 us -> 4.58 us  [the longest x1 1.87 us: local(): zy = lax.all_gather(left[0], 'z')]
    all_gather x2 -> x3, waiting for transfers between devices: 30.5 us -> 34.6 us  [the longest x1 22.3 us: local(): raw = lax.all_gather(eigen_basis, 'z').reshape(nz * rows, columns)]
    pallas_call x1 -> x2, Pallas kernels: 1.78 us -> 5.13 us  [split_columns(): pl.pallas_call(split_kernel, out_shape=jax.ShapeDtypeStruct((copies, 2, r...]
  transfers between devices with their start and end apart: 14 -> 17, of which waited for: 8 -> 10; matrix products, arithmetic and copies ran while one was open for 5% -> 6% of each run, Pallas kernels for 4% -> 6%
where the time goes in v2:
time: 201 us; the launch traced here: 198 us
  waiting for transfers between devices  118 us (59%)
  starting transfers between devices  29 us (14%)
  Pallas kernels  21.5 us (11%)
  between operations  14 us (7%)
  local copies, waits for them, and re-layouts  10.5 us (5%)
  other arithmetic  5.59 us (3%)
    ppermute x11, waiting for transfers between devices, shifted(): lax.ppermute(array, axis, [(k, (k + step) % size) for k in range(size)])  52.7 us
    all_gather x1, waiting for transfers between devices, local(): raw = lax.all_gather(eigen_basis, 'z').reshape(nz * rows, columns)  22.3 us
    all_to_all x1, waiting for transfers between devices, local(): got = lax.all_to_all(sent, ROW, 0, 0, tiled=True)  21.3 us
    all_gather x1, waiting for transfers between devices, local(): zy = lax.all_gather(left[0], 'z')  12.3 us
    ppermute x11, starting transfers between devices, shifted(): lax.ppermute(array, axis, [(k, (k + step) % size) for k in range(size)])  11.8 us
    pallas_call x1, Pallas kernels, last_product(): pl.pallas_call(last_kernel, out_shape=jax.ShapeDtypeStruct(white.shape, j...  9.33 us
    all_to_all x1, starting transfers between devices, local(): got = lax.all_to_all(sent, ROW, 0, 0, tiled=True)  7.42 us
    pallas_call x1, Pallas kernels, first_product(): pl.pallas_call(first_kernel, out_shape=jax.ShapeDtypeStruct((width, 8 * r...  7.07 us
  transfers between devices with their start and end apart: 17, of which 10 were waited for; matrix products, arithmetic and copies ran while one was open for 6% of the time, Pallas kernels for 6%

profile of v2, /device:TPU:32, one launch (start us, length us, event | category | flops | bytes accessed | tf_op | source)
XLA Modules:
  0.0 198.4 jit_solution(3841171939856334486)
XLA Ops:
  6.5 0.7 all-gather.8.cloned.1.call-update
  7.3 0.8 slice.12
  8.1 0.8 broadcast_in_dim.50
  8.9 5.4 %all-to-all-start = ((bf16[8,64,512]{2,1,0:T(8,128)(2,1)}), bf16[8,64,512]{2,1,0:T(8,128)(2,1)S(1)}, u32[]{:S(2)}, u32[]{:S(2)}) async-start(bf16[8,64,512]{2,1,0:T(8,128)(2,1)} %broadcast_in_dim.50), calls=%async_computation | async-start | bytes 1048576 | tf_op jit(solution)/shard_map/all_to_all | solution.py:234
  14.4 4.1 %fusion.8.a0 = bf16[64,4096]{1,0:T(8,128)(2,1)S(1)} fusion(s32[1,64,4096]{2,1,0:T(8,128)S(1)} %copy-done.5, f32[1,64,4096]{2,1,0:T(8,128)} %param.10, f32[1,64,4096]{2,1,0:T(8,128)} %param.9), kind=kLoop, calls=%fused_computation.16 | loop fusion | flops 17563648 | bytes 3670016 | tf_op jit(solution)/shard_map/squeeze | solution.py:235
  18.6 5.9 %all-to-all-done = bf16[8,64,512]{2,1,0:T(8,128)(2,1)S(1)} async-done(((bf16[8,64,512]{2,1,0:T(8,128)(2,1)}), bf16[8,64,512]{2,1,0:T(8,128)(2,1)S(1)}, u32[]{:S(2)}, u32[]{:S(2)}) %all-to-all-start) | async-done | bytes 524320 | tf_op jit(solution)/shard_map/all_to_all | solution.py:234
  24.4 0.8 copy-done.3
  25.2 2.3 %split_columns.2 = bf16[1,2,512,256]{3,2,1,0:T(8,128)(2,1)} custom-call(s32[1]{0:T(128)} %bitcast.first_ref, bf16[512,512]{1,0:T(8,128)(2,1)} %bitcast.46), custom_call_target="tpu_custom_call" | custom-call | tf_op jit(solution)/shard_map/split_columns/pallas_call | solution.py:95
  27.5 22.3 %all-gather.8.cloned.1.call-done = bf16[512,1024]{1,0:T(8,128)(2,1)} async-done(((bf16[64,1024]{1,0:T(8,128)(2,1)}), bf16[512,1024]{1,0:T(8,128)(2,1)}) %all-gather.8.cloned.1.call-update) | async-done | bytes 1048592 | tf_op jit(solution)/shard_map/all_gather | solution.py:232
  49.8 1.9 fusion.10
  51.7 3.1 %collective-permute-start = (bf16[64,4096]{1,0:T(8,128)(2,1)S(1)}, bf16[64,4096]{1,0:T(8,128)(2,1)S(1)}, u32[]{:S(2)}, u32[]{:S(2)}) collective-permute-start(bf16[64,4096]{1,0:T(8,128)(2,1)S(1)} %fusion.8.a0), channel_id=1, source_target_pairs={{0,128},{1,129},{128,0},{129,1},{2,130},{3,131},{130,2},{131,3},{4... | collective-permute-start | bytes 1572872 | tf_op jit(solution)/shard_map/ppermute | solution.py:73
  55.3 2.7 %collective-permute-start.2 = (bf16[64,4096]{1,0:T(8,128)(2,1)S(1)}, bf16[64,4096]{1,0:T(8,128)(2,1)}, u32[]{:S(2)}, u32[]{:S(2)}) collective-permute-start(bf16[64,4096]{1,0:T(8,128)(2,1)S(1)} %fusion.8.a0), channel_id=1, source_target_pairs={{0,129},{1,0},{128,1},{129,128},{2,131},{3,2},{130,3},{131,130},{4... | collective-permute-start | bytes 1572872 | tf_op jit(solution)/shard_map/ppermute | solution.py:73
  58.0 1.9 slice.15.basis_ref
  59.8 2.9 %split_columns.3 = bf16[4,2,512,256]{3,2,1,0:T(8,128)(2,1)} custom-call(s32[1]{0:T(128)} %constant.47.clone.1.first_ref, bf16[512,512]{1,0:T(8,128)(2,1)} %slice.15.basis_ref), custom_call_target="tpu_custom_call" | custom-call | tf_op jit(solution)/shard_map/split_columns/pallas_call | solution.py:95
  62.7 4.3 %all-to-all-start.1 = ((bf16[8,512,256]{2,1,0:T(8,128)(2,1)}), bf16[8,512,256]{2,1,0:T(8,128)(2,1)S(1)}, u32[]{:S(2)}, u32[]{:S(2)}) async-start(bf16[8,512,256]{2,1,0:T(8,128)(2,1)} %bitcast.41), calls=%async_computation.1 | async-start | bytes 4194304 | tf_op jit(solution)/shard_map/all_to_all | solution.py:241
  67.0 1.1 collective-permute-done.a2
  68.1 10.2 %collective-permute-done.1.b0 = bf16[64,4096]{1,0:T(8,128)(2,1)} collective-permute-done((bf16[64,4096]{1,0:T(8,128)(2,1)S(1)}, bf16[64,4096]{1,0:T(8,128)(2,1)}, u32[]{:S(2)}, u32[]{:S(2)}) %collective-permute-start.1) | collective-permute-done | bytes 524320 | tf_op jit(solution)/shard_map/ppermute | solution.py:73
  78.4 1.1 collective-permute-done.2.b2
  79.5 12.3 %all-gather.6.cloned.1.call-done.zy_ref.zy0 = bf16[8,4,128,256]{3,2,1,0:T(8,128)(2,1)} async-done(((bf16[1,4,128,256]{3,2,1,0:T(8,128)(2,1)}), bf16[8,4,128,256]{3,2,1,0:T(8,128)(2,1)}) %all-gather.6.cloned.1.call-update) | async-done | bytes 2097168 | tf_op jit(solution)/shard_map/all_gather | solution.py:243
  94.4 0.6 pad_add_fusion.place_ref
  95.1 0.7 broadcast_select_fusion.mix_ref
  95.7 2.5 %all-to-all-done.1 = bf16[8,512,256]{2,1,0:T(8,128)(2,1)S(1)} async-done(((bf16[8,512,256]{2,1,0:T(8,128)(2,1)}), bf16[8,512,256]{2,1,0:T(8,128)(2,1)S(1)}, u32[]{:S(2)}, u32[]{:S(2)}) %all-to-all-start.1) | async-done | bytes 2097184 | tf_op jit(solution)/shard_map/all_to_all | solution.py:241
  98.3 1.3 copy-done
  99.7 7.1 %first_product.1 = bf16[512,512]{1,0:T(8,128)(2,1)} custom-call(f32[8,4]{1,0:T(8,128)} %broadcast_select_fusion.mix_ref, s32[2]{0:T(128)} %pad_add_fusion.place_ref, bf16[64,4096]{1,0:T(8,128)(2,1)} %copy-done.1, bf16[64,4096]{1,0:T(8,128)(2,1)} %collective-permute-done.3.a1, bf16[64,4096]{1,0:T(8,128)(2,1)} %copy-done.6, ...), custom_call_target="tpu_custom_call" | custom-call | flops 2147483648 | bytes 8388608 | tf_op jit(solution)/shard_map/first_product/pallas_call | solution.py:146
  106.7 7.4 %all-to-all-start.2 = ((bf16[64,8,512]{2,1,0:T(8,128)(2,1)}), bf16[64,8,512]{2,1,0:T(8,128)(2,1)S(1)}, u32[]{:S(2)}, u32[]{:S(2)}) async-start(bf16[64,8,512]{2,1,0:T(8,128)(2,1)} %bitcast.45), calls=%async_computation.2 | async-start | bytes 1048576 | tf_op jit(solution)/shard_map/all_to_all | solution.py:263
  114.1 1.6 collective-permute-start.10
  115.7 21.3 %all-to-all-done.2 = bf16[64,8,512]{2,1,0:T(8,128)(2,1)S(1)} async-done(((bf16[64,8,512]{2,1,0:T(8,128)(2,1)}), bf16[64,8,512]{2,1,0:T(8,128)(2,1)S(1)}, u32[]{:S(2)}, u32[]{:S(2)}) %all-to-all-start.2) | async-done | bytes 524320 | tf_op jit(solution)/shard_map/all_to_all | solution.py:263
  137.1 2.7 %collective-permute-start.8 = (bf16[4,16,4096]{2,1,0:T(8,128)(2,1)S(1)}, bf16[4,16,4096]{2,1,0:T(8,128)(2,1)S(1)}, u32[]{:S(2)}, u32[]{:S(2)}) collective-permute-start(bf16[4,16,4096]{2,1,0:T(8,128)(2,1)S(1)} %bitcast.42), channel_id=1, source_target_pairs={{0,128},{128,0},{1,129},{129,1},{2,130},{130,2},{3,131},{131,3},{4... | collective-permute-start | bytes 1572872 | tf_op jit(solution)/shard_map/ppermute | solution.py:73
  140.2 39.6 %collective-permute-done.8.t2 = bf16[4,16,4096]{2,1,0:T(8,128)(2,1)S(1)} collective-permute-done((bf16[4,16,4096]{2,1,0:T(8,128)(2,1)S(1)}, bf16[4,16,4096]{2,1,0:T(8,128)(2,1)S(1)}, u32[]{:S(2)}, u32[]{:S(2)}) %collective-permute-start.8) | collective-permute-done | bytes 524320 | tf_op jit(solution)/shard_map/ppermute | solution.py:73
  181.1 0.7 collective-permute-done.9.t3
  181.8 0.7 broadcast_in_dim.55.sy_ref
  182.5 9.3 %last_product.1 = f32[64,4,1024]{2,1,0:T(4,128)} custom-call(s32[2]{0:T(128)} %pad_add_fusion.place_ref, bf16[4,16,4096]{2,1,0:T(8,128)(2,1)} %bitcast.44, bf16[4,16,4096]{2,1,0:T(8,128)(2,1)} %collective-permute-done.7.t1, bf16[4,16,4096]{2,1,0:T(8,128)(2,1)} %copy-done.7, bf16[4,16,4096]{2,1,0:T(8,128)(2,1)} %collective-permute-done.9.t3, ...), custom_call_target="tpu_custom_call" | custom-call | flops 2147483648 | bytes 12582912 | tf_op jit(solution)/shard_map/last_product/pallas_call | solution.py:211
  (56 shorter events, 4.4 us)
Async XLA Ops:
  6.5 7.8 %copy-start.5 = (s32[1,64,4096]{2,1,0:T(8,128)S(1)}, s32[1,64,4096]{2,1,0:T(8,128)}, u32[]{:S(2)}) copy-start(s32[1,64,4096]{2,1,0:T(8,128)} %param.8) | copy-start | bytes 3145732
  6.5 43.2 %all-gather.8.cloned.1.call-start = ((), (), s32[]{:S(2)}) async-start(), calls=%async_computation.4 | async-start | bytes 1179648 | tf_op jit(solution)/shard_map/all_gather | solution.py:232
  8.9 15.5 %all-to-all-start = ((bf16[8,64,512]{2,1,0:T(8,128)(2,1)}), bf16[8,64,512]{2,1,0:T(8,128)(2,1)S(1)}, u32[]{:S(2)}, u32[]{:S(2)}) async-start(bf16[8,64,512]{2,1,0:T(8,128)(2,1)} %broadcast_in_dim.50), calls=%async_computation | async-start | bytes 1048576 | tf_op jit(solution)/shard_map/all_to_all | solution.py:234
  14.3 77.5 %all-gather.6.cloned.1.call-start = ((), (), s32[]{:S(2)}) async-start(), calls=%async_computation.3 | async-start | bytes 2359296 | tf_op jit(solution)/shard_map/all_gather | solution.py:243
  18.5 74.8 %copy-start.1 = (bf16[64,4096]{1,0:T(8,128)(2,1)}, bf16[64,4096]{1,0:T(8,128)(2,1)S(1)}, u32[]{:S(2)}) copy-start(bf16[64,4096]{1,0:T(8,128)(2,1)S(1)} %fusion.8.a0) | copy-start | bytes 1572868
  24.4 0.8 copy-start.3
  51.7 16.5 %collective-permute-start = (bf16[64,4096]{1,0:T(8,128)(2,1)S(1)}, bf16[64,4096]{1,0:T(8,128)(2,1)S(1)}, u32[]{:S(2)}, u32[]{:S(2)}) collective-permute-start(bf16[64,4096]{1,0:T(8,128)(2,1)S(1)} %fusion.8.a0), channel_id=1, source_target_pairs={{0,128},{1,129},{128,0},{129,1},{2,130},{3,131},{130,2},{131,3},{4... | collective-permute-start | bytes 1572872 | tf_op jit(solution)/shard_map/ppermute | solution.py:73
  54.7 23.6 %collective-permute-start.1 = (bf16[64,4096]{1,0:T(8,128)(2,1)S(1)}, bf16[64,4096]{1,0:T(8,128)(2,1)}, u32[]{:S(2)}, u32[]{:S(2)}) collective-permute-start(bf16[64,4096]{1,0:T(8,128)(2,1)S(1)} %fusion.8.a0), channel_id=1, source_target_pairs={{0,1},{1,128},{128,129},{129,0},{2,3},{3,130},{130,131},{131,2},{4... | collective-permute-start | bytes 1572872 | tf_op jit(solution)/shard_map/ppermute | solution.py:73
  55.3 24.2 %collective-permute-start.2 = (bf16[64,4096]{1,0:T(8,128)(2,1)S(1)}, bf16[64,4096]{1,0:T(8,128)(2,1)}, u32[]{:S(2)}, u32[]{:S(2)}) collective-permute-start(bf16[64,4096]{1,0:T(8,128)(2,1)S(1)} %fusion.8.a0), channel_id=1, source_target_pairs={{0,129},{1,0},{128,1},{129,128},{2,131},{3,2},{130,3},{131,130},{4... | collective-permute-start | bytes 1572872 | tf_op jit(solution)/shard_map/ppermute | solution.py:73
  62.7 35.6 %all-to-all-start.1 = ((bf16[8,512,256]{2,1,0:T(8,128)(2,1)}), bf16[8,512,256]{2,1,0:T(8,128)(2,1)S(1)}, u32[]{:S(2)}, u32[]{:S(2)}) async-start(bf16[8,512,256]{2,1,0:T(8,128)(2,1)} %bitcast.41), calls=%async_computation.1 | async-start | bytes 4194304 | tf_op jit(solution)/shard_map/all_to_all | solution.py:241
  67.0 114.8 %all-gather.10.cloned.1.call-start = ((), (), s32[]{:S(2)}) async-start(), calls=%async_computation.5 | async-start | bytes 2359296 | tf_op jit(solution)/shard_map/all_gather | solution.py:246
  68.1 30.2 %copy-start.6 = (bf16[64,4096]{1,0:T(8,128)(2,1)}, bf16[64,4096]{1,0:T(8,128)(2,1)S(1)}, u32[]{:S(2)}) copy-start(bf16[64,4096]{1,0:T(8,128)(2,1)S(1)} %collective-permute-done.a2) | copy-start | bytes 1572868
  93.4 4.9 %collective-permute-start.3 = (bf16[64,4096]{1,0:T(8,128)(2,1)S(1)}, bf16[64,4096]{1,0:T(8,128)(2,1)}, u32[]{:S(2)}, u32[]{:S(2)}) collective-permute-start(bf16[64,4096]{1,0:T(8,128)(2,1)S(1)} %fusion.8.a0), channel_id=1, source_target_pairs={{0,64},{64,0},{1,65},{65,1},{2,66},{66,2},{3,67},{67,3},{4,68},{68... | collective-permute-start | bytes 1572872 | tf_op jit(solution)/shard_map/ppermute | solution.py:73
  93.4 4.9 %collective-permute-start.4 = (bf16[64,4096]{1,0:T(8,128)(2,1)S(1)}, bf16[64,4096]{1,0:T(8,128)(2,1)}, u32[]{:S(2)}, u32[]{:S(2)}) collective-permute-start(bf16[64,4096]{1,0:T(8,128)(2,1)S(1)} %collective-permute-done.a2), channel_id=1, source_target_pairs={{0,64},{64,0},{1,65},{65,1},{2,66},{66,2},{3,67},{67,3},{4,68},{68... | collective-permute-start | bytes 1572872 | tf_op jit(solution)/shard_map/ppermute | solution.py:73
  93.9 4.4 %collective-permute-start.5 = (bf16[64,4096]{1,0:T(8,128)(2,1)}, bf16[64,4096]{1,0:T(8,128)(2,1)}, u32[]{:S(2)}, u32[]{:S(2)}) collective-permute-start(bf16[64,4096]{1,0:T(8,128)(2,1)} %collective-permute-done.1.b0), channel_id=1, source_target_pairs={{0,64},{64,0},{1,65},{65,1},{2,66},{66,2},{3,67},{67,3},{4,68},{68... | collective-permute-start | bytes 1572872 | tf_op jit(solution)/shard_map/ppermute | solution.py:73
  94.0 4.3 %collective-permute-start.6 = (bf16[64,4096]{1,0:T(8,128)(2,1)}, bf16[64,4096]{1,0:T(8,128)(2,1)}, u32[]{:S(2)}, u32[]{:S(2)}) collective-permute-start(bf16[64,4096]{1,0:T(8,128)(2,1)} %collective-permute-done.2.b2), channel_id=1, source_target_pairs={{0,64},{64,0},{1,65},{65,1},{2,66},{66,2},{3,67},{67,3},{4,68},{68... | collective-permute-start | bytes 1572872 | tf_op jit(solution)/shard_map/ppermute | solution.py:73
  98.3 1.4 copy-start
  106.7 33.0 %copy-start.8 = (f32[4096]{0:T(1024)S(1)}, f32[4096]{0:T(1024)}, u32[]{:S(2)}) copy-start(f32[4096]{0:T(1024)} %param.12) | copy-start | bytes 49156
  106.7 30.2 %all-to-all-start.2 = ((bf16[64,8,512]{2,1,0:T(8,128)(2,1)}), bf16[64,8,512]{2,1,0:T(8,128)(2,1)S(1)}, u32[]{:S(2)}, u32[]{:S(2)}) async-start(bf16[64,8,512]{2,1,0:T(8,128)(2,1)} %bitcast.45), calls=%async_computation.2 | async-start | bytes 1048576 | tf_op jit(solution)/shard_map/all_to_all | solution.py:263
  114.1 67.0 %collective-permute-start.10 = (bf16[4,2,8,64,256]{4,3,2,1,0:T(8,128)(2,1)}, bf16[4,2,8,64,256]{4,3,2,1,0:T(8,128)(2,1)S(1)}, u32[]{:S(2)}, u32[]{:S(2)}) collective-permute-start(bf16[4,2,8,64,256]{4,3,2,1,0:T(8,128)(2,1)} %bitcast.39), channel_id=1, source_target_pairs={{0,1},{1,0},{2,3},{3,2},{4,5},{5,4},{6,7},{7,6},{8,9},{9,8},{10,11... | collective-permute-start | bytes 6291464 | tf_op jit(solution)/shard_map/ppermute | solution.py:73
  137.1 45.4 %copy-start.2 = (bf16[4,2,8,32,128]{4,2,3,1,0:T(8,128)(2,1)}, bf16[4,2,8,32,128]{4,2,3,1,0:T(8,128)(2,1)S(1)}, u32[]{:S(2)}) copy-start(bf16[4,2,8,32,128]{4,2,3,1,0:T(8,128)(2,1)S(1)} %copy.15) | copy-start | bytes 1572868
  137.1 42.7 %collective-permute-start.8 = (bf16[4,16,4096]{2,1,0:T(8,128)(2,1)S(1)}, bf16[4,16,4096]{2,1,0:T(8,128)(2,1)S(1)}, u32[]{:S(2)}, u32[]{:S(2)}) collective-permute-start(bf16[4,16,4096]{2,1,0:T(8,128)(2,1)S(1)} %bitcast.42), channel_id=1, source_target_pairs={{0,128},{128,0},{1,129},{129,1},{2,130},{130,2},{3,131},{131,3},{4... | collective-permute-start | bytes 1572872 | tf_op jit(solution)/shard_map/ppermute | solution.py:73
  139.9 41.2 %collective-permute-start.7 = (bf16[4,16,4096]{2,1,0:T(8,128)(2,1)S(1)}, bf16[4,16,4096]{2,1,0:T(8,128)(2,1)}, u32[]{:S(2)}, u32[]{:S(2)}) collective-permute-start(bf16[4,16,4096]{2,1,0:T(8,128)(2,1)S(1)} %bitcast.43), channel_id=1, source_target_pairs={{0,64},{64,0},{1,65},{65,1},{2,66},{66,2},{3,67},{67,3},{4,68},{68... | collective-permute-start | bytes 1572872 | tf_op jit(solution)/shard_map/ppermute | solution.py:73
  179.8 2.7 %copy-start.7 = (bf16[4,16,4096]{2,1,0:T(8,128)(2,1)}, bf16[4,16,4096]{2,1,0:T(8,128)(2,1)S(1)}, u32[]{:S(2)}) copy-start(bf16[4,16,4096]{2,1,0:T(8,128)(2,1)S(1)} %collective-permute-done.8.t2) | copy-start | bytes 1572868
  179.8 2.0 %collective-permute-start.9 = (bf16[4,16,4096]{2,1,0:T(8,128)(2,1)S(1)}, bf16[4,16,4096]{2,1,0:T(8,128)(2,1)}, u32[]{:S(2)}, u32[]{:S(2)}) collective-permute-start(bf16[4,16,4096]{2,1,0:T(8,128)(2,1)S(1)} %collective-permute-done.8.t2), channel_id=1, source_target_pairs={{0,64},{64,0},{1,65},{65,1},{2,66},{66,2},{3,67},{67,3},{4,68},{68... | collective-permute-start | bytes 1572872 | tf_op jit(solution)/shard_map/ppermute | solution.py:73
  181.1 1.4 copy-start.4
Sparse Core Ops, SparseCore 0:
  9.1 40.5 all-gather.7
  51.8 39.9 all-gather.5
  93.6 48.9 all-gather.9

commit v3 on v1

v3 whole, which is shorter than its diff:
```python
import math

import jax
import jax.numpy as jnp
from jax import lax
from jax.experimental import pallas as pl
from jax.experimental.pallas import tpu as pltpu
from jax.sharding import Mesh
from jax.sharding import PartitionSpec as P

TM = ("hi", "core")
ROW = ("y", "z", "lo")
RING = ("hi", "lo")

HERMITE_NODES = (
    -2.0201828704560856,
    -0.9585724646138185,
    0.0,
    0.9585724646138185,
    2.0201828704560856,
)
HERMITE_WEIGHTS = (
    0.019953242059045913,
    0.3936193231522412,
    0.9453087204829419,
    0.3936193231522412,
    0.019953242059045913,
)
VMEM = pl.BlockSpec(memory_space=pltpu.VMEM)
SMEM = pl.BlockSpec(memory_space=pltpu.SMEM)


def moments(event_counts, latent_mean, latent_var):
    spread = jnp.sqrt(2.0 * latent_var)
    normal = 1.0 / math.sqrt(math.pi)
    points = [latent_mean + spread * abscissa for abscissa in HERMITE_NODES]
    rate_points = [jnp.exp(value) for value in points]
    mean_rate = sum(
        (weight * normal * value for weight, value in zip(HERMITE_WEIGHTS, rate_points))
    )
    covariance = sum(
        (
            weight * normal * (node_value - latent_mean) * (value - mean_rate)
            for weight, node_value, value in zip(HERMITE_WEIGHTS, points, rate_points)
        )
    )
    rate_var = sum(
        (
            weight * normal * (value - mean_rate) * (value - mean_rate)
            for weight, value in zip(HERMITE_WEIGHTS, rate_points)
        )
    )
    slope_gain = covariance / latent_var
    noise_var = rate_var - slope_gain * covariance + mean_rate
    return slope_gain * (event_counts.astype(latent_mean.dtype) - mean_rate) / noise_var


def time_factor(correlation, total):
    later = jnp.arange(total)[:, None]
    earlier = jnp.arange(total)[None, :]
    distance = jnp.maximum(later - earlier, 0).astype(correlation.dtype)
    lower = jnp.where(later >= earlier, jnp.power(correlation, distance), jnp.zeros_like(distance))
    column_scale = jnp.where(
        earlier == 0,
        jnp.ones_like(distance),
        jnp.sqrt(1.0 - correlation * correlation) * jnp.ones_like(distance),
    )
    return lower * column_scale


def shifted(array, axis, step):
    size = lax.axis_size(axis)
    return lax.ppermute(array, axis, [(k, (k + step) % size) for k in range(size)])


def copies_along(array, axis):
    size = lax.axis_size(axis)
    return lax.all_to_all(
        jnp.broadcast_to(array[None], (size, *array.shape)), axis, 0, 0, tiled=True
    )


def split_kernel(first_ref, basis_ref, kept_ref, sent_ref):
    source = lax.broadcasted_iota(jnp.int32, (256, 128), 0)
    target = lax.broadcasted_iota(jnp.int32, (256, 128), 1)
    for half, ref in ((first_ref[0], kept_ref), (1 - first_ref[0], sent_ref)):
        match = source == (target // 8) * 16 + half * 8 + lax.rem(target, 8)
        chosen = match.astype(jnp.float32).astype(jnp.bfloat16)
        for block in range(basis_ref.shape[1] // 256):
            moved = jnp.dot(
                basis_ref[:, block * 256 : block * 256 + 256],
                chosen,
                preferred_element_type=jnp.float32,
            )
            ref[:, block * 128 : block * 128 + 128] = moved.astype(jnp.bfloat16)


def split_columns(place, basis):
    rows, columns = basis.shape
    half = jax.ShapeDtypeStruct((rows, columns // 2), basis.dtype)
    return pl.pallas_call(
        split_kernel,
        out_shape=(half, half),
        in_specs=[SMEM, VMEM],
        out_specs=(VMEM, VMEM),
        name="split_columns",
    )(place, basis)


def first_kernel(mix_ref, place_ref, *refs):
    blocks, z_refs, y_refs = refs[:8], refs[8:17], refs[17:22]
    out_ref, zy_ref, yz_ref, acc_ref, tmp_ref = refs[22:]
    rows, total = blocks[0].shape
    ny, nz = yz_ref.shape[:2]
    lo, y_here, z_here = place_ref[0], place_ref[2], place_ref[3]

    y_steps = (0, ny - 1, 1, 2)
    for ref, step in zip(z_refs, (0, nz - 1, 1, nz - 2, 2, nz - 3, 3, 4, 4)):
        at = lax.rem(z_here + step, nz)
        first = 2 if ref is z_refs[8] else 0
        for k in range(ref.shape[0]):
            zy_ref[at, lax.rem(y_here + y_steps[first + k], ny)] = ref[k]
    for ref, step in zip(y_refs, (0, ny - 1, 1, 2, 2)):
        at = lax.rem(y_here + step, ny)
        first = nz // 2 if ref is y_refs[4] else 0
        for k in range(ref.shape[0]):
            yz_ref[at, first + k] = ref[k]

    depth = total // ny
    half = zy_ref.shape[-1]
    for y in range(ny):
        field = jnp.concatenate([ref[:, y * depth : (y + 1) * depth] for ref in blocks], axis=0)
        for part in range(2):
            product = jnp.dot(
                field, basis_at(zy_ref, yz_ref, part, y), preferred_element_type=jnp.float32
            )
            span = slice(part * half, part * half + half)
            if y == 0:
                acc_ref[:, span] = product
            else:
                acc_ref[:, span] += product
    for a in range(4):
        for group in range(2):
            mixed = sum(
                mix_ref[group * 4 + t, a]
                * acc_ref[(group * 4 + t) * rows : (group * 4 + t + 1) * rows, :]
                for t in range(4)
            )
            at = lo if group == 0 else 1 - lo
            tmp_ref[pl.ds(pl.multiple_of(at * rows, rows), rows), :] = mixed
        out_ref[:, a * 2 * rows : (a + 1) * 2 * rows] = tmp_ref[...].T.astype(jnp.bfloat16)


def basis_at(zy_ref, yz_ref, part, y):
    if part == 0:
        pieces = [zy_ref[z, y] for z in range(zy_ref.shape[0])]
    else:
        pieces = [yz_ref[y, z] for z in range(yz_ref.shape[1])]
    return jnp.concatenate(pieces, axis=0)


def first_product(mix, place, fields, by_z, by_y):
    rows, depth = fields[0].shape
    ny, (nz, deep, half) = lax.axis_size("y"), by_y[0].shape
    width = 2 * half
    return pl.pallas_call(
        first_kernel,
        out_shape=(
            jax.ShapeDtypeStruct((width, 8 * rows), jnp.bfloat16),
            jax.ShapeDtypeStruct((nz, ny, deep, half), jnp.bfloat16),
            jax.ShapeDtypeStruct((ny, nz, deep, half), jnp.bfloat16),
        ),
        in_specs=[SMEM, SMEM] + [VMEM] * 22,
        out_specs=(VMEM, VMEM, VMEM),
        scratch_shapes=[
            pltpu.VMEM((8 * rows, width), jnp.float32),
            pltpu.VMEM((2 * rows, width), jnp.float32),
        ],
        cost_estimate=pl.CostEstimate(
            flops=2 * 8 * rows * depth * width, bytes_accessed=8 << 20, transcendentals=0
        ),
        name="first_product",
    )(mix, place, *fields, *by_z, *by_y)


def last_kernel(place_ref, slice_ref, *refs):
    fields = refs[:8]
    zy_ref, yz_ref, kept_ref, sent_ref, acc_ref, tmp_ref = refs[8:]
    ny = yz_ref.shape[0]
    times, rows, total = fields[0].shape
    depth = total // ny
    half = zy_ref.shape[-1]
    for y in range(ny):
        field = jnp.concatenate(
            [ref[a, :, y * depth : (y + 1) * depth] for a in range(times) for ref in fields], axis=0
        )
        for part in range(2):
            product = jnp.dot(
                field, basis_at(zy_ref, yz_ref, part, y), preferred_element_type=jnp.float32
            )
            span = slice(part * half, part * half + half)
            if y == 0:
                acc_ref[:, span] = product
            else:
                acc_ref[:, span] += product
    lo = place_ref[0]
    group = rows // 2
    for a in range(times):
        for b in range(8):
            half_of = lo if b < 4 else 1 - lo
            to = pl.multiple_of((slice_ref[b] * 2 + half_of) * group, group)
            base = (a * 8 + b) * rows
            mine = pl.multiple_of(base + lo * group, group)
            theirs = pl.multiple_of(base + (1 - lo) * group, group)
            kept_ref[a, pl.ds(to, group), :] = acc_ref[pl.ds(mine, group), :]
            tmp_ref[pl.ds(to, group), :] = acc_ref[pl.ds(theirs, group), :]
        sent_ref[a] = tmp_ref[...].astype(jnp.bfloat16)


def last_product(place, slices, fields, zy, yz):
    times, rows, total = fields[0].shape
    width = zy.shape[-1] + yz.shape[-1]
    own = (times, 4 * rows, width)
    return pl.pallas_call(
        last_kernel,
        out_shape=(
            jax.ShapeDtypeStruct(own, jnp.float32),
            jax.ShapeDtypeStruct(own, jnp.bfloat16),
        ),
        in_specs=[SMEM, SMEM] + [VMEM] * 10,
        out_specs=(VMEM, VMEM),
        scratch_shapes=[
            pltpu.VMEM((8 * times * rows, width), jnp.float32),
            pltpu.VMEM((4 * rows, width), jnp.float32),
        ],
        cost_estimate=pl.CostEstimate(
            flops=2 * 8 * times * rows * total * width, bytes_accessed=8 << 20, transcendentals=0
        ),
        name="last_product",
    )(place, slices, *fields, zy, yz)


def gradient_kernel(place_ref, kept_ref, got_ref, sx_ref, sy_ref, white_ref, out_ref):
    lo = place_ref[0]
    source = lax.broadcasted_iota(jnp.int32, (256, 256), 0)
    target = lax.broadcasted_iota(jnp.int32, (256, 256), 1)
    within = lax.rem(source, 128)
    which = jnp.where(source < 128, lo, 1 - lo)
    chosen = (target == (within // 8) * 16 + which * 8 + lax.rem(within, 8)).astype(jnp.float32)
    times, rows, half = kept_ref.shape
    for block in range(half // 128):
        here = slice(block * 128, block * 128 + 128)
        span = slice(block * 256, block * 256 + 256)
        pair = jnp.concatenate(
            [
                jnp.concatenate(
                    [kept_ref[a, :, here], got_ref[a, :, here].astype(jnp.float32)], axis=1
                )
                for a in range(times)
            ],
            axis=0,
        )
        natural = jnp.dot(pair, chosen, precision=lax.Precision.HIGHEST)
        for a in range(times):
            scale = sy_ref[:, :1] * sx_ref[:, span]
            out_ref[:, a, span] = (
                scale * natural[a * rows : (a + 1) * rows] - white_ref[:, a, span]
            )


def whitened_gradient(place, kept, got, sx, sy, white):
    return pl.pallas_call(
        gradient_kernel,
        out_shape=jax.ShapeDtypeStruct(white.shape, jnp.float32),
        in_specs=[SMEM] + [VMEM] * 5,
        out_specs=VMEM,
        name="whitened_gradient",
    )(place, kept, got, sx, sy, white)


def around_x(block):
    blocks = [block] + [shifted(block, RING, step) for step in (2, 1, 3)]
    return tuple(copy for b in blocks for copy in (b, shifted(b, "core", 1)))


def local(event_counts, latent_mean, latent_var, eigen_basis, spectrum, correlation, whitened):
    hi, core = lax.axis_index("hi"), lax.axis_index("core")
    y, z, lo = (lax.axis_index(axis) for axis in ROW)
    time = hi * 2 + core
    ny, nz = lax.axis_size("y"), lax.axis_size("z")
    place = jnp.stack([lo, time, y, z]).astype(jnp.int32)

    kept, sent = split_columns(place, eigen_basis)
    other = shifted(sent, "lo", 1)
    mine = jnp.where(lo == 0, jnp.concatenate([kept, other]), jnp.concatenate([other, kept]))
    half = mine.shape[-1] // 2
    z_block, y_block = mine[:, :half], mine[:, half:]

    pseudo = moments(event_counts, latent_mean, latent_var).astype(jnp.bfloat16)[0]
    z_block, y_block, pseudo = lax.optimization_barrier((z_block, y_block, pseudo))

    y_block = copies_along(y_block, "z")
    z_block = jnp.stack([z_block] + [shifted(z_block, "y", step) for step in (1, 3, 2)])
    fields = around_x(pseudo)

    right = left = z_block
    by_z = [z_block]
    for _ in range(3):
        right, left = shifted(right, "z", 1), shifted(left, "z", nz - 1)
        by_z += [right, left]
    by_z += [shifted(right[:2], "z", 1), shifted(left[2:], "z", nz - 1)]
    right, left = shifted(y_block, "y", 1), shifted(y_block, "y", ny - 1)
    by_y = [y_block, right, left]
    by_y += [shifted(right[: nz // 2], "y", 1), shifted(left[nz // 2 :], "y", ny - 1)]

    flips = jnp.array([0, 1, 2, 3], jnp.int32)
    before_flip, after_flip = 2 * (1 - lo), 2 * lo
    crossed = jnp.stack([before_flip, before_flip + 1, after_flip, after_flip + 1])
    slices = lax.bitwise_xor(time, jnp.concatenate([flips, crossed])).astype(jnp.int32)
    factor = time_factor(correlation[0], 4)
    mix = jnp.take(factor, slices, axis=0)
    partial_y, zy, yz = first_product(mix, place, fields, by_z, by_y)

    modes, width = partial_y.shape
    sent = partial_y.reshape(ny * nz, modes // (ny * nz), width)
    got = lax.all_to_all(sent, ("y", "z"), 0, 0, tiled=True)
    got = got.reshape(ny * nz, modes // (ny * nz), 4, width // 4)
    got = got.transpose(2, 1, 0, 3).reshape(4, modes // (ny * nz), -1)
    kept, sent = last_product(place, slices, around_x(got), zy, yz)
    got = shifted(sent, "lo", 1)

    root = jnp.sqrt(spectrum)
    sx = lax.dynamic_slice_in_dim(root, time * 1024, 1024, 0)[None]
    row = (y * nz + z) * 2 + lo
    sy = lax.dynamic_slice_in_dim(root.reshape(4, lax.axis_size(ROW), -1), row, 1, 1).reshape(-1, 1)
    sy = jnp.broadcast_to(sy, (sy.shape[0], 128))
    white = whitened.reshape(-1, *whitened.shape[3:])
    gradient = whitened_gradient(place, kept, got, sx, sy, white)
    return gradient.reshape(whitened.shape)


def solution(mesh):
    finer = Mesh(mesh.devices.reshape(2, 2, 4, 8, 2), ("hi", "core", "y", "z", "lo"))
    placed = (
        P(TM, ROW, None),
        P(TM, ROW, None),
        P(TM, ROW, None),
        P(ROW, TM),
        P(),
        P(),
        P(None, ROW, None, None, TM),
    )
    return jax.shard_map(
        local,
        mesh=finer,
        in_specs=placed,
        out_specs=P(None, ROW, None, None, TM),
        check_vma=False,
    )
```

time: 194 us -> 176 us (0.907)
  blocking collectives: 75 us -> 25.6 us
  starting transfers between devices: 15.3 us -> 45.3 us
  waiting for transfers between devices: 55.4 us -> 69.3 us
  between operations: 14.3 us -> 1.03 us
  Pallas kernels: 18.2 us -> 20.5 us
    ppermute x11 -> x31, waiting for transfers between devices: 25 us -> 69.3 us  [shifted(): lax.ppermute(array, axis, [(k, (k + step) % size) for k in range(size)])]
    all_gather x2 -> x0, waiting for transfers between devices: 30.5 us -> none  [the longest x1 30.5 us: local(): zy = lax.all_gather(copies_along(mine[:, :quarter], 'y'), 'z')]
    ppermute x11 -> x31, starting transfers between devices: 10.9 us -> 36.7 us  [shifted(): lax.ppermute(array, axis, [(k, (k + step) % size) for k in range(size)])]
    all_gather x1 -> x0, blocking collectives: 25.6 us -> none  [local(): yz = copies_along(lax.all_gather(mine[:, quarter:], 'z'), 'y')]
    all_to_all x3 -> x1, blocking collectives: 49.4 us -> 25.6 us  [local(): got = lax.all_to_all(sent, ('y', 'z'), 0, 0, tiled=True)]
    all_to_all x1, starting transfers between devices: 4.36 us -> 8.57 us  [copies_along(): lax.all_to_all(jnp.broadcast_to(array[None], (size, *array.shape)), axis,...]
    pallas_call x3 -> x4, Pallas kernels: 18.2 us -> 20.5 us  [the longest x1 7.87 us: first_product(): pl.pallas_call(first_kernel, out_shape=(jax.ShapeDtypeStruct((width, 8 *...]
  transfers between devices with their start and end apart: 14 -> 32, of which waited for: 8 -> 12; matrix products, arithmetic and copies ran while one was open for 5% -> 5% of each run, Pallas kernels for 4% -> 0%
where the time goes in v3:
time: 176 us; the launch traced here: 175 us
  waiting for transfers between devices  69.3 us (39%)
  starting transfers between devices  45.3 us (26%)
  blocking collectives  25.6 us (15%)
  Pallas kernels  20.5 us (12%)
  local copies, waits for them, and re-layouts  7.64 us (4%)
  other arithmetic  6.11 us (3%)
    ppermute x31, waiting for transfers between devices, shifted(): lax.ppermute(array, axis, [(k, (k + step) % size) for k in range(size)])  69.3 us
    ppermute x31, starting transfers between devices, shifted(): lax.ppermute(array, axis, [(k, (k + step) % size) for k in range(size)])  36.7 us
    all_to_all x1, blocking collectives, local(): got = lax.all_to_all(sent, ('y', 'z'), 0, 0, tiled=True)  25.6 us
    all_to_all x1, starting transfers between devices, copies_along(): lax.all_to_all(jnp.broadcast_to(array[None], (size, *array.shape)), axis,...  8.57 us
    pallas_call x1, Pallas kernels, first_product(): pl.pallas_call(first_kernel, out_shape=(jax.ShapeDtypeStruct((width, 8 *...  7.87 us
    pallas_call x1, Pallas kernels, last_product(): pl.pallas_call(last_kernel, out_shape=(jax.ShapeDtypeStruct(own, jnp.floa...  6.79 us
    squeeze x1, other arithmetic, local(): moments(event_counts, latent_mean, latent_var).astype(jnp.bfloat16)[0]  4.29 us
    pallas_call x1, Pallas kernels, whitened_gradient(): pl.pallas_call(gradient_kernel, out_shape=jax.ShapeDtypeStruct(white.shap...  4.03 us
  transfers between devices with their start and end apart: 32, of which 12 were waited for; matrix products, arithmetic and copies ran while one was open for 5% of the time, Pallas kernels for 0%

profile of v3, /device:TPU:32, one launch (start us, length us, event | category | flops | bytes accessed | tf_op | source)
XLA Modules:
  0.0 175.4 jit_solution(7464541061031248536)
XLA Ops:
  0.6 1.8 %split_columns.1 = (bf16[64,512]{1,0:T(8,128)(2,1)}, bf16[64,512]{1,0:T(8,128)(2,1)}) custom-call(s32[4]{0:T(128)} %pad_add_fusion.first_ref.place_ref, bf16[64,1024]{1,0:T(8,128)(2,1)} %basis_ref.1), custom_call_target="tpu_custom_call" | custom-call | tf_op jit(solution)/shard_map/split_columns/pallas_call | solution.py:101
  2.4 1.5 collective-permute-start
  3.9 4.3 %fusion.8.refs_0_ = bf16[64,4096]{1,0:T(8,128)(2,1)S(1)} fusion(s32[1,64,4096]{2,1,0:T(8,128)} %param.8, f32[1,64,4096]{2,1,0:T(8,128)} %param.10, f32[1,64,4096]{2,1,0:T(8,128)} %param.9), kind=kLoop, calls=%fused_computation.14 | loop fusion | flops 17563648 | bytes 3670016 | tf_op jit(solution)/shard_map/squeeze | solution.py:299
  8.2 3.3 %collective-permute-start.10 = (bf16[128,256]{1,0:T(8,128)(2,1)S(1)}, bf16[128,256]{1,0:T(8,128)(2,1)S(1)}, u32[]{:S(2)}, u32[]{:S(2)}) collective-permute-start(bf16[128,256]{1,0:T(8,128)(2,1)S(1)} %get-tuple-element.18), channel_id=1, source_target_pairs={{0,32},{16,48},{32,0},{48,16},{1,33},{17,49},{33,1},{49,17},{2,34}... | collective-permute-start | bytes 196616 | tf_op jit(solution)/shard_map/ppermute | solution.py:73
  11.5 1.1 collective-permute-start.9
  12.6 1.0 collective-permute-start.8
  14.4 8.6 %all-to-all-start = ((bf16[8,128,256]{2,1,0:T(8,128)(2,1)}), bf16[8,128,256]{2,1,0:T(8,128)(2,1)S(1)}, u32[]{:S(2)}, u32[]{:S(2)}) async-start(bf16[8,128,256]{2,1,0:T(8,128)(2,1)} %broadcast_in_dim.39), calls=%async_computation | async-start | bytes 1048576 | tf_op jit(solution)/shard_map/all_to_all | solution.py:78
  23.0 1.5 collective-permute-start.11
  25.1 14.2 %collective-permute-done.11.refs_9_ = bf16[4,128,256]{2,1,0:T(8,128)(2,1)S(1)} collective-permute-done((bf16[4,128,256]{2,1,0:T(8,128)(2,1)S(1)}, bf16[4,128,256]{2,1,0:T(8,128)(2,1)S(1)}, u32[]{:S(2)}, u32[]{:S(2)}) %collective-permute-start.11) | collective-permute-done | bytes 262176 | tf_op jit(solution)/shard_map/ppermute | solution.py:73
  39.4 1.5 collective-permute-start.13
  40.8 1.5 collective-permute-start.14
  42.4 5.4 %collective-permute-done.13.refs_11_ = bf16[4,128,256]{2,1,0:T(8,128)(2,1)S(1)} collective-permute-done((bf16[4,128,256]{2,1,0:T(8,128)(2,1)S(1)}, bf16[4,128,256]{2,1,0:T(8,128)(2,1)S(1)}, u32[]{:S(2)}, u32[]{:S(2)}) %collective-permute-start.13) | collective-permute-done | bytes 262176 | tf_op jit(solution)/shard_map/ppermute | solution.py:73
  48.3 2.6 %collective-permute-start.16 = (bf16[4,128,256]{2,1,0:T(8,128)(2,1)S(1)}, bf16[4,128,256]{2,1,0:T(8,128)(2,1)S(1)}, u32[]{:S(2)}, u32[]{:S(2)}) collective-permute-start(bf16[4,128,256]{2,1,0:T(8,128)(2,1)S(1)} %collective-permute-done.14.refs_12_), channel_id=1, source_target_pairs={{0,14},{2,0},{4,2},{6,4},{8,6},{10,8},{12,10},{14,12},{1,15},{3,1}... | collective-permute-start | bytes 786440 | tf_op jit(solution)/shard_map/ppermute | solution.py:73
  51.8 2.7 %collective-permute-start.2 = (bf16[64,4096]{1,0:T(8,128)(2,1)S(1)}, bf16[64,4096]{1,0:T(8,128)(2,1)}, u32[]{:S(2)}, u32[]{:S(2)}) collective-permute-start(bf16[64,4096]{1,0:T(8,128)(2,1)S(1)} %fusion.8.refs_0_), channel_id=1, source_target_pairs={{0,128},{1,129},{128,0},{129,1},{2,130},{3,131},{130,2},{131,3},{4... | collective-permute-start | bytes 1572872 | tf_op jit(solution)/shard_map/ppermute | solution.py:73
  54.7 3.0 %collective-permute-start.6 = (bf16[64,4096]{1,0:T(8,128)(2,1)S(1)}, bf16[64,4096]{1,0:T(8,128)(2,1)}, u32[]{:S(2)}, u32[]{:S(2)}) collective-permute-start(bf16[64,4096]{1,0:T(8,128)(2,1)S(1)} %fusion.8.refs_0_), channel_id=1, source_target_pairs={{0,129},{1,0},{128,1},{129,128},{2,131},{3,2},{130,3},{131,130},{4... | collective-permute-start | bytes 1572872 | tf_op jit(solution)/shard_map/ppermute | solution.py:73
  58.7 2.6 %collective-permute-start.20 = (bf16[8,128,256]{2,1,0:T(8,128)(2,1)S(1)}, bf16[8,128,256]{2,1,0:T(8,128)(2,1)S(1)}, u32[]{:S(2)}, u32[]{:S(2)}) collective-permute-start(bf16[8,128,256]{2,1,0:T(8,128)(2,1)S(1)} %all-to-all-done.refs_17_), channel_id=1, source_target_pairs={{0,48},{16,0},{32,16},{48,32},{1,49},{17,1},{33,17},{49,33},{2,50}... | collective-permute-start | bytes 1572872 | tf_op jit(solution)/shard_map/ppermute | solution.py:73
  61.9 6.4 %collective-permute-done.2.refs_2_ = bf16[64,4096]{1,0:T(8,128)(2,1)} collective-permute-done((bf16[64,4096]{1,0:T(8,128)(2,1)S(1)}, bf16[64,4096]{1,0:T(8,128)(2,1)}, u32[]{:S(2)}, u32[]{:S(2)}) %collective-permute-start.2) | collective-permute-done | bytes 524320 | tf_op jit(solution)/shard_map/ppermute | solution.py:73
  68.3 8.0 %collective-permute-done.4.refs_4_ = bf16[64,4096]{1,0:T(8,128)(2,1)} collective-permute-done((bf16[64,4096]{1,0:T(8,128)(2,1)S(1)}, bf16[64,4096]{1,0:T(8,128)(2,1)}, u32[]{:S(2)}, u32[]{:S(2)}) %collective-permute-start.4) | collective-permute-done | bytes 524320 | tf_op jit(solution)/shard_map/ppermute | solution.py:73
  77.5 2.4 %collective-permute-start.18 = (bf16[2,128,256]{2,1,0:T(8,128)(2,1)S(1)}, bf16[2,128,256]{2,1,0:T(8,128)(2,1)}, u32[]{:S(2)}, u32[]{:S(2)}) collective-permute-start(bf16[2,128,256]{2,1,0:T(8,128)(2,1)S(1)} %slice.29), channel_id=1, source_target_pairs={{0,14},{2,0},{4,2},{6,4},{8,6},{10,8},{12,10},{14,12},{1,15},{3,1}... | collective-permute-start | bytes 393224 | tf_op jit(solution)/shard_map/ppermute | solution.py:73
  81.3 2.2 %collective-permute-done.17.refs_15_ = bf16[2,128,256]{2,1,0:T(8,128)(2,1)S(1)} collective-permute-done((bf16[2,128,256]{2,1,0:T(8,128)(2,1)S(1)}, bf16[2,128,256]{2,1,0:T(8,128)(2,1)S(1)}, u32[]{:S(2)}, u32[]{:S(2)}) %collective-permute-start.17) | collective-permute-done | bytes 131104 | tf_op jit(solution)/shard_map/ppermute | solution.py:73
  84.2 2.6 %collective-permute-start.22 = (bf16[4,128,256]{2,1,0:T(8,128)(2,1)}, bf16[4,128,256]{2,1,0:T(8,128)(2,1)S(1)}, u32[]{:S(2)}, u32[]{:S(2)}) collective-permute-start(bf16[4,128,256]{2,1,0:T(8,128)(2,1)} %slice.31), channel_id=1, source_target_pairs={{0,48},{16,0},{32,16},{48,32},{1,49},{17,1},{33,17},{49,33},{2,50}... | collective-permute-start | bytes 786440 | tf_op jit(solution)/shard_map/ppermute | solution.py:73
  88.0 4.8 %collective-permute-done.21.refs_20_ = bf16[4,128,256]{2,1,0:T(8,128)(2,1)S(1)} collective-permute-done((bf16[4,128,256]{2,1,0:T(8,128)(2,1)}, bf16[4,128,256]{2,1,0:T(8,128)(2,1)S(1)}, u32[]{:S(2)}, u32[]{:S(2)}) %collective-permute-start.21) | collective-permute-done | bytes 262176 | tf_op jit(solution)/shard_map/ppermute | solution.py:73
  94.2 7.9 %first_product.1 = (bf16[512,512]{1,0:T(8,128)(2,1)}, bf16[8,4,128,256]{3,2,1,0:T(8,128)(2,1)}, bf16[4,8,128,256]{3,2,1,0:T(8,128)(2,1)}) custom-call(f32[8,4]{1,0:T(8,128)} %broadcast_select_fusion.mix_ref, s32[4]{0:T(128)} %pad_add_fusion.first_ref.place_ref, bf16[64,4096]{1,0:T(8,128)(2,1)} %copy-done.1, bf16[64,4096]{1,0:T(8,128)(2,1)} %copy-done.15, ...), custom_call_target="tpu_custom_call" | custom-call | flops 2147483648 | bytes 8388608 | tf_op jit(solution)/shard_map/first_product/pallas_call | solution.py:166
  102.1 25.6 %all_to_all.10 = bf16[32,16,512]{2,1,0:T(8,128)(2,1)S(1)} all-to-all(bf16[32,16,512]{2,1,0:T(8,128)(2,1)} %bitcast.35), channel_id=1, replica_groups=mesh['hi'=2,'core'=2,'y'=4,'z'=8,'lo'=2] {'y','z'}, dimensions={0} | all-to-all | bytes 1048576 | tf_op jit(solution)/shard_map/all_to_all | solution.py:326
  128.5 1.8 %collective-permute-start.24 = (bf16[4,16,4096]{2,1,0:T(8,128)(2,1)S(1)}, bf16[4,16,4096]{2,1,0:T(8,128)(2,1)S(1)}, u32[]{:S(2)}, u32[]{:S(2)}) collective-permute-start(bf16[4,16,4096]{2,1,0:T(8,128)(2,1)S(1)} %reshape.132.refs_0_), channel_id=1, source_target_pairs={{0,128},{1,129},{128,0},{129,1},{2,130},{3,131},{130,2},{131,3},{4... | collective-permute-start | bytes 1572872 | tf_op jit(solution)/shard_map/ppermute | solution.py:73
  130.3 1.9 %collective-permute-start.26 = (bf16[4,16,4096]{2,1,0:T(8,128)(2,1)S(1)}, bf16[4,16,4096]{2,1,0:T(8,128)(2,1)S(1)}, u32[]{:S(2)}, u32[]{:S(2)}) collective-permute-start(bf16[4,16,4096]{2,1,0:T(8,128)(2,1)S(1)} %reshape.132.refs_0_), channel_id=1, source_target_pairs={{0,1},{1,128},{128,129},{129,0},{2,3},{3,130},{130,131},{131,2},{4... | collective-permute-start | bytes 1572872 | tf_op jit(solution)/shard_map/ppermute | solution.py:73
  132.2 1.3 collective-permute-start.28
  133.5 11.4 %collective-permute-done.24.refs_2_ = bf16[4,16,4096]{2,1,0:T(8,128)(2,1)S(1)} collective-permute-done((bf16[4,16,4096]{2,1,0:T(8,128)(2,1)S(1)}, bf16[4,16,4096]{2,1,0:T(8,128)(2,1)S(1)}, u32[]{:S(2)}, u32[]{:S(2)}) %collective-permute-start.24) | collective-permute-done | bytes 524320 | tf_op jit(solution)/shard_map/ppermute | solution.py:73
  144.9 6.7 %collective-permute-done.26.refs_4_ = bf16[4,16,4096]{2,1,0:T(8,128)(2,1)S(1)} collective-permute-done((bf16[4,16,4096]{2,1,0:T(8,128)(2,1)S(1)}, bf16[4,16,4096]{2,1,0:T(8,128)(2,1)S(1)}, u32[]{:S(2)}, u32[]{:S(2)}) %collective-permute-start.26) | collective-permute-done | bytes 524320 | tf_op jit(solution)/shard_map/ppermute | solution.py:73
  155.3 6.8 %last_product.1 = (f32[4,64,512]{2,1,0:T(8,128)}, bf16[4,64,512]{2,1,0:T(8,128)(2,1)}) custom-call(s32[4]{0:T(128)} %pad_add_fusion.first_ref.place_ref, s32[8]{0:T(128)} %get-tuple-element.26.slice_ref, bf16[4,16,4096]{2,1,0:T(8,128)(2,1)} %copy-done, bf16[4,16,4096]{2,1,0:T(8,128)(2,1)} %copy-done.11, bf16[4,16,4096]{2,1,0:T(8,128)(2,1)} %copy-done.8, ...), custom_call_target="tpu_custom_call" | custom-call | flops 2147483648 | bytes 8388608 | tf_op jit(solution)/shard_map/last_product/pallas_call | solution.py:224
  163.3 7.4 %collective-permute-done.30.got_ref = bf16[4,64,512]{2,1,0:T(8,128)(2,1)S(1)} collective-permute-done((bf16[4,64,512]{2,1,0:T(8,128)(2,1)}, bf16[4,64,512]{2,1,0:T(8,128)(2,1)S(1)}, u32[]{:S(2)}, u32[]{:S(2)}) %collective-permute-start.30) | collective-permute-done | bytes 262176 | tf_op jit(solution)/shard_map/ppermute | solution.py:73
  171.4 4.0 %whitened_gradient.1 = f32[64,4,1024]{2,1,0:T(4,128)} custom-call(s32[4]{0:T(128)} %pad_add_fusion.first_ref.place_ref, f32[4,64,512]{2,1,0:T(8,128)} %get-tuple-element.23.kept_ref, bf16[4,64,512]{2,1,0:T(8,128)(2,1)} %copy-done.22, f32[1,1024]{1,0:T(1,128)} %bitcast.40, f32[64,128]{1,0:T(8,128)} %broadcast_in_dim.42.sy_ref, f32[64,4,1024]{2,1,0:T(4,128)} %bitcast.34), custom_call_target="tpu_custom_call" | custom-call | tf_op jit(solution)/shard_map/whitened_gradient/pallas_call | solution.py:272
  (119 shorter events, 16.7 us)
Async XLA Ops:
  2.4 5.8 %collective-permute-start = (bf16[64,512]{1,0:T(8,128)(2,1)}, bf16[64,512]{1,0:T(8,128)(2,1)S(1)}, u32[]{:S(2)}, u32[]{:S(2)}) collective-permute-start(bf16[64,512]{1,0:T(8,128)(2,1)} %get-tuple-element.16), channel_id=1, source_target_pairs={{0,1},{1,0},{2,3},{3,2},{4,5},{5,4},{6,7},{7,6},{8,9},{9,8},{10,11... | collective-permute-start | bytes 196616 | tf_op jit(solution)/shard_map/ppermute | solution.py:73
  8.2 14.7 %collective-permute-start.10 = (bf16[128,256]{1,0:T(8,128)(2,1)S(1)}, bf16[128,256]{1,0:T(8,128)(2,1)S(1)}, u32[]{:S(2)}, u32[]{:S(2)}) collective-permute-start(bf16[128,256]{1,0:T(8,128)(2,1)S(1)} %get-tuple-element.18), channel_id=1, source_target_pairs={{0,32},{16,48},{32,0},{48,16},{1,33},{17,49},{33,1},{49,17},{2,34}... | collective-permute-start | bytes 196616 | tf_op jit(solution)/shard_map/ppermute | solution.py:73
  11.5 11.5 %collective-permute-start.9 = (bf16[128,256]{1,0:T(8,128)(2,1)S(1)}, bf16[128,256]{1,0:T(8,128)(2,1)S(1)}, u32[]{:S(2)}, u32[]{:S(2)}) collective-permute-start(bf16[128,256]{1,0:T(8,128)(2,1)S(1)} %get-tuple-element.18), channel_id=1, source_target_pairs={{0,48},{16,0},{32,16},{48,32},{1,49},{17,1},{33,17},{49,33},{2,50}... | collective-permute-start | bytes 196616 | tf_op jit(solution)/shard_map/ppermute | solution.py:73
  12.6 10.4 %collective-permute-start.8 = (bf16[128,256]{1,0:T(8,128)(2,1)S(1)}, bf16[128,256]{1,0:T(8,128)(2,1)S(1)}, u32[]{:S(2)}, u32[]{:S(2)}) collective-permute-start(bf16[128,256]{1,0:T(8,128)(2,1)S(1)} %get-tuple-element.18), channel_id=1, source_target_pairs={{0,16},{16,32},{32,48},{48,0},{1,17},{17,33},{33,49},{49,1},{2,18}... | collective-permute-start | bytes 196616 | tf_op jit(solution)/shard_map/ppermute | solution.py:73
  14.4 43.4 %all-to-all-start = ((bf16[8,128,256]{2,1,0:T(8,128)(2,1)}), bf16[8,128,256]{2,1,0:T(8,128)(2,1)S(1)}, u32[]{:S(2)}, u32[]{:S(2)}) async-start(bf16[8,128,256]{2,1,0:T(8,128)(2,1)} %broadcast_in_dim.39), calls=%async_computation | async-start | bytes 1048576 | tf_op jit(solution)/shard_map/all_to_all | solution.py:78
  23.0 16.3 %collective-permute-start.11 = (bf16[4,128,256]{2,1,0:T(8,128)(2,1)S(1)}, bf16[4,128,256]{2,1,0:T(8,128)(2,1)S(1)}, u32[]{:S(2)}, u32[]{:S(2)}) collective-permute-start(bf16[4,128,256]{2,1,0:T(8,128)(2,1)S(1)} %pad_maximum_fusion.refs_8_), channel_id=1, source_target_pairs={{0,2},{2,4},{4,6},{6,8},{8,10},{10,12},{12,14},{14,0},{1,3},{3,5},... | collective-permute-start | bytes 786440 | tf_op jit(solution)/shard_map/ppermute | solution.py:73
  24.6 16.2 %collective-permute-start.12 = (bf16[4,128,256]{2,1,0:T(8,128)(2,1)S(1)}, bf16[4,128,256]{2,1,0:T(8,128)(2,1)S(1)}, u32[]{:S(2)}, u32[]{:S(2)}) collective-permute-start(bf16[4,128,256]{2,1,0:T(8,128)(2,1)S(1)} %pad_maximum_fusion.refs_8_), channel_id=1, source_target_pairs={{0,14},{2,0},{4,2},{6,4},{8,6},{10,8},{12,10},{14,12},{1,15},{3,1}... | collective-permute-start | bytes 786440 | tf_op jit(solution)/shard_map/ppermute | solution.py:73
  25.1 29.6 %collective-permute-start.1 = (bf16[64,4096]{1,0:T(8,128)(2,1)S(1)}, bf16[64,4096]{1,0:T(8,128)(2,1)S(1)}, u32[]{:S(2)}, u32[]{:S(2)}) collective-permute-start(bf16[64,4096]{1,0:T(8,128)(2,1)S(1)} %fusion.8.refs_0_), channel_id=1, source_target_pairs={{0,64},{64,0},{1,65},{65,1},{2,66},{66,2},{3,67},{67,3},{4,68},{68... | collective-permute-start | bytes 1572872 | tf_op jit(solution)/shard_map/ppermute | solution.py:73
  39.4 8.4 %collective-permute-start.13 = (bf16[4,128,256]{2,1,0:T(8,128)(2,1)S(1)}, bf16[4,128,256]{2,1,0:T(8,128)(2,1)S(1)}, u32[]{:S(2)}, u32[]{:S(2)}) collective-permute-start(bf16[4,128,256]{2,1,0:T(8,128)(2,1)S(1)} %collective-permute-done.11.refs_9_), channel_id=1, source_target_pairs={{0,2},{2,4},{4,6},{6,8},{8,10},{10,12},{12,14},{14,0},{1,3},{3,5},... | collective-permute-start | bytes 786440 | tf_op jit(solution)/shard_map/ppermute | solution.py:73
  40.8 7.5 %collective-permute-start.14 = (bf16[4,128,256]{2,1,0:T(8,128)(2,1)S(1)}, bf16[4,128,256]{2,1,0:T(8,128)(2,1)S(1)}, u32[]{:S(2)}, u32[]{:S(2)}) collective-permute-start(bf16[4,128,256]{2,1,0:T(8,128)(2,1)S(1)} %collective-permute-done.12.refs_10_), channel_id=1, source_target_pairs={{0,14},{2,0},{4,2},{6,4},{8,6},{10,8},{12,10},{14,12},{1,15},{3,1}... | collective-permute-start | bytes 786440 | tf_op jit(solution)/shard_map/ppermute | solution.py:73
  47.8 10.0 %collective-permute-start.15 = (bf16[4,128,256]{2,1,0:T(8,128)(2,1)S(1)}, bf16[4,128,256]{2,1,0:T(8,128)(2,1)S(1)}, u32[]{:S(2)}, u32[]{:S(2)}) collective-permute-start(bf16[4,128,256]{2,1,0:T(8,128)(2,1)S(1)} %collective-permute-done.13.refs_11_), channel_id=1, source_target_pairs={{0,2},{2,4},{4,6},{6,8},{8,10},{10,12},{12,14},{14,0},{1,3},{3,5},... | collective-permute-start | bytes 786440 | tf_op jit(solution)/shard_map/ppermute | solution.py:73
  48.3 10.4 %collective-permute-start.16 = (bf16[4,128,256]{2,1,0:T(8,128)(2,1)S(1)}, bf16[4,128,256]{2,1,0:T(8,128)(2,1)S(1)}, u32[]{:S(2)}, u32[]{:S(2)}) collective-permute-start(bf16[4,128,256]{2,1,0:T(8,128)(2,1)S(1)} %collective-permute-done.14.refs_12_), channel_id=1, source_target_pairs={{0,14},{2,0},{4,2},{6,4},{8,6},{10,8},{12,10},{14,12},{1,15},{3,1}... | collective-permute-start | bytes 786440 | tf_op jit(solution)/shard_map/ppermute | solution.py:73
  51.8 16.5 %collective-permute-start.2 = (bf16[64,4096]{1,0:T(8,128)(2,1)S(1)}, bf16[64,4096]{1,0:T(8,128)(2,1)}, u32[]{:S(2)}, u32[]{:S(2)}) collective-permute-start(bf16[64,4096]{1,0:T(8,128)(2,1)S(1)} %fusion.8.refs_0_), channel_id=1, source_target_pairs={{0,128},{1,129},{128,0},{129,1},{2,130},{3,131},{130,2},{131,3},{4... | collective-permute-start | bytes 1572872 | tf_op jit(solution)/shard_map/ppermute | solution.py:73
  54.5 21.8 %collective-permute-start.4 = (bf16[64,4096]{1,0:T(8,128)(2,1)S(1)}, bf16[64,4096]{1,0:T(8,128)(2,1)}, u32[]{:S(2)}, u32[]{:S(2)}) collective-permute-start(bf16[64,4096]{1,0:T(8,128)(2,1)S(1)} %fusion.8.refs_0_), channel_id=1, source_target_pairs={{0,1},{1,128},{128,129},{129,0},{2,3},{3,130},{130,131},{131,2},{4... | collective-permute-start | bytes 1572872 | tf_op jit(solution)/shard_map/ppermute | solution.py:73
  54.7 21.6 %collective-permute-start.6 = (bf16[64,4096]{1,0:T(8,128)(2,1)S(1)}, bf16[64,4096]{1,0:T(8,128)(2,1)}, u32[]{:S(2)}, u32[]{:S(2)}) collective-permute-start(bf16[64,4096]{1,0:T(8,128)(2,1)S(1)} %fusion.8.refs_0_), channel_id=1, source_target_pairs={{0,129},{1,0},{128,1},{129,128},{2,131},{3,2},{130,3},{131,130},{4... | collective-permute-start | bytes 1572872 | tf_op jit(solution)/shard_map/ppermute | solution.py:73
  57.8 19.0 %collective-permute-start.19 = (bf16[8,128,256]{2,1,0:T(8,128)(2,1)S(1)}, bf16[8,128,256]{2,1,0:T(8,128)(2,1)S(1)}, u32[]{:S(2)}, u32[]{:S(2)}) collective-permute-start(bf16[8,128,256]{2,1,0:T(8,128)(2,1)S(1)} %all-to-all-done.refs_17_), channel_id=1, source_target_pairs={{0,16},{16,32},{32,48},{48,0},{1,17},{17,33},{33,49},{49,1},{2,18}... | collective-permute-start | bytes 1572872 | tf_op jit(solution)/shard_map/ppermute | solution.py:73
  58.7 18.8 %collective-permute-start.20 = (bf16[8,128,256]{2,1,0:T(8,128)(2,1)S(1)}, bf16[8,128,256]{2,1,0:T(8,128)(2,1)S(1)}, u32[]{:S(2)}, u32[]{:S(2)}) collective-permute-start(bf16[8,128,256]{2,1,0:T(8,128)(2,1)S(1)} %all-to-all-done.refs_17_), channel_id=1, source_target_pairs={{0,48},{16,0},{32,16},{48,32},{1,49},{17,1},{33,17},{49,33},{2,50}... | collective-permute-start | bytes 1572872 | tf_op jit(solution)/shard_map/ppermute | solution.py:73
  68.3 19.7 %collective-permute-start.3 = (bf16[64,4096]{1,0:T(8,128)(2,1)}, bf16[64,4096]{1,0:T(8,128)(2,1)}, u32[]{:S(2)}, u32[]{:S(2)}) collective-permute-start(bf16[64,4096]{1,0:T(8,128)(2,1)} %collective-permute-done.2.refs_2_), channel_id=1, source_target_pairs={{0,64},{64,0},{1,65},{65,1},{2,66},{66,2},{3,67},{67,3},{4,68},{68... | collective-permute-start | bytes 1572872 | tf_op jit(solution)/shard_map/ppermute | solution.py:73
  76.3 11.7 %collective-permute-start.5 = (bf16[64,4096]{1,0:T(8,128)(2,1)}, bf16[64,4096]{1,0:T(8,128)(2,1)}, u32[]{:S(2)}, u32[]{:S(2)}) collective-permute-start(bf16[64,4096]{1,0:T(8,128)(2,1)} %collective-permute-done.4.refs_4_), channel_id=1, source_target_pairs={{0,64},{64,0},{1,65},{65,1},{2,66},{66,2},{3,67},{67,3},{4,68},{68... | collective-permute-start | bytes 1572872 | tf_op jit(solution)/shard_map/ppermute | solution.py:73
  76.3 11.7 %collective-permute-start.7 = (bf16[64,4096]{1,0:T(8,128)(2,1)}, bf16[64,4096]{1,0:T(8,128)(2,1)}, u32[]{:S(2)}, u32[]{:S(2)}) collective-permute-start(bf16[64,4096]{1,0:T(8,128)(2,1)} %collective-permute-done.6.refs_6_), channel_id=1, source_target_pairs={{0,64},{64,0},{1,65},{65,1},{2,66},{66,2},{3,67},{67,3},{4,68},{68... | collective-permute-start | bytes 1572872 | tf_op jit(solution)/shard_map/ppermute | solution.py:73
  76.8 6.7 %collective-permute-start.17 = (bf16[2,128,256]{2,1,0:T(8,128)(2,1)S(1)}, bf16[2,128,256]{2,1,0:T(8,128)(2,1)S(1)}, u32[]{:S(2)}, u32[]{:S(2)}) collective-permute-start(bf16[2,128,256]{2,1,0:T(8,128)(2,1)S(1)} %slice.28), channel_id=1, source_target_pairs={{0,2},{2,4},{4,6},{6,8},{8,10},{10,12},{12,14},{14,0},{1,3},{3,5},... | collective-permute-start | bytes 393224 | tf_op jit(solution)/shard_map/ppermute | solution.py:73
  77.5 6.7 %collective-permute-start.18 = (bf16[2,128,256]{2,1,0:T(8,128)(2,1)S(1)}, bf16[2,128,256]{2,1,0:T(8,128)(2,1)}, u32[]{:S(2)}, u32[]{:S(2)}) collective-permute-start(bf16[2,128,256]{2,1,0:T(8,128)(2,1)S(1)} %slice.29), channel_id=1, source_target_pairs={{0,14},{2,0},{4,2},{6,4},{8,6},{10,8},{12,10},{14,12},{1,15},{3,1}... | collective-permute-start | bytes 393224 | tf_op jit(solution)/shard_map/ppermute | solution.py:73
  83.5 9.3 %collective-permute-start.21 = (bf16[4,128,256]{2,1,0:T(8,128)(2,1)}, bf16[4,128,256]{2,1,0:T(8,128)(2,1)S(1)}, u32[]{:S(2)}, u32[]{:S(2)}) collective-permute-start(bf16[4,128,256]{2,1,0:T(8,128)(2,1)} %slice.30), channel_id=1, source_target_pairs={{0,16},{16,32},{32,48},{48,0},{1,17},{17,33},{33,49},{49,1},{2,18}... | collective-permute-start | bytes 786440 | tf_op jit(solution)/shard_map/ppermute | solution.py:73
  84.2 8.6 %collective-permute-start.22 = (bf16[4,128,256]{2,1,0:T(8,128)(2,1)}, bf16[4,128,256]{2,1,0:T(8,128)(2,1)S(1)}, u32[]{:S(2)}, u32[]{:S(2)}) collective-permute-start(bf16[4,128,256]{2,1,0:T(8,128)(2,1)} %slice.31), channel_id=1, source_target_pairs={{0,48},{16,0},{32,16},{48,32},{1,49},{17,1},{33,17},{49,33},{2,50}... | collective-permute-start | bytes 786440 | tf_op jit(solution)/shard_map/ppermute | solution.py:73
  128.5 16.5 %collective-permute-start.24 = (bf16[4,16,4096]{2,1,0:T(8,128)(2,1)S(1)}, bf16[4,16,4096]{2,1,0:T(8,128)(2,1)S(1)}, u32[]{:S(2)}, u32[]{:S(2)}) collective-permute-start(bf16[4,16,4096]{2,1,0:T(8,128)(2,1)S(1)} %reshape.132.refs_0_), channel_id=1, source_target_pairs={{0,128},{1,129},{128,0},{129,1},{2,130},{3,131},{130,2},{131,3},{4... | collective-permute-start | bytes 1572872 | tf_op jit(solution)/shard_map/ppermute | solution.py:73
  130.3 21.3 %collective-permute-start.26 = (bf16[4,16,4096]{2,1,0:T(8,128)(2,1)S(1)}, bf16[4,16,4096]{2,1,0:T(8,128)(2,1)S(1)}, u32[]{:S(2)}, u32[]{:S(2)}) collective-permute-start(bf16[4,16,4096]{2,1,0:T(8,128)(2,1)S(1)} %reshape.132.refs_0_), channel_id=1, source_target_pairs={{0,1},{1,128},{128,129},{129,0},{2,3},{3,130},{130,131},{131,2},{4... | collective-permute-start | bytes 1572872 | tf_op jit(solution)/shard_map/ppermute | solution.py:73
  132.2 20.3 %collective-permute-start.28 = (bf16[4,16,4096]{2,1,0:T(8,128)(2,1)S(1)}, bf16[4,16,4096]{2,1,0:T(8,128)(2,1)S(1)}, u32[]{:S(2)}, u32[]{:S(2)}) collective-permute-start(bf16[4,16,4096]{2,1,0:T(8,128)(2,1)S(1)} %reshape.132.refs_0_), channel_id=1, source_target_pairs={{0,129},{1,0},{128,1},{129,128},{2,131},{3,2},{130,3},{131,130},{4... | collective-permute-start | bytes 1572872 | tf_op jit(solution)/shard_map/ppermute | solution.py:73
  133.5 19.0 %collective-permute-start.23 = (bf16[4,16,4096]{2,1,0:T(8,128)(2,1)S(1)}, bf16[4,16,4096]{2,1,0:T(8,128)(2,1)S(1)}, u32[]{:S(2)}, u32[]{:S(2)}) collective-permute-start(bf16[4,16,4096]{2,1,0:T(8,128)(2,1)S(1)} %reshape.132.refs_0_), channel_id=1, source_target_pairs={{0,64},{64,0},{1,65},{65,1},{2,66},{66,2},{3,67},{67,3},{4,68},{68... | collective-permute-start | bytes 1572872 | tf_op jit(solution)/shard_map/ppermute | solution.py:73
  144.9 7.6 %collective-permute-start.25 = (bf16[4,16,4096]{2,1,0:T(8,128)(2,1)S(1)}, bf16[4,16,4096]{2,1,0:T(8,128)(2,1)S(1)}, u32[]{:S(2)}, u32[]{:S(2)}) collective-permute-start(bf16[4,16,4096]{2,1,0:T(8,128)(2,1)S(1)} %collective-permute-done.24.refs_2_), channel_id=1, source_target_pairs={{0,64},{64,0},{1,65},{65,1},{2,66},{66,2},{3,67},{67,3},{4,68},{68... | collective-permute-start | bytes 1572872 | tf_op jit(solution)/shard_map/ppermute | solution.py:73
  151.6 1.9 %collective-permute-start.27 = (bf16[4,16,4096]{2,1,0:T(8,128)(2,1)S(1)}, bf16[4,16,4096]{2,1,0:T(8,128)(2,1)S(1)}, u32[]{:S(2)}, u32[]{:S(2)}) collective-permute-start(bf16[4,16,4096]{2,1,0:T(8,128)(2,1)S(1)} %collective-permute-done.26.refs_4_), channel_id=1, source_target_pairs={{0,64},{64,0},{1,65},{65,1},{2,66},{66,2},{3,67},{67,3},{4,68},{68... | collective-permute-start | bytes 1572872 | tf_op jit(solution)/shard_map/ppermute | solution.py:73
  152.5 1.9 %collective-permute-start.29 = (bf16[4,16,4096]{2,1,0:T(8,128)(2,1)S(1)}, bf16[4,16,4096]{2,1,0:T(8,128)(2,1)S(1)}, u32[]{:S(2)}, u32[]{:S(2)}) collective-permute-start(bf16[4,16,4096]{2,1,0:T(8,128)(2,1)S(1)} %collective-permute-done.28.refs_6_), channel_id=1, source_target_pairs={{0,64},{64,0},{1,65},{65,1},{2,66},{66,2},{3,67},{67,3},{4,68},{68... | collective-permute-start | bytes 1572872 | tf_op jit(solution)/shard_map/ppermute | solution.py:73
  162.1 8.6 %collective-permute-start.30 = (bf16[4,64,512]{2,1,0:T(8,128)(2,1)}, bf16[4,64,512]{2,1,0:T(8,128)(2,1)S(1)}, u32[]{:S(2)}, u32[]{:S(2)}) collective-permute-start(bf16[4,64,512]{2,1,0:T(8,128)(2,1)} %get-tuple-element.24), channel_id=1, source_target_pairs={{0,1},{1,0},{2,3},{3,2},{4,5},{5,4},{6,7},{7,6},{8,9},{9,8},{10,11... | collective-permute-start | bytes 786440 | tf_op jit(solution)/shard_map/ppermute | solution.py:73
  (26 other events, 423.3 us)

commit v4 on v3

v4 whole, which is shorter than its diff:
```python
import math

import jax
import jax.numpy as jnp
from jax import lax
from jax.experimental import pallas as pl
from jax.experimental.pallas import tpu as pltpu
from jax.sharding import Mesh
from jax.sharding import PartitionSpec as P

TM = ("hi", "core")
ROW = ("y", "z", "lo")
RING = ("hi", "lo")

HERMITE_NODES = (
    -2.0201828704560856,
    -0.9585724646138185,
    0.0,
    0.9585724646138185,
    2.0201828704560856,
)
HERMITE_WEIGHTS = (
    0.019953242059045913,
    0.3936193231522412,
    0.9453087204829419,
    0.3936193231522412,
    0.019953242059045913,
)
VMEM = pl.BlockSpec(memory_space=pltpu.VMEM)
SMEM = pl.BlockSpec(memory_space=pltpu.SMEM)


def moments(event_counts, latent_mean, latent_var):
    spread = jnp.sqrt(2.0 * latent_var)
    normal = 1.0 / math.sqrt(math.pi)
    points = [latent_mean + spread * abscissa for abscissa in HERMITE_NODES]
    rate_points = [jnp.exp(value) for value in points]
    mean_rate = sum(
        (weight * normal * value for weight, value in zip(HERMITE_WEIGHTS, rate_points))
    )
    covariance = sum(
        (
            weight * normal * (node_value - latent_mean) * (value - mean_rate)
            for weight, node_value, value in zip(HERMITE_WEIGHTS, points, rate_points)
        )
    )
    rate_var = sum(
        (
            weight * normal * (value - mean_rate) * (value - mean_rate)
            for weight, value in zip(HERMITE_WEIGHTS, rate_points)
        )
    )
    slope_gain = covariance / latent_var
    noise_var = rate_var - slope_gain * covariance + mean_rate
    return slope_gain * (event_counts.astype(latent_mean.dtype) - mean_rate) / noise_var


def time_factor(correlation, total):
    later = jnp.arange(total)[:, None]
    earlier = jnp.arange(total)[None, :]
    distance = jnp.maximum(later - earlier, 0).astype(correlation.dtype)
    lower = jnp.where(later >= earlier, jnp.power(correlation, distance), jnp.zeros_like(distance))
    column_scale = jnp.where(
        earlier == 0,
        jnp.ones_like(distance),
        jnp.sqrt(1.0 - correlation * correlation) * jnp.ones_like(distance),
    )
    return lower * column_scale


def shifted(array, axis, step):
    size = lax.axis_size(axis)
    return lax.ppermute(array, axis, [(k, (k + step) % size) for k in range(size)])


def split_kernel(first_ref, basis_ref, kept_ref, sent_ref):
    source = lax.broadcasted_iota(jnp.int32, (256, 128), 0)
    target = lax.broadcasted_iota(jnp.int32, (256, 128), 1)
    for half, ref in ((first_ref[0], kept_ref), (1 - first_ref[0], sent_ref)):
        match = source == (target // 8) * 16 + half * 8 + lax.rem(target, 8)
        chosen = match.astype(jnp.float32).astype(jnp.bfloat16)
        for block in range(basis_ref.shape[1] // 256):
            moved = jnp.dot(
                basis_ref[:, block * 256 : block * 256 + 256],
                chosen,
                preferred_element_type=jnp.float32,
            )
            ref[:, block * 128 : block * 128 + 128] = moved.astype(jnp.bfloat16)


def split_columns(place, basis):
    rows, columns = basis.shape
    half = jax.ShapeDtypeStruct((rows, columns // 2), basis.dtype)
    return pl.pallas_call(
        split_kernel,
        out_shape=(half, half),
        in_specs=[SMEM, VMEM],
        out_specs=(VMEM, VMEM),
        name="split_columns",
    )(place, basis)


def columns_at(ref, index):
    return pl.ds(pl.multiple_of(index * 128, 128), 128)


def product_of(place_ref, load, steps, pieces, acc_ref):
    y_here, z_here = place_ref[2], place_ref[3]
    for (step, parts), ref in zip(steps, pieces):
        at = lax.rem(z_here + step, 8)
        where = [columns_at(ref, lax.rem(y_here + part, 4) * 8 + at) for part in parts]
        field = jnp.concatenate([load(span) for span in where], axis=1)
        basis = jnp.concatenate([ref[k] for k in range(len(parts))], axis=0)
        acc_ref[...] += jnp.dot(field, basis, preferred_element_type=jnp.float32)


NEAR = tuple((step, (0, 3, 1, 2)) for step in (0, 7, 1, 6, 2, 5, 3))
FAR = ((4, (0, 3)), (4, (1, 2)))


def near_kernel(place_ref, *refs):
    blocks, pieces, acc_ref = refs[:8], refs[8:-1], refs[-1]
    acc_ref[...] = jnp.zeros_like(acc_ref)

    def load(span):
        return jnp.concatenate([ref[:, span] for ref in blocks], axis=0)

    product_of(place_ref, load, NEAR, pieces, acc_ref)


def near_product(place, fields, pieces):
    rows = sum(field.shape[0] for field in fields)
    width = pieces[0].shape[-1]
    return pl.pallas_call(
        near_kernel,
        out_shape=jax.ShapeDtypeStruct((rows, width), jnp.float32),
        in_specs=[SMEM] + [VMEM] * 15,
        out_specs=VMEM,
        cost_estimate=pl.CostEstimate(
            flops=2 * rows * 3584 * width, bytes_accessed=8 << 20, transcendentals=0
        ),
        name="near_product",
    )(place, *fields, *pieces)


def first_kernel(mix_ref, place_ref, *refs):
    blocks, pieces, near_ref, out_ref, acc_ref, tmp_ref = refs[:8], refs[8:10], *refs[10:]
    rows = blocks[0].shape[0]
    lo = place_ref[0]
    acc_ref[...] = near_ref[...]

    def load(span):
        return jnp.concatenate([ref[:, span] for ref in blocks], axis=0)

    product_of(place_ref, load, FAR, pieces, acc_ref)
    for a in range(4):
        for group in range(2):
            mixed = sum(
                mix_ref[group * 4 + t, a]
                * acc_ref[(group * 4 + t) * rows : (group * 4 + t + 1) * rows, :]
                for t in range(4)
            )
            at = lo if group == 0 else 1 - lo
            tmp_ref[pl.ds(pl.multiple_of(at * rows, rows), rows), :] = mixed
        out_ref[:, a * 2 * rows : (a + 1) * 2 * rows] = tmp_ref[...].T.astype(jnp.bfloat16)


def first_product(mix, place, fields, pieces, near):
    rows = fields[0].shape[0]
    width = near.shape[-1]
    return pl.pallas_call(
        first_kernel,
        out_shape=jax.ShapeDtypeStruct((width, 8 * rows), jnp.bfloat16),
        in_specs=[SMEM, SMEM] + [VMEM] * 11,
        out_specs=VMEM,
        scratch_shapes=[
            pltpu.VMEM((8 * rows, width), jnp.float32),
            pltpu.VMEM((2 * rows, width), jnp.float32),
        ],
        cost_estimate=pl.CostEstimate(
            flops=2 * 8 * rows * 512 * width, bytes_accessed=4 << 20, transcendentals=0
        ),
        name="first_product",
    )(mix, place, *fields, *pieces, near)


def load_bands(fields, span):
    times = fields[0].shape[0]
    return jnp.concatenate([ref[a, :, span] for a in range(times) for ref in fields], axis=0)


def band_kernel(place_ref, *refs):
    fields, pieces, acc_ref = refs[:-10], refs[-10:-1], refs[-1]
    acc_ref[...] = jnp.zeros_like(acc_ref)
    product_of(place_ref, lambda span: load_bands(fields, span), NEAR + FAR, pieces, acc_ref)


def band_product(place, fields, pieces):
    times, rows, total = fields[0].shape
    width = pieces[0].shape[-1]
    count = len(fields) * times * rows
    return pl.pallas_call(
        band_kernel,
        out_shape=jax.ShapeDtypeStruct((count, width), jnp.float32),
        in_specs=[SMEM] + [VMEM] * (len(fields) + 9),
        out_specs=VMEM,
        cost_estimate=pl.CostEstimate(
            flops=2 * count * total * width, bytes_accessed=6 << 20, transcendentals=0
        ),
        name="band_product",
    )(place, *fields, *pieces)


def last_kernel(place_ref, slice_ref, *refs):
    fields, pieces, done = refs[:2], refs[2:11], refs[11:13]
    kept_ref, sent_ref, acc_ref, tmp_ref = refs[13:]
    times, rows, _ = fields[0].shape
    acc_ref[...] = jnp.zeros_like(acc_ref)
    product_of(place_ref, lambda span: load_bands(fields, span), NEAR + FAR, pieces, acc_ref)
    lo = place_ref[0]
    group = rows // 2
    sources = [(done[0], 2, 0), (acc_ref, 2, 0), (done[1], 4, 0), (done[1], 4, 2)]
    for a in range(times):
        for b in range(8):
            ref, count, first = sources[b // 2]
            half_of = lo if b < 4 else 1 - lo
            to = pl.multiple_of((slice_ref[b] * 2 + half_of) * group, group)
            base = (a * count + first + b % 2) * rows
            mine = pl.multiple_of(base + lo * group, group)
            theirs = pl.multiple_of(base + (1 - lo) * group, group)
            kept_ref[a, pl.ds(to, group), :] = ref[pl.ds(mine, group), :]
            tmp_ref[pl.ds(to, group), :] = ref[pl.ds(theirs, group), :]
        sent_ref[a] = tmp_ref[...].astype(jnp.bfloat16)


def last_product(place, slices, fields, pieces, done):
    times, rows, total = fields[0].shape
    width = pieces[0].shape[-1]
    own = (times, 4 * rows, width)
    return pl.pallas_call(
        last_kernel,
        out_shape=(
            jax.ShapeDtypeStruct(own, jnp.float32),
            jax.ShapeDtypeStruct(own, jnp.bfloat16),
        ),
        in_specs=[SMEM, SMEM] + [VMEM] * 13,
        out_specs=(VMEM, VMEM),
        scratch_shapes=[
            pltpu.VMEM((2 * times * rows, width), jnp.float32),
            pltpu.VMEM((4 * rows, width), jnp.float32),
        ],
        cost_estimate=pl.CostEstimate(
            flops=4 * times * rows * total * width, bytes_accessed=6 << 20, transcendentals=0
        ),
        name="last_product",
    )(place, slices, *fields, *pieces, *done)


def gradient_kernel(place_ref, kept_ref, got_ref, sx_ref, sy_ref, white_ref, out_ref):
    lo = place_ref[0]
    source = lax.broadcasted_iota(jnp.int32, (256, 256), 0)
    target = lax.broadcasted_iota(jnp.int32, (256, 256), 1)
    within = lax.rem(source, 128)
    which = jnp.where(source < 128, lo, 1 - lo)
    chosen = (target == (within // 8) * 16 + which * 8 + lax.rem(within, 8)).astype(jnp.float32)
    times, rows, half = kept_ref.shape
    for block in range(half // 128):
        here = slice(block * 128, block * 128 + 128)
        span = slice(block * 256, block * 256 + 256)
        pair = jnp.concatenate(
            [
                jnp.concatenate(
                    [kept_ref[a, :, here], got_ref[a, :, here].astype(jnp.float32)], axis=1
                )
                for a in range(times)
            ],
            axis=0,
        )
        natural = jnp.dot(pair, chosen, precision=lax.Precision.HIGHEST)
        for a in range(times):
            scale = sy_ref[:, :1] * sx_ref[:, span]
            out_ref[:, a, span] = (
                scale * natural[a * rows : (a + 1) * rows] - white_ref[:, a, span]
            )


def whitened_gradient(place, kept, got, sx, sy, white):
    return pl.pallas_call(
        gradient_kernel,
        out_shape=jax.ShapeDtypeStruct(white.shape, jnp.float32),
        in_specs=[SMEM] + [VMEM] * 5,
        out_specs=VMEM,
        name="whitened_gradient",
    )(place, kept, got, sx, sy, white)


def with_core(block):
    return block, shifted(block, "core", 1)


def local(event_counts, latent_mean, latent_var, eigen_basis, spectrum, correlation, whitened):
    hi, core = lax.axis_index("hi"), lax.axis_index("core")
    y, z, lo = (lax.axis_index(axis) for axis in ROW)
    time = hi * 2 + core
    ny, nz = lax.axis_size("y"), lax.axis_size("z")
    place = jnp.stack([lo, time, y, z]).astype(jnp.int32)

    kept, sent = split_columns(place, eigen_basis)
    other = shifted(sent, "lo", 1)
    mine = jnp.where(lo == 0, jnp.concatenate([kept, other]), jnp.concatenate([other, kept]))
    pseudo = moments(event_counts, latent_mean, latent_var).astype(jnp.bfloat16)[0]
    mine, pseudo = lax.optimization_barrier((mine, pseudo))
    far, before, after = [shifted(pseudo, RING, step) for step in (2, 1, 3)]
    block = jnp.stack([mine] + [shifted(mine, "y", step) for step in (1, 3, 2)])
    own = with_core(pseudo)

    flips = jnp.array([0, 1, 2, 3], jnp.int32)
    before_flip, after_flip = 2 * (1 - lo), 2 * lo
    crossed = jnp.stack([before_flip, before_flip + 1, after_flip, after_flip + 1])
    slices = lax.bitwise_xor(time, jnp.concatenate([flips, crossed])).astype(jnp.int32)
    factor = time_factor(correlation[0], 4)
    mix = jnp.take(factor, slices, axis=0)
    root = jnp.sqrt(spectrum)
    sx = lax.dynamic_slice_in_dim(root, time * 1024, 1024, 0)[None]
    row = (y * nz + z) * 2 + lo
    sy = lax.dynamic_slice_in_dim(root.reshape(4, lax.axis_size(ROW), -1), row, 1, 1).reshape(-1, 1)
    sy = jnp.broadcast_to(sy, (sy.shape[0], 128))

    right, left = shifted(block, "z", 1), shifted(block, "z", nz - 1)
    pieces = [block, right, left]
    right, left, before, after = lax.optimization_barrier((right, left, before, after))
    before, after = with_core(before), with_core(after)
    right, left = shifted(right, "z", 1), shifted(left, "z", nz - 1)
    pieces += [right, left]
    right, left, far, own, mix, sx, sy = lax.optimization_barrier(
        (right, left, far, own, mix, sx, sy)
    )
    far = with_core(far)
    right, left = shifted(right, "z", 1), shifted(left, "z", nz - 1)
    pieces += [right, left]
    right, left, far, before, after = lax.optimization_barrier((right, left, far, before, after))
    last = [shifted(right[:2], "z", 1), shifted(left[2:], "z", nz - 1)]

    fields = (*own, *far, *before, *after)
    near = near_product(place, fields, pieces)
    partial_y = first_product(mix, place, fields, last, near)
    pieces += last

    modes, width = partial_y.shape
    sent = partial_y.reshape(ny * nz, modes // (ny * nz), width)
    got = lax.all_to_all(sent, ("y", "z"), 0, 0, tiled=True)
    got = got.reshape(ny * nz, modes // (ny * nz), 4, width // 4)
    got = got.transpose(2, 1, 0, 3).reshape(4, modes // (ny * nz), -1)
    far, before, after = [shifted(got, RING, step) for step in (2, 1, 3)]
    done = (
        band_product(place, with_core(got), pieces),
        band_product(place, (*with_core(before), *with_core(after)), pieces),
    )
    kept, sent = last_product(place, slices, with_core(far), pieces, done)
    got = shifted(sent, "lo", 1)

    white = whitened.reshape(-1, *whitened.shape[3:])
    gradient = whitened_gradient(place, kept, got, sx, sy, white)
    return gradient.reshape(whitened.shape)


def solution(mesh):
    finer = Mesh(mesh.devices.reshape(2, 2, 4, 8, 2), ("hi", "core", "y", "z", "lo"))
    placed = (
        P(TM, ROW, None),
        P(TM, ROW, None),
        P(TM, ROW, None),
        P(ROW, TM),
        P(),
        P(),
        P(None, ROW, None, None, TM),
    )
    return jax.shard_map(
        local,
        mesh=finer,
        in_specs=placed,
        out_specs=P(None, ROW, None, None, TM),
        check_vma=False,
    )
```

time: 176 us -> 155 us (0.88)
  starting transfers between devices: 45.3 us -> 23.9 us
  Pallas kernels: 20.5 us -> 29.7 us
  waiting for transfers between devices: 69.3 us -> 64 us
  blocking collectives: 25.6 us -> 21.3 us
    ppermute x31 -> x27, starting transfers between devices: 36.7 us -> 23.9 us  [shifted(): lax.ppermute(array, axis, [(k, (k + step) % size) for k in range(size)])]
    pallas_call x1 -> x4, Pallas kernels: 7.87 us -> 19.5 us  [the longest x2 8.77 us: band_product(): pl.pallas_call(band_kernel, out_shape=jax.ShapeDtypeStruct((count, width)...]
    all_to_all x1 -> x0, starting transfers between devices: 8.57 us -> none  [copies_along(): lax.all_to_all(jnp.broadcast_to(array[None], (size, *array.shape)), axis,...]
    ppermute x31 -> x27, waiting for transfers between devices: 69.3 us -> 64 us  [shifted(): lax.ppermute(array, axis, [(k, (k + step) % size) for k in range(size)])]
    all_to_all x1, blocking collectives: 25.6 us -> 21.3 us  [local(): got = lax.all_to_all(sent, ('y', 'z'), 0, 0, tiled=True)]
    pallas_call x1, Pallas kernels: 6.79 us -> 4.36 us  [last_product(): pl.pallas_call(last_kernel, out_shape=(jax.ShapeDtypeStruct(own, jnp.floa...]
    unnamed x52 -> x46, local copies, waits for them, and re-layouts: 2.31 us -> 3.81 us
  transfers between devices with their start and end apart: 32 -> 27, of which waited for: 12 -> 11; matrix products, arithmetic and copies ran while one was open for 5% -> 5% of each run, Pallas kernels for 0% -> 10%
where the time goes in v4:
time: 155 us
  waiting for transfers between devices  64 us (41%)
  Pallas kernels  29.7 us (19%)
  starting transfers between devices  23.9 us (15%)
  blocking collectives  21.3 us (14%)
  local copies, waits for them, and re-layouts  8.37 us (5%)
  other arithmetic  6.2 us (4%)
    ppermute x27, waiting for transfers between devices, shifted(): lax.ppermute(array, axis, [(k, (k + step) % size) for k in range(size)])  64 us
    ppermute x27, starting transfers between devices, shifted(): lax.ppermute(array, axis, [(k, (k + step) % size) for k in range(size)])  23.9 us
    all_to_all x1, blocking collectives, local(): got = lax.all_to_all(sent, ('y', 'z'), 0, 0, tiled=True)  21.3 us
    pallas_call x2, Pallas kernels, band_product(): pl.pallas_call(band_kernel, out_shape=jax.ShapeDtypeStruct((count, width)...  8.77 us
    pallas_call x1, Pallas kernels, near_product(): pl.pallas_call(near_kernel, out_shape=jax.ShapeDtypeStruct((rows, width),...  6.31 us
    pallas_call x1, Pallas kernels, first_product(): pl.pallas_call(first_kernel, out_shape=jax.ShapeDtypeStruct((width, 8 * r...  4.41 us
    pallas_call x1, Pallas kernels, last_product(): pl.pallas_call(last_kernel, out_shape=(jax.ShapeDtypeStruct(own, jnp.floa...  4.36 us
    squeeze x1, other arithmetic, local(): moments(event_counts, latent_mean, latent_var).astype(jnp.bfloat16)[0]  4.29 us
  transfers between devices with their start and end apart: 27, of which 11 were waited for; matrix products, arithmetic and copies ran while one was open for 5% of the time, Pallas kernels for 10%

profile of v4, /device:TPU:32, one launch (start us, length us, event | category | flops | bytes accessed | tf_op | source)
XLA Modules:
  0.0 154.5 jit_solution(4856867575398925253)
XLA Ops:
  0.6 1.8 %split_columns.1 = (bf16[64,512]{1,0:T(8,128)(2,1)}, bf16[64,512]{1,0:T(8,128)(2,1)}) custom-call(s32[4]{0:T(128)} %pad_add_fusion.first_ref.place_ref, bf16[64,1024]{1,0:T(8,128)(2,1)} %basis_ref.1), custom_call_target="tpu_custom_call" | custom-call | tf_op jit(solution)/shard_map/split_columns/pallas_call | solution.py:94
  2.4 1.5 collective-permute-start
  3.9 4.3 %fusion.8.refs_0_ = bf16[64,4096]{1,0:T(8,128)(2,1)S(1)} fusion(s32[1,64,4096]{2,1,0:T(8,128)} %param.8, f32[1,64,4096]{2,1,0:T(8,128)} %param.10, f32[1,64,4096]{2,1,0:T(8,128)} %param.9), kind=kLoop, calls=%fused_computation.15 | loop fusion | flops 17563648 | bytes 3670016 | tf_op jit(solution)/shard_map/squeeze | solution.py:311
  8.2 3.3 %collective-permute-start.3 = (bf16[128,512]{1,0:T(8,128)(2,1)S(1)}, bf16[128,512]{1,0:T(8,128)(2,1)S(1)}, u32[]{:S(2)}, u32[]{:S(2)}) collective-permute-start(bf16[128,512]{1,0:T(8,128)(2,1)S(1)} %maximum_select_fusion), channel_id=1, source_target_pairs={{0,32},{16,48},{32,0},{48,16},{1,33},{17,49},{33,1},{49,17},{2,34}... | collective-permute-start | bytes 393224 | tf_op jit(solution)/shard_map/ppermute | solution.py:73
  11.5 1.1 collective-permute-start.2
  12.6 1.0 collective-permute-start.1
  15.2 2.1 %collective-permute-start.7 = (bf16[64,4096]{1,0:T(8,128)(2,1)S(1)}, bf16[64,4096]{1,0:T(8,128)(2,1)S(1)}, u32[]{:S(2)}, u32[]{:S(2)}) collective-permute-start(bf16[64,4096]{1,0:T(8,128)(2,1)S(1)} %fusion.8.refs_0_), channel_id=1, source_target_pairs={{0,129},{1,0},{128,1},{129,128},{2,131},{3,2},{130,3},{131,130},{4... | collective-permute-start | bytes 1572872 | tf_op jit(solution)/shard_map/ppermute | solution.py:73
  17.9 0.8 collective-permute-done.1
  19.0 1.9 %collective-permute-start.4 = (bf16[4,128,512]{2,1,0:T(8,128)(2,1)S(1)}, bf16[4,128,512]{2,1,0:T(8,128)(2,1)S(1)}, u32[]{:S(2)}, u32[]{:S(2)}) collective-permute-start(bf16[4,128,512]{2,1,0:T(8,128)(2,1)S(1)} %pad_maximum_fusion.refs_8_.refs_2_.refs_4_), channel_id=1, source_target_pairs={{0,2},{2,4},{4,6},{6,8},{8,10},{10,12},{12,14},{14,0},{1,3},{3,5},... | collective-permute-start | bytes 1572872 | tf_op jit(solution)/shard_map/ppermute | solution.py:73
  21.1 6.7 %collective-permute-done.7.refs_6_ = bf16[64,4096]{1,0:T(8,128)(2,1)S(1)} collective-permute-done((bf16[64,4096]{1,0:T(8,128)(2,1)S(1)}, bf16[64,4096]{1,0:T(8,128)(2,1)S(1)}, u32[]{:S(2)}, u32[]{:S(2)}) %collective-permute-start.7) | collective-permute-done | bytes 524320 | tf_op jit(solution)/shard_map/ppermute | solution.py:73
  27.8 2.7 %collective-permute-start.10 = (bf16[64,4096]{1,0:T(8,128)(2,1)S(1)}, bf16[64,4096]{1,0:T(8,128)(2,1)}, u32[]{:S(2)}, u32[]{:S(2)}) collective-permute-start(bf16[64,4096]{1,0:T(8,128)(2,1)S(1)} %fusion.8.refs_0_), channel_id=1, source_target_pairs={{0,128},{1,129},{128,0},{129,1},{2,130},{3,131},{130,2},{131,3},{4... | collective-permute-start | bytes 1572872 | tf_op jit(solution)/shard_map/ppermute | solution.py:73
  30.5 11.5 %collective-permute-done.6.refs_4_ = bf16[64,4096]{1,0:T(8,128)(2,1)S(1)} collective-permute-done((bf16[64,4096]{1,0:T(8,128)(2,1)S(1)}, bf16[64,4096]{1,0:T(8,128)(2,1)S(1)}, u32[]{:S(2)}, u32[]{:S(2)}) %collective-permute-start.6) | collective-permute-done | bytes 524320 | tf_op jit(solution)/shard_map/ppermute | solution.py:73
  42.1 2.0 %collective-permute-start.8 = (bf16[4,128,512]{2,1,0:T(8,128)(2,1)S(1)}, bf16[4,128,512]{2,1,0:T(8,128)(2,1)S(1)}, u32[]{:S(2)}, u32[]{:S(2)}) collective-permute-start(bf16[4,128,512]{2,1,0:T(8,128)(2,1)S(1)} %collective-permute-done.4.refs_9_.refs_3_.refs_5_), channel_id=1, source_target_pairs={{0,2},{2,4},{4,6},{6,8},{8,10},{10,12},{12,14},{14,0},{1,3},{3,5},... | collective-permute-start | bytes 1572872 | tf_op jit(solution)/shard_map/ppermute | solution.py:73
  46.5 5.5 %collective-permute-done.8.refs_11_.refs_5_.refs_7_ = bf16[4,128,512]{2,1,0:T(8,128)(2,1)S(1)} collective-permute-done((bf16[4,128,512]{2,1,0:T(8,128)(2,1)S(1)}, bf16[4,128,512]{2,1,0:T(8,128)(2,1)S(1)}, u32[]{:S(2)}, u32[]{:S(2)}) %collective-permute-start.8) | collective-permute-done | bytes 524320 | tf_op jit(solution)/shard_map/ppermute | solution.py:73
  52.0 1.5 collective-permute-done.9.refs_12_.refs_6_.refs_8_
  53.5 0.8 broadcast_in_dim.35.sy_ref
  54.3 2.8 %collective-permute-start.12 = (bf16[4,128,512]{2,1,0:T(8,128)(2,1)S(1)}, bf16[4,128,512]{2,1,0:T(8,128)(2,1)S(1)}, u32[]{:S(2)}, u32[]{:S(2)}) collective-permute-start(bf16[4,128,512]{2,1,0:T(8,128)(2,1)S(1)} %collective-permute-done.8.refs_11_.refs_5_.refs_7_), channel_id=1, source_target_pairs={{0,2},{2,4},{4,6},{6,8},{8,10},{10,12},{12,14},{14,0},{1,3},{3,5},... | collective-permute-start | bytes 1572872 | tf_op jit(solution)/shard_map/ppermute | solution.py:73
  57.2 6.9 %collective-permute-done.12.refs_13_.refs_7_.refs_9_ = bf16[4,128,512]{2,1,0:T(8,128)(2,1)S(1)} collective-permute-done((bf16[4,128,512]{2,1,0:T(8,128)(2,1)S(1)}, bf16[4,128,512]{2,1,0:T(8,128)(2,1)S(1)}, u32[]{:S(2)}, u32[]{:S(2)}) %collective-permute-start.12) | collective-permute-done | bytes 524320 | tf_op jit(solution)/shard_map/ppermute | solution.py:73
  64.1 5.9 %collective-permute-done.13.refs_14_.refs_8_.refs_10_ = bf16[4,128,512]{2,1,0:T(8,128)(2,1)S(1)} collective-permute-done((bf16[4,128,512]{2,1,0:T(8,128)(2,1)S(1)}, bf16[4,128,512]{2,1,0:T(8,128)(2,1)S(1)}, u32[]{:S(2)}, u32[]{:S(2)}) %collective-permute-start.13) | collective-permute-done | bytes 524320 | tf_op jit(solution)/shard_map/ppermute | solution.py:73
  71.5 2.1 %collective-permute-start.17 = (bf16[2,128,512]{2,1,0:T(8,128)(2,1)}, bf16[2,128,512]{2,1,0:T(8,128)(2,1)S(1)}, u32[]{:S(2)}, u32[]{:S(2)}) collective-permute-start(bf16[2,128,512]{2,1,0:T(8,128)(2,1)} %slice.6), channel_id=1, source_target_pairs={{0,2},{2,4},{4,6},{6,8},{8,10},{10,12},{12,14},{14,0},{1,3},{3,5},... | collective-permute-start | bytes 786440 | tf_op jit(solution)/shard_map/ppermute | solution.py:73
  73.6 6.3 %near_product.1.refs_10_ = f32[512,512]{1,0:T(8,128)} custom-call(s32[4]{0:T(128)} %pad_add_fusion.first_ref.place_ref, bf16[64,4096]{1,0:T(8,128)(2,1)} %copy-done.7, bf16[64,4096]{1,0:T(8,128)(2,1)} %collective-permute-done.11.refs_1_, bf16[64,4096]{1,0:T(8,128)(2,1)} %collective-permute-done.10.refs_2_, bf16[64,4096]{1,0:T(8,128)(2,1)} %collective-permute-done.14.refs_3_, ...), custom_call_target="tpu_custom_call" | custom-call | flops 1879048192 | bytes 8388608 | tf_op jit(solution)/shard_map/near_product/pallas_call | solution.py:134
  81.4 4.4 %first_product.1 = bf16[512,512]{1,0:T(8,128)(2,1)} custom-call(f32[8,4]{1,0:T(8,128)} %broadcast_select_fusion.mix_ref, s32[4]{0:T(128)} %pad_add_fusion.first_ref.place_ref, bf16[64,4096]{1,0:T(8,128)(2,1)} %copy-done.7, bf16[64,4096]{1,0:T(8,128)(2,1)} %collective-permute-done.11.refs_1_, bf16[64,4096]{1,0:T(8,128)(2,1)} %collective-permute-done.10.refs_2_, ...), custom_call_target="tpu_custom_call" | custom-call | flops 268435456 | bytes 4194304 | tf_op jit(solution)/shard_map/first_product/pallas_call | solution.py:171
  85.8 21.3 %all_to_all.5 = bf16[32,16,512]{2,1,0:T(8,128)(2,1)S(1)} all-to-all(bf16[32,16,512]{2,1,0:T(8,128)(2,1)} %bitcast.33), channel_id=1, replica_groups=mesh['hi'=2,'core'=2,'y'=4,'z'=8,'lo'=2] {'y','z'}, dimensions={0} | all-to-all | bytes 1048576 | tf_op jit(solution)/shard_map/all_to_all | solution.py:351
  107.9 2.0 %collective-permute-start.22 = (bf16[4,16,4096]{2,1,0:T(8,128)(2,1)S(1)}, bf16[4,16,4096]{2,1,0:T(8,128)(2,1)S(1)}, u32[]{:S(2)}, u32[]{:S(2)}) collective-permute-start(bf16[4,16,4096]{2,1,0:T(8,128)(2,1)S(1)} %reshape.132.refs_0_), channel_id=1, source_target_pairs={{0,1},{1,128},{128,129},{129,0},{2,3},{3,130},{130,131},{131,2},{4... | collective-permute-start | bytes 1572872 | tf_op jit(solution)/shard_map/ppermute | solution.py:73
  109.9 7.8 %collective-permute-done.24.refs_2_ = bf16[4,16,4096]{2,1,0:T(8,128)(2,1)S(1)} collective-permute-done((bf16[4,16,4096]{2,1,0:T(8,128)(2,1)S(1)}, bf16[4,16,4096]{2,1,0:T(8,128)(2,1)S(1)}, u32[]{:S(2)}, u32[]{:S(2)}) %collective-permute-start.24) | collective-permute-done | bytes 524320 | tf_op jit(solution)/shard_map/ppermute | solution.py:73
  117.7 8.0 %collective-permute-done.22.refs_0_ = bf16[4,16,4096]{2,1,0:T(8,128)(2,1)S(1)} collective-permute-done((bf16[4,16,4096]{2,1,0:T(8,128)(2,1)S(1)}, bf16[4,16,4096]{2,1,0:T(8,128)(2,1)S(1)}, u32[]{:S(2)}, u32[]{:S(2)}) %collective-permute-start.22) | collective-permute-done | bytes 524320 | tf_op jit(solution)/shard_map/ppermute | solution.py:73
  126.3 3.9 %band_product.2.refs_11_ = f32[128,512]{1,0:T(8,128)} custom-call(s32[4]{0:T(128)} %pad_add_fusion.first_ref.place_ref, bf16[4,16,4096]{2,1,0:T(8,128)(2,1)} %copy-done.14, bf16[4,16,4096]{2,1,0:T(8,128)(2,1)} %collective-permute-done.21.refs_1_, bf16[4,128,512]{2,1,0:T(8,128)(2,1)} %copy-done, bf16[4,128,512]{2,1,0:T(8,128)(2,1)} %copy-done.4, ...), custom_call_target="tpu_custom_call" | custom-call | flops 536870912 | bytes 6291456 | tf_op jit(solution)/shard_map/band_product/pallas_call | solution.py:202
  131.0 4.9 %band_product.3.refs_12_ = f32[256,512]{1,0:T(8,128)} custom-call(s32[4]{0:T(128)} %pad_add_fusion.first_ref.place_ref, bf16[4,16,4096]{2,1,0:T(8,128)(2,1)} %copy-done.18, bf16[4,16,4096]{2,1,0:T(8,128)(2,1)} %collective-permute-done.23.refs_1_, bf16[4,16,4096]{2,1,0:T(8,128)(2,1)} %copy-done.17, bf16[4,16,4096]{2,1,0:T(8,128)(2,1)} %copy-done.19, ...), custom_call_target="tpu_custom_call" | custom-call | flops 1073741824 | bytes 6291456 | tf_op jit(solution)/shard_map/band_product/pallas_call | solution.py:202
  135.9 0.8 copy-done.16
  136.7 4.4 %last_product.1 = (f32[4,64,512]{2,1,0:T(8,128)}, bf16[4,64,512]{2,1,0:T(8,128)(2,1)}) custom-call(s32[4]{0:T(128)} %pad_add_fusion.first_ref.place_ref, s32[8]{0:T(128)} %get-tuple-element.58.slice_ref, bf16[4,16,4096]{2,1,0:T(8,128)(2,1)} %copy-done.15, bf16[4,16,4096]{2,1,0:T(8,128)(2,1)} %copy-done.16, bf16[4,128,512]{2,1,0:T(8,128)(2,1)} %copy-done, ...), custom_call_target="tpu_custom_call" | custom-call | flops 536870912 | bytes 6291456 | tf_op jit(solution)/shard_map/last_product/pallas_call | solution.py:240
  141.1 8.7 %collective-permute-done.26.got_ref = bf16[4,64,512]{2,1,0:T(8,128)(2,1)S(1)} collective-permute-done((bf16[4,64,512]{2,1,0:T(8,128)(2,1)}, bf16[4,64,512]{2,1,0:T(8,128)(2,1)S(1)}, u32[]{:S(2)}, u32[]{:S(2)}) %collective-permute-start.26) | collective-permute-done | bytes 262176 | tf_op jit(solution)/shard_map/ppermute | solution.py:73
  150.5 4.0 %whitened_gradient.1 = f32[64,4,1024]{2,1,0:T(4,128)} custom-call(s32[4]{0:T(128)} %pad_add_fusion.first_ref.place_ref, f32[4,64,512]{2,1,0:T(8,128)} %get-tuple-element.53.kept_ref, bf16[4,64,512]{2,1,0:T(8,128)(2,1)} %copy-done.20, f32[1,1024]{1,0:T(1,128)} %bitcast.40, f32[64,128]{1,0:T(8,128)} %broadcast_in_dim.35.sy_ref, f32[64,4,1024]{2,1,0:T(4,128)} %bitcast.35), custom_call_target="tpu_custom_call" | custom-call | tf_op jit(solution)/shard_map/whitened_gradient/pallas_call | solution.py:288
  (102 shorter events, 10.8 us)
Async XLA Ops:
  2.4 5.8 %collective-permute-start = (bf16[64,512]{1,0:T(8,128)(2,1)}, bf16[64,512]{1,0:T(8,128)(2,1)S(1)}, u32[]{:S(2)}, u32[]{:S(2)}) collective-permute-start(bf16[64,512]{1,0:T(8,128)(2,1)} %get-tuple-element.32), channel_id=1, source_target_pairs={{0,1},{1,0},{2,3},{3,2},{4,5},{5,4},{6,7},{7,6},{8,9},{9,8},{10,11... | collective-permute-start | bytes 196616 | tf_op jit(solution)/shard_map/ppermute | solution.py:73
  8.2 9.1 %collective-permute-start.3 = (bf16[128,512]{1,0:T(8,128)(2,1)S(1)}, bf16[128,512]{1,0:T(8,128)(2,1)S(1)}, u32[]{:S(2)}, u32[]{:S(2)}) collective-permute-start(bf16[128,512]{1,0:T(8,128)(2,1)S(1)} %maximum_select_fusion), channel_id=1, source_target_pairs={{0,32},{16,48},{32,0},{48,16},{1,33},{17,49},{33,1},{49,17},{2,34}... | collective-permute-start | bytes 393224 | tf_op jit(solution)/shard_map/ppermute | solution.py:73
  11.5 6.4 %collective-permute-start.2 = (bf16[128,512]{1,0:T(8,128)(2,1)S(1)}, bf16[128,512]{1,0:T(8,128)(2,1)S(1)}, u32[]{:S(2)}, u32[]{:S(2)}) collective-permute-start(bf16[128,512]{1,0:T(8,128)(2,1)S(1)} %maximum_select_fusion), channel_id=1, source_target_pairs={{0,48},{16,0},{32,16},{48,32},{1,49},{17,1},{33,17},{49,33},{2,50}... | collective-permute-start | bytes 393224 | tf_op jit(solution)/shard_map/ppermute | solution.py:73
  12.6 6.2 %collective-permute-start.1 = (bf16[128,512]{1,0:T(8,128)(2,1)S(1)}, bf16[128,512]{1,0:T(8,128)(2,1)S(1)}, u32[]{:S(2)}, u32[]{:S(2)}) collective-permute-start(bf16[128,512]{1,0:T(8,128)(2,1)S(1)} %maximum_select_fusion), channel_id=1, source_target_pairs={{0,16},{16,32},{32,48},{48,0},{1,17},{17,33},{33,49},{49,1},{2,18}... | collective-permute-start | bytes 393224 | tf_op jit(solution)/shard_map/ppermute | solution.py:73
  15.2 12.5 %collective-permute-start.7 = (bf16[64,4096]{1,0:T(8,128)(2,1)S(1)}, bf16[64,4096]{1,0:T(8,128)(2,1)S(1)}, u32[]{:S(2)}, u32[]{:S(2)}) collective-permute-start(bf16[64,4096]{1,0:T(8,128)(2,1)S(1)} %fusion.8.refs_0_), channel_id=1, source_target_pairs={{0,129},{1,0},{128,1},{129,128},{2,131},{3,2},{130,3},{131,130},{4... | collective-permute-start | bytes 1572872 | tf_op jit(solution)/shard_map/ppermute | solution.py:73
  17.3 24.7 %collective-permute-start.6 = (bf16[64,4096]{1,0:T(8,128)(2,1)S(1)}, bf16[64,4096]{1,0:T(8,128)(2,1)S(1)}, u32[]{:S(2)}, u32[]{:S(2)}) collective-permute-start(bf16[64,4096]{1,0:T(8,128)(2,1)S(1)} %fusion.8.refs_0_), channel_id=1, source_target_pairs={{0,1},{1,128},{128,129},{129,0},{2,3},{3,130},{130,131},{131,2},{4... | collective-permute-start | bytes 1572872 | tf_op jit(solution)/shard_map/ppermute | solution.py:73
  18.8 52.7 %copy-start = (bf16[4,128,512]{2,1,0:T(8,128)(2,1)}, bf16[4,128,512]{2,1,0:T(8,128)(2,1)S(1)}, u32[]{:S(2)}) copy-start(bf16[4,128,512]{2,1,0:T(8,128)(2,1)S(1)} %pad_maximum_fusion.refs_8_.refs_2_.refs_4_) | copy-start | bytes 1572868
  18.8 23.2 %collective-permute-start.5 = (bf16[4,128,512]{2,1,0:T(8,128)(2,1)S(1)}, bf16[4,128,512]{2,1,0:T(8,128)(2,1)S(1)}, u32[]{:S(2)}, u32[]{:S(2)}) collective-permute-start(bf16[4,128,512]{2,1,0:T(8,128)(2,1)S(1)} %pad_maximum_fusion.refs_8_.refs_2_.refs_4_), channel_id=1, source_target_pairs={{0,14},{2,0},{4,2},{6,4},{8,6},{10,8},{12,10},{14,12},{1,15},{3,1}... | collective-permute-start | bytes 1572872 | tf_op jit(solution)/shard_map/ppermute | solution.py:73
  19.0 23.0 %collective-permute-start.4 = (bf16[4,128,512]{2,1,0:T(8,128)(2,1)S(1)}, bf16[4,128,512]{2,1,0:T(8,128)(2,1)S(1)}, u32[]{:S(2)}, u32[]{:S(2)}) collective-permute-start(bf16[4,128,512]{2,1,0:T(8,128)(2,1)S(1)} %pad_maximum_fusion.refs_8_.refs_2_.refs_4_), channel_id=1, source_target_pairs={{0,2},{2,4},{4,6},{6,8},{8,10},{10,12},{12,14},{14,0},{1,3},{3,5},... | collective-permute-start | bytes 1572872 | tf_op jit(solution)/shard_map/ppermute | solution.py:73
  21.0 25.0 %collective-permute-start.11 = (bf16[64,4096]{1,0:T(8,128)(2,1)S(1)}, bf16[64,4096]{1,0:T(8,128)(2,1)}, u32[]{:S(2)}, u32[]{:S(2)}) collective-permute-start(bf16[64,4096]{1,0:T(8,128)(2,1)S(1)} %fusion.8.refs_0_), channel_id=1, source_target_pairs={{0,64},{64,0},{1,65},{65,1},{2,66},{66,2},{3,67},{67,3},{4,68},{68... | collective-permute-start | bytes 1572872 | tf_op jit(solution)/shard_map/ppermute | solution.py:73
  27.8 18.8 %collective-permute-start.10 = (bf16[64,4096]{1,0:T(8,128)(2,1)S(1)}, bf16[64,4096]{1,0:T(8,128)(2,1)}, u32[]{:S(2)}, u32[]{:S(2)}) collective-permute-start(bf16[64,4096]{1,0:T(8,128)(2,1)S(1)} %fusion.8.refs_0_), channel_id=1, source_target_pairs={{0,128},{1,129},{128,0},{129,1},{2,130},{3,131},{130,2},{131,3},{4... | collective-permute-start | bytes 1572872 | tf_op jit(solution)/shard_map/ppermute | solution.py:73
  42.0 31.6 %copy-start.3 = (bf16[4,128,512]{2,1,0:T(8,128)(2,1)}, bf16[4,128,512]{2,1,0:T(8,128)(2,1)S(1)}, u32[]{:S(2)}) copy-start(bf16[4,128,512]{2,1,0:T(8,128)(2,1)S(1)} %collective-permute-done.5.refs_10_.refs_4_.refs_6_) | copy-start | bytes 1572868
  42.0 31.6 %copy-start.4 = (bf16[4,128,512]{2,1,0:T(8,128)(2,1)}, bf16[4,128,512]{2,1,0:T(8,128)(2,1)S(1)}, u32[]{:S(2)}) copy-start(bf16[4,128,512]{2,1,0:T(8,128)(2,1)S(1)} %collective-permute-done.4.refs_9_.refs_3_.refs_5_) | copy-start | bytes 1572868
  42.1 10.0 %collective-permute-start.8 = (bf16[4,128,512]{2,1,0:T(8,128)(2,1)S(1)}, bf16[4,128,512]{2,1,0:T(8,128)(2,1)S(1)}, u32[]{:S(2)}, u32[]{:S(2)}) collective-permute-start(bf16[4,128,512]{2,1,0:T(8,128)(2,1)S(1)} %collective-permute-done.4.refs_9_.refs_3_.refs_5_), channel_id=1, source_target_pairs={{0,2},{2,4},{4,6},{6,8},{8,10},{10,12},{12,14},{14,0},{1,3},{3,5},... | collective-permute-start | bytes 1572872 | tf_op jit(solution)/shard_map/ppermute | solution.py:73
  44.0 9.5 %collective-permute-start.9 = (bf16[4,128,512]{2,1,0:T(8,128)(2,1)S(1)}, bf16[4,128,512]{2,1,0:T(8,128)(2,1)S(1)}, u32[]{:S(2)}, u32[]{:S(2)}) collective-permute-start(bf16[4,128,512]{2,1,0:T(8,128)(2,1)S(1)} %collective-permute-done.5.refs_10_.refs_4_.refs_6_), channel_id=1, source_target_pairs={{0,14},{2,0},{4,2},{6,4},{8,6},{10,8},{12,10},{14,12},{1,15},{3,1}... | collective-permute-start | bytes 1572872 | tf_op jit(solution)/shard_map/ppermute | solution.py:73
  46.0 11.1 %collective-permute-start.15 = (bf16[64,4096]{1,0:T(8,128)(2,1)}, bf16[64,4096]{1,0:T(8,128)(2,1)S(1)}, u32[]{:S(2)}, u32[]{:S(2)}) collective-permute-start(bf16[64,4096]{1,0:T(8,128)(2,1)} %copy-done.11), channel_id=1, source_target_pairs={{0,64},{64,0},{1,65},{65,1},{2,66},{66,2},{3,67},{67,3},{4,68},{68... | collective-permute-start | bytes 1572872 | tf_op jit(solution)/shard_map/ppermute | solution.py:73
  46.0 11.2 %collective-permute-start.16 = (bf16[64,4096]{1,0:T(8,128)(2,1)}, bf16[64,4096]{1,0:T(8,128)(2,1)S(1)}, u32[]{:S(2)}, u32[]{:S(2)}) collective-permute-start(bf16[64,4096]{1,0:T(8,128)(2,1)} %copy-done.10), channel_id=1, source_target_pairs={{0,64},{64,0},{1,65},{65,1},{2,66},{66,2},{3,67},{67,3},{4,68},{68... | collective-permute-start | bytes 1572872 | tf_op jit(solution)/shard_map/ppermute | solution.py:73
  52.0 21.6 %copy-start.5 = (bf16[4,128,512]{2,1,0:T(8,128)(2,1)}, bf16[4,128,512]{2,1,0:T(8,128)(2,1)S(1)}, u32[]{:S(2)}) copy-start(bf16[4,128,512]{2,1,0:T(8,128)(2,1)S(1)} %collective-permute-done.8.refs_11_.refs_5_.refs_7_) | copy-start | bytes 1572868
  53.5 20.1 %copy-start.6 = (bf16[4,128,512]{2,1,0:T(8,128)(2,1)}, bf16[4,128,512]{2,1,0:T(8,128)(2,1)S(1)}, u32[]{:S(2)}) copy-start(bf16[4,128,512]{2,1,0:T(8,128)(2,1)S(1)} %collective-permute-done.9.refs_12_.refs_6_.refs_8_) | copy-start | bytes 1572868
  54.3 9.8 %collective-permute-start.12 = (bf16[4,128,512]{2,1,0:T(8,128)(2,1)S(1)}, bf16[4,128,512]{2,1,0:T(8,128)(2,1)S(1)}, u32[]{:S(2)}, u32[]{:S(2)}) collective-permute-start(bf16[4,128,512]{2,1,0:T(8,128)(2,1)S(1)} %collective-permute-done.8.refs_11_.refs_5_.refs_7_), channel_id=1, source_target_pairs={{0,2},{2,4},{4,6},{6,8},{8,10},{10,12},{12,14},{14,0},{1,3},{3,5},... | collective-permute-start | bytes 1572872 | tf_op jit(solution)/shard_map/ppermute | solution.py:73
  57.1 12.8 %collective-permute-start.13 = (bf16[4,128,512]{2,1,0:T(8,128)(2,1)S(1)}, bf16[4,128,512]{2,1,0:T(8,128)(2,1)S(1)}, u32[]{:S(2)}, u32[]{:S(2)}) collective-permute-start(bf16[4,128,512]{2,1,0:T(8,128)(2,1)S(1)} %collective-permute-done.9.refs_12_.refs_6_.refs_8_), channel_id=1, source_target_pairs={{0,14},{2,0},{4,2},{6,4},{8,6},{10,8},{12,10},{14,12},{1,15},{3,1}... | collective-permute-start | bytes 1572872 | tf_op jit(solution)/shard_map/ppermute | solution.py:73
  57.1 12.8 %collective-permute-start.14 = (bf16[64,4096]{1,0:T(8,128)(2,1)}, bf16[64,4096]{1,0:T(8,128)(2,1)}, u32[]{:S(2)}, u32[]{:S(2)}) collective-permute-start(bf16[64,4096]{1,0:T(8,128)(2,1)} %collective-permute-done.10.refs_2_), channel_id=1, source_target_pairs={{0,64},{64,0},{1,65},{65,1},{2,66},{66,2},{3,67},{67,3},{4,68},{68... | collective-permute-start | bytes 1572872 | tf_op jit(solution)/shard_map/ppermute | solution.py:73
  71.5 8.4 %collective-permute-start.18 = (bf16[2,128,512]{2,1,0:T(8,128)(2,1)}, bf16[2,128,512]{2,1,0:T(8,128)(2,1)S(1)}, u32[]{:S(2)}, u32[]{:S(2)}) collective-permute-start(bf16[2,128,512]{2,1,0:T(8,128)(2,1)} %slice.7), channel_id=1, source_target_pairs={{0,14},{2,0},{4,2},{6,4},{8,6},{10,8},{12,10},{14,12},{1,15},{3,1}... | collective-permute-start | bytes 786440 | tf_op jit(solution)/shard_map/ppermute | solution.py:73
  71.5 8.4 %collective-permute-start.17 = (bf16[2,128,512]{2,1,0:T(8,128)(2,1)}, bf16[2,128,512]{2,1,0:T(8,128)(2,1)S(1)}, u32[]{:S(2)}, u32[]{:S(2)}) collective-permute-start(bf16[2,128,512]{2,1,0:T(8,128)(2,1)} %slice.6), channel_id=1, source_target_pairs={{0,2},{2,4},{4,6},{6,8},{8,10},{10,12},{12,14},{14,0},{1,3},{3,5},... | collective-permute-start | bytes 786440 | tf_op jit(solution)/shard_map/ppermute | solution.py:73
  107.8 9.9 %collective-permute-start.24 = (bf16[4,16,4096]{2,1,0:T(8,128)(2,1)S(1)}, bf16[4,16,4096]{2,1,0:T(8,128)(2,1)S(1)}, u32[]{:S(2)}, u32[]{:S(2)}) collective-permute-start(bf16[4,16,4096]{2,1,0:T(8,128)(2,1)S(1)} %reshape.132.refs_0_), channel_id=1, source_target_pairs={{0,129},{1,0},{128,1},{129,128},{2,131},{3,2},{130,3},{131,130},{4... | collective-permute-start | bytes 1572872 | tf_op jit(solution)/shard_map/ppermute | solution.py:73
  107.9 17.9 %collective-permute-start.22 = (bf16[4,16,4096]{2,1,0:T(8,128)(2,1)S(1)}, bf16[4,16,4096]{2,1,0:T(8,128)(2,1)S(1)}, u32[]{:S(2)}, u32[]{:S(2)}) collective-permute-start(bf16[4,16,4096]{2,1,0:T(8,128)(2,1)S(1)} %reshape.132.refs_0_), channel_id=1, source_target_pairs={{0,1},{1,128},{128,129},{129,0},{2,3},{3,130},{130,131},{131,2},{4... | collective-permute-start | bytes 1572872 | tf_op jit(solution)/shard_map/ppermute | solution.py:73
  109.9 15.8 %collective-permute-start.19 = (bf16[4,16,4096]{2,1,0:T(8,128)(2,1)S(1)}, bf16[4,16,4096]{2,1,0:T(8,128)(2,1)S(1)}, u32[]{:S(2)}, u32[]{:S(2)}) collective-permute-start(bf16[4,16,4096]{2,1,0:T(8,128)(2,1)S(1)} %reshape.132.refs_0_), channel_id=1, source_target_pairs={{0,128},{1,129},{128,0},{129,1},{2,130},{3,131},{130,2},{131,3},{4... | collective-permute-start | bytes 1572872 | tf_op jit(solution)/shard_map/ppermute | solution.py:73
  109.9 16.4 %collective-permute-start.21 = (bf16[4,16,4096]{2,1,0:T(8,128)(2,1)S(1)}, bf16[4,16,4096]{2,1,0:T(8,128)(2,1)}, u32[]{:S(2)}, u32[]{:S(2)}) collective-permute-start(bf16[4,16,4096]{2,1,0:T(8,128)(2,1)S(1)} %reshape.132.refs_0_), channel_id=1, source_target_pairs={{0,64},{64,0},{1,65},{65,1},{2,66},{66,2},{3,67},{67,3},{4,68},{68... | collective-permute-start | bytes 1572872 | tf_op jit(solution)/shard_map/ppermute | solution.py:73
  117.7 12.5 %collective-permute-start.25 = (bf16[4,16,4096]{2,1,0:T(8,128)(2,1)S(1)}, bf16[4,16,4096]{2,1,0:T(8,128)(2,1)S(1)}, u32[]{:S(2)}, u32[]{:S(2)}) collective-permute-start(bf16[4,16,4096]{2,1,0:T(8,128)(2,1)S(1)} %collective-permute-done.24.refs_2_), channel_id=1, source_target_pairs={{0,64},{64,0},{1,65},{65,1},{2,66},{66,2},{3,67},{67,3},{4,68},{68... | collective-permute-start | bytes 1572872 | tf_op jit(solution)/shard_map/ppermute | solution.py:73
  125.7 4.5 %collective-permute-start.23 = (bf16[4,16,4096]{2,1,0:T(8,128)(2,1)S(1)}, bf16[4,16,4096]{2,1,0:T(8,128)(2,1)}, u32[]{:S(2)}, u32[]{:S(2)}) collective-permute-start(bf16[4,16,4096]{2,1,0:T(8,128)(2,1)S(1)} %collective-permute-done.22.refs_0_), channel_id=1, source_target_pairs={{0,64},{64,0},{1,65},{65,1},{2,66},{66,2},{3,67},{67,3},{4,68},{68... | collective-permute-start | bytes 1572872 | tf_op jit(solution)/shard_map/ppermute | solution.py:73
  125.7 10.1 %collective-permute-start.20 = (bf16[4,16,4096]{2,1,0:T(8,128)(2,1)S(1)}, bf16[4,16,4096]{2,1,0:T(8,128)(2,1)S(1)}, u32[]{:S(2)}, u32[]{:S(2)}) collective-permute-start(bf16[4,16,4096]{2,1,0:T(8,128)(2,1)S(1)} %collective-permute-done.19.refs_0_), channel_id=1, source_target_pairs={{0,64},{64,0},{1,65},{65,1},{2,66},{66,2},{3,67},{67,3},{4,68},{68... | collective-permute-start | bytes 1572872 | tf_op jit(solution)/shard_map/ppermute | solution.py:73
  141.0 8.7 %collective-permute-start.26 = (bf16[4,64,512]{2,1,0:T(8,128)(2,1)}, bf16[4,64,512]{2,1,0:T(8,128)(2,1)S(1)}, u32[]{:S(2)}, u32[]{:S(2)}) collective-permute-start(bf16[4,64,512]{2,1,0:T(8,128)(2,1)} %get-tuple-element.54), channel_id=1, source_target_pairs={{0,1},{1,0},{2,3},{3,2},{4,5},{5,4},{6,7},{7,6},{8,9},{9,8},{10,11... | collective-permute-start | bytes 786440 | tf_op jit(solution)/shard_map/ppermute | solution.py:73
  (18 other events, 125.8 us)

commit v5 on v4

--- a/solution.py
+++ b/solution.py
@@ -26,6 +26,7 @@
     0.3936193231522412,
     0.019953242059045913,
 )
+GRANT = 20 << 20
 VMEM = pl.BlockSpec(memory_space=pltpu.VMEM)
 SMEM = pl.BlockSpec(memory_space=pltpu.SMEM)
 
@@ -96,6 +97,7 @@
         out_shape=(half, half),
         in_specs=[SMEM, VMEM],
         out_specs=(VMEM, VMEM),
+        compiler_params=pltpu.CompilerParams(vmem_limit_bytes=GRANT),
         name="split_columns",
     )(place, basis)
 
@@ -136,6 +138,7 @@
         out_shape=jax.ShapeDtypeStruct((rows, width), jnp.float32),
         in_specs=[SMEM] + [VMEM] * 15,
         out_specs=VMEM,
+        compiler_params=pltpu.CompilerParams(vmem_limit_bytes=GRANT),
         cost_estimate=pl.CostEstimate(
             flops=2 * rows * 3584 * width, bytes_accessed=8 << 20, transcendentals=0
         ),
@@ -177,6 +180,7 @@
             pltpu.VMEM((8 * rows, width), jnp.float32),
             pltpu.VMEM((2 * rows, width), jnp.float32),
         ],
+        compiler_params=pltpu.CompilerParams(vmem_limit_bytes=GRANT),
         cost_estimate=pl.CostEstimate(
             flops=2 * 8 * rows * 512 * width, bytes_accessed=4 << 20, transcendentals=0
         ),
@@ -184,114 +188,102 @@
     )(mix, place, *fields, *pieces, near)
 
 
-def load_bands(fields, span):
-    times = fields[0].shape[0]
-    return jnp.concatenate([ref[a, :, span] for a in range(times) for ref in fields], axis=0)
-
-
-def band_kernel(place_ref, *refs):
-    fields, pieces, acc_ref = refs[:-10], refs[-10:-1], refs[-1]
+def load_bands(fields, which, span):
+    return jnp.concatenate([ref[which, :, span] for ref in fields], axis=0)
+
+
+def natural_rows(place_ref, slice_ref, acc_ref, rows_ref):
+    times, group = 4, 8
+    for b in range(8):
+        half_of = place_ref[0] if b < 4 else 1 - place_ref[0]
+        to = pl.multiple_of((slice_ref[b] * 2 + half_of) * group, group)
+        for a in range(times):
+            first = (b * times + a) * group
+            rows_ref[a, pl.ds(to, group), :] = acc_ref[first : first + group, :]
+
+
+def moved_columns(half):
+    source = lax.broadcasted_iota(jnp.int32, (128, 256), 0)
+    target = lax.broadcasted_iota(jnp.int32, (128, 256), 1)
+    return (target == (source // 8) * 16 + half * 8 + lax.rem(source, 8)).astype(jnp.float32)
+
+
+def sent_kernel(place_ref, slice_ref, *refs):
+    fields, pieces, (sent_ref, acc_ref, rows_ref) = refs[:8], refs[8:17], refs[17:]
     acc_ref[...] = jnp.zeros_like(acc_ref)
-    product_of(place_ref, lambda span: load_bands(fields, span), NEAR + FAR, pieces, acc_ref)
-
-
-def band_product(place, fields, pieces):
-    times, rows, total = fields[0].shape
+    which = 1 - place_ref[0]
+    product_of(
+        place_ref, lambda span: load_bands(fields, which, span), NEAR + FAR, pieces, acc_ref
+    )
+    natural_rows(place_ref, slice_ref, acc_ref, rows_ref)
+    sent_ref[...] = rows_ref[...].astype(jnp.bfloat16)
+
+
+def kept_kernel(place_ref, slice_ref, *refs):
+    fields, pieces, (sx_ref, sy_ref, white_ref) = refs[:8], refs[8:17], refs[17:20]
+    kept_ref, acc_ref, rows_ref = refs[20:]
+    acc_ref[...] = jnp.zeros_like(acc_ref)
+    lo = place_ref[0]
+    product_of(place_ref, lambda span: load_bands(fields, lo, span), NEAR + FAR, pieces, acc_ref)
+    natural_rows(place_ref, slice_ref, acc_ref, rows_ref)
+    chosen = moved_columns(lo)
+    for block in range(rows_ref.shape[-1] // 128):
+        span = slice(block * 256, block * 256 + 256)
+        scale = sy_ref[:, :1] * sx_ref[:, span]
+        for a in range(rows_ref.shape[0]):
+            moved = jnp.dot(
+                rows_ref[a, :, block * 128 : block * 128 + 128],
+                chosen,
+                precision=lax.Precision.HIGHEST,
+            )
+            kept_ref[a, :, span] = scale * moved - white_ref[:, a, span]
+
+
+def band_products(kernel, name, place, slices, fields, pieces, more, out_shape):
+    _, rows, total = fields[0].shape
     width = pieces[0].shape[-1]
-    count = len(fields) * times * rows
-    return pl.pallas_call(
-        band_kernel,
-        out_shape=jax.ShapeDtypeStruct((count, width), jnp.float32),
-        in_specs=[SMEM] + [VMEM] * (len(fields) + 9),
+    count = len(fields) * rows
+    return pl.pallas_call(
+        kernel,
+        out_shape=out_shape,
+        in_specs=[SMEM, SMEM] + [VMEM] * (17 + len(more)),
         out_specs=VMEM,
+        scratch_shapes=[
+            pltpu.VMEM((count, width), jnp.float32),
+            pltpu.VMEM((4, count // 4, width), jnp.float32),
+        ],
+        compiler_params=pltpu.CompilerParams(vmem_limit_bytes=GRANT),
         cost_estimate=pl.CostEstimate(
             flops=2 * count * total * width, bytes_accessed=6 << 20, transcendentals=0
         ),
-        name="band_product",
-    )(place, *fields, *pieces)
-
-
-def last_kernel(place_ref, slice_ref, *refs):
-    fields, pieces, done = refs[:2], refs[2:11], refs[11:13]
-    kept_ref, sent_ref, acc_ref, tmp_ref = refs[13:]
-    times, rows, _ = fields[0].shape
-    acc_ref[...] = jnp.zeros_like(acc_ref)
-    product_of(place_ref, lambda span: load_bands(fields, span), NEAR + FAR, pieces, acc_ref)
-    lo = place_ref[0]
-    group = rows // 2
-    sources = [(done[0], 2, 0), (acc_ref, 2, 0), (done[1], 4, 0), (done[1], 4, 2)]
-    for a in range(times):
-        for b in range(8):
-            ref, count, first = sources[b // 2]
-            half_of = lo if b < 4 else 1 - lo
-            to = pl.multiple_of((slice_ref[b] * 2 + half_of) * group, group)
-            base = (a * count + first + b % 2) * rows
-            mine = pl.multiple_of(base + lo * group, group)
-            theirs = pl.multiple_of(base + (1 - lo) * group, group)
-            kept_ref[a, pl.ds(to, group), :] = ref[pl.ds(mine, group), :]
-            tmp_ref[pl.ds(to, group), :] = ref[pl.ds(theirs, group), :]
-        sent_ref[a] = tmp_ref[...].astype(jnp.bfloat16)
-
-
-def last_product(place, slices, fields, pieces, done):
-    times, rows, total = fields[0].shape
-    width = pieces[0].shape[-1]
-    own = (times, 4 * rows, width)
-    return pl.pallas_call(
-        last_kernel,
-        out_shape=(
-            jax.ShapeDtypeStruct(own, jnp.float32),
-            jax.ShapeDtypeStruct(own, jnp.bfloat16),
-        ),
-        in_specs=[SMEM, SMEM] + [VMEM] * 13,
-        out_specs=(VMEM, VMEM),
-        scratch_shapes=[
-            pltpu.VMEM((2 * times * rows, width), jnp.float32),
-            pltpu.VMEM((4 * rows, width), jnp.float32),
-        ],
-        cost_estimate=pl.CostEstimate(
-            flops=4 * times * rows * total * width, bytes_accessed=6 << 20, transcendentals=0
-        ),
-        name="last_product",
-    )(place, slices, *fields, *pieces, *done)
-
-
-def gradient_kernel(place_ref, kept_ref, got_ref, sx_ref, sy_ref, white_ref, out_ref):
-    lo = place_ref[0]
-    source = lax.broadcasted_iota(jnp.int32, (256, 256), 0)
-    target = lax.broadcasted_iota(jnp.int32, (256, 256), 1)
-    within = lax.rem(source, 128)
-    which = jnp.where(source < 128, lo, 1 - lo)
-    chosen = (target == (within // 8) * 16 + which * 8 + lax.rem(within, 8)).astype(jnp.float32)
-    times, rows, half = kept_ref.shape
-    for block in range(half // 128):
-        here = slice(block * 128, block * 128 + 128)
+        name=name,
+    )(place, slices, *fields, *pieces, *more)
+
+
+def gradient_kernel(place_ref, kept_ref, got_ref, sx_ref, sy_ref, out_ref):
+    chosen = moved_columns(1 - place_ref[0]).astype(jnp.bfloat16)
+    for block in range(got_ref.shape[-1] // 128):
         span = slice(block * 256, block * 256 + 256)
-        pair = jnp.concatenate(
-            [
-                jnp.concatenate(
-                    [kept_ref[a, :, here], got_ref[a, :, here].astype(jnp.float32)], axis=1
-                )
-                for a in range(times)
-            ],
-            axis=0,
-        )
-        natural = jnp.dot(pair, chosen, precision=lax.Precision.HIGHEST)
-        for a in range(times):
-            scale = sy_ref[:, :1] * sx_ref[:, span]
-            out_ref[:, a, span] = (
-                scale * natural[a * rows : (a + 1) * rows] - white_ref[:, a, span]
+        scale = sy_ref[:, :1] * sx_ref[:, span]
+        for a in range(got_ref.shape[0]):
+            moved = jnp.dot(
+                got_ref[a, :, block * 128 : block * 128 + 128],
+                chosen,
+                preferred_element_type=jnp.float32,
             )
-
-
-def whitened_gradient(place, kept, got, sx, sy, white):
+            out_ref[:, a, span] = kept_ref[a, :, span] + scale * moved
+
+
+def whitened_gradient(place, kept, got, sx, sy):
+    times, rows, width = kept.shape
     return pl.pallas_call(
         gradient_kernel,
-        out_shape=jax.ShapeDtypeStruct(white.shape, jnp.float32),
-        in_specs=[SMEM] + [VMEM] * 5,
+        out_shape=jax.ShapeDtypeStruct((rows, times, width), jnp.float32),
+        in_specs=[SMEM] + [VMEM] * 4,
         out_specs=VMEM,
+        compiler_params=pltpu.CompilerParams(vmem_limit_bytes=GRANT),
         name="whitened_gradient",
-    )(place, kept, got, sx, sy, white)
+    )(place, kept, got, sx, sy)
 
 
 def with_core(block):
@@ -349,18 +341,19 @@
     modes, width = partial_y.shape
     sent = partial_y.reshape(ny * nz, modes // (ny * nz), width)
     got = lax.all_to_all(sent, ("y", "z"), 0, 0, tiled=True)
-    got = got.reshape(ny * nz, modes // (ny * nz), 4, width // 4)
-    got = got.transpose(2, 1, 0, 3).reshape(4, modes // (ny * nz), -1)
+    got = got.reshape(ny * nz, 2, modes // (2 * ny * nz), 4, width // 4)
+    got = got.transpose(1, 3, 2, 0, 4).reshape(2, 4 * (modes // (2 * ny * nz)), -1)
     far, before, after = [shifted(got, RING, step) for step in (2, 1, 3)]
-    done = (
-        band_product(place, with_core(got), pieces),
-        band_product(place, (*with_core(before), *with_core(after)), pieces),
-    )
-    kept, sent = last_product(place, slices, with_core(far), pieces, done)
+    bands = tuple(b for block in (got, far, before, after) for b in with_core(block))
+    white = whitened.reshape(-1, *whitened.shape[3:])
+    part = (4, white.shape[0], pieces[0].shape[-1])
+    sent = jax.ShapeDtypeStruct(part, jnp.bfloat16)
+    sent = band_products(sent_kernel, "sent_rows", place, slices, bands, pieces, (), sent)
     got = shifted(sent, "lo", 1)
-
-    white = whitened.reshape(-1, *whitened.shape[3:])
-    gradient = whitened_gradient(place, kept, got, sx, sy, white)
+    kept = jax.ShapeDtypeStruct((*part[:2], 2 * part[2]), jnp.float32)
+    more = (sx, sy, white)
+    kept = band_products(kept_kernel, "kept_rows", place, slices, bands, pieces, more, kept)
+    gradient = whitened_gradient(place, kept, got, sx, sy)
     return gradient.reshape(whitened.shape)
 
 

time: 155 us -> 135 us (0.87)
  Pallas kernels: 29.7 us -> 13 us
  local copies, waits for them, and re-layouts: 8.37 us -> 2.1 us
  blocking collectives: 21.3 us -> 24.2 us
  waiting for transfers between devices: 64 us -> 65.7 us
  other arithmetic: 6.2 us -> 4.58 us
    pallas_call x4 -> x3, Pallas kernels: 17.2 us -> 6.85 us  [the longest x2 4.72 us: band_products(): pl.pallas_call(kernel, out_shape=out_shape, in_specs=[SMEM, SMEM] + [VMEM...]
    pallas_call x1, Pallas kernels: 6.31 us -> 3.3 us  [near_product(): pl.pallas_call(near_kernel, out_shape=jax.ShapeDtypeStruct((rows, width),...]
    all_to_all x1, blocking collectives: 21.3 us -> 24.2 us  [local(): got = lax.all_to_all(sent, ('y', 'z'), 0, 0, tiled=True)]
    unnamed x46 -> x14, local copies, waits for them, and re-layouts: 3.81 us -> 0.95 us
    pallas_call x1, Pallas kernels: 4.41 us -> 2.11 us  [first_product(): pl.pallas_call(first_kernel, out_shape=jax.ShapeDtypeStruct((width, 8 * r...]
    ppermute x27, waiting for transfers between devices: 64 us -> 65.7 us  [shifted(): lax.ppermute(array, axis, [(k, (k + step) % size) for k in range(size)])]
  transfers between devices with their start and end apart: 27 -> 27, of which waited for: 11 -> 15; matrix products, arithmetic and copies ran while one was open for 5% -> 4% of each run, Pallas kernels for 10% -> 5%
where the time goes in v5:
time: 135 us
  waiting for transfers between devices  65.7 us (49%)
  starting transfers between devices  24.7 us (18%)
  blocking collectives  24.2 us (18%)
  Pallas kernels  13 us (10%)
  other arithmetic  4.58 us (3%)
  local copies, waits for them, and re-layouts  2.1 us (2%)
    ppermute x27, waiting for transfers between devices, shifted(): lax.ppermute(array, axis, [(k, (k + step) % size) for k in range(size)])  65.7 us
    ppermute x27, starting transfers between devices, shifted(): lax.ppermute(array, axis, [(k, (k + step) % size) for k in range(size)])  24.7 us
    all_to_all x1, blocking collectives, local(): got = lax.all_to_all(sent, ('y', 'z'), 0, 0, tiled=True)  24.2 us
    pallas_call x2, Pallas kernels, band_products(): pl.pallas_call(kernel, out_shape=out_shape, in_specs=[SMEM, SMEM] + [VMEM...  4.72 us
    squeeze x1, other arithmetic, local(): moments(event_counts, latent_mean, latent_var).astype(jnp.bfloat16)[0]  4.29 us
    pallas_call x1, Pallas kernels, near_product(): pl.pallas_call(near_kernel, out_shape=jax.ShapeDtypeStruct((rows, width),...  3.3 us
  transfers between devices with their start and end apart: 27, of which 15 were waited for; matrix products, arithmetic and copies ran while one was open for 4% of the time, Pallas kernels for 5%

profile of v5, /device:TPU:32, one launch (start us, length us, event | category | flops | bytes accessed | tf_op | source)
XLA Modules:
  0.0 135.2 jit_solution(5564742871612783064)
XLA Ops:
  0.1 0.9 copy-done.5
  1.8 1.6 %collective-permute-start = (bf16[64,512]{1,0:T(8,128)(2,1)S(1)}, bf16[64,512]{1,0:T(8,128)(2,1)S(1)}, u32[]{:S(2)}, u32[]{:S(2)}) collective-permute-start(bf16[64,512]{1,0:T(8,128)(2,1)S(1)} %get-tuple-element.30), channel_id=1, source_target_pairs={{0,1},{1,0},{2,3},{3,2},{4,5},{5,4},{6,7},{7,6},{8,9},{9,8},{10,11... | collective-permute-start | bytes 196616 | tf_op jit(solution)/shard_map/ppermute | solution.py:74
  3.3 4.3 %fusion.8.refs_0_ = bf16[64,4096]{1,0:T(8,128)(2,1)S(1)} fusion(s32[1,64,4096]{2,1,0:T(8,128)} %param.8, f32[1,64,4096]{2,1,0:T(8,128)} %param.10, f32[1,64,4096]{2,1,0:T(8,128)} %param.9), kind=kLoop, calls=%fused_computation.16 | loop fusion | flops 17563648 | bytes 3670016 | tf_op jit(solution)/shard_map/squeeze | solution.py:303
  7.7 3.3 %collective-permute-start.3 = (bf16[128,512]{1,0:T(8,128)(2,1)S(1)}, bf16[128,512]{1,0:T(8,128)(2,1)S(1)}, u32[]{:S(2)}, u32[]{:S(2)}) collective-permute-start(bf16[128,512]{1,0:T(8,128)(2,1)S(1)} %maximum_select_fusion), channel_id=1, source_target_pairs={{0,32},{16,48},{32,0},{48,16},{1,33},{17,49},{33,1},{49,17},{2,34}... | collective-permute-start | bytes 393224 | tf_op jit(solution)/shard_map/ppermute | solution.py:74
  11.0 1.1 collective-permute-start.2
  12.0 1.0 collective-permute-start.1
  14.1 2.1 %collective-permute-start.7 = (bf16[64,4096]{1,0:T(8,128)(2,1)S(1)}, bf16[64,4096]{1,0:T(8,128)(2,1)S(1)}, u32[]{:S(2)}, u32[]{:S(2)}) collective-permute-start(bf16[64,4096]{1,0:T(8,128)(2,1)S(1)} %fusion.8.refs_0_), channel_id=1, source_target_pairs={{0,129},{1,0},{128,1},{129,128},{2,131},{3,2},{130,3},{131,130},{4... | collective-permute-start | bytes 1572872 | tf_op jit(solution)/shard_map/ppermute | solution.py:74
  16.2 1.2 collective-permute-done.2
  17.4 0.8 collective-permute-done.1
  18.5 1.9 %collective-permute-start.4 = (bf16[4,128,512]{2,1,0:T(8,128)(2,1)S(1)}, bf16[4,128,512]{2,1,0:T(8,128)(2,1)S(1)}, u32[]{:S(2)}, u32[]{:S(2)}) collective-permute-start(bf16[4,128,512]{2,1,0:T(8,128)(2,1)S(1)} %pad_maximum_fusion.refs_8_), channel_id=1, source_target_pairs={{0,2},{2,4},{4,6},{6,8},{8,10},{10,12},{12,14},{14,0},{1,3},{3,5},... | collective-permute-start | bytes 1572872 | tf_op jit(solution)/shard_map/ppermute | solution.py:74
  20.5 6.1 %collective-permute-done.7.refs_6_ = bf16[64,4096]{1,0:T(8,128)(2,1)S(1)} collective-permute-done((bf16[64,4096]{1,0:T(8,128)(2,1)S(1)}, bf16[64,4096]{1,0:T(8,128)(2,1)S(1)}, u32[]{:S(2)}, u32[]{:S(2)}) %collective-permute-start.7) | collective-permute-done | bytes 524320 | tf_op jit(solution)/shard_map/ppermute | solution.py:74
  26.6 2.7 %collective-permute-start.10 = (bf16[64,4096]{1,0:T(8,128)(2,1)S(1)}, bf16[64,4096]{1,0:T(8,128)(2,1)}, u32[]{:S(2)}, u32[]{:S(2)}) collective-permute-start(bf16[64,4096]{1,0:T(8,128)(2,1)S(1)} %fusion.8.refs_0_), channel_id=1, source_target_pairs={{0,128},{1,129},{128,0},{129,1},{2,130},{3,131},{130,2},{131,3},{4... | collective-permute-start | bytes 1572872 | tf_op jit(solution)/shard_map/ppermute | solution.py:74
  29.4 11.5 %collective-permute-done.6.refs_4_ = bf16[64,4096]{1,0:T(8,128)(2,1)S(1)} collective-permute-done((bf16[64,4096]{1,0:T(8,128)(2,1)S(1)}, bf16[64,4096]{1,0:T(8,128)(2,1)S(1)}, u32[]{:S(2)}, u32[]{:S(2)}) %collective-permute-start.6) | collective-permute-done | bytes 524320 | tf_op jit(solution)/shard_map/ppermute | solution.py:74
  40.9 2.0 %collective-permute-start.8 = (bf16[4,128,512]{2,1,0:T(8,128)(2,1)S(1)}, bf16[4,128,512]{2,1,0:T(8,128)(2,1)S(1)}, u32[]{:S(2)}, u32[]{:S(2)}) collective-permute-start(bf16[4,128,512]{2,1,0:T(8,128)(2,1)S(1)} %collective-permute-done.4.refs_9_), channel_id=1, source_target_pairs={{0,2},{2,4},{4,6},{6,8},{8,10},{10,12},{12,14},{14,0},{1,3},{3,5},... | collective-permute-start | bytes 1572872 | tf_op jit(solution)/shard_map/ppermute | solution.py:74
  44.3 8.1 %collective-permute-done.8.refs_11_ = bf16[4,128,512]{2,1,0:T(8,128)(2,1)S(1)} collective-permute-done((bf16[4,128,512]{2,1,0:T(8,128)(2,1)S(1)}, bf16[4,128,512]{2,1,0:T(8,128)(2,1)S(1)}, u32[]{:S(2)}, u32[]{:S(2)}) %collective-permute-start.8) | collective-permute-done | bytes 524320 | tf_op jit(solution)/shard_map/ppermute | solution.py:74
  52.4 1.5 %collective-permute-done.9.refs_12_ = bf16[4,128,512]{2,1,0:T(8,128)(2,1)S(1)} collective-permute-done((bf16[4,128,512]{2,1,0:T(8,128)(2,1)S(1)}, bf16[4,128,512]{2,1,0:T(8,128)(2,1)S(1)}, u32[]{:S(2)}, u32[]{:S(2)}) %collective-permute-start.9) | collective-permute-done | bytes 524320 | tf_op jit(solution)/shard_map/ppermute | solution.py:74
  53.9 3.1 %collective-permute-start.12 = (bf16[4,128,512]{2,1,0:T(8,128)(2,1)S(1)}, bf16[4,128,512]{2,1,0:T(8,128)(2,1)S(1)}, u32[]{:S(2)}, u32[]{:S(2)}) collective-permute-start(bf16[4,128,512]{2,1,0:T(8,128)(2,1)S(1)} %collective-permute-done.8.refs_11_), channel_id=1, source_target_pairs={{0,2},{2,4},{4,6},{6,8},{8,10},{10,12},{12,14},{14,0},{1,3},{3,5},... | collective-permute-start | bytes 1572872 | tf_op jit(solution)/shard_map/ppermute | solution.py:74
  57.0 7.2 %collective-permute-done.12.refs_13_ = bf16[4,128,512]{2,1,0:T(8,128)(2,1)S(1)} collective-permute-done((bf16[4,128,512]{2,1,0:T(8,128)(2,1)S(1)}, bf16[4,128,512]{2,1,0:T(8,128)(2,1)S(1)}, u32[]{:S(2)}, u32[]{:S(2)}) %collective-permute-start.12) | collective-permute-done | bytes 524320 | tf_op jit(solution)/shard_map/ppermute | solution.py:74
  64.2 6.3 %collective-permute-done.13.refs_14_ = bf16[4,128,512]{2,1,0:T(8,128)(2,1)S(1)} collective-permute-done((bf16[4,128,512]{2,1,0:T(8,128)(2,1)S(1)}, bf16[4,128,512]{2,1,0:T(8,128)(2,1)S(1)}, u32[]{:S(2)}, u32[]{:S(2)}) %collective-permute-start.13) | collective-permute-done | bytes 524320 | tf_op jit(solution)/shard_map/ppermute | solution.py:74
  70.6 2.1 %collective-permute-start.17 = (bf16[2,128,512]{2,1,0:T(8,128)(2,1)S(1)}, bf16[2,128,512]{2,1,0:T(8,128)(2,1)S(1)}, u32[]{:S(2)}, u32[]{:S(2)}) collective-permute-start(bf16[2,128,512]{2,1,0:T(8,128)(2,1)S(1)} %slice.6), channel_id=1, source_target_pairs={{0,2},{2,4},{4,6},{6,8},{8,10},{10,12},{12,14},{14,0},{1,3},{3,5},... | collective-permute-start | bytes 786440 | tf_op jit(solution)/shard_map/ppermute | solution.py:74
  72.7 3.3 %near_product.1.refs_10_ = f32[512,512]{1,0:T(8,128)S(1)} custom-call(s32[4]{0:T(128)S(1)} %pad_add_fusion.first_ref.place_ref, bf16[64,4096]{1,0:T(8,128)(2,1)S(1)} %fusion.8.refs_0_, bf16[64,4096]{1,0:T(8,128)(2,1)} %collective-permute-done.11.refs_1_, bf16[64,4096]{1,0:T(8,128)(2,1)} %collective-permute-done.10.refs_2_, ...), custom_call_target="tpu_custom_call" | custom-call | flops 1879048192 | bytes 8388608 | tf_op jit(solution)/shard_map/near_product/pallas_call | solution.py:136
  76.0 1.0 collective-permute-done.18.refs_9_.refs_16_
  77.4 2.1 %first_product.1 = bf16[512,512]{1,0:T(8,128)(2,1)S(1)} custom-call(f32[8,4]{1,0:T(8,128)S(1)} %broadcast_select_fusion.mix_ref, s32[4]{0:T(128)S(1)} %pad_add_fusion.first_ref.place_ref, bf16[64,4096]{1,0:T(8,128)(2,1)S(1)} %fusion.8.refs_0_, bf16[64,4096]{1,0:T(8,128)(2,1)} %collective-permute-done.11.refs_1_, ...), custom_call_target="tpu_custom_call" | custom-call | flops 268435456 | bytes 4194304 | tf_op jit(solution)/shard_map/first_product/pallas_call | solution.py:174
  79.5 24.2 %all_to_all.5 = bf16[32,16,512]{2,1,0:T(8,128)(2,1)S(1)} all-to-all(bf16[32,16,512]{2,1,0:T(8,128)(2,1)S(1)} %bitcast.37), channel_id=1, replica_groups=mesh['hi'=2,'core'=2,'y'=4,'z'=8,'lo'=2] {'y','z'}, dimensions={0} | all-to-all | bytes 1048576 | tf_op jit(solution)/shard_map/all_to_all | solution.py:343
  103.8 2.0 %collective-permute-start.22 = (bf16[2,32,4096]{2,1,0:T(8,128)(2,1)S(1)}, bf16[2,32,4096]{2,1,0:T(8,128)(2,1)S(1)}, u32[]{:S(2)}, u32[]{:S(2)}) collective-permute-start(bf16[2,32,4096]{2,1,0:T(8,128)(2,1)S(1)} %copy_bitcast_fusion.refs_0_), channel_id=1, source_target_pairs={{0,1},{1,128},{128,129},{129,0},{2,3},{3,130},{130,131},{131,2},{4... | collective-permute-start | bytes 1572872 | tf_op jit(solution)/shard_map/ppermute | solution.py:74
  105.8 7.1 %collective-permute-done.24.refs_6_ = bf16[2,32,4096]{2,1,0:T(8,128)(2,1)S(1)} collective-permute-done((bf16[2,32,4096]{2,1,0:T(8,128)(2,1)S(1)}, bf16[2,32,4096]{2,1,0:T(8,128)(2,1)S(1)}, u32[]{:S(2)}, u32[]{:S(2)}) %collective-permute-start.24) | collective-permute-done | bytes 524320 | tf_op jit(solution)/shard_map/ppermute | solution.py:74
  113.0 6.9 %collective-permute-done.22.refs_4_ = bf16[2,32,4096]{2,1,0:T(8,128)(2,1)S(1)} collective-permute-done((bf16[2,32,4096]{2,1,0:T(8,128)(2,1)S(1)}, bf16[2,32,4096]{2,1,0:T(8,128)(2,1)S(1)}, u32[]{:S(2)}, u32[]{:S(2)}) %collective-permute-start.22) | collective-permute-done | bytes 524320 | tf_op jit(solution)/shard_map/ppermute | solution.py:74
  120.4 1.4 %collective-permute-done.23.refs_5_ = bf16[2,32,4096]{2,1,0:T(8,128)(2,1)S(1)} collective-permute-done((bf16[2,32,4096]{2,1,0:T(8,128)(2,1)S(1)}, bf16[2,32,4096]{2,1,0:T(8,128)(2,1)S(1)}, u32[]{:S(2)}, u32[]{:S(2)}) %collective-permute-start.23) | collective-permute-done | bytes 524320 | tf_op jit(solution)/shard_map/ppermute | solution.py:74
  122.6 1.9 %sent_rows.1 = bf16[4,64,512]{2,1,0:T(8,128)(2,1)S(1)} custom-call(s32[4]{0:T(128)S(1)} %pad_add_fusion.first_ref.place_ref, s32[8]{0:T(128)S(1)} %get-tuple-element.54.slice_ref, bf16[2,32,4096]{2,1,0:T(8,128)(2,1)S(1)} %copy_bitcast_fusion.refs_0_, bf16[2,32,4096]{2,1,0:T(8,128)(2,1)S(1)} %collective-permute-done.19.refs_1_, ...), custom_call_target="tpu_custom_call" | custom-call | flops 1073741824 | bytes 6291456 | tf_op jit(solution)/shard_map/sent_rows/pallas_call | solution.py:246
  124.8 2.9 %kept_rows.1.kept_ref = f32[4,64,1024]{2,1,0:T(8,128)S(1)} custom-call(s32[4]{0:T(128)S(1)} %pad_add_fusion.first_ref.place_ref, s32[8]{0:T(128)S(1)} %get-tuple-element.54.slice_ref, bf16[2,32,4096]{2,1,0:T(8,128)(2,1)S(1)} %copy_bitcast_fusion.refs_0_, bf16[2,32,4096]{2,1,0:T(8,128)(2,1)S(1)} %collective-permute-done.19.refs_1_, ...), custom_call_target="tpu_custom_call" | custom-call | flops 1073741824 | bytes 6291456 | tf_op jit(solution)/shard_map/kept_rows/pallas_call | solution.py:246
  127.6 5.5 %collective-permute-done.26.got_ref = bf16[4,64,512]{2,1,0:T(8,128)(2,1)S(1)} collective-permute-done((bf16[4,64,512]{2,1,0:T(8,128)(2,1)S(1)}, bf16[4,64,512]{2,1,0:T(8,128)(2,1)S(1)}, u32[]{:S(2)}, u32[]{:S(2)}) %collective-permute-start.26) | collective-permute-done | bytes 262176 | tf_op jit(solution)/shard_map/ppermute | solution.py:74
  133.1 2.1 %whitened_gradient.1 = f32[64,4,1024]{2,1,0:T(4,128)} custom-call(s32[4]{0:T(128)S(1)} %pad_add_fusion.first_ref.place_ref, f32[4,64,1024]{2,1,0:T(8,128)S(1)} %kept_rows.1.kept_ref, bf16[4,64,512]{2,1,0:T(8,128)(2,1)S(1)} %collective-permute-done.26.got_ref, f32[1,1024]{1,0:T(1,128)S(1)} %bitcast.40, f32[64,128]{1,0:T(8,128)S(1)} %broadcast_in_dim.35.refs_18_.sy_ref), custom_call_target="tpu_custom_call" | custom-call | tf_op jit(solution)/shard_map/whitened_gradient/pallas_call | solution.py:279
  (67 shorter events, 5.3 us)
Async XLA Ops:
  1.8 5.9 %collective-permute-start = (bf16[64,512]{1,0:T(8,128)(2,1)S(1)}, bf16[64,512]{1,0:T(8,128)(2,1)S(1)}, u32[]{:S(2)}, u32[]{:S(2)}) collective-permute-start(bf16[64,512]{1,0:T(8,128)(2,1)S(1)} %get-tuple-element.30), channel_id=1, source_target_pairs={{0,1},{1,0},{2,3},{3,2},{4,5},{5,4},{6,7},{7,6},{8,9},{9,8},{10,11... | collective-permute-start | bytes 196616 | tf_op jit(solution)/shard_map/ppermute | solution.py:74
  7.7 8.5 %collective-permute-start.3 = (bf16[128,512]{1,0:T(8,128)(2,1)S(1)}, bf16[128,512]{1,0:T(8,128)(2,1)S(1)}, u32[]{:S(2)}, u32[]{:S(2)}) collective-permute-start(bf16[128,512]{1,0:T(8,128)(2,1)S(1)} %maximum_select_fusion), channel_id=1, source_target_pairs={{0,32},{16,48},{32,0},{48,16},{1,33},{17,49},{33,1},{49,17},{2,34}... | collective-permute-start | bytes 393224 | tf_op jit(solution)/shard_map/ppermute | solution.py:74
  11.0 6.4 %collective-permute-start.2 = (bf16[128,512]{1,0:T(8,128)(2,1)S(1)}, bf16[128,512]{1,0:T(8,128)(2,1)S(1)}, u32[]{:S(2)}, u32[]{:S(2)}) collective-permute-start(bf16[128,512]{1,0:T(8,128)(2,1)S(1)} %maximum_select_fusion), channel_id=1, source_target_pairs={{0,48},{16,0},{32,16},{48,32},{1,49},{17,1},{33,17},{49,33},{2,50}... | collective-permute-start | bytes 393224 | tf_op jit(solution)/shard_map/ppermute | solution.py:74
  12.0 6.2 %collective-permute-start.1 = (bf16[128,512]{1,0:T(8,128)(2,1)S(1)}, bf16[128,512]{1,0:T(8,128)(2,1)S(1)}, u32[]{:S(2)}, u32[]{:S(2)}) collective-permute-start(bf16[128,512]{1,0:T(8,128)(2,1)S(1)} %maximum_select_fusion), channel_id=1, source_target_pairs={{0,16},{16,32},{32,48},{48,0},{1,17},{17,33},{33,49},{49,1},{2,18}... | collective-permute-start | bytes 393224 | tf_op jit(solution)/shard_map/ppermute | solution.py:74
  14.1 12.5 %collective-permute-start.7 = (bf16[64,4096]{1,0:T(8,128)(2,1)S(1)}, bf16[64,4096]{1,0:T(8,128)(2,1)S(1)}, u32[]{:S(2)}, u32[]{:S(2)}) collective-permute-start(bf16[64,4096]{1,0:T(8,128)(2,1)S(1)} %fusion.8.refs_0_), channel_id=1, source_target_pairs={{0,129},{1,0},{128,1},{129,128},{2,131},{3,2},{130,3},{131,130},{4... | collective-permute-start | bytes 1572872 | tf_op jit(solution)/shard_map/ppermute | solution.py:74
  16.2 24.7 %collective-permute-start.6 = (bf16[64,4096]{1,0:T(8,128)(2,1)S(1)}, bf16[64,4096]{1,0:T(8,128)(2,1)S(1)}, u32[]{:S(2)}, u32[]{:S(2)}) collective-permute-start(bf16[64,4096]{1,0:T(8,128)(2,1)S(1)} %fusion.8.refs_0_), channel_id=1, source_target_pairs={{0,1},{1,128},{128,129},{129,0},{2,3},{3,130},{130,131},{131,2},{4... | collective-permute-start | bytes 1572872 | tf_op jit(solution)/shard_map/ppermute | solution.py:74
  18.3 22.6 %collective-permute-start.5 = (bf16[4,128,512]{2,1,0:T(8,128)(2,1)S(1)}, bf16[4,128,512]{2,1,0:T(8,128)(2,1)S(1)}, u32[]{:S(2)}, u32[]{:S(2)}) collective-permute-start(bf16[4,128,512]{2,1,0:T(8,128)(2,1)S(1)} %pad_maximum_fusion.refs_8_), channel_id=1, source_target_pairs={{0,14},{2,0},{4,2},{6,4},{8,6},{10,8},{12,10},{14,12},{1,15},{3,1}... | collective-permute-start | bytes 1572872 | tf_op jit(solution)/shard_map/ppermute | solution.py:74
  18.5 22.4 %collective-permute-start.4 = (bf16[4,128,512]{2,1,0:T(8,128)(2,1)S(1)}, bf16[4,128,512]{2,1,0:T(8,128)(2,1)S(1)}, u32[]{:S(2)}, u32[]{:S(2)}) collective-permute-start(bf16[4,128,512]{2,1,0:T(8,128)(2,1)S(1)} %pad_maximum_fusion.refs_8_), channel_id=1, source_target_pairs={{0,2},{2,4},{4,6},{6,8},{8,10},{10,12},{12,14},{14,0},{1,3},{3,5},... | collective-permute-start | bytes 1572872 | tf_op jit(solution)/shard_map/ppermute | solution.py:74
  20.4 23.4 %collective-permute-start.11 = (bf16[64,4096]{1,0:T(8,128)(2,1)S(1)}, bf16[64,4096]{1,0:T(8,128)(2,1)}, u32[]{:S(2)}, u32[]{:S(2)}) collective-permute-start(bf16[64,4096]{1,0:T(8,128)(2,1)S(1)} %fusion.8.refs_0_), channel_id=1, source_target_pairs={{0,64},{64,0},{1,65},{65,1},{2,66},{66,2},{3,67},{67,3},{4,68},{68... | collective-permute-start | bytes 1572872 | tf_op jit(solution)/shard_map/ppermute | solution.py:74
  26.6 14.3 %copy-start = (bf16[64,4096]{1,0:T(8,128)(2,1)}, bf16[64,4096]{1,0:T(8,128)(2,1)S(1)}, u32[]{:S(2)}) copy-start(bf16[64,4096]{1,0:T(8,128)(2,1)S(1)} %collective-permute-done.7.refs_6_) | copy-start | bytes 1572868
  26.6 17.7 %collective-permute-start.10 = (bf16[64,4096]{1,0:T(8,128)(2,1)S(1)}, bf16[64,4096]{1,0:T(8,128)(2,1)}, u32[]{:S(2)}, u32[]{:S(2)}) collective-permute-start(bf16[64,4096]{1,0:T(8,128)(2,1)S(1)} %fusion.8.refs_0_), channel_id=1, source_target_pairs={{0,128},{1,129},{128,0},{129,1},{2,130},{3,131},{130,2},{131,3},{4... | collective-permute-start | bytes 1572872 | tf_op jit(solution)/shard_map/ppermute | solution.py:74
  40.9 2.0 %copy-start.2 = (bf16[64,4096]{1,0:T(8,128)(2,1)}, bf16[64,4096]{1,0:T(8,128)(2,1)S(1)}, u32[]{:S(2)}) copy-start(bf16[64,4096]{1,0:T(8,128)(2,1)S(1)} %collective-permute-done.6.refs_4_) | copy-start | bytes 1572868
  40.9 11.5 %collective-permute-start.8 = (bf16[4,128,512]{2,1,0:T(8,128)(2,1)S(1)}, bf16[4,128,512]{2,1,0:T(8,128)(2,1)S(1)}, u32[]{:S(2)}, u32[]{:S(2)}) collective-permute-start(bf16[4,128,512]{2,1,0:T(8,128)(2,1)S(1)} %collective-permute-done.4.refs_9_), channel_id=1, source_target_pairs={{0,2},{2,4},{4,6},{6,8},{8,10},{10,12},{12,14},{14,0},{1,3},{3,5},... | collective-permute-start | bytes 1572872 | tf_op jit(solution)/shard_map/ppermute | solution.py:74
  42.9 11.0 %collective-permute-start.9 = (bf16[4,128,512]{2,1,0:T(8,128)(2,1)S(1)}, bf16[4,128,512]{2,1,0:T(8,128)(2,1)S(1)}, u32[]{:S(2)}, u32[]{:S(2)}) collective-permute-start(bf16[4,128,512]{2,1,0:T(8,128)(2,1)S(1)} %collective-permute-done.5.refs_10_), channel_id=1, source_target_pairs={{0,14},{2,0},{4,2},{6,4},{8,6},{10,8},{12,10},{14,12},{1,15},{3,1}... | collective-permute-start | bytes 1572872 | tf_op jit(solution)/shard_map/ppermute | solution.py:74
  43.8 13.2 %collective-permute-start.15 = (bf16[64,4096]{1,0:T(8,128)(2,1)}, bf16[64,4096]{1,0:T(8,128)(2,1)S(1)}, u32[]{:S(2)}, u32[]{:S(2)}) collective-permute-start(bf16[64,4096]{1,0:T(8,128)(2,1)} %copy-done.2), channel_id=1, source_target_pairs={{0,64},{64,0},{1,65},{65,1},{2,66},{66,2},{3,67},{67,3},{4,68},{68... | collective-permute-start | bytes 1572872 | tf_op jit(solution)/shard_map/ppermute | solution.py:74
  43.8 13.2 %collective-permute-start.16 = (bf16[64,4096]{1,0:T(8,128)(2,1)}, bf16[64,4096]{1,0:T(8,128)(2,1)S(1)}, u32[]{:S(2)}, u32[]{:S(2)}) collective-permute-start(bf16[64,4096]{1,0:T(8,128)(2,1)} %copy-done), channel_id=1, source_target_pairs={{0,64},{64,0},{1,65},{65,1},{2,66},{66,2},{3,67},{67,3},{4,68},{68... | collective-permute-start | bytes 1572872 | tf_op jit(solution)/shard_map/ppermute | solution.py:74
  53.9 18.8 %copy-start.1 = (bf16[64,4096]{1,0:T(8,128)(2,1)S(1)}, bf16[64,4096]{1,0:T(8,128)(2,1)}, u32[]{:S(2)}) copy-start(bf16[64,4096]{1,0:T(8,128)(2,1)} %copy-done) | copy-start | bytes 1572868
  53.9 18.8 %copy-start.3 = (bf16[64,4096]{1,0:T(8,128)(2,1)S(1)}, bf16[64,4096]{1,0:T(8,128)(2,1)}, u32[]{:S(2)}) copy-start(bf16[64,4096]{1,0:T(8,128)(2,1)} %copy-done.2) | copy-start | bytes 1572868
  53.9 10.3 %collective-permute-start.12 = (bf16[4,128,512]{2,1,0:T(8,128)(2,1)S(1)}, bf16[4,128,512]{2,1,0:T(8,128)(2,1)S(1)}, u32[]{:S(2)}, u32[]{:S(2)}) collective-permute-start(bf16[4,128,512]{2,1,0:T(8,128)(2,1)S(1)} %collective-permute-done.8.refs_11_), channel_id=1, source_target_pairs={{0,2},{2,4},{4,6},{6,8},{8,10},{10,12},{12,14},{14,0},{1,3},{3,5},... | collective-permute-start | bytes 1572872 | tf_op jit(solution)/shard_map/ppermute | solution.py:74
  57.0 13.5 %collective-permute-start.13 = (bf16[4,128,512]{2,1,0:T(8,128)(2,1)S(1)}, bf16[4,128,512]{2,1,0:T(8,128)(2,1)S(1)}, u32[]{:S(2)}, u32[]{:S(2)}) collective-permute-start(bf16[4,128,512]{2,1,0:T(8,128)(2,1)S(1)} %collective-permute-done.9.refs_12_), channel_id=1, source_target_pairs={{0,14},{2,0},{4,2},{6,4},{8,6},{10,8},{12,10},{14,12},{1,15},{3,1}... | collective-permute-start | bytes 1572872 | tf_op jit(solution)/shard_map/ppermute | solution.py:74
  57.0 13.5 %collective-permute-start.14 = (bf16[64,4096]{1,0:T(8,128)(2,1)}, bf16[64,4096]{1,0:T(8,128)(2,1)S(1)}, u32[]{:S(2)}, u32[]{:S(2)}) collective-permute-start(bf16[64,4096]{1,0:T(8,128)(2,1)} %collective-permute-done.10.refs_2_), channel_id=1, source_target_pairs={{0,64},{64,0},{1,65},{65,1},{2,66},{66,2},{3,67},{67,3},{4,68},{68... | collective-permute-start | bytes 1572872 | tf_op jit(solution)/shard_map/ppermute | solution.py:74
  70.5 6.5 %collective-permute-start.18 = (bf16[2,128,512]{2,1,0:T(8,128)(2,1)S(1)}, bf16[2,128,512]{2,1,0:T(8,128)(2,1)S(1)}, u32[]{:S(2)}, u32[]{:S(2)}) collective-permute-start(bf16[2,128,512]{2,1,0:T(8,128)(2,1)S(1)} %slice.7), channel_id=1, source_target_pairs={{0,14},{2,0},{4,2},{6,4},{8,6},{10,8},{12,10},{14,12},{1,15},{3,1}... | collective-permute-start | bytes 786440 | tf_op jit(solution)/shard_map/ppermute | solution.py:74
  70.6 6.7 %collective-permute-start.17 = (bf16[2,128,512]{2,1,0:T(8,128)(2,1)S(1)}, bf16[2,128,512]{2,1,0:T(8,128)(2,1)S(1)}, u32[]{:S(2)}, u32[]{:S(2)}) collective-permute-start(bf16[2,128,512]{2,1,0:T(8,128)(2,1)S(1)} %slice.6), channel_id=1, source_target_pairs={{0,2},{2,4},{4,6},{6,8},{8,10},{10,12},{12,14},{14,0},{1,3},{3,5},... | collective-permute-start | bytes 786440 | tf_op jit(solution)/shard_map/ppermute | solution.py:74
  103.7 9.3 %collective-permute-start.24 = (bf16[2,32,4096]{2,1,0:T(8,128)(2,1)S(1)}, bf16[2,32,4096]{2,1,0:T(8,128)(2,1)S(1)}, u32[]{:S(2)}, u32[]{:S(2)}) collective-permute-start(bf16[2,32,4096]{2,1,0:T(8,128)(2,1)S(1)} %copy_bitcast_fusion.refs_0_), channel_id=1, source_target_pairs={{0,129},{1,0},{128,1},{129,128},{2,131},{3,2},{130,3},{131,130},{4... | collective-permute-start | bytes 1572872 | tf_op jit(solution)/shard_map/ppermute | solution.py:74
  103.8 16.1 %collective-permute-start.22 = (bf16[2,32,4096]{2,1,0:T(8,128)(2,1)S(1)}, bf16[2,32,4096]{2,1,0:T(8,128)(2,1)S(1)}, u32[]{:S(2)}, u32[]{:S(2)}) collective-permute-start(bf16[2,32,4096]{2,1,0:T(8,128)(2,1)S(1)} %copy_bitcast_fusion.refs_0_), channel_id=1, source_target_pairs={{0,1},{1,128},{128,129},{129,0},{2,3},{3,130},{130,131},{131,2},{4... | collective-permute-start | bytes 1572872 | tf_op jit(solution)/shard_map/ppermute | solution.py:74
  105.8 14.1 %collective-permute-start.20 = (bf16[2,32,4096]{2,1,0:T(8,128)(2,1)S(1)}, bf16[2,32,4096]{2,1,0:T(8,128)(2,1)S(1)}, u32[]{:S(2)}, u32[]{:S(2)}) collective-permute-start(bf16[2,32,4096]{2,1,0:T(8,128)(2,1)S(1)} %copy_bitcast_fusion.refs_0_), channel_id=1, source_target_pairs={{0,128},{1,129},{128,0},{129,1},{2,130},{3,131},{130,2},{131,3},{4... | collective-permute-start | bytes 1572872 | tf_op jit(solution)/shard_map/ppermute | solution.py:74
  105.8 14.6 %collective-permute-start.19 = (bf16[2,32,4096]{2,1,0:T(8,128)(2,1)S(1)}, bf16[2,32,4096]{2,1,0:T(8,128)(2,1)S(1)}, u32[]{:S(2)}, u32[]{:S(2)}) collective-permute-start(bf16[2,32,4096]{2,1,0:T(8,128)(2,1)S(1)} %copy_bitcast_fusion.refs_0_), channel_id=1, source_target_pairs={{0,64},{64,0},{1,65},{65,1},{2,66},{66,2},{3,67},{67,3},{4,68},{68... | collective-permute-start | bytes 1572872 | tf_op jit(solution)/shard_map/ppermute | solution.py:74
  113.0 7.4 %collective-permute-start.25 = (bf16[2,32,4096]{2,1,0:T(8,128)(2,1)S(1)}, bf16[2,32,4096]{2,1,0:T(8,128)(2,1)S(1)}, u32[]{:S(2)}, u32[]{:S(2)}) collective-permute-start(bf16[2,32,4096]{2,1,0:T(8,128)(2,1)S(1)} %collective-permute-done.24.refs_6_), channel_id=1, source_target_pairs={{0,64},{64,0},{1,65},{65,1},{2,66},{66,2},{3,67},{67,3},{4,68},{68... | collective-permute-start | bytes 1572872 | tf_op jit(solution)/shard_map/ppermute | solution.py:74
  119.9 1.9 %collective-permute-start.23 = (bf16[2,32,4096]{2,1,0:T(8,128)(2,1)S(1)}, bf16[2,32,4096]{2,1,0:T(8,128)(2,1)S(1)}, u32[]{:S(2)}, u32[]{:S(2)}) collective-permute-start(bf16[2,32,4096]{2,1,0:T(8,128)(2,1)S(1)} %collective-permute-done.22.refs_4_), channel_id=1, source_target_pairs={{0,64},{64,0},{1,65},{65,1},{2,66},{66,2},{3,67},{67,3},{4,68},{68... | collective-permute-start | bytes 1572872 | tf_op jit(solution)/shard_map/ppermute | solution.py:74
  119.9 2.7 %collective-permute-start.21 = (bf16[2,32,4096]{2,1,0:T(8,128)(2,1)S(1)}, bf16[2,32,4096]{2,1,0:T(8,128)(2,1)S(1)}, u32[]{:S(2)}, u32[]{:S(2)}) collective-permute-start(bf16[2,32,4096]{2,1,0:T(8,128)(2,1)S(1)} %collective-permute-done.20.refs_2_), channel_id=1, source_target_pairs={{0,64},{64,0},{1,65},{65,1},{2,66},{66,2},{3,67},{67,3},{4,68},{68... | collective-permute-start | bytes 1572872 | tf_op jit(solution)/shard_map/ppermute | solution.py:74
  122.6 2.2 %copy-start.4 = (f32[4,1,16,4,1024]{4,3,2,1,0:T(4,128)S(1)}, f32[4,1,16,4,1024]{4,3,2,1,0:T(4,128)}, u32[]{:S(2)}) copy-start(f32[4,1,16,4,1024]{4,3,2,1,0:T(4,128)} %param.14) | copy-start | bytes 3145732
  124.4 8.7 %collective-permute-start.26 = (bf16[4,64,512]{2,1,0:T(8,128)(2,1)S(1)}, bf16[4,64,512]{2,1,0:T(8,128)(2,1)S(1)}, u32[]{:S(2)}, u32[]{:S(2)}) collective-permute-start(bf16[4,64,512]{2,1,0:T(8,128)(2,1)S(1)} %sent_rows.1), channel_id=1, source_target_pairs={{0,1},{1,0},{2,3},{3,2},{4,5},{5,4},{6,7},{7,6},{8,9},{9,8},{10,11... | collective-permute-start | bytes 786440 | tf_op jit(solution)/shard_map/ppermute | solution.py:74
  (2 other events, 1.6 us)

commit v6 on v5

--- a/solution.py
+++ b/solution.py
@@ -102,27 +102,49 @@
     )(place, basis)
 
 
-def columns_at(ref, index):
+def columns_at(index):
     return pl.ds(pl.multiple_of(index * 128, 128), 128)
 
 
-def product_of(place_ref, load, steps, pieces, acc_ref):
+def product_of(place_ref, load, spec, pieces, acc_ref):
+    acc_ref[...] = jnp.zeros_like(acc_ref)
     y_here, z_here = place_ref[2], place_ref[3]
-    for (step, parts), ref in zip(steps, pieces):
-        at = lax.rem(z_here + step, 8)
-        where = [columns_at(ref, lax.rem(y_here + part, 4) * 8 + at) for part in parts]
+    for blocks, ref in zip(spec, pieces):
+        where = [
+            columns_at(lax.rem(y_here + dy, 4) * 8 + lax.rem(z_here + dz, 8)) for dz, dy in blocks
+        ]
         field = jnp.concatenate([load(span) for span in where], axis=1)
-        basis = jnp.concatenate([ref[k] for k in range(len(parts))], axis=0)
+        basis = jnp.concatenate([ref[k] for k in range(len(blocks))], axis=0)
         acc_ref[...] += jnp.dot(field, basis, preferred_element_type=jnp.float32)
 
 
-NEAR = tuple((step, (0, 3, 1, 2)) for step in (0, 7, 1, 6, 2, 5, 3))
-FAR = ((4, (0, 3)), (4, (1, 2)))
+NEAR = (
+    ((0, 0), (0, 1)),
+    ((0, 2),),
+    ((0, 3),),
+    ((7, 0), (7, 1)),
+    ((1, 0), (1, 1)),
+    ((7, 2), (1, 2)),
+    ((7, 3), (1, 3)),
+    ((6, 0), (6, 1)),
+    ((2, 0), (2, 1)),
+    ((6, 2), (2, 2)),
+    ((6, 3), (2, 3)),
+    ((5, 0), (5, 1)),
+    ((3, 0), (3, 1)),
+)
+FAR = (
+    ((5, 2), (3, 2)),
+    ((5, 3), (3, 3)),
+    ((4, 0),),
+    ((4, 1),),
+    ((4, 2),),
+    ((4, 3),),
+)
 
 
 def near_kernel(place_ref, *refs):
     blocks, pieces, acc_ref = refs[:8], refs[8:-1], refs[-1]
-    acc_ref[...] = jnp.zeros_like(acc_ref)
 
     def load(span):
         return jnp.concatenate([ref[:, span] for ref in blocks], axis=0)
@@ -136,26 +158,26 @@
     return pl.pallas_call(
         near_kernel,
         out_shape=jax.ShapeDtypeStruct((rows, width), jnp.float32),
-        in_specs=[SMEM] + [VMEM] * 15,
+        in_specs=[SMEM] + [VMEM] * (8 + len(pieces)),
         out_specs=VMEM,
         compiler_params=pltpu.CompilerParams(vmem_limit_bytes=GRANT),
         cost_estimate=pl.CostEstimate(
-            flops=2 * rows * 3584 * width, bytes_accessed=8 << 20, transcendentals=0
+            flops=2 * rows * 3072 * width, bytes_accessed=8 << 20, transcendentals=0
         ),
         name="near_product",
     )(place, *fields, *pieces)
 
 
 def first_kernel(mix_ref, place_ref, *refs):
-    blocks, pieces, near_ref, out_ref, acc_ref, tmp_ref = refs[:8], refs[8:10], *refs[10:]
+    blocks, pieces, (near_ref, out_ref, acc_ref, tmp_ref) = refs[:8], refs[8:-4], refs[-4:]
     rows = blocks[0].shape[0]
     lo = place_ref[0]
-    acc_ref[...] = near_ref[...]
 
     def load(span):
         return jnp.concatenate([ref[:, span] for ref in blocks], axis=0)
 
     product_of(place_ref, load, FAR, pieces, acc_ref)
+    acc_ref[...] += near_ref[...]
     for a in range(4):
         for group in range(2):
             mixed = sum(
@@ -174,7 +196,7 @@
     return pl.pallas_call(
         first_kernel,
         out_shape=jax.ShapeDtypeStruct((width, 8 * rows), jnp.bfloat16),
-        in_specs=[SMEM, SMEM] + [VMEM] * 11,
+        in_specs=[SMEM, SMEM] + [VMEM] * (9 + len(pieces)),
         out_specs=VMEM,
         scratch_shapes=[
             pltpu.VMEM((8 * rows, width), jnp.float32),
@@ -182,7 +204,7 @@
         ],
         compiler_params=pltpu.CompilerParams(vmem_limit_bytes=GRANT),
         cost_estimate=pl.CostEstimate(
-            flops=2 * 8 * rows * 512 * width, bytes_accessed=4 << 20, transcendentals=0
+            flops=2 * 8 * rows * 1024 * width, bytes_accessed=4 << 20, transcendentals=0
         ),
         name="first_product",
     )(mix, place, *fields, *pieces, near)
@@ -192,14 +214,8 @@
     return jnp.concatenate([ref[which, :, span] for ref in fields], axis=0)
 
 
-def natural_rows(place_ref, slice_ref, acc_ref, rows_ref):
-    times, group = 4, 8
-    for b in range(8):
-        half_of = place_ref[0] if b < 4 else 1 - place_ref[0]
-        to = pl.multiple_of((slice_ref[b] * 2 + half_of) * group, group)
-        for a in range(times):
-            first = (b * times + a) * group
-            rows_ref[a, pl.ds(to, group), :] = acc_ref[first : first + group, :]
+def natural_place(slice_ref, half_of, block):
+    return pl.multiple_of((slice_ref[block] * 2 + half_of) * 8, 8)
 
 
 def moved_columns(half):
@@ -208,24 +224,44 @@
     return (target == (source // 8) * 16 + half * 8 + lax.rem(source, 8)).astype(jnp.float32)
 
 
-def sent_kernel(place_ref, slice_ref, *refs):
-    fields, pieces, (sent_ref, acc_ref, rows_ref) = refs[:8], refs[8:17], refs[17:]
-    acc_ref[...] = jnp.zeros_like(acc_ref)
+def sent_kernel(place_ref, *refs):
+    count = len(refs) - len(NEAR + FAR) - 2
+    fields, pieces, (sent_ref, acc_ref) = refs[:count], refs[count:-2], refs[-2:]
     which = 1 - place_ref[0]
     product_of(
         place_ref, lambda span: load_bands(fields, which, span), NEAR + FAR, pieces, acc_ref
     )
-    natural_rows(place_ref, slice_ref, acc_ref, rows_ref)
-    sent_ref[...] = rows_ref[...].astype(jnp.bfloat16)
+    sent_ref[...] = acc_ref[...].astype(jnp.bfloat16)
+
+
+def sent_rows(place, fields, pieces):
+    count = sum(field.shape[1] for field in fields)
+    total, width = fields[0].shape[-1], pieces[0].shape[-1]
+    return pl.pallas_call(
+        sent_kernel,
+        out_shape=jax.ShapeDtypeStruct((count, width), jnp.bfloat16),
+        in_specs=[SMEM] + [VMEM] * (len(fields) + len(pieces)),
+        out_specs=VMEM,
+        scratch_shapes=[pltpu.VMEM((count, width), jnp.float32)],
+        compiler_params=pltpu.CompilerParams(vmem_limit_bytes=GRANT),
+        cost_estimate=pl.CostEstimate(
+            flops=2 * count * total * width, bytes_accessed=6 << 20, transcendentals=0
+        ),
+        name="sent_rows",
+    )(place, *fields, *pieces)
 
 
 def kept_kernel(place_ref, slice_ref, *refs):
-    fields, pieces, (sx_ref, sy_ref, white_ref) = refs[:8], refs[8:17], refs[17:20]
-    kept_ref, acc_ref, rows_ref = refs[20:]
-    acc_ref[...] = jnp.zeros_like(acc_ref)
+    count = len(refs) - len(NEAR + FAR) - 6
+    fields, pieces = refs[:count], refs[count:-6]
+    sx_ref, sy_ref, white_ref, kept_ref, acc_ref, rows_ref = refs[-6:]
     lo = place_ref[0]
     product_of(place_ref, lambda span: load_bands(fields, lo, span), NEAR + FAR, pieces, acc_ref)
-    natural_rows(place_ref, slice_ref, acc_ref, rows_ref)
+    for b in range(8):
+        to = natural_place(slice_ref, lo if b < 4 else 1 - lo, b)
+        for a in range(4):
+            first = (b * 4 + a) * 8
+            rows_ref[a, pl.ds(to, 8), :] = acc_ref[first : first + 8, :]
     chosen = moved_columns(lo)
     for block in range(rows_ref.shape[-1] // 128):
         span = slice(block * 256, block * 256 + 256)
@@ -239,51 +275,55 @@
             kept_ref[a, :, span] = scale * moved - white_ref[:, a, span]
 
 
-def band_products(kernel, name, place, slices, fields, pieces, more, out_shape):
-    _, rows, total = fields[0].shape
-    width = pieces[0].shape[-1]
-    count = len(fields) * rows
-    return pl.pallas_call(
-        kernel,
-        out_shape=out_shape,
-        in_specs=[SMEM, SMEM] + [VMEM] * (17 + len(more)),
+def kept_rows(place, slices, fields, pieces, sx, sy, white):
+    count = sum(field.shape[1] for field in fields)
+    total, width = fields[0].shape[-1], pieces[0].shape[-1]
+    rows, times, columns = white.shape
+    return pl.pallas_call(
+        kept_kernel,
+        out_shape=jax.ShapeDtypeStruct((times, rows, columns), jnp.float32),
+        in_specs=[SMEM, SMEM] + [VMEM] * (len(fields) + len(pieces) + 3),
         out_specs=VMEM,
         scratch_shapes=[
             pltpu.VMEM((count, width), jnp.float32),
-            pltpu.VMEM((4, count // 4, width), jnp.float32),
+            pltpu.VMEM((times, rows, width), jnp.float32),
         ],
         compiler_params=pltpu.CompilerParams(vmem_limit_bytes=GRANT),
         cost_estimate=pl.CostEstimate(
             flops=2 * count * total * width, bytes_accessed=6 << 20, transcendentals=0
         ),
-        name=name,
-    )(place, slices, *fields, *pieces, *more)
-
-
-def gradient_kernel(place_ref, kept_ref, got_ref, sx_ref, sy_ref, out_ref):
-    chosen = moved_columns(1 - place_ref[0]).astype(jnp.bfloat16)
-    for block in range(got_ref.shape[-1] // 128):
+        name="kept_rows",
+    )(place, slices, *fields, *pieces, sx, sy, white)
+
+
+def gradient_kernel(place_ref, slice_ref, kept_ref, early_ref, late_ref, sx_ref, sy_ref, out_ref):
+    lo = place_ref[0]
+    chosen = moved_columns(1 - lo).astype(jnp.bfloat16)
+    for block in range(early_ref.shape[-1] // 128):
+        here = slice(block * 128, block * 128 + 128)
         span = slice(block * 256, block * 256 + 256)
-        scale = sy_ref[:, :1] * sx_ref[:, span]
-        for a in range(got_ref.shape[0]):
-            moved = jnp.dot(
-                got_ref[a, :, block * 128 : block * 128 + 128],
-                chosen,
-                preferred_element_type=jnp.float32,
-            )
-            out_ref[:, a, span] = kept_ref[a, :, span] + scale * moved
-
-
-def whitened_gradient(place, kept, got, sx, sy):
+        for ref, sources in ((early_ref, (0, 1, 4, 5, 6, 7)), (late_ref, (2, 3))):
+            moved = jnp.dot(ref[:, here], chosen, preferred_element_type=jnp.float32)
+            for k, b in enumerate(sources):
+                to = natural_place(slice_ref, 1 - lo if b < 4 else lo, b)
+                scale = sy_ref[pl.ds(to, 8), :1] * sx_ref[:, span]
+                for a in range(4):
+                    first = (k * 4 + a) * 8
+                    out_ref[pl.ds(to, 8), a, span] = (
+                        kept_ref[a, pl.ds(to, 8), span] + scale * moved[first : first + 8]
+                    )
+
+
+def whitened_gradient(place, slices, kept, early, late, sx, sy):
     times, rows, width = kept.shape
     return pl.pallas_call(
         gradient_kernel,
         out_shape=jax.ShapeDtypeStruct((rows, times, width), jnp.float32),
-        in_specs=[SMEM] + [VMEM] * 4,
+        in_specs=[SMEM, SMEM] + [VMEM] * 5,
         out_specs=VMEM,
         compiler_params=pltpu.CompilerParams(vmem_limit_bytes=GRANT),
         name="whitened_gradient",
-    )(place, kept, got, sx, sy)
+    )(place, slices, kept, early, late, sx, sy)
 
 
 def with_core(block):
@@ -302,14 +342,16 @@
     mine = jnp.where(lo == 0, jnp.concatenate([kept, other]), jnp.concatenate([other, kept]))
     pseudo = moments(event_counts, latent_mean, latent_var).astype(jnp.bfloat16)[0]
     mine, pseudo = lax.optimization_barrier((mine, pseudo))
+    next_y = shifted(mine, "y", 3)
     far, before, after = [shifted(pseudo, RING, step) for step in (2, 1, 3)]
-    block = jnp.stack([mine] + [shifted(mine, "y", step) for step in (1, 3, 2)])
+    block = jnp.stack([mine, next_y])
     own = with_core(pseudo)
 
     flips = jnp.array([0, 1, 2, 3], jnp.int32)
     before_flip, after_flip = 2 * (1 - lo), 2 * lo
     crossed = jnp.stack([before_flip, before_flip + 1, after_flip, after_flip + 1])
     slices = lax.bitwise_xor(time, jnp.concatenate([flips, crossed])).astype(jnp.int32)
+    swapped = jnp.concatenate([slices[:4], slices[6:], slices[4:6]])
     factor = time_factor(correlation[0], 4)
     mix = jnp.take(factor, slices, axis=0)
     root = jnp.sqrt(spectrum)
@@ -318,20 +360,35 @@
     sy = lax.dynamic_slice_in_dim(root.reshape(4, lax.axis_size(ROW), -1), row, 1, 1).reshape(-1, 1)
     sy = jnp.broadcast_to(sy, (sy.shape[0], 128))
 
+    def from_neighbours(blocks):
+        second = jnp.concatenate([b[-1:] for b in blocks])
+        first = jnp.concatenate([b[:1] for b in blocks])
+        return [shifted(second, "y", 3), shifted(first, "y", 1)]
+
     right, left = shifted(block, "z", 1), shifted(block, "z", nz - 1)
-    pieces = [block, right, left]
+    beside = from_neighbours([block])
     right, left, before, after = lax.optimization_barrier((right, left, before, after))
+    pieces = [block]
+    next_right, next_left = shifted(right, "z", 1), shifted(left, "z", nz - 1)
+    beside_next = from_neighbours([right, left])
     before, after = with_core(before), with_core(after)
-    right, left = shifted(right, "z", 1), shifted(left, "z", nz - 1)
+    next_right, next_left, beside, beside_next, far, own, mix, sx, sy = lax.optimization_barrier(
+        (next_right, next_left, beside, beside_next, far, own, mix, sx, sy)
+    )
+    pieces += [*beside, right, left, *beside_next]
+    right, left = next_right, next_left
+    next_right, next_left = shifted(right, "z", 1), shifted(left, "z", nz - 1)
+    beside = from_neighbours([right, left])
+    far = with_core(far)
+    next_right, next_left, beside, far, before, after = lax.optimization_barrier(
+        (next_right, next_left, beside, far, before, after)
+    )
+    pieces += [right, left, *beside]
+    right, left = next_right, next_left
     pieces += [right, left]
-    right, left, far, own, mix, sx, sy = lax.optimization_barrier(
-        (right, left, far, own, mix, sx, sy)
-    )
-    far = with_core(far)
-    right, left = shifted(right, "z", 1), shifted(left, "z", nz - 1)
-    pieces += [right, left]
-    right, left, far, before, after = lax.optimization_barrier((right, left, far, before, after))
-    last = [shifted(right[:2], "z", 1), shifted(left[2:], "z", nz - 1)]
+    ends = [shifted(right[:1], "z", 1), shifted(left[1:], "z", nz - 1)]
+    last = [*from_neighbours([right, left]), *ends]
+    last += [shifted(ends[1], "y", 3), shifted(ends[0], "y", 1)]
 
     fields = (*own, *far, *before, *after)
     near = near_product(place, fields, pieces)
@@ -343,17 +400,18 @@
     got = lax.all_to_all(sent, ("y", "z"), 0, 0, tiled=True)
     got = got.reshape(ny * nz, 2, modes // (2 * ny * nz), 4, width // 4)
     got = got.transpose(1, 3, 2, 0, 4).reshape(2, 4 * (modes // (2 * ny * nz)), -1)
-    far, before, after = [shifted(got, RING, step) for step in (2, 1, 3)]
-    bands = tuple(b for block in (got, far, before, after) for b in with_core(block))
+    own, before, after = with_core(got), shifted(got, RING, 1), shifted(got, RING, 3)
+    middle = got.shape[1] // 2
+    far = [shifted(before[:, :middle], RING, 1), shifted(after[:, middle:], RING, 3)]
+    before, after = with_core(before), with_core(after)
+    early = sent_rows(place, (*own, *before, *after), pieces)
+    far, early = lax.optimization_barrier((far, early))
+    got_early = shifted(early, "lo", 1)
+    far = (*far, *(shifted(half, "core", 1) for half in far))
+    got_late = shifted(sent_rows(place, far, pieces), "lo", 1)
     white = whitened.reshape(-1, *whitened.shape[3:])
-    part = (4, white.shape[0], pieces[0].shape[-1])
-    sent = jax.ShapeDtypeStruct(part, jnp.bfloat16)
-    sent = band_products(sent_kernel, "sent_rows", place, slices, bands, pieces, (), sent)
-    got = shifted(sent, "lo", 1)
-    kept = jax.ShapeDtypeStruct((*part[:2], 2 * part[2]), jnp.float32)
-    more = (sx, sy, white)
-    kept = band_products(kept_kernel, "kept_rows", place, slices, bands, pieces, more, kept)
-    gradient = whitened_gradient(place, kept, got, sx, sy)
+    kept = kept_rows(place, slices, (*own, *far, *before, *after), pieces, sx, sy, white)
+    gradient = whitened_gradient(place, swapped, kept, got_early, got_late, sx, sy)
     return gradient.reshape(whitened.shape)
 
 

time: 135 us -> 141 us (1.044)
  waiting for transfers between devices: 65.7 us -> 43.1 us
  starting transfers between devices: 24.7 us -> 47 us
  local copies, waits for them, and re-layouts: 2.1 us -> 5.28 us
  blocking collectives: 24.2 us -> 22 us
  other arithmetic: 4.58 us -> 6.64 us
  Pallas kernels: 13 us -> 15 us
    ppermute x27 -> x38, waiting for transfers between devices: 65.7 us -> 43.1 us  [shifted(): lax.ppermute(array, axis, [(k, (k + step) % size) for k in range(size)])]
    ppermute x27 -> x38, starting transfers between devices: 24.7 us -> 47 us  [shifted(): lax.ppermute(array, axis, [(k, (k + step) % size) for k in range(size)])]
    all_to_all x1, blocking collectives: 24.2 us -> 22 us  [local(): got = lax.all_to_all(sent, ('y', 'z'), 0, 0, tiled=True)]
    pallas_call x2 -> x3, Pallas kernels: 4.72 us -> 6.22 us  [the longest x2 3.13 us: sent_rows(): pl.pallas_call(sent_kernel, out_shape=jax.ShapeDtypeStruct((count, width)...]
  transfers between devices with their start and end apart: 27 -> 38, of which waited for: 15 -> 12; matrix products, arithmetic and copies ran while one was open for 4% -> 7% of each run, Pallas kernels for 5% -> 7%
where the time goes in v6:
time: 141 us; the launch traced here: 140 us
  starting transfers between devices  47 us (33%)
  waiting for transfers between devices  43.1 us (31%)
  blocking collectives  22 us (16%)
  Pallas kernels  15 us (11%)
  other arithmetic  6.64 us (5%)
  local copies, waits for them, and re-layouts  5.28 us (4%)
    ppermute x38, starting transfers between devices, shifted(): lax.ppermute(array, axis, [(k, (k + step) % size) for k in range(size)])  47 us
    ppermute x38, waiting for transfers between devices, shifted(): lax.ppermute(array, axis, [(k, (k + step) % size) for k in range(size)])  43.1 us
    all_to_all x1, blocking collectives, local(): got = lax.all_to_all(sent, ('y', 'z'), 0, 0, tiled=True)  22 us
    squeeze x1, other arithmetic, local(): moments(event_counts, latent_mean, latent_var).astype(jnp.bfloat16)[0]  4.3 us
    pallas_call x1, Pallas kernels, near_product(): pl.pallas_call(near_kernel, out_shape=jax.ShapeDtypeStruct((rows, width),...  3.17 us
    pallas_call x2, Pallas kernels, sent_rows(): pl.pallas_call(sent_kernel, out_shape=jax.ShapeDtypeStruct((count, width)...  3.13 us
    pallas_call x1, Pallas kernels, kept_rows(): pl.pallas_call(kept_kernel, out_shape=jax.ShapeDtypeStruct((times, rows,...  3.09 us
  transfers between devices with their start and end apart: 38, of which 12 were waited for; matrix products, arithmetic and copies ran while one was open for 7% of the time, Pallas kernels for 7%

profile of v6, /device:TPU:32, one launch (start us, length us, event | category | flops | bytes accessed | tf_op | source)
XLA Modules:
  0.0 140.1 jit_solution(5618245644531715676)
XLA Ops:
  4.0 4.3 %fusion.8.refs_0_ = bf16[64,4096]{1,0:T(8,128)(2,1)S(1)} fusion(s32[1,64,4096]{2,1,0:T(8,128)} %param.8, f32[1,64,4096]{2,1,0:T(8,128)} %param.10, f32[1,64,4096]{2,1,0:T(8,128)} %param.9), kind=kLoop, calls=%fused_computation.15 | loop fusion | flops 17563648 | bytes 3670016 | tf_op jit(solution)/shard_map/squeeze | solution.py:343
  8.5 3.1 %collective-permute-start.1 = (bf16[128,512]{1,0:T(8,128)(2,1)S(1)}, bf16[128,512]{1,0:T(8,128)(2,1)S(1)}, u32[]{:S(2)}, u32[]{:S(2)}) collective-permute-start(bf16[128,512]{1,0:T(8,128)(2,1)S(1)} %maximum_select_fusion), channel_id=1, source_target_pairs={{0,48},{16,0},{32,16},{48,32},{1,49},{17,1},{33,17},{49,33},{2,50}... | collective-permute-start | bytes 393224 | tf_op jit(solution)/shard_map/ppermute | solution.py:74
  12.2 2.7 %collective-permute-start.5 = (bf16[64,4096]{1,0:T(8,128)(2,1)S(1)}, bf16[64,4096]{1,0:T(8,128)(2,1)}, u32[]{:S(2)}, u32[]{:S(2)}) collective-permute-start(bf16[64,4096]{1,0:T(8,128)(2,1)S(1)} %fusion.8.refs_0_), channel_id=1, source_target_pairs={{0,129},{1,0},{128,1},{129,128},{2,131},{3,2},{130,3},{131,130},{4... | collective-permute-start | bytes 1572872 | tf_op jit(solution)/shard_map/ppermute | solution.py:74
  14.9 2.0 %collective-permute-start.2 = (bf16[2,128,512]{2,1,0:T(8,128)(2,1)S(1)}, bf16[2,128,512]{2,1,0:T(8,128)(2,1)S(1)}, u32[]{:S(2)}, u32[]{:S(2)}) collective-permute-start(bf16[2,128,512]{2,1,0:T(8,128)(2,1)S(1)} %pad_maximum_fusion.refs_8_.refs_6_.refs_10_.refs_4_), channel_id=1, source_target_pairs={{0,2},{2,4},{4,6},{6,8},{8,10},{10,12},{12,14},{14,0},{1,3},{3,5},... | collective-permute-start | bytes 786440 | tf_op jit(solution)/shard_map/ppermute | solution.py:74
  17.7 1.9 %collective-permute-start.12 = (bf16[64,4096]{1,0:T(8,128)(2,1)S(1)}, bf16[64,4096]{1,0:T(8,128)(2,1)S(1)}, u32[]{:S(2)}, u32[]{:S(2)}) collective-permute-start(bf16[64,4096]{1,0:T(8,128)(2,1)S(1)} %fusion.8.refs_0_), channel_id=1, source_target_pairs={{0,128},{1,129},{128,0},{129,1},{2,130},{3,131},{130,2},{131,3},{4... | collective-permute-start | bytes 1572872 | tf_op jit(solution)/shard_map/ppermute | solution.py:74
  19.7 2.3 %collective-permute-done.2.refs_11_.refs_9_.refs_13_.refs_7_ = bf16[2,128,512]{2,1,0:T(8,128)(2,1)S(1)} collective-permute-done((bf16[2,128,512]{2,1,0:T(8,128)(2,1)S(1)}, bf16[2,128,512]{2,1,0:T(8,128)(2,1)S(1)}, u32[]{:S(2)}, u32[]{:S(2)}) %collective-permute-start.2) | collective-permute-done | bytes 262176 | tf_op jit(solution)/shard_map/ppermute | solution.py:74
  21.9 1.8 %collective-permute-done.3.refs_12_.refs_10_.refs_14_.refs_8_ = bf16[2,128,512]{2,1,0:T(8,128)(2,1)S(1)} collective-permute-done((bf16[2,128,512]{2,1,0:T(8,128)(2,1)S(1)}, bf16[2,128,512]{2,1,0:T(8,128)(2,1)S(1)}, u32[]{:S(2)}, u32[]{:S(2)}) %collective-permute-start.3) | collective-permute-done | bytes 262176 | tf_op jit(solution)/shard_map/ppermute | solution.py:74
  23.8 3.7 %collective-permute-done.4.refs_4_ = bf16[64,4096]{1,0:T(8,128)(2,1)S(1)} collective-permute-done((bf16[64,4096]{1,0:T(8,128)(2,1)S(1)}, bf16[64,4096]{1,0:T(8,128)(2,1)S(1)}, u32[]{:S(2)}, u32[]{:S(2)}) %collective-permute-start.4) | collective-permute-done | bytes 524320 | tf_op jit(solution)/shard_map/ppermute | solution.py:74
  28.2 8.4 %collective-permute-done.5.refs_6_ = bf16[64,4096]{1,0:T(8,128)(2,1)} collective-permute-done((bf16[64,4096]{1,0:T(8,128)(2,1)S(1)}, bf16[64,4096]{1,0:T(8,128)(2,1)}, u32[]{:S(2)}, u32[]{:S(2)}) %collective-permute-start.5) | collective-permute-done | bytes 524320 | tf_op jit(solution)/shard_map/ppermute | solution.py:74
  36.5 1.9 %collective-permute-start.6 = (bf16[2,128,512]{2,1,0:T(8,128)(2,1)S(1)}, bf16[2,128,512]{2,1,0:T(8,128)(2,1)S(1)}, u32[]{:S(2)}, u32[]{:S(2)}) collective-permute-start(bf16[2,128,512]{2,1,0:T(8,128)(2,1)S(1)} %collective-permute-done.2.refs_11_.refs_9_.refs_13_.refs_7_), channel_id=1, source_target_pairs={{0,2},{2,4},{4,6},{6,8},{8,10},{10,12},{12,14},{14,0},{1,3},{3,5},... | collective-permute-start | bytes 786440 | tf_op jit(solution)/shard_map/ppermute | solution.py:74
  40.2 3.2 %collective-permute-start.10 = (bf16[2,128,512]{2,1,0:T(8,128)(2,1)S(1)}, bf16[2,128,512]{2,1,0:T(8,128)(2,1)S(1)}, u32[]{:S(2)}, u32[]{:S(2)}) collective-permute-start(bf16[2,128,512]{2,1,0:T(8,128)(2,1)S(1)} %pad_maximum_fusion.1), channel_id=1, source_target_pairs={{0,48},{16,0},{32,16},{48,32},{1,49},{17,1},{33,17},{49,33},{2,50}... | collective-permute-start | bytes 786440 | tf_op jit(solution)/shard_map/ppermute | solution.py:74
  47.9 2.0 %collective-permute-start.14 = (bf16[2,128,512]{2,1,0:T(8,128)(2,1)S(1)}, bf16[2,128,512]{2,1,0:T(8,128)(2,1)S(1)}, u32[]{:S(2)}, u32[]{:S(2)}) collective-permute-start(bf16[2,128,512]{2,1,0:T(8,128)(2,1)S(1)} %collective-permute-done.6.refs_15_.refs_13_.refs_17_.refs_11_), channel_id=1, source_target_pairs={{0,2},{2,4},{4,6},{6,8},{8,10},{10,12},{12,14},{14,0},{1,3},{3,5},... | collective-permute-start | bytes 786440 | tf_op jit(solution)/shard_map/ppermute | solution.py:74
  50.1 3.4 %collective-permute-start.16 = (bf16[2,128,512]{2,1,0:T(8,128)(2,1)S(1)}, bf16[2,128,512]{2,1,0:T(8,128)(2,1)S(1)}, u32[]{:S(2)}, u32[]{:S(2)}) collective-permute-start(bf16[2,128,512]{2,1,0:T(8,128)(2,1)S(1)} %pad_maximum_fusion.3), channel_id=1, source_target_pairs={{0,48},{16,0},{32,16},{48,32},{1,49},{17,1},{33,17},{49,33},{2,50}... | collective-permute-start | bytes 786440 | tf_op jit(solution)/shard_map/ppermute | solution.py:74
  53.4 2.2 %collective-permute-start.15 = (bf16[2,128,512]{2,1,0:T(8,128)(2,1)S(1)}, bf16[2,128,512]{2,1,0:T(8,128)(2,1)S(1)}, u32[]{:S(2)}, u32[]{:S(2)}) collective-permute-start(bf16[2,128,512]{2,1,0:T(8,128)(2,1)S(1)} %collective-permute-done.7.refs_16_.refs_14_.refs_18_.refs_12_), channel_id=1, source_target_pairs={{0,14},{2,0},{4,2},{6,4},{8,6},{10,8},{12,10},{14,12},{1,15},{3,1}... | collective-permute-start | bytes 786440 | tf_op jit(solution)/shard_map/ppermute | solution.py:74
  55.6 4.7 %collective-permute-done.17.refs_18_.refs_16_.refs_20_.refs_14_ = bf16[2,128,512]{2,1,0:T(8,128)(2,1)S(1)} collective-permute-done((bf16[2,128,512]{2,1,0:T(8,128)(2,1)S(1)}, bf16[2,128,512]{2,1,0:T(8,128)(2,1)S(1)}, u32[]{:S(2)}, u32[]{:S(2)}) %collective-permute-start.17) | collective-permute-done | bytes 262176 | tf_op jit(solution)/shard_map/ppermute | solution.py:74
  60.3 3.0 %collective-permute-done.15.refs_20_.refs_18_.refs_22_.refs_16_ = bf16[2,128,512]{2,1,0:T(8,128)(2,1)S(1)} collective-permute-done((bf16[2,128,512]{2,1,0:T(8,128)(2,1)S(1)}, bf16[2,128,512]{2,1,0:T(8,128)(2,1)S(1)}, u32[]{:S(2)}, u32[]{:S(2)}) %collective-permute-start.15) | collective-permute-done | bytes 262176 | tf_op jit(solution)/shard_map/ppermute | solution.py:74
  63.3 3.2 %collective-permute-start.23 = (bf16[1,128,512]{2,1,0:T(8,128)(2,1)S(1)}, bf16[1,128,512]{2,1,0:T(8,128)(2,1)S(1)}, u32[]{:S(2)}, u32[]{:S(2)}) collective-permute-start(bf16[1,128,512]{2,1,0:T(8,128)(2,1)S(1)} %get-tuple-element.73), channel_id=1, source_target_pairs={{0,2},{2,4},{4,6},{6,8},{8,10},{10,12},{12,14},{14,0},{1,3},{3,5},... | collective-permute-start | bytes 393224 | tf_op jit(solution)/shard_map/ppermute | solution.py:74
  66.8 3.2 %collective-permute-start.21 = (bf16[2,128,512]{2,1,0:T(8,128)(2,1)S(1)}, bf16[2,128,512]{2,1,0:T(8,128)(2,1)S(1)}, u32[]{:S(2)}, u32[]{:S(2)}) collective-permute-start(bf16[2,128,512]{2,1,0:T(8,128)(2,1)S(1)} %pad_maximum_fusion.5), channel_id=1, source_target_pairs={{0,48},{16,0},{32,16},{48,32},{1,49},{17,1},{33,17},{49,33},{2,50}... | collective-permute-start | bytes 786440 | tf_op jit(solution)/shard_map/ppermute | solution.py:74
  70.0 2.6 %collective-permute-done.24.refs_11_.refs_22_.refs_26_.refs_20_ = bf16[1,128,512]{2,1,0:T(8,128)(2,1)S(1)} collective-permute-done((bf16[1,128,512]{2,1,0:T(8,128)(2,1)S(1)}, bf16[1,128,512]{2,1,0:T(8,128)(2,1)S(1)}, u32[]{:S(2)}, u32[]{:S(2)}) %collective-permute-start.24) | collective-permute-done | bytes 131104 | tf_op jit(solution)/shard_map/ppermute | solution.py:74
  72.6 3.1 %collective-permute-start.25 = (bf16[1,128,512]{2,1,0:T(8,128)(2,1)S(1)}, bf16[1,128,512]{2,1,0:T(8,128)(2,1)S(1)}, u32[]{:S(2)}, u32[]{:S(2)}) collective-permute-start(bf16[1,128,512]{2,1,0:T(8,128)(2,1)S(1)} %collective-permute-done.24.refs_11_.refs_22_.refs_26_.refs_20_), channel_id=1, source_target_pairs={{0,48},{16,0},{32,16},{48,32},{1,49},{17,1},{33,17},{49,33},{2,50}... | collective-permute-start | bytes 393224 | tf_op jit(solution)/shard_map/ppermute | solution.py:74
  75.8 3.2 %near_product.1.refs_14_ = f32[512,512]{1,0:T(8,128)S(1)} custom-call(s32[4]{0:T(128)S(1)} %pad_add_fusion.first_ref.place_ref, bf16[64,4096]{1,0:T(8,128)(2,1)S(1)} %fusion.8.refs_0_, bf16[64,4096]{1,0:T(8,128)(2,1)} %collective-permute-done.13.refs_1_, bf16[64,4096]{1,0:T(8,128)(2,1)S(1)} %copy-done.1, ...), custom_call_target="tpu_custom_call" | custom-call | flops 1610612736 | bytes 8388608 | tf_op jit(solution)/shard_map/near_product/pallas_call | solution.py:158
  79.0 3.0 %collective-permute-done.26.refs_13_.refs_24_.refs_28_.refs_22_ = bf16[1,128,512]{2,1,0:T(8,128)(2,1)S(1)} collective-permute-done((bf16[1,128,512]{2,1,0:T(8,128)(2,1)S(1)}, bf16[1,128,512]{2,1,0:T(8,128)(2,1)S(1)}, u32[]{:S(2)}, u32[]{:S(2)}) %collective-permute-start.26) | collective-permute-done | bytes 131104 | tf_op jit(solution)/shard_map/ppermute | solution.py:74
  81.9 2.7 %first_product.1 = bf16[512,512]{1,0:T(8,128)(2,1)S(1)} custom-call(f32[8,4]{1,0:T(8,128)S(1)} %broadcast_select_fusion.mix_ref, s32[4]{0:T(128)S(1)} %pad_add_fusion.first_ref.place_ref, bf16[64,4096]{1,0:T(8,128)(2,1)S(1)} %fusion.8.refs_0_, bf16[64,4096]{1,0:T(8,128)(2,1)} %collective-permute-done.13.refs_1_, bf16[64,4096]{1,0:T(8,128)(2,1)S(1)} %copy-done.1, ...), custom_call_target="tpu_custom_call" | custom-call | flops 536870912 | bytes 4194304 | tf_op jit(solution)/shard_map/first_product/pallas_call | solution.py:196
  84.6 22.0 %all_to_all.5 = bf16[32,16,512]{2,1,0:T(8,128)(2,1)S(1)} all-to-all(bf16[32,16,512]{2,1,0:T(8,128)(2,1)S(1)} %bitcast.36), channel_id=1, replica_groups=mesh['hi'=2,'core'=2,'y'=4,'z'=8,'lo'=2] {'y','z'}, dimensions={0} | all-to-all | bytes 1048576 | tf_op jit(solution)/shard_map/all_to_all | solution.py:400
  106.7 1.7 %collective-permute-start.28 = (bf16[2,32,4096]{2,1,0:T(8,128)(2,1)S(1)}, bf16[2,32,4096]{2,1,0:T(8,128)(2,1)S(1)}, u32[]{:S(2)}, u32[]{:S(2)}) collective-permute-start(bf16[2,32,4096]{2,1,0:T(8,128)(2,1)S(1)} %copy_bitcast_fusion.refs_0_), channel_id=1, source_target_pairs={{0,1},{1,128},{128,129},{129,0},{2,3},{3,130},{130,131},{131,2},{4... | collective-permute-start | bytes 1572872 | tf_op jit(solution)/shard_map/ppermute | solution.py:74
  108.4 2.2 %collective-permute-start.30 = (bf16[2,32,4096]{2,1,0:T(8,128)(2,1)S(1)}, bf16[2,32,4096]{2,1,0:T(8,128)(2,1)S(1)}, u32[]{:S(2)}, u32[]{:S(2)}) collective-permute-start(bf16[2,32,4096]{2,1,0:T(8,128)(2,1)S(1)} %copy_bitcast_fusion.refs_0_), channel_id=1, source_target_pairs={{0,129},{1,0},{128,1},{129,128},{2,131},{3,2},{130,3},{131,130},{4... | collective-permute-start | bytes 1572872 | tf_op jit(solution)/shard_map/ppermute | solution.py:74
  110.6 8.3 %collective-permute-done.28.refs_2_.refs_6_ = bf16[2,32,4096]{2,1,0:T(8,128)(2,1)S(1)} collective-permute-done((bf16[2,32,4096]{2,1,0:T(8,128)(2,1)S(1)}, bf16[2,32,4096]{2,1,0:T(8,128)(2,1)S(1)}, u32[]{:S(2)}, u32[]{:S(2)}) %collective-permute-start.28) | collective-permute-done | bytes 524320 | tf_op jit(solution)/shard_map/ppermute | solution.py:74
  120.2 2.7 %collective-permute-start.31 = (bf16[2,16,4096]{2,1,0:T(8,128)(2,1)S(1)}, bf16[2,16,4096]{2,1,0:T(8,128)(2,1)S(1)}, u32[]{:S(2)}, u32[]{:S(2)}) collective-permute-start(bf16[2,16,4096]{2,1,0:T(8,128)(2,1)S(1)} %slice.73), channel_id=1, source_target_pairs={{0,129},{1,0},{128,1},{129,128},{2,131},{3,2},{130,3},{131,130},{4... | collective-permute-start | bytes 786440 | tf_op jit(solution)/shard_map/ppermute | solution.py:74
  122.9 1.7 %sent_rows.2 = bf16[192,512]{1,0:T(8,128)(2,1)S(1)} custom-call(s32[4]{0:T(128)S(1)} %pad_add_fusion.first_ref.place_ref, bf16[2,32,4096]{2,1,0:T(8,128)(2,1)S(1)} %copy_bitcast_fusion.refs_0_, bf16[2,32,4096]{2,1,0:T(8,128)(2,1)S(1)} %collective-permute-done.27.refs_1_, bf16[2,32,4096]{2,1,0:T(8,128)(2,1)S(1)} %collective-permute-done.28.refs_2_.refs_6_, ...), custom_call_target="tpu_custom_call" | custom-call | flops 805306368 | bytes 6291456 | tf_op jit(solution)/shard_map/sent_rows/pallas_call | solution.py:240
  124.7 4.4 %collective-permute-done.29.refs_2_.refs_0_ = bf16[2,16,4096]{2,1,0:T(8,128)(2,1)S(1)} collective-permute-done((bf16[2,16,4096]{2,1,0:T(8,128)(2,1)S(1)}, bf16[2,16,4096]{2,1,0:T(8,128)(2,1)S(1)}, u32[]{:S(2)}, u32[]{:S(2)}) %collective-permute-start.29) | collective-permute-done | bytes 262176 | tf_op jit(solution)/shard_map/ppermute | solution.py:74
  133.9 3.1 %kept_rows.1.kept_ref = f32[4,64,1024]{2,1,0:T(8,128)S(1)} custom-call(s32[4]{0:T(128)S(1)} %pad_add_fusion.first_ref.place_ref, s32[8]{0:T(128)S(1)} %get-tuple-element.72.slice_ref, bf16[2,32,4096]{2,1,0:T(8,128)(2,1)S(1)} %copy_bitcast_fusion.refs_0_, bf16[2,32,4096]{2,1,0:T(8,128)(2,1)S(1)} %collective-permute-done.27.refs_1_, ...), custom_call_target="tpu_custom_call" | custom-call | flops 1073741824 | bytes 6291456 | tf_op jit(solution)/shard_map/kept_rows/pallas_call | solution.py:282
  137.9 2.2 %whitened_gradient.1 = f32[64,4,1024]{2,1,0:T(4,128)} custom-call(s32[4]{0:T(128)S(1)} %pad_add_fusion.first_ref.place_ref, s32[8]{0:T(128)S(1)} %pad_add_fusion.1.slice_ref, f32[4,64,1024]{2,1,0:T(8,128)S(1)} %kept_rows.1.kept_ref, bf16[192,512]{1,0:T(8,128)(2,1)S(1)} %collective-permute-done.36.early_ref, ...), custom_call_target="tpu_custom_call" | custom-call | tf_op jit(solution)/shard_map/whitened_gradient/pallas_call | solution.py:319
  (101 shorter events, 19.2 us)
Async XLA Ops:
  1.8 6.7 %collective-permute-start = (bf16[64,512]{1,0:T(8,128)(2,1)S(1)}, bf16[64,512]{1,0:T(8,128)(2,1)S(1)}, u32[]{:S(2)}, u32[]{:S(2)}) collective-permute-start(bf16[64,512]{1,0:T(8,128)(2,1)S(1)} %get-tuple-element.39), channel_id=1, source_target_pairs={{0,1},{1,0},{2,3},{3,2},{4,5},{5,4},{6,7},{7,6},{8,9},{9,8},{10,11... | collective-permute-start | bytes 196616 | tf_op jit(solution)/shard_map/ppermute | solution.py:74
  8.5 6.4 %collective-permute-start.1 = (bf16[128,512]{1,0:T(8,128)(2,1)S(1)}, bf16[128,512]{1,0:T(8,128)(2,1)S(1)}, u32[]{:S(2)}, u32[]{:S(2)}) collective-permute-start(bf16[128,512]{1,0:T(8,128)(2,1)S(1)} %maximum_select_fusion), channel_id=1, source_target_pairs={{0,48},{16,0},{32,16},{48,32},{1,49},{17,1},{33,17},{49,33},{2,50}... | collective-permute-start | bytes 393224 | tf_op jit(solution)/shard_map/ppermute | solution.py:74
  11.6 15.8 %collective-permute-start.4 = (bf16[64,4096]{1,0:T(8,128)(2,1)S(1)}, bf16[64,4096]{1,0:T(8,128)(2,1)S(1)}, u32[]{:S(2)}, u32[]{:S(2)}) collective-permute-start(bf16[64,4096]{1,0:T(8,128)(2,1)S(1)} %fusion.8.refs_0_), channel_id=1, source_target_pairs={{0,1},{1,128},{128,129},{129,0},{2,3},{3,130},{130,131},{131,2},{4... | collective-permute-start | bytes 1572872 | tf_op jit(solution)/shard_map/ppermute | solution.py:74
  12.2 24.3 %collective-permute-start.5 = (bf16[64,4096]{1,0:T(8,128)(2,1)S(1)}, bf16[64,4096]{1,0:T(8,128)(2,1)}, u32[]{:S(2)}, u32[]{:S(2)}) collective-permute-start(bf16[64,4096]{1,0:T(8,128)(2,1)S(1)} %fusion.8.refs_0_), channel_id=1, source_target_pairs={{0,129},{1,0},{128,1},{129,128},{2,131},{3,2},{130,3},{131,130},{4... | collective-permute-start | bytes 1572872 | tf_op jit(solution)/shard_map/ppermute | solution.py:74
  14.9 7.0 %collective-permute-start.2 = (bf16[2,128,512]{2,1,0:T(8,128)(2,1)S(1)}, bf16[2,128,512]{2,1,0:T(8,128)(2,1)S(1)}, u32[]{:S(2)}, u32[]{:S(2)}) collective-permute-start(bf16[2,128,512]{2,1,0:T(8,128)(2,1)S(1)} %pad_maximum_fusion.refs_8_.refs_6_.refs_10_.refs_4_), channel_id=1, source_target_pairs={{0,2},{2,4},{4,6},{6,8},{8,10},{10,12},{12,14},{14,0},{1,3},{3,5},... | collective-permute-start | bytes 786440 | tf_op jit(solution)/shard_map/ppermute | solution.py:74
  16.9 6.8 %collective-permute-start.3 = (bf16[2,128,512]{2,1,0:T(8,128)(2,1)S(1)}, bf16[2,128,512]{2,1,0:T(8,128)(2,1)S(1)}, u32[]{:S(2)}, u32[]{:S(2)}) collective-permute-start(bf16[2,128,512]{2,1,0:T(8,128)(2,1)S(1)} %pad_maximum_fusion.refs_8_.refs_6_.refs_10_.refs_4_), channel_id=1, source_target_pairs={{0,14},{2,0},{4,2},{6,4},{8,6},{10,8},{12,10},{14,12},{1,15},{3,1}... | collective-permute-start | bytes 786440 | tf_op jit(solution)/shard_map/ppermute | solution.py:74
  17.7 21.7 %collective-permute-start.12 = (bf16[64,4096]{1,0:T(8,128)(2,1)S(1)}, bf16[64,4096]{1,0:T(8,128)(2,1)S(1)}, u32[]{:S(2)}, u32[]{:S(2)}) collective-permute-start(bf16[64,4096]{1,0:T(8,128)(2,1)S(1)} %fusion.8.refs_0_), channel_id=1, source_target_pairs={{0,128},{1,129},{128,0},{129,1},{2,130},{3,131},{130,2},{131,3},{4... | collective-permute-start | bytes 1572872 | tf_op jit(solution)/shard_map/ppermute | solution.py:74
  21.9 25.3 %collective-permute-start.13 = (bf16[64,4096]{1,0:T(8,128)(2,1)S(1)}, bf16[64,4096]{1,0:T(8,128)(2,1)}, u32[]{:S(2)}, u32[]{:S(2)}) collective-permute-start(bf16[64,4096]{1,0:T(8,128)(2,1)S(1)} %fusion.8.refs_0_), channel_id=1, source_target_pairs={{0,64},{64,0},{1,65},{65,1},{2,66},{66,2},{3,67},{67,3},{4,68},{68... | collective-permute-start | bytes 1572872 | tf_op jit(solution)/shard_map/ppermute | solution.py:74
  23.7 15.5 %collective-permute-start.9 = (bf16[1,128,512]{2,1,0:T(8,128)(2,1)S(1)}, bf16[1,128,512]{2,1,0:T(8,128)(2,1)S(1)}, u32[]{:S(2)}, u32[]{:S(2)}) collective-permute-start(bf16[1,128,512]{2,1,0:T(8,128)(2,1)S(1)} %bitcast.42), channel_id=1, source_target_pairs={{0,16},{16,32},{32,48},{48,0},{1,17},{17,33},{33,49},{49,1},{2,18}... | collective-permute-start | bytes 393224 | tf_op jit(solution)/shard_map/ppermute | solution.py:74
  27.4 12.0 %collective-permute-start.8 = (bf16[1,128,512]{2,1,0:T(8,128)(2,1)S(1)}, bf16[1,128,512]{2,1,0:T(8,128)(2,1)S(1)}, u32[]{:S(2)}, u32[]{:S(2)}) collective-permute-start(bf16[1,128,512]{2,1,0:T(8,128)(2,1)S(1)} %bitcast.44), channel_id=1, source_target_pairs={{0,48},{16,0},{32,16},{48,32},{1,49},{17,1},{33,17},{49,33},{2,50}... | collective-permute-start | bytes 393224 | tf_op jit(solution)/shard_map/ppermute | solution.py:74
  36.5 11.2 %collective-permute-start.6 = (bf16[2,128,512]{2,1,0:T(8,128)(2,1)S(1)}, bf16[2,128,512]{2,1,0:T(8,128)(2,1)S(1)}, u32[]{:S(2)}, u32[]{:S(2)}) collective-permute-start(bf16[2,128,512]{2,1,0:T(8,128)(2,1)S(1)} %collective-permute-done.2.refs_11_.refs_9_.refs_13_.refs_7_), channel_id=1, source_target_pairs={{0,2},{2,4},{4,6},{6,8},{8,10},{10,12},{12,14},{14,0},{1,3},{3,5},... | collective-permute-start | bytes 786440 | tf_op jit(solution)/shard_map/ppermute | solution.py:74
  39.2 8.5 %collective-permute-start.7 = (bf16[2,128,512]{2,1,0:T(8,128)(2,1)S(1)}, bf16[2,128,512]{2,1,0:T(8,128)(2,1)S(1)}, u32[]{:S(2)}, u32[]{:S(2)}) collective-permute-start(bf16[2,128,512]{2,1,0:T(8,128)(2,1)S(1)} %collective-permute-done.3.refs_12_.refs_10_.refs_14_.refs_8_), channel_id=1, source_target_pairs={{0,14},{2,0},{4,2},{6,4},{8,6},{10,8},{12,10},{14,12},{1,15},{3,1}... | collective-permute-start | bytes 786440 | tf_op jit(solution)/shard_map/ppermute | solution.py:74
  39.4 7.8 %collective-permute-start.11 = (bf16[2,128,512]{2,1,0:T(8,128)(2,1)}, bf16[2,128,512]{2,1,0:T(8,128)(2,1)S(1)}, u32[]{:S(2)}, u32[]{:S(2)}) collective-permute-start(bf16[2,128,512]{2,1,0:T(8,128)(2,1)} %pad_maximum_fusion.2), channel_id=1, source_target_pairs={{0,16},{16,32},{32,48},{48,0},{1,17},{17,33},{33,49},{49,1},{2,18}... | collective-permute-start | bytes 786440 | tf_op jit(solution)/shard_map/ppermute | solution.py:74
  40.2 7.5 %collective-permute-start.10 = (bf16[2,128,512]{2,1,0:T(8,128)(2,1)S(1)}, bf16[2,128,512]{2,1,0:T(8,128)(2,1)S(1)}, u32[]{:S(2)}, u32[]{:S(2)}) collective-permute-start(bf16[2,128,512]{2,1,0:T(8,128)(2,1)S(1)} %pad_maximum_fusion.1), channel_id=1, source_target_pairs={{0,48},{16,0},{32,16},{48,32},{1,49},{17,1},{33,17},{49,33},{2,50}... | collective-permute-start | bytes 786440 | tf_op jit(solution)/shard_map/ppermute | solution.py:74
  47.3 6.2 %collective-permute-start.20 = (bf16[64,4096]{1,0:T(8,128)(2,1)}, bf16[64,4096]{1,0:T(8,128)(2,1)S(1)}, u32[]{:S(2)}, u32[]{:S(2)}) collective-permute-start(bf16[64,4096]{1,0:T(8,128)(2,1)} %collective-permute-done.5.refs_6_), channel_id=1, source_target_pairs={{0,64},{64,0},{1,65},{65,1},{2,66},{66,2},{3,67},{67,3},{4,68},{68... | collective-permute-start | bytes 1572872 | tf_op jit(solution)/shard_map/ppermute | solution.py:74
  47.9 12.4 %collective-permute-start.14 = (bf16[2,128,512]{2,1,0:T(8,128)(2,1)S(1)}, bf16[2,128,512]{2,1,0:T(8,128)(2,1)S(1)}, u32[]{:S(2)}, u32[]{:S(2)}) collective-permute-start(bf16[2,128,512]{2,1,0:T(8,128)(2,1)S(1)} %collective-permute-done.6.refs_15_.refs_13_.refs_17_.refs_11_), channel_id=1, source_target_pairs={{0,2},{2,4},{4,6},{6,8},{8,10},{10,12},{12,14},{14,0},{1,3},{3,5},... | collective-permute-start | bytes 786440 | tf_op jit(solution)/shard_map/ppermute | solution.py:74
  49.9 13.4 %collective-permute-start.18 = (bf16[64,4096]{1,0:T(8,128)(2,1)S(1)}, bf16[64,4096]{1,0:T(8,128)(2,1)S(1)}, u32[]{:S(2)}, u32[]{:S(2)}) collective-permute-start(bf16[64,4096]{1,0:T(8,128)(2,1)S(1)} %copy-done.1), channel_id=1, source_target_pairs={{0,64},{64,0},{1,65},{65,1},{2,66},{66,2},{3,67},{67,3},{4,68},{68... | collective-permute-start | bytes 1572872 | tf_op jit(solution)/shard_map/ppermute | solution.py:74
  49.9 10.3 %collective-permute-start.17 = (bf16[2,128,512]{2,1,0:T(8,128)(2,1)S(1)}, bf16[2,128,512]{2,1,0:T(8,128)(2,1)S(1)}, u32[]{:S(2)}, u32[]{:S(2)}) collective-permute-start(bf16[2,128,512]{2,1,0:T(8,128)(2,1)S(1)} %pad_maximum_fusion.4), channel_id=1, source_target_pairs={{0,16},{16,32},{32,48},{48,0},{1,17},{17,33},{33,49},{49,1},{2,18}... | collective-permute-start | bytes 786440 | tf_op jit(solution)/shard_map/ppermute | solution.py:74
  50.1 10.2 %collective-permute-start.16 = (bf16[2,128,512]{2,1,0:T(8,128)(2,1)S(1)}, bf16[2,128,512]{2,1,0:T(8,128)(2,1)S(1)}, u32[]{:S(2)}, u32[]{:S(2)}) collective-permute-start(bf16[2,128,512]{2,1,0:T(8,128)(2,1)S(1)} %pad_maximum_fusion.3), channel_id=1, source_target_pairs={{0,48},{16,0},{32,16},{48,32},{1,49},{17,1},{33,17},{49,33},{2,50}... | collective-permute-start | bytes 786440 | tf_op jit(solution)/shard_map/ppermute | solution.py:74
  53.4 9.8 %collective-permute-start.15 = (bf16[2,128,512]{2,1,0:T(8,128)(2,1)S(1)}, bf16[2,128,512]{2,1,0:T(8,128)(2,1)S(1)}, u32[]{:S(2)}, u32[]{:S(2)}) collective-permute-start(bf16[2,128,512]{2,1,0:T(8,128)(2,1)S(1)} %collective-permute-done.7.refs_16_.refs_14_.refs_18_.refs_12_), channel_id=1, source_target_pairs={{0,14},{2,0},{4,2},{6,4},{8,6},{10,8},{12,10},{14,12},{1,15},{3,1}... | collective-permute-start | bytes 786440 | tf_op jit(solution)/shard_map/ppermute | solution.py:74
  63.3 12.5 %collective-permute-start.23 = (bf16[1,128,512]{2,1,0:T(8,128)(2,1)S(1)}, bf16[1,128,512]{2,1,0:T(8,128)(2,1)S(1)}, u32[]{:S(2)}, u32[]{:S(2)}) collective-permute-start(bf16[1,128,512]{2,1,0:T(8,128)(2,1)S(1)} %get-tuple-element.73), channel_id=1, source_target_pairs={{0,2},{2,4},{4,6},{6,8},{8,10},{10,12},{12,14},{14,0},{1,3},{3,5},... | collective-permute-start | bytes 393224 | tf_op jit(solution)/shard_map/ppermute | solution.py:74
  66.5 12.4 %collective-permute-start.22 = (bf16[2,128,512]{2,1,0:T(8,128)(2,1)S(1)}, bf16[2,128,512]{2,1,0:T(8,128)(2,1)S(1)}, u32[]{:S(2)}, u32[]{:S(2)}) collective-permute-start(bf16[2,128,512]{2,1,0:T(8,128)(2,1)S(1)} %pad_maximum_fusion.6), channel_id=1, source_target_pairs={{0,16},{16,32},{32,48},{48,0},{1,17},{17,33},{33,49},{49,1},{2,18}... | collective-permute-start | bytes 786440 | tf_op jit(solution)/shard_map/ppermute | solution.py:74
  66.6 6.0 %collective-permute-start.24 = (bf16[1,128,512]{2,1,0:T(8,128)(2,1)S(1)}, bf16[1,128,512]{2,1,0:T(8,128)(2,1)S(1)}, u32[]{:S(2)}, u32[]{:S(2)}) collective-permute-start(bf16[1,128,512]{2,1,0:T(8,128)(2,1)S(1)} %get-tuple-element.76), channel_id=1, source_target_pairs={{0,14},{2,0},{4,2},{6,4},{8,6},{10,8},{12,10},{14,12},{1,15},{3,1}... | collective-permute-start | bytes 393224 | tf_op jit(solution)/shard_map/ppermute | solution.py:74
  66.8 12.2 %collective-permute-start.21 = (bf16[2,128,512]{2,1,0:T(8,128)(2,1)S(1)}, bf16[2,128,512]{2,1,0:T(8,128)(2,1)S(1)}, u32[]{:S(2)}, u32[]{:S(2)}) collective-permute-start(bf16[2,128,512]{2,1,0:T(8,128)(2,1)S(1)} %pad_maximum_fusion.5), channel_id=1, source_target_pairs={{0,48},{16,0},{32,16},{48,32},{1,49},{17,1},{33,17},{49,33},{2,50}... | collective-permute-start | bytes 786440 | tf_op jit(solution)/shard_map/ppermute | solution.py:74
  72.6 6.3 %collective-permute-start.25 = (bf16[1,128,512]{2,1,0:T(8,128)(2,1)S(1)}, bf16[1,128,512]{2,1,0:T(8,128)(2,1)S(1)}, u32[]{:S(2)}, u32[]{:S(2)}) collective-permute-start(bf16[1,128,512]{2,1,0:T(8,128)(2,1)S(1)} %collective-permute-done.24.refs_11_.refs_22_.refs_26_.refs_20_), channel_id=1, source_target_pairs={{0,48},{16,0},{32,16},{48,32},{1,49},{17,1},{33,17},{49,33},{2,50}... | collective-permute-start | bytes 393224 | tf_op jit(solution)/shard_map/ppermute | solution.py:74
  75.8 6.2 %collective-permute-start.26 = (bf16[1,128,512]{2,1,0:T(8,128)(2,1)S(1)}, bf16[1,128,512]{2,1,0:T(8,128)(2,1)S(1)}, u32[]{:S(2)}, u32[]{:S(2)}) collective-permute-start(bf16[1,128,512]{2,1,0:T(8,128)(2,1)S(1)} %collective-permute-done.23.refs_10_.refs_21_.refs_25_.refs_19_), channel_id=1, source_target_pairs={{0,16},{16,32},{32,48},{48,0},{1,17},{17,33},{33,49},{49,1},{2,18}... | collective-permute-start | bytes 393224 | tf_op jit(solution)/shard_map/ppermute | solution.py:74
  106.7 12.3 %collective-permute-start.28 = (bf16[2,32,4096]{2,1,0:T(8,128)(2,1)S(1)}, bf16[2,32,4096]{2,1,0:T(8,128)(2,1)S(1)}, u32[]{:S(2)}, u32[]{:S(2)}) collective-permute-start(bf16[2,32,4096]{2,1,0:T(8,128)(2,1)S(1)} %copy_bitcast_fusion.refs_0_), channel_id=1, source_target_pairs={{0,1},{1,128},{128,129},{129,0},{2,3},{3,130},{130,131},{131,2},{4... | collective-permute-start | bytes 1572872 | tf_op jit(solution)/shard_map/ppermute | solution.py:74
  108.4 10.5 %collective-permute-start.30 = (bf16[2,32,4096]{2,1,0:T(8,128)(2,1)S(1)}, bf16[2,32,4096]{2,1,0:T(8,128)(2,1)S(1)}, u32[]{:S(2)}, u32[]{:S(2)}) collective-permute-start(bf16[2,32,4096]{2,1,0:T(8,128)(2,1)S(1)} %copy_bitcast_fusion.refs_0_), channel_id=1, source_target_pairs={{0,129},{1,0},{128,1},{129,128},{2,131},{3,2},{130,3},{131,130},{4... | collective-permute-start | bytes 1572872 | tf_op jit(solution)/shard_map/ppermute | solution.py:74
  110.6 12.3 %collective-permute-start.27 = (bf16[2,32,4096]{2,1,0:T(8,128)(2,1)S(1)}, bf16[2,32,4096]{2,1,0:T(8,128)(2,1)S(1)}, u32[]{:S(2)}, u32[]{:S(2)}) collective-permute-start(bf16[2,32,4096]{2,1,0:T(8,128)(2,1)S(1)} %copy_bitcast_fusion.refs_0_), channel_id=1, source_target_pairs={{0,64},{64,0},{1,65},{65,1},{2,66},{66,2},{3,67},{67,3},{4,68},{68... | collective-permute-start | bytes 1572872 | tf_op jit(solution)/shard_map/ppermute | solution.py:74
  119.5 9.6 %collective-permute-start.29 = (bf16[2,16,4096]{2,1,0:T(8,128)(2,1)S(1)}, bf16[2,16,4096]{2,1,0:T(8,128)(2,1)S(1)}, u32[]{:S(2)}, u32[]{:S(2)}) collective-permute-start(bf16[2,16,4096]{2,1,0:T(8,128)(2,1)S(1)} %slice.72), channel_id=1, source_target_pairs={{0,1},{1,128},{128,129},{129,0},{2,3},{3,130},{130,131},{131,2},{4... | collective-permute-start | bytes 786440 | tf_op jit(solution)/shard_map/ppermute | solution.py:74
  120.2 8.9 %collective-permute-start.31 = (bf16[2,16,4096]{2,1,0:T(8,128)(2,1)S(1)}, bf16[2,16,4096]{2,1,0:T(8,128)(2,1)S(1)}, u32[]{:S(2)}, u32[]{:S(2)}) collective-permute-start(bf16[2,16,4096]{2,1,0:T(8,128)(2,1)S(1)} %slice.73), channel_id=1, source_target_pairs={{0,129},{1,0},{128,1},{129,128},{2,131},{3,2},{130,3},{131,130},{4... | collective-permute-start | bytes 786440 | tf_op jit(solution)/shard_map/ppermute | solution.py:74
  129.7 7.5 %collective-permute-start.36 = (bf16[192,512]{1,0:T(8,128)(2,1)S(1)}, bf16[192,512]{1,0:T(8,128)(2,1)S(1)}, u32[]{:S(2)}, u32[]{:S(2)}) collective-permute-start(bf16[192,512]{1,0:T(8,128)(2,1)S(1)} %sent_rows.2), channel_id=1, source_target_pairs={{0,1},{1,0},{2,3},{3,2},{4,5},{5,4},{6,7},{7,6},{8,9},{9,8},{10,11... | collective-permute-start | bytes 589832 | tf_op jit(solution)/shard_map/ppermute | solution.py:74
  (12 other events, 33.1 us)

commit v7 on v6

--- a/solution.py
+++ b/solution.py
@@ -74,6 +74,13 @@
     return lax.ppermute(array, axis, [(k, (k + step) % size) for k in range(size)])
 
 
+def copies_along(array, axis):
+    size = lax.axis_size(axis)
+    return lax.all_to_all(
+        jnp.broadcast_to(array[None], (size, *array.shape)), axis, 0, 0, tiled=True
+    )
+
+
 def split_kernel(first_ref, basis_ref, kept_ref, sent_ref):
     source = lax.broadcasted_iota(jnp.int32, (256, 128), 0)
     target = lax.broadcasted_iota(jnp.int32, (256, 128), 1)
@@ -118,85 +125,56 @@
         acc_ref[...] += jnp.dot(field, basis, preferred_element_type=jnp.float32)
 
 
-NEAR = (
-    ((0, 0), (0, 1)),
-    ((0, 2),),
-    ((0, 3),),
-    ((7, 0), (7, 1)),
-    ((1, 0), (1, 1)),
-    ((7, 2), (1, 2)),
-    ((7, 3), (1, 3)),
-    ((6, 0), (6, 1)),
-    ((2, 0), (2, 1)),
-    ((6, 2), (2, 2)),
-    ((6, 3), (2, 3)),
-    ((5, 0), (5, 1)),
-    ((3, 0), (3, 1)),
-)
-FAR = (
-    ((5, 2), (3, 2)),
-    ((5, 3), (3, 3)),
-    ((4, 0),),
-    ((4, 1),),
-    ((4, 2),),
-    ((4, 3),),
-)
+NEAR = tuple(tuple((dz, dy) for dy in (0, 3, 1, 2)) for dz in (0, 7, 1, 6, 2, 5, 3))
+FAR = (((4, 0), (4, 3)), ((4, 1), (4, 2)))
+
+
+def load_fields(refs, span):
+    return jnp.concatenate([ref[x, :, span] for ref in refs for x in range(4)], axis=0)
 
 
 def near_kernel(place_ref, *refs):
-    blocks, pieces, acc_ref = refs[:8], refs[8:-1], refs[-1]
-
-    def load(span):
-        return jnp.concatenate([ref[:, span] for ref in blocks], axis=0)
-
-    product_of(place_ref, load, NEAR, pieces, acc_ref)
+    fields, pieces, acc_ref = refs[:2], refs[2:-1], refs[-1]
+    product_of(place_ref, lambda span: load_fields(fields, span), NEAR, pieces, acc_ref)
 
 
 def near_product(place, fields, pieces):
-    rows = sum(field.shape[0] for field in fields)
+    rows = 8 * fields[0].shape[1]
     width = pieces[0].shape[-1]
     return pl.pallas_call(
         near_kernel,
         out_shape=jax.ShapeDtypeStruct((rows, width), jnp.float32),
-        in_specs=[SMEM] + [VMEM] * (8 + len(pieces)),
+        in_specs=[SMEM] + [VMEM] * (2 + len(pieces)),
         out_specs=VMEM,
         compiler_params=pltpu.CompilerParams(vmem_limit_bytes=GRANT),
         cost_estimate=pl.CostEstimate(
-            flops=2 * rows * 3072 * width, bytes_accessed=8 << 20, transcendentals=0
+            flops=2 * rows * 3584 * width, bytes_accessed=8 << 20, transcendentals=0
         ),
         name="near_product",
     )(place, *fields, *pieces)
 
 
 def first_kernel(mix_ref, place_ref, *refs):
-    blocks, pieces, (near_ref, out_ref, acc_ref, tmp_ref) = refs[:8], refs[8:-4], refs[-4:]
-    rows = blocks[0].shape[0]
-    lo = place_ref[0]
-
-    def load(span):
-        return jnp.concatenate([ref[:, span] for ref in blocks], axis=0)
-
-    product_of(place_ref, load, FAR, pieces, acc_ref)
+    fields, pieces, (near_ref, out_ref, acc_ref, tmp_ref) = refs[:2], refs[2:-4], refs[-4:]
+    rows = fields[0].shape[1]
+    product_of(place_ref, lambda span: load_fields(fields, span), FAR, pieces, acc_ref)
     acc_ref[...] += near_ref[...]
     for a in range(4):
-        for group in range(2):
-            mixed = sum(
-                mix_ref[group * 4 + t, a]
-                * acc_ref[(group * 4 + t) * rows : (group * 4 + t + 1) * rows, :]
-                for t in range(4)
+        for lo in range(2):
+            blocks = [core * 4 + hi * 2 + lo for core in range(2) for hi in range(2)]
+            tmp_ref[lo * rows : (lo + 1) * rows, :] = sum(
+                mix_ref[b, a] * acc_ref[b * rows : (b + 1) * rows, :] for b in blocks
             )
-            at = lo if group == 0 else 1 - lo
-            tmp_ref[pl.ds(pl.multiple_of(at * rows, rows), rows), :] = mixed
         out_ref[:, a * 2 * rows : (a + 1) * 2 * rows] = tmp_ref[...].T.astype(jnp.bfloat16)
 
 
 def first_product(mix, place, fields, pieces, near):
-    rows = fields[0].shape[0]
+    rows = fields[0].shape[1]
     width = near.shape[-1]
     return pl.pallas_call(
         first_kernel,
         out_shape=jax.ShapeDtypeStruct((width, 8 * rows), jnp.bfloat16),
-        in_specs=[SMEM, SMEM] + [VMEM] * (9 + len(pieces)),
+        in_specs=[SMEM, SMEM] + [VMEM] * (3 + len(pieces)),
         out_specs=VMEM,
         scratch_shapes=[
             pltpu.VMEM((8 * rows, width), jnp.float32),
@@ -204,7 +182,7 @@
         ],
         compiler_params=pltpu.CompilerParams(vmem_limit_bytes=GRANT),
         cost_estimate=pl.CostEstimate(
-            flops=2 * 8 * rows * 1024 * width, bytes_accessed=4 << 20, transcendentals=0
+            flops=2 * 8 * rows * 512 * width, bytes_accessed=4 << 20, transcendentals=0
         ),
         name="first_product",
     )(mix, place, *fields, *pieces, near)
@@ -342,10 +320,8 @@
     mine = jnp.where(lo == 0, jnp.concatenate([kept, other]), jnp.concatenate([other, kept]))
     pseudo = moments(event_counts, latent_mean, latent_var).astype(jnp.bfloat16)[0]
     mine, pseudo = lax.optimization_barrier((mine, pseudo))
-    next_y = shifted(mine, "y", 3)
-    far, before, after = [shifted(pseudo, RING, step) for step in (2, 1, 3)]
-    block = jnp.stack([mine, next_y])
-    own = with_core(pseudo)
+    block = jnp.stack([mine] + [shifted(mine, "y", step) for step in (1, 3, 2)])
+    field = copies_along(pseudo, RING).reshape(4, *pseudo.shape)
 
     flips = jnp.array([0, 1, 2, 3], jnp.int32)
     before_flip, after_flip = 2 * (1 - lo), 2 * lo
@@ -353,44 +329,25 @@
     slices = lax.bitwise_xor(time, jnp.concatenate([flips, crossed])).astype(jnp.int32)
     swapped = jnp.concatenate([slices[:4], slices[6:], slices[4:6]])
     factor = time_factor(correlation[0], 4)
-    mix = jnp.take(factor, slices, axis=0)
+    early_slices = jnp.arange(4) // 2 * 2
+    mix = jnp.take(factor, jnp.concatenate([early_slices + core, early_slices + 1 - core]), axis=0)
     root = jnp.sqrt(spectrum)
     sx = lax.dynamic_slice_in_dim(root, time * 1024, 1024, 0)[None]
     row = (y * nz + z) * 2 + lo
     sy = lax.dynamic_slice_in_dim(root.reshape(4, lax.axis_size(ROW), -1), row, 1, 1).reshape(-1, 1)
     sy = jnp.broadcast_to(sy, (sy.shape[0], 128))
 
-    def from_neighbours(blocks):
-        second = jnp.concatenate([b[-1:] for b in blocks])
-        first = jnp.concatenate([b[:1] for b in blocks])
-        return [shifted(second, "y", 3), shifted(first, "y", 1)]
-
     right, left = shifted(block, "z", 1), shifted(block, "z", nz - 1)
-    beside = from_neighbours([block])
-    right, left, before, after = lax.optimization_barrier((right, left, before, after))
-    pieces = [block]
-    next_right, next_left = shifted(right, "z", 1), shifted(left, "z", nz - 1)
-    beside_next = from_neighbours([right, left])
-    before, after = with_core(before), with_core(after)
-    next_right, next_left, beside, beside_next, far, own, mix, sx, sy = lax.optimization_barrier(
-        (next_right, next_left, beside, beside_next, far, own, mix, sx, sy)
-    )
-    pieces += [*beside, right, left, *beside_next]
-    right, left = next_right, next_left
-    next_right, next_left = shifted(right, "z", 1), shifted(left, "z", nz - 1)
-    beside = from_neighbours([right, left])
-    far = with_core(far)
-    next_right, next_left, beside, far, before, after = lax.optimization_barrier(
-        (next_right, next_left, beside, far, before, after)
-    )
-    pieces += [right, left, *beside]
-    right, left = next_right, next_left
+    pieces = [block, right, left]
+    right, left = shifted(right, "z", 1), shifted(left, "z", nz - 1)
     pieces += [right, left]
-    ends = [shifted(right[:1], "z", 1), shifted(left[1:], "z", nz - 1)]
-    last = [*from_neighbours([right, left]), *ends]
-    last += [shifted(ends[1], "y", 3), shifted(ends[0], "y", 1)]
-
-    fields = (*own, *far, *before, *after)
+    right, left, field, mix, sx, sy = lax.optimization_barrier((right, left, field, mix, sx, sy))
+    fields = with_core(field)
+    right, left = shifted(right, "z", 1), shifted(left, "z", nz - 1)
+    pieces += [right, left]
+    right, left, fields = lax.optimization_barrier((right, left, fields))
+    last = [shifted(right[:2], "z", 1), shifted(left[2:], "z", nz - 1)]
+
     near = near_product(place, fields, pieces)
     partial_y = first_product(mix, place, fields, last, near)
     pieces += last

time: 141 us -> 146 us (1.035)
  starting transfers between devices: 47 us -> 29.4 us
  waiting for transfers between devices: 43.1 us -> 60.2 us
  blocking collectives: 22 us -> 25.1 us
  Pallas kernels: 15 us -> 17.7 us
  local copies, waits for them, and re-layouts: 5.28 us -> 7.41 us
  other arithmetic: 6.64 us -> 4.82 us
    ppermute x38 -> x24, starting transfers between devices: 47 us -> 25.3 us  [shifted(): lax.ppermute(array, axis, [(k, (k + step) % size) for k in range(size)])]
    ppermute x38 -> x24, waiting for transfers between devices: 43.1 us -> 60.2 us  [shifted(): lax.ppermute(array, axis, [(k, (k + step) % size) for k in range(size)])]
    all_to_all x0 -> x1, starting transfers between devices: none -> 4.13 us  [copies_along(): lax.all_to_all(jnp.broadcast_to(array[None], (size, *array.shape)), axis,...]
    all_to_all x1, blocking collectives: 22 us -> 25.1 us  [local(): got = lax.all_to_all(sent, ('y', 'z'), 0, 0, tiled=True)]
    pallas_call x2, Pallas kernels: 3.13 us -> 5.4 us  [sent_rows(): pl.pallas_call(sent_kernel, out_shape=jax.ShapeDtypeStruct((count, width)...]
    broadcast_in_dim x0 -> x1, local copies, waits for them, and re-layouts: none -> 1.6 us  [copies_along(): jnp.broadcast_to(array[None], (size, *array.shape))]
  transfers between devices with their start and end apart: 38 -> 25, of which waited for: 12 -> 15; matrix products, arithmetic and copies ran while one was open for 7% -> 5% of each run, Pallas kernels for 7% -> 9%
where the time goes in v7:
time: 146 us
  waiting for transfers between devices  60.2 us (41%)
  starting transfers between devices  29.4 us (20%)
  blocking collectives  25.1 us (17%)
  Pallas kernels  17.7 us (12%)
  local copies, waits for them, and re-layouts  7.41 us (5%)
  other arithmetic  4.82 us (3%)
    ppermute x24, waiting for transfers between devices, shifted(): lax.ppermute(array, axis, [(k, (k + step) % size) for k in range(size)])  60.2 us
    ppermute x24, starting transfers between devices, shifted(): lax.ppermute(array, axis, [(k, (k + step) % size) for k in range(size)])  25.3 us
    all_to_all x1, blocking collectives, local(): got = lax.all_to_all(sent, ('y', 'z'), 0, 0, tiled=True)  25.1 us
    pallas_call x2, Pallas kernels, sent_rows(): pl.pallas_call(sent_kernel, out_shape=jax.ShapeDtypeStruct((count, width)...  5.4 us
    pallas_call x1, Pallas kernels, kept_rows(): pl.pallas_call(kept_kernel, out_shape=jax.ShapeDtypeStruct((times, rows,...  4.47 us
    squeeze x1, other arithmetic, local(): moments(event_counts, latent_mean, latent_var).astype(jnp.bfloat16)[0]  4.29 us
    all_to_all x1, starting transfers between devices, copies_along(): lax.all_to_all(jnp.broadcast_to(array[None], (size, *array.shape)), axis,...  4.13 us
    pallas_call x1, Pallas kernels, near_product(): pl.pallas_call(near_kernel, out_shape=jax.ShapeDtypeStruct((rows, width),...  3.46 us
  transfers between devices with their start and end apart: 25, of which 15 were waited for; matrix products, arithmetic and copies ran while one was open for 5% of the time, Pallas kernels for 9%

profile of v7, /device:TPU:32, one launch (start us, length us, event | category | flops | bytes accessed | tf_op | source)
XLA Modules:
  0.0 145.6 jit_solution(13522319845537243679)
XLA Ops:
  1.8 1.6 %collective-permute-start = (bf16[64,512]{1,0:T(8,128)(2,1)S(1)}, bf16[64,512]{1,0:T(8,128)(2,1)S(1)}, u32[]{:S(2)}, u32[]{:S(2)}) collective-permute-start(bf16[64,512]{1,0:T(8,128)(2,1)S(1)} %get-tuple-element.23), channel_id=1, source_target_pairs={{0,1},{1,0},{2,3},{3,2},{4,5},{5,4},{6,7},{7,6},{8,9},{9,8},{10,11... | collective-permute-start | bytes 196616 | tf_op jit(solution)/shard_map/ppermute | solution.py:74
  3.3 4.3 %fusion.8 = bf16[64,4096]{1,0:T(8,128)(2,1)S(1)} fusion(s32[1,64,4096]{2,1,0:T(8,128)} %param.8, f32[1,64,4096]{2,1,0:T(8,128)} %param.10, f32[1,64,4096]{2,1,0:T(8,128)} %param.9), kind=kLoop, calls=%fused_computation.16 | loop fusion | flops 17563648 | bytes 3670016 | tf_op jit(solution)/shard_map/squeeze | solution.py:321
  7.7 1.6 %broadcast_in_dim.36 = bf16[4,64,4096]{2,1,0:T(8,128)(2,1)} broadcast(bf16[64,4096]{1,0:T(8,128)(2,1)S(1)} %fusion.8), dimensions={1,2} | broadcast | bytes 2621440 | tf_op jit(solution)/shard_map/broadcast_in_dim | solution.py:80
  9.3 4.1 %all-to-all-start = ((bf16[4,64,4096]{2,1,0:T(8,128)(2,1)}), bf16[4,64,4096]{2,1,0:T(8,128)(2,1)S(1)}, u32[]{:S(2)}, u32[]{:S(2)}) async-start(bf16[4,64,4096]{2,1,0:T(8,128)(2,1)} %broadcast_in_dim.36), calls=%async_computation | async-start | bytes 4194304 | tf_op jit(solution)/shard_map/all_to_all | solution.py:79
  13.4 3.2 %collective-permute-start.3 = (bf16[128,512]{1,0:T(8,128)(2,1)S(1)}, bf16[128,512]{1,0:T(8,128)(2,1)S(1)}, u32[]{:S(2)}, u32[]{:S(2)}) collective-permute-start(bf16[128,512]{1,0:T(8,128)(2,1)S(1)} %maximum_select_fusion), channel_id=1, source_target_pairs={{0,32},{16,48},{32,0},{48,16},{1,33},{17,49},{33,1},{49,17},{2,34}... | collective-permute-start | bytes 393224 | tf_op jit(solution)/shard_map/ppermute | solution.py:74
  16.6 1.1 collective-permute-start.2
  19.6 1.3 collective-permute-done.3
  20.9 1.8 %collective-permute-done.2 = bf16[128,512]{1,0:T(8,128)(2,1)S(1)} collective-permute-done((bf16[128,512]{1,0:T(8,128)(2,1)S(1)}, bf16[128,512]{1,0:T(8,128)(2,1)S(1)}, u32[]{:S(2)}, u32[]{:S(2)}) %collective-permute-start.2) | collective-permute-done | bytes 131104 | tf_op jit(solution)/shard_map/ppermute | solution.py:74
  22.7 1.1 collective-permute-done.1
  24.1 1.9 %collective-permute-start.4 = (bf16[4,128,512]{2,1,0:T(8,128)(2,1)S(1)}, bf16[4,128,512]{2,1,0:T(8,128)(2,1)}, u32[]{:S(2)}, u32[]{:S(2)}) collective-permute-start(bf16[4,128,512]{2,1,0:T(8,128)(2,1)S(1)} %pad_maximum_fusion.refs_2_.refs_6_.refs_10_.refs_4_), channel_id=1, source_target_pairs={{0,2},{2,4},{4,6},{6,8},{8,10},{10,12},{12,14},{14,0},{1,3},{3,5},... | collective-permute-start | bytes 1572872 | tf_op jit(solution)/shard_map/ppermute | solution.py:74
  26.1 10.1 %collective-permute-done.6.refs_4_.refs_8_.refs_12_.refs_6_ = bf16[4,128,512]{2,1,0:T(8,128)(2,1)S(1)} collective-permute-done((bf16[4,128,512]{2,1,0:T(8,128)(2,1)S(1)}, bf16[4,128,512]{2,1,0:T(8,128)(2,1)S(1)}, u32[]{:S(2)}, u32[]{:S(2)}) %collective-permute-start.6) | collective-permute-done | bytes 524320 | tf_op jit(solution)/shard_map/ppermute | solution.py:74
  36.2 3.3 %collective-permute-start.7 = (bf16[4,128,512]{2,1,0:T(8,128)(2,1)S(1)}, bf16[4,128,512]{2,1,0:T(8,128)(2,1)}, u32[]{:S(2)}, u32[]{:S(2)}) collective-permute-start(bf16[4,128,512]{2,1,0:T(8,128)(2,1)S(1)} %collective-permute-done.6.refs_4_.refs_8_.refs_12_.refs_6_), channel_id=1, source_target_pairs={{0,14},{2,0},{4,2},{6,4},{8,6},{10,8},{12,10},{14,12},{1,15},{3,1}... | collective-permute-start | bytes 1572872 | tf_op jit(solution)/shard_map/ppermute | solution.py:74
  41.1 7.1 %collective-permute-done.7.refs_6_.refs_10_.refs_14_.refs_8_ = bf16[4,128,512]{2,1,0:T(8,128)(2,1)} collective-permute-done((bf16[4,128,512]{2,1,0:T(8,128)(2,1)S(1)}, bf16[4,128,512]{2,1,0:T(8,128)(2,1)}, u32[]{:S(2)}, u32[]{:S(2)}) %collective-permute-start.7) | collective-permute-done | bytes 524320 | tf_op jit(solution)/shard_map/ppermute | solution.py:74
  48.2 5.3 %collective-permute-done.5.refs_5_.refs_9_.refs_13_.refs_7_ = bf16[4,128,512]{2,1,0:T(8,128)(2,1)} collective-permute-done((bf16[4,128,512]{2,1,0:T(8,128)(2,1)}, bf16[4,128,512]{2,1,0:T(8,128)(2,1)}, u32[]{:S(2)}, u32[]{:S(2)}) %collective-permute-start.5) | collective-permute-done | bytes 524320 | tf_op jit(solution)/shard_map/ppermute | solution.py:74
  53.7 3.0 %collective-permute-start.9 = (bf16[4,128,512]{2,1,0:T(8,128)(2,1)}, bf16[4,128,512]{2,1,0:T(8,128)(2,1)S(1)}, u32[]{:S(2)}, u32[]{:S(2)}) collective-permute-start(bf16[4,128,512]{2,1,0:T(8,128)(2,1)} %collective-permute-done.7.refs_6_.refs_10_.refs_14_.refs_8_), channel_id=1, source_target_pairs={{0,14},{2,0},{4,2},{6,4},{8,6},{10,8},{12,10},{14,12},{1,15},{3,1}... | collective-permute-start | bytes 1572872 | tf_op jit(solution)/shard_map/ppermute | solution.py:74
  56.7 12.6 %collective-permute-done.8.refs_7_.refs_11_.refs_15_.refs_9_ = bf16[4,128,512]{2,1,0:T(8,128)(2,1)S(1)} collective-permute-done((bf16[4,128,512]{2,1,0:T(8,128)(2,1)}, bf16[4,128,512]{2,1,0:T(8,128)(2,1)S(1)}, u32[]{:S(2)}, u32[]{:S(2)}) %collective-permute-start.8) | collective-permute-done | bytes 524320 | tf_op jit(solution)/shard_map/ppermute | solution.py:74
  69.4 3.0 %collective-permute-start.12 = (bf16[2,128,512]{2,1,0:T(8,128)(2,1)S(1)}, bf16[2,128,512]{2,1,0:T(8,128)(2,1)S(1)}, u32[]{:S(2)}, u32[]{:S(2)}) collective-permute-start(bf16[2,128,512]{2,1,0:T(8,128)(2,1)S(1)} %slice.25), channel_id=1, source_target_pairs={{0,14},{2,0},{4,2},{6,4},{8,6},{10,8},{12,10},{14,12},{1,15},{3,1}... | collective-permute-start | bytes 786440 | tf_op jit(solution)/shard_map/ppermute | solution.py:74
  73.5 3.5 %near_product.1.refs_4_ = f32[512,512]{1,0:T(8,128)S(1)} custom-call(s32[4]{0:T(128)S(1)} %pad_add_fusion.first_ref.place_ref, bf16[4,64,4096]{2,1,0:T(8,128)(2,1)S(1)} %all-to-all-done.refs_0_, bf16[4,64,4096]{2,1,0:T(8,128)(2,1)S(1)} %collective-permute-done.10.refs_1_, bf16[4,128,512]{2,1,0:T(8,128)(2,1)S(1)} %pad_maximum_fusion.refs_2_.refs_6_.refs_10_.refs_4_, ...), custom_call_target="tpu_custom_call" | custom-call | flops 1879048192 | bytes 8388608 | tf_op jit(solution)/shard_map/near_product/pallas_call | solution.py:144
  77.8 3.1 %collective-permute-done.11.refs_2_.refs_13_.refs_17_.refs_11_ = bf16[2,128,512]{2,1,0:T(8,128)(2,1)S(1)} collective-permute-done((bf16[2,128,512]{2,1,0:T(8,128)(2,1)S(1)}, bf16[2,128,512]{2,1,0:T(8,128)(2,1)S(1)}, u32[]{:S(2)}, u32[]{:S(2)}) %collective-permute-start.11) | collective-permute-done | bytes 262176 | tf_op jit(solution)/shard_map/ppermute | solution.py:74
  80.9 1.4 first_product.1
  82.4 25.1 %all_to_all.10 = bf16[32,16,512]{2,1,0:T(8,128)(2,1)S(1)} all-to-all(bf16[32,16,512]{2,1,0:T(8,128)(2,1)S(1)} %bitcast.38), channel_id=1, replica_groups=mesh['hi'=2,'core'=2,'y'=4,'z'=8,'lo'=2] {'y','z'}, dimensions={0} | all-to-all | bytes 1048576 | tf_op jit(solution)/shard_map/all_to_all | solution.py:357
  107.5 2.5 %collective-permute-start.16 = (bf16[2,32,4096]{2,1,0:T(8,128)(2,1)S(1)}, bf16[2,32,4096]{2,1,0:T(8,128)(2,1)}, u32[]{:S(2)}, u32[]{:S(2)}) collective-permute-start(bf16[2,32,4096]{2,1,0:T(8,128)(2,1)S(1)} %copy_bitcast_fusion.refs_0_), channel_id=1, source_target_pairs={{0,129},{1,0},{128,1},{129,128},{2,131},{3,2},{130,3},{131,130},{4... | collective-permute-start | bytes 1572872 | tf_op jit(solution)/shard_map/ppermute | solution.py:74
  110.0 8.1 %collective-permute-done.16.refs_4_.refs_8_ = bf16[2,32,4096]{2,1,0:T(8,128)(2,1)} collective-permute-done((bf16[2,32,4096]{2,1,0:T(8,128)(2,1)S(1)}, bf16[2,32,4096]{2,1,0:T(8,128)(2,1)}, u32[]{:S(2)}, u32[]{:S(2)}) %collective-permute-start.16) | collective-permute-done | bytes 524320 | tf_op jit(solution)/shard_map/ppermute | solution.py:74
  118.1 3.3 %collective-permute-done.14.refs_2_.refs_6_ = bf16[2,32,4096]{2,1,0:T(8,128)(2,1)} collective-permute-done((bf16[2,32,4096]{2,1,0:T(8,128)(2,1)S(1)}, bf16[2,32,4096]{2,1,0:T(8,128)(2,1)}, u32[]{:S(2)}, u32[]{:S(2)}) %collective-permute-start.14) | collective-permute-done | bytes 524320 | tf_op jit(solution)/shard_map/ppermute | solution.py:74
  124.3 1.3 collective-permute-start.15
  125.7 3.2 %sent_rows.2 = bf16[192,512]{1,0:T(8,128)(2,1)S(1)} custom-call(s32[4]{0:T(128)S(1)} %pad_add_fusion.first_ref.place_ref, bf16[2,32,4096]{2,1,0:T(8,128)(2,1)S(1)} %copy_bitcast_fusion.refs_0_, bf16[2,32,4096]{2,1,0:T(8,128)(2,1)} %collective-permute-done.13.refs_1_, bf16[2,32,4096]{2,1,0:T(8,128)(2,1)} %collective-permute-done.14.refs_2_.refs_6_, ...), custom_call_target="tpu_custom_call" | custom-call | flops 805306368 | bytes 6291456 | tf_op jit(solution)/shard_map/sent_rows/pallas_call | solution.py:218
  128.9 2.4 %collective-permute-done.17.refs_3_.refs_1_ = bf16[2,16,4096]{2,1,0:T(8,128)(2,1)S(1)} collective-permute-done((bf16[2,16,4096]{2,1,0:T(8,128)(2,1)S(1)}, bf16[2,16,4096]{2,1,0:T(8,128)(2,1)S(1)}, u32[]{:S(2)}, u32[]{:S(2)}) %collective-permute-start.17) | collective-permute-done | bytes 262176 | tf_op jit(solution)/shard_map/ppermute | solution.py:74
  131.3 2.3 %collective-permute-done.15.refs_2_.refs_0_ = bf16[2,16,4096]{2,1,0:T(8,128)(2,1)S(1)} collective-permute-done((bf16[2,16,4096]{2,1,0:T(8,128)(2,1)S(1)}, bf16[2,16,4096]{2,1,0:T(8,128)(2,1)S(1)}, u32[]{:S(2)}, u32[]{:S(2)}) %collective-permute-start.15) | collective-permute-done | bytes 262176 | tf_op jit(solution)/shard_map/ppermute | solution.py:74
  135.5 2.2 %sent_rows.3 = bf16[64,512]{1,0:T(8,128)(2,1)S(1)} custom-call(s32[4]{0:T(128)S(1)} %pad_add_fusion.first_ref.place_ref, bf16[2,16,4096]{2,1,0:T(8,128)(2,1)S(1)} %collective-permute-done.15.refs_2_.refs_0_, bf16[2,16,4096]{2,1,0:T(8,128)(2,1)S(1)} %collective-permute-done.17.refs_3_.refs_1_, ...), custom_call_target="tpu_custom_call" | custom-call | flops 268435456 | bytes 6291456 | tf_op jit(solution)/shard_map/sent_rows/pallas_call | solution.py:218
  137.7 1.2 collective-permute-start.23
  138.9 4.5 %kept_rows.1.kept_ref = f32[4,64,1024]{2,1,0:T(8,128)S(1)} custom-call(s32[4]{0:T(128)S(1)} %pad_add_fusion.first_ref.place_ref, s32[8]{0:T(128)S(1)} %broadcast_xor_fusion.slice_ref, bf16[2,32,4096]{2,1,0:T(8,128)(2,1)S(1)} %copy_bitcast_fusion.refs_0_, bf16[2,32,4096]{2,1,0:T(8,128)(2,1)} %collective-permute-done.13.refs_1_, ...), custom_call_target="tpu_custom_call" | custom-call | flops 1073741824 | bytes 6291456 | tf_op jit(solution)/shard_map/kept_rows/pallas_call | solution.py:260
  143.4 2.2 %whitened_gradient.1 = f32[64,4,1024]{2,1,0:T(4,128)} custom-call(s32[4]{0:T(128)S(1)} %pad_add_fusion.first_ref.place_ref, s32[8]{0:T(128)S(1)} %pad_add_fusion.1.slice_ref, f32[4,64,1024]{2,1,0:T(8,128)S(1)} %kept_rows.1.kept_ref, bf16[192,512]{1,0:T(8,128)(2,1)S(1)} %collective-permute-done.22.early_ref, ...), custom_call_target="tpu_custom_call" | custom-call | tf_op jit(solution)/shard_map/whitened_gradient/pallas_call | solution.py:297
  (76 shorter events, 11.9 us)
Async XLA Ops:
  1.8 5.9 %collective-permute-start = (bf16[64,512]{1,0:T(8,128)(2,1)S(1)}, bf16[64,512]{1,0:T(8,128)(2,1)S(1)}, u32[]{:S(2)}, u32[]{:S(2)}) collective-permute-start(bf16[64,512]{1,0:T(8,128)(2,1)S(1)} %get-tuple-element.23), channel_id=1, source_target_pairs={{0,1},{1,0},{2,3},{3,2},{4,5},{5,4},{6,7},{7,6},{8,9},{9,8},{10,11... | collective-permute-start | bytes 196616 | tf_op jit(solution)/shard_map/ppermute | solution.py:74
  9.3 10.1 %copy-start.9 = (f32[4096]{0:T(1024)S(1)}, f32[4096]{0:T(1024)}, u32[]{:S(2)}) copy-start(f32[4096]{0:T(1024)} %param.12) | copy-start | bytes 49156
  9.3 44.2 %all-to-all-start = ((bf16[4,64,4096]{2,1,0:T(8,128)(2,1)}), bf16[4,64,4096]{2,1,0:T(8,128)(2,1)S(1)}, u32[]{:S(2)}, u32[]{:S(2)}) async-start(bf16[4,64,4096]{2,1,0:T(8,128)(2,1)} %broadcast_in_dim.36), calls=%async_computation | async-start | bytes 4194304 | tf_op jit(solution)/shard_map/all_to_all | solution.py:79
  13.4 7.5 %collective-permute-start.3 = (bf16[128,512]{1,0:T(8,128)(2,1)S(1)}, bf16[128,512]{1,0:T(8,128)(2,1)S(1)}, u32[]{:S(2)}, u32[]{:S(2)}) collective-permute-start(bf16[128,512]{1,0:T(8,128)(2,1)S(1)} %maximum_select_fusion), channel_id=1, source_target_pairs={{0,32},{16,48},{32,0},{48,16},{1,33},{17,49},{33,1},{49,17},{2,34}... | collective-permute-start | bytes 393224 | tf_op jit(solution)/shard_map/ppermute | solution.py:74
  16.6 6.1 %collective-permute-start.2 = (bf16[128,512]{1,0:T(8,128)(2,1)S(1)}, bf16[128,512]{1,0:T(8,128)(2,1)S(1)}, u32[]{:S(2)}, u32[]{:S(2)}) collective-permute-start(bf16[128,512]{1,0:T(8,128)(2,1)S(1)} %maximum_select_fusion), channel_id=1, source_target_pairs={{0,48},{16,0},{32,16},{48,32},{1,49},{17,1},{33,17},{49,33},{2,50}... | collective-permute-start | bytes 393224 | tf_op jit(solution)/shard_map/ppermute | solution.py:74
  17.7 6.2 %collective-permute-start.1 = (bf16[128,512]{1,0:T(8,128)(2,1)S(1)}, bf16[128,512]{1,0:T(8,128)(2,1)S(1)}, u32[]{:S(2)}, u32[]{:S(2)}) collective-permute-start(bf16[128,512]{1,0:T(8,128)(2,1)S(1)} %maximum_select_fusion), channel_id=1, source_target_pairs={{0,16},{16,32},{32,48},{48,0},{1,17},{17,33},{33,49},{49,1},{2,18}... | collective-permute-start | bytes 393224 | tf_op jit(solution)/shard_map/ppermute | solution.py:74
  23.9 12.3 %collective-permute-start.6 = (bf16[4,128,512]{2,1,0:T(8,128)(2,1)S(1)}, bf16[4,128,512]{2,1,0:T(8,128)(2,1)S(1)}, u32[]{:S(2)}, u32[]{:S(2)}) collective-permute-start(bf16[4,128,512]{2,1,0:T(8,128)(2,1)S(1)} %pad_maximum_fusion.refs_2_.refs_6_.refs_10_.refs_4_), channel_id=1, source_target_pairs={{0,14},{2,0},{4,2},{6,4},{8,6},{10,8},{12,10},{14,12},{1,15},{3,1}... | collective-permute-start | bytes 1572872 | tf_op jit(solution)/shard_map/ppermute | solution.py:74
  24.1 16.2 %collective-permute-start.4 = (bf16[4,128,512]{2,1,0:T(8,128)(2,1)S(1)}, bf16[4,128,512]{2,1,0:T(8,128)(2,1)}, u32[]{:S(2)}, u32[]{:S(2)}) collective-permute-start(bf16[4,128,512]{2,1,0:T(8,128)(2,1)S(1)} %pad_maximum_fusion.refs_2_.refs_6_.refs_10_.refs_4_), channel_id=1, source_target_pairs={{0,2},{2,4},{4,6},{6,8},{8,10},{10,12},{12,14},{14,0},{1,3},{3,5},... | collective-permute-start | bytes 1572872 | tf_op jit(solution)/shard_map/ppermute | solution.py:74
  36.2 12.0 %collective-permute-start.7 = (bf16[4,128,512]{2,1,0:T(8,128)(2,1)S(1)}, bf16[4,128,512]{2,1,0:T(8,128)(2,1)}, u32[]{:S(2)}, u32[]{:S(2)}) collective-permute-start(bf16[4,128,512]{2,1,0:T(8,128)(2,1)S(1)} %collective-permute-done.6.refs_4_.refs_8_.refs_12_.refs_6_), channel_id=1, source_target_pairs={{0,14},{2,0},{4,2},{6,4},{8,6},{10,8},{12,10},{14,12},{1,15},{3,1}... | collective-permute-start | bytes 1572872 | tf_op jit(solution)/shard_map/ppermute | solution.py:74
  40.3 13.1 %collective-permute-start.5 = (bf16[4,128,512]{2,1,0:T(8,128)(2,1)}, bf16[4,128,512]{2,1,0:T(8,128)(2,1)}, u32[]{:S(2)}, u32[]{:S(2)}) collective-permute-start(bf16[4,128,512]{2,1,0:T(8,128)(2,1)} %collective-permute-done.4.refs_3_.refs_7_.refs_11_.refs_5_), channel_id=1, source_target_pairs={{0,2},{2,4},{4,6},{6,8},{8,10},{10,12},{12,14},{14,0},{1,3},{3,5},... | collective-permute-start | bytes 1572872 | tf_op jit(solution)/shard_map/ppermute | solution.py:74
  53.5 15.8 %collective-permute-start.10 = (bf16[4,64,4096]{2,1,0:T(8,128)(2,1)S(1)}, bf16[4,64,4096]{2,1,0:T(8,128)(2,1)S(1)}, u32[]{:S(2)}, u32[]{:S(2)}) collective-permute-start(bf16[4,64,4096]{2,1,0:T(8,128)(2,1)S(1)} %all-to-all-done.refs_0_), channel_id=1, source_target_pairs={{0,64},{64,0},{1,65},{65,1},{2,66},{66,2},{3,67},{67,3},{4,68},{68... | collective-permute-start | bytes 6291464 | tf_op jit(solution)/shard_map/ppermute | solution.py:74
  53.6 15.7 %collective-permute-start.8 = (bf16[4,128,512]{2,1,0:T(8,128)(2,1)}, bf16[4,128,512]{2,1,0:T(8,128)(2,1)S(1)}, u32[]{:S(2)}, u32[]{:S(2)}) collective-permute-start(bf16[4,128,512]{2,1,0:T(8,128)(2,1)} %collective-permute-done.5.refs_5_.refs_9_.refs_13_.refs_7_), channel_id=1, source_target_pairs={{0,2},{2,4},{4,6},{6,8},{8,10},{10,12},{12,14},{14,0},{1,3},{3,5},... | collective-permute-start | bytes 1572872 | tf_op jit(solution)/shard_map/ppermute | solution.py:74
  53.7 15.7 %collective-permute-start.9 = (bf16[4,128,512]{2,1,0:T(8,128)(2,1)}, bf16[4,128,512]{2,1,0:T(8,128)(2,1)S(1)}, u32[]{:S(2)}, u32[]{:S(2)}) collective-permute-start(bf16[4,128,512]{2,1,0:T(8,128)(2,1)} %collective-permute-done.7.refs_6_.refs_10_.refs_14_.refs_8_), channel_id=1, source_target_pairs={{0,14},{2,0},{4,2},{6,4},{8,6},{10,8},{12,10},{14,12},{1,15},{3,1}... | collective-permute-start | bytes 1572872 | tf_op jit(solution)/shard_map/ppermute | solution.py:74
  69.3 7.6 %copy-start = (bf16[4,128,512]{2,1,0:T(8,128)(2,1)}, bf16[4,128,512]{2,1,0:T(8,128)(2,1)S(1)}, u32[]{:S(2)}) copy-start(bf16[4,128,512]{2,1,0:T(8,128)(2,1)S(1)} %collective-permute-done.9.refs_8_.refs_12_.refs_16_.refs_10_) | copy-start | bytes 1572868
  69.4 8.4 %collective-permute-start.12 = (bf16[2,128,512]{2,1,0:T(8,128)(2,1)S(1)}, bf16[2,128,512]{2,1,0:T(8,128)(2,1)S(1)}, u32[]{:S(2)}, u32[]{:S(2)}) collective-permute-start(bf16[2,128,512]{2,1,0:T(8,128)(2,1)S(1)} %slice.25), channel_id=1, source_target_pairs={{0,14},{2,0},{4,2},{6,4},{8,6},{10,8},{12,10},{14,12},{1,15},{3,1}... | collective-permute-start | bytes 786440 | tf_op jit(solution)/shard_map/ppermute | solution.py:74
  72.4 8.5 %collective-permute-start.11 = (bf16[2,128,512]{2,1,0:T(8,128)(2,1)S(1)}, bf16[2,128,512]{2,1,0:T(8,128)(2,1)S(1)}, u32[]{:S(2)}, u32[]{:S(2)}) collective-permute-start(bf16[2,128,512]{2,1,0:T(8,128)(2,1)S(1)} %slice.24), channel_id=1, source_target_pairs={{0,2},{2,4},{4,6},{6,8},{8,10},{10,12},{12,14},{14,0},{1,3},{3,5},... | collective-permute-start | bytes 786440 | tf_op jit(solution)/shard_map/ppermute | solution.py:74
  80.9 1.4 copy-start.5
  82.3 43.4 %copy-start.1 = (bf16[4,128,512]{2,1,0:T(8,128)(2,1)S(1)}, bf16[4,128,512]{2,1,0:T(8,128)(2,1)}, u32[]{:S(2)}) copy-start(bf16[4,128,512]{2,1,0:T(8,128)(2,1)} %copy-done) | copy-start | bytes 1572868
  82.3 43.4 %copy-start.4 = (bf16[4,128,512]{2,1,0:T(8,128)(2,1)S(1)}, bf16[4,128,512]{2,1,0:T(8,128)(2,1)}, u32[]{:S(2)}) copy-start(bf16[4,128,512]{2,1,0:T(8,128)(2,1)} %copy-done.2) | copy-start | bytes 1572868
  82.3 43.4 %copy-start.6 = (bf16[2,128,512]{2,1,0:T(8,128)(2,1)S(1)}, bf16[2,128,512]{2,1,0:T(8,128)(2,1)}, u32[]{:S(2)}) copy-start(bf16[2,128,512]{2,1,0:T(8,128)(2,1)} %copy-done.5) | copy-start | bytes 786436
  107.5 10.6 %collective-permute-start.16 = (bf16[2,32,4096]{2,1,0:T(8,128)(2,1)S(1)}, bf16[2,32,4096]{2,1,0:T(8,128)(2,1)}, u32[]{:S(2)}, u32[]{:S(2)}) collective-permute-start(bf16[2,32,4096]{2,1,0:T(8,128)(2,1)S(1)} %copy_bitcast_fusion.refs_0_), channel_id=1, source_target_pairs={{0,129},{1,0},{128,1},{129,128},{2,131},{3,2},{130,3},{131,130},{4... | collective-permute-start | bytes 1572872 | tf_op jit(solution)/shard_map/ppermute | solution.py:74
  110.0 11.4 %collective-permute-start.14 = (bf16[2,32,4096]{2,1,0:T(8,128)(2,1)S(1)}, bf16[2,32,4096]{2,1,0:T(8,128)(2,1)}, u32[]{:S(2)}, u32[]{:S(2)}) collective-permute-start(bf16[2,32,4096]{2,1,0:T(8,128)(2,1)S(1)} %copy_bitcast_fusion.refs_0_), channel_id=1, source_target_pairs={{0,1},{1,128},{128,129},{129,0},{2,3},{3,130},{130,131},{131,2},{4... | collective-permute-start | bytes 1572872 | tf_op jit(solution)/shard_map/ppermute | solution.py:74
  110.0 15.7 %collective-permute-start.13 = (bf16[2,32,4096]{2,1,0:T(8,128)(2,1)S(1)}, bf16[2,32,4096]{2,1,0:T(8,128)(2,1)}, u32[]{:S(2)}, u32[]{:S(2)}) collective-permute-start(bf16[2,32,4096]{2,1,0:T(8,128)(2,1)S(1)} %copy_bitcast_fusion.refs_0_), channel_id=1, source_target_pairs={{0,64},{64,0},{1,65},{65,1},{2,66},{66,2},{3,67},{67,3},{4,68},{68... | collective-permute-start | bytes 1572872 | tf_op jit(solution)/shard_map/ppermute | solution.py:74
  118.1 7.6 %collective-permute-start.19 = (bf16[2,32,4096]{2,1,0:T(8,128)(2,1)}, bf16[2,32,4096]{2,1,0:T(8,128)(2,1)}, u32[]{:S(2)}, u32[]{:S(2)}) collective-permute-start(bf16[2,32,4096]{2,1,0:T(8,128)(2,1)} %collective-permute-done.16.refs_4_.refs_8_), channel_id=1, source_target_pairs={{0,64},{64,0},{1,65},{65,1},{2,66},{66,2},{3,67},{67,3},{4,68},{68... | collective-permute-start | bytes 1572872 | tf_op jit(solution)/shard_map/ppermute | solution.py:74
  121.4 4.2 %collective-permute-start.18 = (bf16[2,32,4096]{2,1,0:T(8,128)(2,1)}, bf16[2,32,4096]{2,1,0:T(8,128)(2,1)}, u32[]{:S(2)}, u32[]{:S(2)}) collective-permute-start(bf16[2,32,4096]{2,1,0:T(8,128)(2,1)} %collective-permute-done.14.refs_2_.refs_6_), channel_id=1, source_target_pairs={{0,64},{64,0},{1,65},{65,1},{2,66},{66,2},{3,67},{67,3},{4,68},{68... | collective-permute-start | bytes 1572872 | tf_op jit(solution)/shard_map/ppermute | solution.py:74
  122.5 8.8 %collective-permute-start.17 = (bf16[2,16,4096]{2,1,0:T(8,128)(2,1)S(1)}, bf16[2,16,4096]{2,1,0:T(8,128)(2,1)S(1)}, u32[]{:S(2)}, u32[]{:S(2)}) collective-permute-start(bf16[2,16,4096]{2,1,0:T(8,128)(2,1)S(1)} %slice.31), channel_id=1, source_target_pairs={{0,129},{1,0},{128,1},{129,128},{2,131},{3,2},{130,3},{131,130},{4... | collective-permute-start | bytes 786440 | tf_op jit(solution)/shard_map/ppermute | solution.py:74
  124.3 9.2 %collective-permute-start.15 = (bf16[2,16,4096]{2,1,0:T(8,128)(2,1)S(1)}, bf16[2,16,4096]{2,1,0:T(8,128)(2,1)S(1)}, u32[]{:S(2)}, u32[]{:S(2)}) collective-permute-start(bf16[2,16,4096]{2,1,0:T(8,128)(2,1)S(1)} %slice.30), channel_id=1, source_target_pairs={{0,1},{1,128},{128,129},{129,0},{2,3},{3,130},{130,131},{131,2},{4... | collective-permute-start | bytes 786440 | tf_op jit(solution)/shard_map/ppermute | solution.py:74
  133.6 1.5 %collective-permute-start.20 = (bf16[2,16,4096]{2,1,0:T(8,128)(2,1)S(1)}, bf16[2,16,4096]{2,1,0:T(8,128)(2,1)S(1)}, u32[]{:S(2)}, u32[]{:S(2)}) collective-permute-start(bf16[2,16,4096]{2,1,0:T(8,128)(2,1)S(1)} %collective-permute-done.15.refs_2_.refs_0_), channel_id=1, source_target_pairs={{0,64},{64,0},{1,65},{65,1},{2,66},{66,2},{3,67},{67,3},{4,68},{68... | collective-permute-start | bytes 786440 | tf_op jit(solution)/shard_map/ppermute | solution.py:74
  133.6 1.9 %collective-permute-start.21 = (bf16[2,16,4096]{2,1,0:T(8,128)(2,1)S(1)}, bf16[2,16,4096]{2,1,0:T(8,128)(2,1)S(1)}, u32[]{:S(2)}, u32[]{:S(2)}) collective-permute-start(bf16[2,16,4096]{2,1,0:T(8,128)(2,1)S(1)} %collective-permute-done.17.refs_3_.refs_1_), channel_id=1, source_target_pairs={{0,64},{64,0},{1,65},{65,1},{2,66},{66,2},{3,67},{67,3},{4,68},{68... | collective-permute-start | bytes 786440 | tf_op jit(solution)/shard_map/ppermute | solution.py:74
  134.2 9.2 %collective-permute-start.22 = (bf16[192,512]{1,0:T(8,128)(2,1)S(1)}, bf16[192,512]{1,0:T(8,128)(2,1)S(1)}, u32[]{:S(2)}, u32[]{:S(2)}) collective-permute-start(bf16[192,512]{1,0:T(8,128)(2,1)S(1)} %sent_rows.2), channel_id=1, source_target_pairs={{0,1},{1,0},{2,3},{3,2},{4,5},{5,4},{6,7},{7,6},{8,9},{9,8},{10,11... | collective-permute-start | bytes 589832 | tf_op jit(solution)/shard_map/ppermute | solution.py:74
  134.8 4.1 %copy-start.7 = (f32[4,1,16,4,1024]{4,3,2,1,0:T(4,128)S(1)}, f32[4,1,16,4,1024]{4,3,2,1,0:T(4,128)}, u32[]{:S(2)}) copy-start(f32[4,1,16,4,1024]{4,3,2,1,0:T(4,128)} %param.14) | copy-start | bytes 3145732
  137.7 5.7 %collective-permute-start.23 = (bf16[64,512]{1,0:T(8,128)(2,1)S(1)}, bf16[64,512]{1,0:T(8,128)(2,1)S(1)}, u32[]{:S(2)}, u32[]{:S(2)}) collective-permute-start(bf16[64,512]{1,0:T(8,128)(2,1)S(1)} %sent_rows.3), channel_id=1, source_target_pairs={{0,1},{1,0},{2,3},{3,2},{4,5},{5,4},{6,7},{7,6},{8,9},{9,8},{10,11... | collective-permute-start | bytes 196616 | tf_op jit(solution)/shard_map/ppermute | solution.py:74
  (3 other events, 2.7 us)

commit v8 on v6

--- a/solution.py
+++ b/solution.py
@@ -118,29 +118,8 @@
         acc_ref[...] += jnp.dot(field, basis, preferred_element_type=jnp.float32)
 
 
-NEAR = (
-    ((0, 0), (0, 1)),
-    ((0, 2),),
-    ((0, 3),),
-    ((7, 0), (7, 1)),
-    ((1, 0), (1, 1)),
-    ((7, 2), (1, 2)),
-    ((7, 3), (1, 3)),
-    ((6, 0), (6, 1)),
-    ((2, 0), (2, 1)),
-    ((6, 2), (2, 2)),
-    ((6, 3), (2, 3)),
-    ((5, 0), (5, 1)),
-    ((3, 0), (3, 1)),
-)
-FAR = (
-    ((5, 2), (3, 2)),
-    ((5, 3), (3, 3)),
-    ((4, 0),),
-    ((4, 1),),
-    ((4, 2),),
-    ((4, 3),),
-)
+NEAR = tuple(tuple((dz, dy) for dy in (0, 3, 1, 2)) for dz in (0, 7, 1, 6, 2, 5, 3))
+FAR = (((4, 0), (4, 3)), ((4, 1), (4, 2)))
 
 
 def near_kernel(place_ref, *refs):
@@ -211,7 +190,9 @@
 
 
 def load_bands(fields, which, span):
-    return jnp.concatenate([ref[which, :, span] for ref in fields], axis=0)
+    return jnp.concatenate(
+        [ref[part, which, :, span] for ref in fields for part in range(ref.shape[0])], axis=0
+    )
 
 
 def natural_place(slice_ref, half_of, block):
@@ -235,7 +216,7 @@
 
 
 def sent_rows(place, fields, pieces):
-    count = sum(field.shape[1] for field in fields)
+    count = sum(field.shape[0] * field.shape[2] for field in fields)
     total, width = fields[0].shape[-1], pieces[0].shape[-1]
     return pl.pallas_call(
         sent_kernel,
@@ -276,7 +257,7 @@
 
 
 def kept_rows(place, slices, fields, pieces, sx, sy, white):
-    count = sum(field.shape[1] for field in fields)
+    count = sum(field.shape[0] * field.shape[2] for field in fields)
     total, width = fields[0].shape[-1], pieces[0].shape[-1]
     rows, times, columns = white.shape
     return pl.pallas_call(
@@ -342,9 +323,8 @@
     mine = jnp.where(lo == 0, jnp.concatenate([kept, other]), jnp.concatenate([other, kept]))
     pseudo = moments(event_counts, latent_mean, latent_var).astype(jnp.bfloat16)[0]
     mine, pseudo = lax.optimization_barrier((mine, pseudo))
-    next_y = shifted(mine, "y", 3)
     far, before, after = [shifted(pseudo, RING, step) for step in (2, 1, 3)]
-    block = jnp.stack([mine, next_y])
+    block = jnp.stack([mine] + [shifted(mine, "y", step) for step in (1, 3, 2)])
     own = with_core(pseudo)
 
     flips = jnp.array([0, 1, 2, 3], jnp.int32)
@@ -360,35 +340,20 @@
     sy = lax.dynamic_slice_in_dim(root.reshape(4, lax.axis_size(ROW), -1), row, 1, 1).reshape(-1, 1)
     sy = jnp.broadcast_to(sy, (sy.shape[0], 128))
 
-    def from_neighbours(blocks):
-        second = jnp.concatenate([b[-1:] for b in blocks])
-        first = jnp.concatenate([b[:1] for b in blocks])
-        return [shifted(second, "y", 3), shifted(first, "y", 1)]
-
     right, left = shifted(block, "z", 1), shifted(block, "z", nz - 1)
-    beside = from_neighbours([block])
+    pieces = [block, right, left]
     right, left, before, after = lax.optimization_barrier((right, left, before, after))
-    pieces = [block]
-    next_right, next_left = shifted(right, "z", 1), shifted(left, "z", nz - 1)
-    beside_next = from_neighbours([right, left])
     before, after = with_core(before), with_core(after)
-    next_right, next_left, beside, beside_next, far, own, mix, sx, sy = lax.optimization_barrier(
-        (next_right, next_left, beside, beside_next, far, own, mix, sx, sy)
-    )
-    pieces += [*beside, right, left, *beside_next]
-    right, left = next_right, next_left
-    next_right, next_left = shifted(right, "z", 1), shifted(left, "z", nz - 1)
-    beside = from_neighbours([right, left])
+    right, left = shifted(right, "z", 1), shifted(left, "z", nz - 1)
+    pieces += [right, left]
+    right, left, far, own, mix, sx, sy = lax.optimization_barrier(
+        (right, left, far, own, mix, sx, sy)
+    )
     far = with_core(far)
-    next_right, next_left, beside, far, before, after = lax.optimization_barrier(
-        (next_right, next_left, beside, far, before, after)
-    )
-    pieces += [right, left, *beside]
-    right, left = next_right, next_left
+    right, left = shifted(right, "z", 1), shifted(left, "z", nz - 1)
     pieces += [right, left]
-    ends = [shifted(right[:1], "z", 1), shifted(left[1:], "z", nz - 1)]
-    last = [*from_neighbours([right, left]), *ends]
-    last += [shifted(ends[1], "y", 3), shifted(ends[0], "y", 1)]
+    right, left, far, before, after = lax.optimization_barrier((right, left, far, before, after))
+    last = [shifted(right[:2], "z", 1), shifted(left[2:], "z", nz - 1)]
 
     fields = (*own, *far, *before, *after)
     near = near_product(place, fields, pieces)
@@ -398,11 +363,13 @@
     modes, width = partial_y.shape
     sent = partial_y.reshape(ny * nz, modes // (ny * nz), width)
     got = lax.all_to_all(sent, ("y", "z"), 0, 0, tiled=True)
-    got = got.reshape(ny * nz, 2, modes // (2 * ny * nz), 4, width // 4)
-    got = got.transpose(1, 3, 2, 0, 4).reshape(2, 4 * (modes // (2 * ny * nz)), -1)
+    group = modes // (2 * ny * nz)
+    got = got.reshape(ny * nz, 2, group, 2, 2, width // 4)
+    got = got.transpose(3, 1, 4, 2, 0, 5).reshape(2, 2, 2 * group, -1)
     own, before, after = with_core(got), shifted(got, RING, 1), shifted(got, RING, 3)
-    middle = got.shape[1] // 2
-    far = [shifted(before[:, :middle], RING, 1), shifted(after[:, middle:], RING, 3)]
+    before, after, far = lax.optimization_barrier((before, after, (before[:1], after[1:])))
+    far = [shifted(far[0], RING, 1), shifted(far[1], RING, 3)]
+    own, before, after = lax.optimization_barrier((own, before, after))
     before, after = with_core(before), with_core(after)
     early = sent_rows(place, (*own, *before, *after), pieces)
     far, early = lax.optimization_barrier((far, early))

time: 141 us -> 136 us (0.965)
  waiting for transfers between devices: 43.1 us -> 59.6 us
  starting transfers between devices: 47 us -> 34.7 us
  local copies, waits for them, and re-layouts: 5.28 us -> 2.2 us
  blocking collectives: 22 us -> 19.9 us
  other arithmetic: 6.64 us -> 4.66 us
    ppermute x38 -> x30, waiting for transfers between devices: 43.1 us -> 59.6 us  [shifted(): lax.ppermute(array, axis, [(k, (k + step) % size) for k in range(size)])]
    ppermute x38 -> x30, starting transfers between devices: 47 us -> 34.7 us  [shifted(): lax.ppermute(array, axis, [(k, (k + step) % size) for k in range(size)])]
    all_to_all x1, blocking collectives: 22 us -> 19.9 us  [local(): got = lax.all_to_all(sent, ('y', 'z'), 0, 0, tiled=True)]
  transfers between devices with their start and end apart: 38 -> 30, of which waited for: 12 -> 17; matrix products, arithmetic and copies ran while one was open for 7% -> 4% of each run, Pallas kernels for 7% -> 7%
where the time goes in v8:
time: 136 us
  waiting for transfers between devices  59.6 us (44%)
  starting transfers between devices  34.7 us (26%)
  blocking collectives  19.9 us (15%)
  Pallas kernels  14.2 us (10%)
  other arithmetic  4.66 us (3%)
  local copies, waits for them, and re-layouts  2.2 us (2%)
    ppermute x30, waiting for transfers between devices, shifted(): lax.ppermute(array, axis, [(k, (k + step) % size) for k in range(size)])  59.6 us
    ppermute x30, starting transfers between devices, shifted(): lax.ppermute(array, axis, [(k, (k + step) % size) for k in range(size)])  34.7 us
    all_to_all x1, blocking collectives, local(): got = lax.all_to_all(sent, ('y', 'z'), 0, 0, tiled=True)  19.9 us
    squeeze x1, other arithmetic, local(): moments(event_counts, latent_mean, latent_var).astype(jnp.bfloat16)[0]  4.29 us
    pallas_call x1, Pallas kernels, near_product(): pl.pallas_call(near_kernel, out_shape=jax.ShapeDtypeStruct((rows, width),...  3.31 us
    pallas_call x2, Pallas kernels, sent_rows(): pl.pallas_call(sent_kernel, out_shape=jax.ShapeDtypeStruct((count, width)...  2.94 us
    pallas_call x1, Pallas kernels, kept_rows(): pl.pallas_call(kept_kernel, out_shape=jax.ShapeDtypeStruct((times, rows,...  2.87 us
  transfers between devices with their start and end apart: 30, of which 17 were waited for; matrix products, arithmetic and copies ran while one was open for 4% of the time, Pallas kernels for 7%

profile of v8, /device:TPU:32, one launch (start us, length us, event | category | flops | bytes accessed | tf_op | source)
XLA Modules:
  0.0 136.2 jit_solution(7215467128814109840)
XLA Ops:
  1.8 1.6 %collective-permute-start = (bf16[64,512]{1,0:T(8,128)(2,1)S(1)}, bf16[64,512]{1,0:T(8,128)(2,1)S(1)}, u32[]{:S(2)}, u32[]{:S(2)}) collective-permute-start(bf16[64,512]{1,0:T(8,128)(2,1)S(1)} %get-tuple-element.41), channel_id=1, source_target_pairs={{0,1},{1,0},{2,3},{3,2},{4,5},{5,4},{6,7},{7,6},{8,9},{9,8},{10,11... | collective-permute-start | bytes 196616 | tf_op jit(solution)/shard_map/ppermute | solution.py:74
  3.3 4.3 %fusion.8.refs_0_ = bf16[64,4096]{1,0:T(8,128)(2,1)S(1)} fusion(s32[1,64,4096]{2,1,0:T(8,128)} %param.8, f32[1,64,4096]{2,1,0:T(8,128)} %param.10, f32[1,64,4096]{2,1,0:T(8,128)} %param.9), kind=kLoop, calls=%fused_computation.16 | loop fusion | flops 17563648 | bytes 3670016 | tf_op jit(solution)/shard_map/squeeze | solution.py:324
  7.7 1.7 %collective-permute-start.1 = (bf16[128,512]{1,0:T(8,128)(2,1)S(1)}, bf16[128,512]{1,0:T(8,128)(2,1)S(1)}, u32[]{:S(2)}, u32[]{:S(2)}) collective-permute-start(bf16[128,512]{1,0:T(8,128)(2,1)S(1)} %maximum_select_fusion), channel_id=1, source_target_pairs={{0,16},{16,32},{32,48},{48,0},{1,17},{17,33},{33,49},{49,1},{2,18}... | collective-permute-start | bytes 393224 | tf_op jit(solution)/shard_map/ppermute | solution.py:74
  9.3 1.7 %collective-permute-start.2 = (bf16[128,512]{1,0:T(8,128)(2,1)S(1)}, bf16[128,512]{1,0:T(8,128)(2,1)S(1)}, u32[]{:S(2)}, u32[]{:S(2)}) collective-permute-start(bf16[128,512]{1,0:T(8,128)(2,1)S(1)} %maximum_select_fusion), channel_id=1, source_target_pairs={{0,48},{16,0},{32,16},{48,32},{1,49},{17,1},{33,17},{49,33},{2,50}... | collective-permute-start | bytes 393224 | tf_op jit(solution)/shard_map/ppermute | solution.py:74
  11.0 2.0 %collective-permute-start.3 = (bf16[128,512]{1,0:T(8,128)(2,1)S(1)}, bf16[128,512]{1,0:T(8,128)(2,1)S(1)}, u32[]{:S(2)}, u32[]{:S(2)}) collective-permute-start(bf16[128,512]{1,0:T(8,128)(2,1)S(1)} %maximum_select_fusion), channel_id=1, source_target_pairs={{0,32},{16,48},{32,0},{48,16},{1,33},{17,49},{33,1},{49,17},{2,34}... | collective-permute-start | bytes 393224 | tf_op jit(solution)/shard_map/ppermute | solution.py:74
  14.6 2.7 %collective-permute-start.7 = (bf16[64,4096]{1,0:T(8,128)(2,1)S(1)}, bf16[64,4096]{1,0:T(8,128)(2,1)S(1)}, u32[]{:S(2)}, u32[]{:S(2)}) collective-permute-start(bf16[64,4096]{1,0:T(8,128)(2,1)S(1)} %fusion.8.refs_0_), channel_id=1, source_target_pairs={{0,129},{1,0},{128,1},{129,128},{2,131},{3,2},{130,3},{131,130},{4... | collective-permute-start | bytes 1572872 | tf_op jit(solution)/shard_map/ppermute | solution.py:74
  18.1 2.0 %collective-permute-start.4 = (bf16[4,128,512]{2,1,0:T(8,128)(2,1)S(1)}, bf16[4,128,512]{2,1,0:T(8,128)(2,1)S(1)}, u32[]{:S(2)}, u32[]{:S(2)}) collective-permute-start(bf16[4,128,512]{2,1,0:T(8,128)(2,1)S(1)} %pad_maximum_fusion.refs_8_.refs_6_.refs_10_.refs_4_), channel_id=1, source_target_pairs={{0,2},{2,4},{4,6},{6,8},{8,10},{10,12},{12,14},{14,0},{1,3},{3,5},... | collective-permute-start | bytes 1572872 | tf_op jit(solution)/shard_map/ppermute | solution.py:74
  20.2 2.8 %collective-permute-start.10 = (bf16[64,4096]{1,0:T(8,128)(2,1)S(1)}, bf16[64,4096]{1,0:T(8,128)(2,1)}, u32[]{:S(2)}, u32[]{:S(2)}) collective-permute-start(bf16[64,4096]{1,0:T(8,128)(2,1)S(1)} %fusion.8.refs_0_), channel_id=1, source_target_pairs={{0,128},{1,129},{128,0},{129,1},{2,130},{3,131},{130,2},{131,3},{4... | collective-permute-start | bytes 1572872 | tf_op jit(solution)/shard_map/ppermute | solution.py:74
  23.0 6.8 %collective-permute-done.6.refs_4_ = bf16[64,4096]{1,0:T(8,128)(2,1)S(1)} collective-permute-done((bf16[64,4096]{1,0:T(8,128)(2,1)S(1)}, bf16[64,4096]{1,0:T(8,128)(2,1)S(1)}, u32[]{:S(2)}, u32[]{:S(2)}) %collective-permute-start.6) | collective-permute-done | bytes 524320 | tf_op jit(solution)/shard_map/ppermute | solution.py:74
  29.8 8.5 %collective-permute-done.7.refs_6_ = bf16[64,4096]{1,0:T(8,128)(2,1)S(1)} collective-permute-done((bf16[64,4096]{1,0:T(8,128)(2,1)S(1)}, bf16[64,4096]{1,0:T(8,128)(2,1)S(1)}, u32[]{:S(2)}, u32[]{:S(2)}) %collective-permute-start.7) | collective-permute-done | bytes 524320 | tf_op jit(solution)/shard_map/ppermute | solution.py:74
  38.4 2.0 %collective-permute-start.8 = (bf16[4,128,512]{2,1,0:T(8,128)(2,1)S(1)}, bf16[4,128,512]{2,1,0:T(8,128)(2,1)S(1)}, u32[]{:S(2)}, u32[]{:S(2)}) collective-permute-start(bf16[4,128,512]{2,1,0:T(8,128)(2,1)S(1)} %collective-permute-done.4.refs_9_.refs_7_.refs_11_.refs_5_), channel_id=1, source_target_pairs={{0,2},{2,4},{4,6},{6,8},{8,10},{10,12},{12,14},{14,0},{1,3},{3,5},... | collective-permute-start | bytes 1572872 | tf_op jit(solution)/shard_map/ppermute | solution.py:74
  41.7 6.8 %collective-permute-done.8.refs_11_.refs_9_.refs_13_.refs_7_ = bf16[4,128,512]{2,1,0:T(8,128)(2,1)S(1)} collective-permute-done((bf16[4,128,512]{2,1,0:T(8,128)(2,1)S(1)}, bf16[4,128,512]{2,1,0:T(8,128)(2,1)S(1)}, u32[]{:S(2)}, u32[]{:S(2)}) %collective-permute-start.8) | collective-permute-done | bytes 524320 | tf_op jit(solution)/shard_map/ppermute | solution.py:74
  48.6 2.7 %collective-permute-done.9.refs_12_.refs_10_.refs_14_.refs_8_ = bf16[4,128,512]{2,1,0:T(8,128)(2,1)S(1)} collective-permute-done((bf16[4,128,512]{2,1,0:T(8,128)(2,1)S(1)}, bf16[4,128,512]{2,1,0:T(8,128)(2,1)S(1)}, u32[]{:S(2)}, u32[]{:S(2)}) %collective-permute-start.9) | collective-permute-done | bytes 524320 | tf_op jit(solution)/shard_map/ppermute | solution.py:74
  51.4 3.0 %collective-permute-start.12 = (bf16[4,128,512]{2,1,0:T(8,128)(2,1)S(1)}, bf16[4,128,512]{2,1,0:T(8,128)(2,1)S(1)}, u32[]{:S(2)}, u32[]{:S(2)}) collective-permute-start(bf16[4,128,512]{2,1,0:T(8,128)(2,1)S(1)} %collective-permute-done.8.refs_11_.refs_9_.refs_13_.refs_7_), channel_id=1, source_target_pairs={{0,2},{2,4},{4,6},{6,8},{8,10},{10,12},{12,14},{14,0},{1,3},{3,5},... | collective-permute-start | bytes 1572872 | tf_op jit(solution)/shard_map/ppermute | solution.py:74
  54.5 7.3 %collective-permute-done.12.refs_13_.refs_11_.refs_15_.refs_9_ = bf16[4,128,512]{2,1,0:T(8,128)(2,1)S(1)} collective-permute-done((bf16[4,128,512]{2,1,0:T(8,128)(2,1)S(1)}, bf16[4,128,512]{2,1,0:T(8,128)(2,1)S(1)}, u32[]{:S(2)}, u32[]{:S(2)}) %collective-permute-start.12) | collective-permute-done | bytes 524320 | tf_op jit(solution)/shard_map/ppermute | solution.py:74
  61.8 5.4 %collective-permute-done.13.refs_14_.refs_12_.refs_16_.refs_10_ = bf16[4,128,512]{2,1,0:T(8,128)(2,1)S(1)} collective-permute-done((bf16[4,128,512]{2,1,0:T(8,128)(2,1)S(1)}, bf16[4,128,512]{2,1,0:T(8,128)(2,1)S(1)}, u32[]{:S(2)}, u32[]{:S(2)}) %collective-permute-start.13) | collective-permute-done | bytes 524320 | tf_op jit(solution)/shard_map/ppermute | solution.py:74
  67.2 2.4 %collective-permute-start.17 = (bf16[2,128,512]{2,1,0:T(8,128)(2,1)S(1)}, bf16[2,128,512]{2,1,0:T(8,128)(2,1)S(1)}, u32[]{:S(2)}, u32[]{:S(2)}) collective-permute-start(bf16[2,128,512]{2,1,0:T(8,128)(2,1)S(1)} %slice.24), channel_id=1, source_target_pairs={{0,2},{2,4},{4,6},{6,8},{8,10},{10,12},{12,14},{14,0},{1,3},{3,5},... | collective-permute-start | bytes 786440 | tf_op jit(solution)/shard_map/ppermute | solution.py:74
  69.7 3.3 %near_product.1.refs_10_ = f32[512,512]{1,0:T(8,128)S(1)} custom-call(s32[4]{0:T(128)S(1)} %pad_add_fusion.first_ref.place_ref, bf16[64,4096]{1,0:T(8,128)(2,1)S(1)} %fusion.8.refs_0_, bf16[64,4096]{1,0:T(8,128)(2,1)} %collective-permute-done.11.refs_1_, bf16[64,4096]{1,0:T(8,128)(2,1)} %collective-permute-done.10.refs_2_, ...), custom_call_target="tpu_custom_call" | custom-call | flops 1610612736 | bytes 8388608 | tf_op jit(solution)/shard_map/near_product/pallas_call | solution.py:137
  73.6 2.4 %collective-permute-done.18.refs_9_.refs_14_.refs_18_.refs_12_ = bf16[2,128,512]{2,1,0:T(8,128)(2,1)S(1)} collective-permute-done((bf16[2,128,512]{2,1,0:T(8,128)(2,1)S(1)}, bf16[2,128,512]{2,1,0:T(8,128)(2,1)S(1)}, u32[]{:S(2)}, u32[]{:S(2)}) %collective-permute-start.18) | collective-permute-done | bytes 262176 | tf_op jit(solution)/shard_map/ppermute | solution.py:74
  76.0 2.1 %first_product.1 = bf16[512,512]{1,0:T(8,128)(2,1)S(1)} custom-call(f32[8,4]{1,0:T(8,128)S(1)} %broadcast_select_fusion.mix_ref, s32[4]{0:T(128)S(1)} %pad_add_fusion.first_ref.place_ref, bf16[64,4096]{1,0:T(8,128)(2,1)S(1)} %fusion.8.refs_0_, bf16[64,4096]{1,0:T(8,128)(2,1)} %collective-permute-done.11.refs_1_, ...), custom_call_target="tpu_custom_call" | custom-call | flops 536870912 | bytes 4194304 | tf_op jit(solution)/shard_map/first_product/pallas_call | solution.py:175
  78.1 19.9 %all_to_all.5 = bf16[32,16,512]{2,1,0:T(8,128)(2,1)S(1)} all-to-all(bf16[32,16,512]{2,1,0:T(8,128)(2,1)S(1)} %bitcast.42), channel_id=1, replica_groups=mesh['hi'=2,'core'=2,'y'=4,'z'=8,'lo'=2] {'y','z'}, dimensions={0} | all-to-all | bytes 1048576 | tf_op jit(solution)/shard_map/all_to_all | solution.py:365
  98.2 5.9 %collective-permute-start.20 = (bf16[2,2,16,4096]{3,2,1,0:T(8,128)(2,1)S(1)}, bf16[2,2,16,4096]{3,2,1,0:T(8,128)(2,1)S(1)}, u32[]{:S(2)}, u32[]{:S(2)}) collective-permute-start(bf16[2,2,16,4096]{3,2,1,0:T(8,128)(2,1)S(1)} %bitcast.37), channel_id=1, source_target_pairs={{0,1},{1,128},{128,129},{129,0},{2,3},{3,130},{130,131},{131,2},{4... | collective-permute-start | bytes 1572872 | tf_op jit(solution)/shard_map/ppermute | solution.py:74
  104.1 7.8 %collective-permute-done.20.refs_2_.refs_6_ = bf16[2,2,16,4096]{3,2,1,0:T(8,128)(2,1)S(1)} collective-permute-done((bf16[2,2,16,4096]{3,2,1,0:T(8,128)(2,1)S(1)}, bf16[2,2,16,4096]{3,2,1,0:T(8,128)(2,1)S(1)}, u32[]{:S(2)}, u32[]{:S(2)}) %collective-permute-start.20) | collective-permute-done | bytes 524320 | tf_op jit(solution)/shard_map/ppermute | solution.py:74
  111.9 2.9 %collective-permute-done.21.refs_4_.refs_8_ = bf16[2,2,16,4096]{3,2,1,0:T(8,128)(2,1)S(1)} collective-permute-done((bf16[2,2,16,4096]{3,2,1,0:T(8,128)(2,1)S(1)}, bf16[2,2,16,4096]{3,2,1,0:T(8,128)(2,1)S(1)}, u32[]{:S(2)}, u32[]{:S(2)}) %collective-permute-start.21) | collective-permute-done | bytes 524320 | tf_op jit(solution)/shard_map/ppermute | solution.py:74
  115.4 1.7 %collective-permute-start.22 = (bf16[1,2,16,4096]{3,2,1,0:T(8,128)(2,1)S(1)}, bf16[1,2,16,4096]{3,2,1,0:T(8,128)(2,1)S(1)}, u32[]{:S(2)}, u32[]{:S(2)}) collective-permute-start(bf16[1,2,16,4096]{3,2,1,0:T(8,128)(2,1)S(1)} %slice.30), channel_id=1, source_target_pairs={{0,1},{1,128},{128,129},{129,0},{2,3},{3,130},{130,131},{131,2},{4... | collective-permute-start | bytes 786440 | tf_op jit(solution)/shard_map/ppermute | solution.py:74
  117.1 1.5 %collective-permute-start.23 = (bf16[1,2,16,4096]{3,2,1,0:T(8,128)(2,1)S(1)}, bf16[1,2,16,4096]{3,2,1,0:T(8,128)(2,1)S(1)}, u32[]{:S(2)}, u32[]{:S(2)}) collective-permute-start(bf16[1,2,16,4096]{3,2,1,0:T(8,128)(2,1)S(1)} %slice.31), channel_id=1, source_target_pairs={{0,129},{1,0},{128,1},{129,128},{2,131},{3,2},{130,3},{131,130},{4... | collective-permute-start | bytes 786440 | tf_op jit(solution)/shard_map/ppermute | solution.py:74
  118.6 1.6 %sent_rows.2 = bf16[192,512]{1,0:T(8,128)(2,1)S(1)} custom-call(s32[4]{0:T(128)S(1)} %pad_add_fusion.first_ref.place_ref, bf16[2,2,16,4096]{3,2,1,0:T(8,128)(2,1)S(1)} %bitcast.40, bf16[2,2,16,4096]{3,2,1,0:T(8,128)(2,1)S(1)} %collective-permute-done.19.refs_1_, bf16[2,2,16,4096]{3,2,1,0:T(8,128)(2,1)S(1)} %collective-permute-done.20.refs_2_.refs_6_, ...), custom_call_target="tpu_custom_call" | custom-call | flops 805306368 | bytes 6291456 | tf_op jit(solution)/shard_map/sent_rows/pallas_call | solution.py:221
  120.2 4.7 %collective-permute-done.22.refs_2_.refs_0_ = bf16[1,2,16,4096]{3,2,1,0:T(8,128)(2,1)S(1)} collective-permute-done((bf16[1,2,16,4096]{3,2,1,0:T(8,128)(2,1)S(1)}, bf16[1,2,16,4096]{3,2,1,0:T(8,128)(2,1)S(1)}, u32[]{:S(2)}, u32[]{:S(2)}) %collective-permute-start.22) | collective-permute-done | bytes 262176 | tf_op jit(solution)/shard_map/ppermute | solution.py:74
  127.1 1.4 %sent_rows.3 = bf16[64,512]{1,0:T(8,128)(2,1)S(1)} custom-call(s32[4]{0:T(128)S(1)} %pad_add_fusion.first_ref.place_ref, bf16[1,2,16,4096]{3,2,1,0:T(8,128)(2,1)S(1)} %collective-permute-done.22.refs_2_.refs_0_, bf16[1,2,16,4096]{3,2,1,0:T(8,128)(2,1)S(1)} %collective-permute-done.23.refs_3_.refs_1_, ...), custom_call_target="tpu_custom_call" | custom-call | flops 268435456 | bytes 6291456 | tf_op jit(solution)/shard_map/sent_rows/pallas_call | solution.py:221
  129.3 2.9 %kept_rows.1.kept_ref = f32[4,64,1024]{2,1,0:T(8,128)S(1)} custom-call(s32[4]{0:T(128)S(1)} %pad_add_fusion.first_ref.place_ref, s32[8]{0:T(128)S(1)} %get-tuple-element.76.slice_ref, bf16[2,2,16,4096]{3,2,1,0:T(8,128)(2,1)S(1)} %bitcast.41, bf16[2,2,16,4096]{3,2,1,0:T(8,128)(2,1)S(1)} %collective-permute-done.19.refs_1_, ...), custom_call_target="tpu_custom_call" | custom-call | flops 1073741824 | bytes 6291456 | tf_op jit(solution)/shard_map/kept_rows/pallas_call | solution.py:263
  132.2 1.1 collective-permute-done.28.early_ref
  134.0 2.2 %whitened_gradient.1 = f32[64,4,1024]{2,1,0:T(4,128)} custom-call(s32[4]{0:T(128)S(1)} %pad_add_fusion.first_ref.place_ref, s32[8]{0:T(128)S(1)} %pad_add_fusion.1.slice_ref, f32[4,64,1024]{2,1,0:T(8,128)S(1)} %kept_rows.1.kept_ref, bf16[192,512]{1,0:T(8,128)(2,1)S(1)} %collective-permute-done.28.early_ref, ...), custom_call_target="tpu_custom_call" | custom-call | tf_op jit(solution)/shard_map/whitened_gradient/pallas_call | solution.py:300
  (78 shorter events, 10.2 us)
Async XLA Ops:
  1.8 5.9 %collective-permute-start = (bf16[64,512]{1,0:T(8,128)(2,1)S(1)}, bf16[64,512]{1,0:T(8,128)(2,1)S(1)}, u32[]{:S(2)}, u32[]{:S(2)}) collective-permute-start(bf16[64,512]{1,0:T(8,128)(2,1)S(1)} %get-tuple-element.41), channel_id=1, source_target_pairs={{0,1},{1,0},{2,3},{3,2},{4,5},{5,4},{6,7},{7,6},{8,9},{9,8},{10,11... | collective-permute-start | bytes 196616 | tf_op jit(solution)/shard_map/ppermute | solution.py:74
  7.7 9.6 %collective-permute-start.1 = (bf16[128,512]{1,0:T(8,128)(2,1)S(1)}, bf16[128,512]{1,0:T(8,128)(2,1)S(1)}, u32[]{:S(2)}, u32[]{:S(2)}) collective-permute-start(bf16[128,512]{1,0:T(8,128)(2,1)S(1)} %maximum_select_fusion), channel_id=1, source_target_pairs={{0,16},{16,32},{32,48},{48,0},{1,17},{17,33},{33,49},{49,1},{2,18}... | collective-permute-start | bytes 393224 | tf_op jit(solution)/shard_map/ppermute | solution.py:74
  9.3 7.9 %collective-permute-start.2 = (bf16[128,512]{1,0:T(8,128)(2,1)S(1)}, bf16[128,512]{1,0:T(8,128)(2,1)S(1)}, u32[]{:S(2)}, u32[]{:S(2)}) collective-permute-start(bf16[128,512]{1,0:T(8,128)(2,1)S(1)} %maximum_select_fusion), channel_id=1, source_target_pairs={{0,48},{16,0},{32,16},{48,32},{1,49},{17,1},{33,17},{49,33},{2,50}... | collective-permute-start | bytes 393224 | tf_op jit(solution)/shard_map/ppermute | solution.py:74
  11.0 7.0 %collective-permute-start.3 = (bf16[128,512]{1,0:T(8,128)(2,1)S(1)}, bf16[128,512]{1,0:T(8,128)(2,1)S(1)}, u32[]{:S(2)}, u32[]{:S(2)}) collective-permute-start(bf16[128,512]{1,0:T(8,128)(2,1)S(1)} %maximum_select_fusion), channel_id=1, source_target_pairs={{0,32},{16,48},{32,0},{48,16},{1,33},{17,49},{33,1},{49,17},{2,34}... | collective-permute-start | bytes 393224 | tf_op jit(solution)/shard_map/ppermute | solution.py:74
  14.0 15.7 %collective-permute-start.6 = (bf16[64,4096]{1,0:T(8,128)(2,1)S(1)}, bf16[64,4096]{1,0:T(8,128)(2,1)S(1)}, u32[]{:S(2)}, u32[]{:S(2)}) collective-permute-start(bf16[64,4096]{1,0:T(8,128)(2,1)S(1)} %fusion.8.refs_0_), channel_id=1, source_target_pairs={{0,1},{1,128},{128,129},{129,0},{2,3},{3,130},{130,131},{131,2},{4... | collective-permute-start | bytes 1572872 | tf_op jit(solution)/shard_map/ppermute | solution.py:74
  14.6 23.8 %collective-permute-start.7 = (bf16[64,4096]{1,0:T(8,128)(2,1)S(1)}, bf16[64,4096]{1,0:T(8,128)(2,1)S(1)}, u32[]{:S(2)}, u32[]{:S(2)}) collective-permute-start(bf16[64,4096]{1,0:T(8,128)(2,1)S(1)} %fusion.8.refs_0_), channel_id=1, source_target_pairs={{0,129},{1,0},{128,1},{129,128},{2,131},{3,2},{130,3},{131,130},{4... | collective-permute-start | bytes 1572872 | tf_op jit(solution)/shard_map/ppermute | solution.py:74
  18.1 20.3 %collective-permute-start.4 = (bf16[4,128,512]{2,1,0:T(8,128)(2,1)S(1)}, bf16[4,128,512]{2,1,0:T(8,128)(2,1)S(1)}, u32[]{:S(2)}, u32[]{:S(2)}) collective-permute-start(bf16[4,128,512]{2,1,0:T(8,128)(2,1)S(1)} %pad_maximum_fusion.refs_8_.refs_6_.refs_10_.refs_4_), channel_id=1, source_target_pairs={{0,2},{2,4},{4,6},{6,8},{8,10},{10,12},{12,14},{14,0},{1,3},{3,5},... | collective-permute-start | bytes 1572872 | tf_op jit(solution)/shard_map/ppermute | solution.py:74
  20.1 18.3 %collective-permute-start.5 = (bf16[4,128,512]{2,1,0:T(8,128)(2,1)S(1)}, bf16[4,128,512]{2,1,0:T(8,128)(2,1)S(1)}, u32[]{:S(2)}, u32[]{:S(2)}) collective-permute-start(bf16[4,128,512]{2,1,0:T(8,128)(2,1)S(1)} %pad_maximum_fusion.refs_8_.refs_6_.refs_10_.refs_4_), channel_id=1, source_target_pairs={{0,14},{2,0},{4,2},{6,4},{8,6},{10,8},{12,10},{14,12},{1,15},{3,1}... | collective-permute-start | bytes 1572872 | tf_op jit(solution)/shard_map/ppermute | solution.py:74
  20.2 21.0 %collective-permute-start.10 = (bf16[64,4096]{1,0:T(8,128)(2,1)S(1)}, bf16[64,4096]{1,0:T(8,128)(2,1)}, u32[]{:S(2)}, u32[]{:S(2)}) collective-permute-start(bf16[64,4096]{1,0:T(8,128)(2,1)S(1)} %fusion.8.refs_0_), channel_id=1, source_target_pairs={{0,128},{1,129},{128,0},{129,1},{2,130},{3,131},{130,2},{131,3},{4... | collective-permute-start | bytes 1572872 | tf_op jit(solution)/shard_map/ppermute | solution.py:74
  29.8 11.9 %collective-permute-start.11 = (bf16[64,4096]{1,0:T(8,128)(2,1)S(1)}, bf16[64,4096]{1,0:T(8,128)(2,1)}, u32[]{:S(2)}, u32[]{:S(2)}) collective-permute-start(bf16[64,4096]{1,0:T(8,128)(2,1)S(1)} %fusion.8.refs_0_), channel_id=1, source_target_pairs={{0,64},{64,0},{1,65},{65,1},{2,66},{66,2},{3,67},{67,3},{4,68},{68... | collective-permute-start | bytes 1572872 | tf_op jit(solution)/shard_map/ppermute | solution.py:74
  38.4 10.2 %collective-permute-start.8 = (bf16[4,128,512]{2,1,0:T(8,128)(2,1)S(1)}, bf16[4,128,512]{2,1,0:T(8,128)(2,1)S(1)}, u32[]{:S(2)}, u32[]{:S(2)}) collective-permute-start(bf16[4,128,512]{2,1,0:T(8,128)(2,1)S(1)} %collective-permute-done.4.refs_9_.refs_7_.refs_11_.refs_5_), channel_id=1, source_target_pairs={{0,2},{2,4},{4,6},{6,8},{8,10},{10,12},{12,14},{14,0},{1,3},{3,5},... | collective-permute-start | bytes 1572872 | tf_op jit(solution)/shard_map/ppermute | solution.py:74
  40.4 11.0 %collective-permute-start.9 = (bf16[4,128,512]{2,1,0:T(8,128)(2,1)S(1)}, bf16[4,128,512]{2,1,0:T(8,128)(2,1)S(1)}, u32[]{:S(2)}, u32[]{:S(2)}) collective-permute-start(bf16[4,128,512]{2,1,0:T(8,128)(2,1)S(1)} %collective-permute-done.5.refs_10_.refs_8_.refs_12_.refs_6_), channel_id=1, source_target_pairs={{0,14},{2,0},{4,2},{6,4},{8,6},{10,8},{12,10},{14,12},{1,15},{3,1}... | collective-permute-start | bytes 1572872 | tf_op jit(solution)/shard_map/ppermute | solution.py:74
  41.2 13.2 %collective-permute-start.15 = (bf16[64,4096]{1,0:T(8,128)(2,1)}, bf16[64,4096]{1,0:T(8,128)(2,1)S(1)}, u32[]{:S(2)}, u32[]{:S(2)}) collective-permute-start(bf16[64,4096]{1,0:T(8,128)(2,1)} %copy-done), channel_id=1, source_target_pairs={{0,64},{64,0},{1,65},{65,1},{2,66},{66,2},{3,67},{67,3},{4,68},{68... | collective-permute-start | bytes 1572872 | tf_op jit(solution)/shard_map/ppermute | solution.py:74
  41.3 13.2 %collective-permute-start.16 = (bf16[64,4096]{1,0:T(8,128)(2,1)}, bf16[64,4096]{1,0:T(8,128)(2,1)S(1)}, u32[]{:S(2)}, u32[]{:S(2)}) collective-permute-start(bf16[64,4096]{1,0:T(8,128)(2,1)} %copy-done.2), channel_id=1, source_target_pairs={{0,64},{64,0},{1,65},{65,1},{2,66},{66,2},{3,67},{67,3},{4,68},{68... | collective-permute-start | bytes 1572872 | tf_op jit(solution)/shard_map/ppermute | solution.py:74
  51.4 18.3 %copy-start.1 = (bf16[64,4096]{1,0:T(8,128)(2,1)S(1)}, bf16[64,4096]{1,0:T(8,128)(2,1)}, u32[]{:S(2)}) copy-start(bf16[64,4096]{1,0:T(8,128)(2,1)} %copy-done) | copy-start | bytes 1572868
  51.4 18.3 %copy-start.3 = (bf16[64,4096]{1,0:T(8,128)(2,1)S(1)}, bf16[64,4096]{1,0:T(8,128)(2,1)}, u32[]{:S(2)}) copy-start(bf16[64,4096]{1,0:T(8,128)(2,1)} %copy-done.2) | copy-start | bytes 1572868
  51.4 10.4 %collective-permute-start.12 = (bf16[4,128,512]{2,1,0:T(8,128)(2,1)S(1)}, bf16[4,128,512]{2,1,0:T(8,128)(2,1)S(1)}, u32[]{:S(2)}, u32[]{:S(2)}) collective-permute-start(bf16[4,128,512]{2,1,0:T(8,128)(2,1)S(1)} %collective-permute-done.8.refs_11_.refs_9_.refs_13_.refs_7_), channel_id=1, source_target_pairs={{0,2},{2,4},{4,6},{6,8},{8,10},{10,12},{12,14},{14,0},{1,3},{3,5},... | collective-permute-start | bytes 1572872 | tf_op jit(solution)/shard_map/ppermute | solution.py:74
  54.4 12.7 %collective-permute-start.13 = (bf16[4,128,512]{2,1,0:T(8,128)(2,1)S(1)}, bf16[4,128,512]{2,1,0:T(8,128)(2,1)S(1)}, u32[]{:S(2)}, u32[]{:S(2)}) collective-permute-start(bf16[4,128,512]{2,1,0:T(8,128)(2,1)S(1)} %collective-permute-done.9.refs_12_.refs_10_.refs_14_.refs_8_), channel_id=1, source_target_pairs={{0,14},{2,0},{4,2},{6,4},{8,6},{10,8},{12,10},{14,12},{1,15},{3,1}... | collective-permute-start | bytes 1572872 | tf_op jit(solution)/shard_map/ppermute | solution.py:74
  54.4 12.7 %collective-permute-start.14 = (bf16[64,4096]{1,0:T(8,128)(2,1)}, bf16[64,4096]{1,0:T(8,128)(2,1)S(1)}, u32[]{:S(2)}, u32[]{:S(2)}) collective-permute-start(bf16[64,4096]{1,0:T(8,128)(2,1)} %collective-permute-done.10.refs_2_), channel_id=1, source_target_pairs={{0,64},{64,0},{1,65},{65,1},{2,66},{66,2},{3,67},{67,3},{4,68},{68... | collective-permute-start | bytes 1572872 | tf_op jit(solution)/shard_map/ppermute | solution.py:74
  67.2 6.4 %collective-permute-start.17 = (bf16[2,128,512]{2,1,0:T(8,128)(2,1)S(1)}, bf16[2,128,512]{2,1,0:T(8,128)(2,1)S(1)}, u32[]{:S(2)}, u32[]{:S(2)}) collective-permute-start(bf16[2,128,512]{2,1,0:T(8,128)(2,1)S(1)} %slice.24), channel_id=1, source_target_pairs={{0,2},{2,4},{4,6},{6,8},{8,10},{10,12},{12,14},{14,0},{1,3},{3,5},... | collective-permute-start | bytes 786440 | tf_op jit(solution)/shard_map/ppermute | solution.py:74
  69.6 6.4 %collective-permute-start.18 = (bf16[2,128,512]{2,1,0:T(8,128)(2,1)S(1)}, bf16[2,128,512]{2,1,0:T(8,128)(2,1)S(1)}, u32[]{:S(2)}, u32[]{:S(2)}) collective-permute-start(bf16[2,128,512]{2,1,0:T(8,128)(2,1)S(1)} %slice.25), channel_id=1, source_target_pairs={{0,14},{2,0},{4,2},{6,4},{8,6},{10,8},{12,10},{14,12},{1,15},{3,1}... | collective-permute-start | bytes 786440 | tf_op jit(solution)/shard_map/ppermute | solution.py:74
  98.2 13.7 %collective-permute-start.20 = (bf16[2,2,16,4096]{3,2,1,0:T(8,128)(2,1)S(1)}, bf16[2,2,16,4096]{3,2,1,0:T(8,128)(2,1)S(1)}, u32[]{:S(2)}, u32[]{:S(2)}) collective-permute-start(bf16[2,2,16,4096]{3,2,1,0:T(8,128)(2,1)S(1)} %bitcast.37), channel_id=1, source_target_pairs={{0,1},{1,128},{128,129},{129,0},{2,3},{3,130},{130,131},{131,2},{4... | collective-permute-start | bytes 1572872 | tf_op jit(solution)/shard_map/ppermute | solution.py:74
  104.1 10.7 %collective-permute-start.21 = (bf16[2,2,16,4096]{3,2,1,0:T(8,128)(2,1)S(1)}, bf16[2,2,16,4096]{3,2,1,0:T(8,128)(2,1)S(1)}, u32[]{:S(2)}, u32[]{:S(2)}) collective-permute-start(bf16[2,2,16,4096]{3,2,1,0:T(8,128)(2,1)S(1)} %bitcast.38), channel_id=1, source_target_pairs={{0,129},{1,0},{128,1},{129,128},{2,131},{3,2},{130,3},{131,130},{4... | collective-permute-start | bytes 1572872 | tf_op jit(solution)/shard_map/ppermute | solution.py:74
  104.1 10.7 %collective-permute-start.19 = (bf16[2,2,16,4096]{3,2,1,0:T(8,128)(2,1)S(1)}, bf16[2,2,16,4096]{3,2,1,0:T(8,128)(2,1)S(1)}, u32[]{:S(2)}, u32[]{:S(2)}) collective-permute-start(bf16[2,2,16,4096]{3,2,1,0:T(8,128)(2,1)S(1)} %bitcast.39), channel_id=1, source_target_pairs={{0,64},{64,0},{1,65},{65,1},{2,66},{66,2},{3,67},{67,3},{4,68},{68... | collective-permute-start | bytes 1572872 | tf_op jit(solution)/shard_map/ppermute | solution.py:74
  114.8 3.8 %collective-permute-start.24 = (bf16[2,2,16,4096]{3,2,1,0:T(8,128)(2,1)S(1)}, bf16[2,2,16,4096]{3,2,1,0:T(8,128)(2,1)S(1)}, u32[]{:S(2)}, u32[]{:S(2)}) collective-permute-start(bf16[2,2,16,4096]{3,2,1,0:T(8,128)(2,1)S(1)} %collective-permute-done.20.refs_2_.refs_6_), channel_id=1, source_target_pairs={{0,64},{64,0},{1,65},{65,1},{2,66},{66,2},{3,67},{67,3},{4,68},{68... | collective-permute-start | bytes 1572872 | tf_op jit(solution)/shard_map/ppermute | solution.py:74
  114.9 3.7 %collective-permute-start.25 = (bf16[2,2,16,4096]{3,2,1,0:T(8,128)(2,1)S(1)}, bf16[2,2,16,4096]{3,2,1,0:T(8,128)(2,1)S(1)}, u32[]{:S(2)}, u32[]{:S(2)}) collective-permute-start(bf16[2,2,16,4096]{3,2,1,0:T(8,128)(2,1)S(1)} %collective-permute-done.21.refs_4_.refs_8_), channel_id=1, source_target_pairs={{0,64},{64,0},{1,65},{65,1},{2,66},{66,2},{3,67},{67,3},{4,68},{68... | collective-permute-start | bytes 1572872 | tf_op jit(solution)/shard_map/ppermute | solution.py:74
  115.4 9.5 %collective-permute-start.22 = (bf16[1,2,16,4096]{3,2,1,0:T(8,128)(2,1)S(1)}, bf16[1,2,16,4096]{3,2,1,0:T(8,128)(2,1)S(1)}, u32[]{:S(2)}, u32[]{:S(2)}) collective-permute-start(bf16[1,2,16,4096]{3,2,1,0:T(8,128)(2,1)S(1)} %slice.30), channel_id=1, source_target_pairs={{0,1},{1,128},{128,129},{129,0},{2,3},{3,130},{130,131},{131,2},{4... | collective-permute-start | bytes 786440 | tf_op jit(solution)/shard_map/ppermute | solution.py:74
  117.1 8.0 %collective-permute-start.23 = (bf16[1,2,16,4096]{3,2,1,0:T(8,128)(2,1)S(1)}, bf16[1,2,16,4096]{3,2,1,0:T(8,128)(2,1)S(1)}, u32[]{:S(2)}, u32[]{:S(2)}) collective-permute-start(bf16[1,2,16,4096]{3,2,1,0:T(8,128)(2,1)S(1)} %slice.31), channel_id=1, source_target_pairs={{0,129},{1,0},{128,1},{129,128},{2,131},{3,2},{130,3},{131,130},{4... | collective-permute-start | bytes 786440 | tf_op jit(solution)/shard_map/ppermute | solution.py:74
  125.1 1.5 %collective-permute-start.26 = (bf16[1,2,16,4096]{3,2,1,0:T(8,128)(2,1)S(1)}, bf16[1,2,16,4096]{3,2,1,0:T(8,128)(2,1)S(1)}, u32[]{:S(2)}, u32[]{:S(2)}) collective-permute-start(bf16[1,2,16,4096]{3,2,1,0:T(8,128)(2,1)S(1)} %collective-permute-done.22.refs_2_.refs_0_), channel_id=1, source_target_pairs={{0,64},{64,0},{1,65},{65,1},{2,66},{66,2},{3,67},{67,3},{4,68},{68... | collective-permute-start | bytes 786440 | tf_op jit(solution)/shard_map/ppermute | solution.py:74
  125.1 1.9 %collective-permute-start.27 = (bf16[1,2,16,4096]{3,2,1,0:T(8,128)(2,1)S(1)}, bf16[1,2,16,4096]{3,2,1,0:T(8,128)(2,1)S(1)}, u32[]{:S(2)}, u32[]{:S(2)}) collective-permute-start(bf16[1,2,16,4096]{3,2,1,0:T(8,128)(2,1)S(1)} %collective-permute-done.23.refs_3_.refs_1_), channel_id=1, source_target_pairs={{0,64},{64,0},{1,65},{65,1},{2,66},{66,2},{3,67},{67,3},{4,68},{68... | collective-permute-start | bytes 786440 | tf_op jit(solution)/shard_map/ppermute | solution.py:74
  125.7 7.5 %collective-permute-start.28 = (bf16[192,512]{1,0:T(8,128)(2,1)S(1)}, bf16[192,512]{1,0:T(8,128)(2,1)S(1)}, u32[]{:S(2)}, u32[]{:S(2)}) collective-permute-start(bf16[192,512]{1,0:T(8,128)(2,1)S(1)} %sent_rows.2), channel_id=1, source_target_pairs={{0,1},{1,0},{2,3},{3,2},{4,5},{5,4},{6,7},{7,6},{8,9},{9,8},{10,11... | collective-permute-start | bytes 589832 | tf_op jit(solution)/shard_map/ppermute | solution.py:74
  128.5 5.5 %collective-permute-start.29 = (bf16[64,512]{1,0:T(8,128)(2,1)S(1)}, bf16[64,512]{1,0:T(8,128)(2,1)S(1)}, u32[]{:S(2)}, u32[]{:S(2)}) collective-permute-start(bf16[64,512]{1,0:T(8,128)(2,1)S(1)} %sent_rows.3), channel_id=1, source_target_pairs={{0,1},{1,0},{2,3},{3,2},{4,5},{5,4},{6,7},{7,6},{8,9},{9,8},{10,11... | collective-permute-start | bytes 196616 | tf_op jit(solution)/shard_map/ppermute | solution.py:74
  (5 other events, 20.6 us)

commit v9 on v8

--- a/solution.py
+++ b/solution.py
@@ -323,9 +323,11 @@
     mine = jnp.where(lo == 0, jnp.concatenate([kept, other]), jnp.concatenate([other, kept]))
     pseudo = moments(event_counts, latent_mean, latent_var).astype(jnp.bfloat16)[0]
     mine, pseudo = lax.optimization_barrier((mine, pseudo))
-    far, before, after = [shifted(pseudo, RING, step) for step in (2, 1, 3)]
+    before, after = shifted(pseudo, RING, 1), shifted(pseudo, RING, 3)
     block = jnp.stack([mine] + [shifted(mine, "y", step) for step in (1, 3, 2)])
-    own = with_core(pseudo)
+    block, pseudo = lax.optimization_barrier((block, pseudo))
+    own = lax.optimization_barrier(with_core(pseudo))
+    far = shifted(own[0], RING, 2)
 
     flips = jnp.array([0, 1, 2, 3], jnp.int32)
     before_flip, after_flip = 2 * (1 - lo), 2 * lo

time: 136 us -> 131 us (0.963)
  waiting for transfers between devices: 59.6 us -> 52.8 us
  local copies, waits for them, and re-layouts: 2.2 us -> 4.03 us
    ppermute x30, waiting for transfers between devices: 59.6 us -> 52.8 us  [shifted(): lax.ppermute(array, axis, [(k, (k + step) % size) for k in range(size)])]
    unnamed x14 -> x18, local copies, waits for them, and re-layouts: 0.93 us -> 2.76 us
  transfers between devices with their start and end apart: 30 -> 30, of which waited for: 17 -> 13; matrix products, arithmetic and copies ran while one was open for 4% -> 4% of each run, Pallas kernels for 7% -> 7%
where the time goes in v9:
time: 131 us; the launch traced here: 130 us
  waiting for transfers between devices  52.8 us (40%)
  starting transfers between devices  34.2 us (26%)
  blocking collectives  19.9 us (15%)
  Pallas kernels  13.9 us (11%)
  other arithmetic  4.66 us (4%)
  local copies, waits for them, and re-layouts  4.03 us (3%)
    ppermute x30, waiting for transfers between devices, shifted(): lax.ppermute(array, axis, [(k, (k + step) % size) for k in range(size)])  52.8 us
    ppermute x30, starting transfers between devices, shifted(): lax.ppermute(array, axis, [(k, (k + step) % size) for k in range(size)])  34.2 us
    all_to_all x1, blocking collectives, local(): got = lax.all_to_all(sent, ('y', 'z'), 0, 0, tiled=True)  19.9 us
    squeeze x1, other arithmetic, local(): moments(event_counts, latent_mean, latent_var).astype(jnp.bfloat16)[0]  4.29 us
    pallas_call x1, Pallas kernels, near_product(): pl.pallas_call(near_kernel, out_shape=jax.ShapeDtypeStruct((rows, width),...  3.14 us
    pallas_call x2, Pallas kernels, sent_rows(): pl.pallas_call(sent_kernel, out_shape=jax.ShapeDtypeStruct((count, width)...  2.96 us
    pallas_call x1, Pallas kernels, kept_rows(): pl.pallas_call(kept_kernel, out_shape=jax.ShapeDtypeStruct((times, rows,...  2.87 us
    unnamed x18, local copies, waits for them, and re-layouts  2.76 us
  transfers between devices with their start and end apart: 30, of which 13 were waited for; matrix products, arithmetic and copies ran while one was open for 4% of the time, Pallas kernels for 7%

profile of v9, /device:TPU:32, one launch (start us, length us, event | category | flops | bytes accessed | tf_op | source)
XLA Modules:
  0.0 130.5 jit_solution(14277895519761158333)
XLA Ops:
  1.8 1.6 %collective-permute-start = (bf16[64,512]{1,0:T(8,128)(2,1)S(1)}, bf16[64,512]{1,0:T(8,128)(2,1)S(1)}, u32[]{:S(2)}, u32[]{:S(2)}) collective-permute-start(bf16[64,512]{1,0:T(8,128)(2,1)S(1)} %get-tuple-element.45), channel_id=1, source_target_pairs={{0,1},{1,0},{2,3},{3,2},{4,5},{5,4},{6,7},{7,6},{8,9},{9,8},{10,11... | collective-permute-start | bytes 196616 | tf_op jit(solution)/shard_map/ppermute | solution.py:74
  3.3 4.3 %fusion.8.refs_0_ = bf16[64,4096]{1,0:T(8,128)(2,1)S(1)} fusion(s32[1,64,4096]{2,1,0:T(8,128)} %param.8, f32[1,64,4096]{2,1,0:T(8,128)} %param.10, f32[1,64,4096]{2,1,0:T(8,128)} %param.9), kind=kLoop, calls=%fused_computation.16 | loop fusion | flops 17563648 | bytes 3670016 | tf_op jit(solution)/shard_map/squeeze | solution.py:324
  7.7 1.7 %collective-permute-start.1 = (bf16[128,512]{1,0:T(8,128)(2,1)S(1)}, bf16[128,512]{1,0:T(8,128)(2,1)S(1)}, u32[]{:S(2)}, u32[]{:S(2)}) collective-permute-start(bf16[128,512]{1,0:T(8,128)(2,1)S(1)} %maximum_select_fusion), channel_id=1, source_target_pairs={{0,16},{16,32},{32,48},{48,0},{1,17},{17,33},{33,49},{49,1},{2,18}... | collective-permute-start | bytes 393224 | tf_op jit(solution)/shard_map/ppermute | solution.py:74
  9.3 1.7 %collective-permute-start.2 = (bf16[128,512]{1,0:T(8,128)(2,1)S(1)}, bf16[128,512]{1,0:T(8,128)(2,1)S(1)}, u32[]{:S(2)}, u32[]{:S(2)}) collective-permute-start(bf16[128,512]{1,0:T(8,128)(2,1)S(1)} %maximum_select_fusion), channel_id=1, source_target_pairs={{0,48},{16,0},{32,16},{48,32},{1,49},{17,1},{33,17},{49,33},{2,50}... | collective-permute-start | bytes 393224 | tf_op jit(solution)/shard_map/ppermute | solution.py:74
  11.0 2.0 %collective-permute-start.3 = (bf16[128,512]{1,0:T(8,128)(2,1)S(1)}, bf16[128,512]{1,0:T(8,128)(2,1)S(1)}, u32[]{:S(2)}, u32[]{:S(2)}) collective-permute-start(bf16[128,512]{1,0:T(8,128)(2,1)S(1)} %maximum_select_fusion), channel_id=1, source_target_pairs={{0,32},{16,48},{32,0},{48,16},{1,33},{17,49},{33,1},{49,17},{2,34}... | collective-permute-start | bytes 393224 | tf_op jit(solution)/shard_map/ppermute | solution.py:74
  14.6 2.7 %collective-permute-start.7 = (bf16[64,4096]{1,0:T(8,128)(2,1)S(1)}, bf16[64,4096]{1,0:T(8,128)(2,1)S(1)}, u32[]{:S(2)}, u32[]{:S(2)}) collective-permute-start(bf16[64,4096]{1,0:T(8,128)(2,1)S(1)} %fusion.8.refs_0_), channel_id=1, source_target_pairs={{0,129},{1,0},{128,1},{129,128},{2,131},{3,2},{130,3},{131,130},{4... | collective-permute-start | bytes 1572872 | tf_op jit(solution)/shard_map/ppermute | solution.py:74
  18.1 2.0 %collective-permute-start.4 = (bf16[4,128,512]{2,1,0:T(8,128)(2,1)S(1)}, bf16[4,128,512]{2,1,0:T(8,128)(2,1)S(1)}, u32[]{:S(2)}, u32[]{:S(2)}) collective-permute-start(bf16[4,128,512]{2,1,0:T(8,128)(2,1)S(1)} %pad_maximum_fusion.refs_8_.refs_6_.refs_10_.refs_4_), channel_id=1, source_target_pairs={{0,2},{2,4},{4,6},{6,8},{8,10},{10,12},{12,14},{14,0},{1,3},{3,5},... | collective-permute-start | bytes 1572872 | tf_op jit(solution)/shard_map/ppermute | solution.py:74
  20.2 1.9 %collective-permute-done.10.refs_1_ = bf16[64,4096]{1,0:T(8,128)(2,1)S(1)} collective-permute-done((bf16[64,4096]{1,0:T(8,128)(2,1)S(1)}, bf16[64,4096]{1,0:T(8,128)(2,1)S(1)}, u32[]{:S(2)}, u32[]{:S(2)}) %collective-permute-start.10) | collective-permute-done | bytes 524320 | tf_op jit(solution)/shard_map/ppermute | solution.py:74
  22.9 2.7 %collective-permute-start.11 = (bf16[64,4096]{1,0:T(8,128)(2,1)S(1)}, bf16[64,4096]{1,0:T(8,128)(2,1)}, u32[]{:S(2)}, u32[]{:S(2)}) collective-permute-start(bf16[64,4096]{1,0:T(8,128)(2,1)S(1)} %fusion.8.refs_0_), channel_id=1, source_target_pairs={{0,128},{1,129},{128,0},{129,1},{2,130},{3,131},{130,2},{131,3},{4... | collective-permute-start | bytes 1572872 | tf_op jit(solution)/shard_map/ppermute | solution.py:74
  25.6 2.8 %collective-permute-done.6.refs_4_ = bf16[64,4096]{1,0:T(8,128)(2,1)S(1)} collective-permute-done((bf16[64,4096]{1,0:T(8,128)(2,1)S(1)}, bf16[64,4096]{1,0:T(8,128)(2,1)S(1)}, u32[]{:S(2)}, u32[]{:S(2)}) %collective-permute-start.6) | collective-permute-done | bytes 524320 | tf_op jit(solution)/shard_map/ppermute | solution.py:74
  28.4 9.9 %collective-permute-done.7.refs_6_ = bf16[64,4096]{1,0:T(8,128)(2,1)S(1)} collective-permute-done((bf16[64,4096]{1,0:T(8,128)(2,1)S(1)}, bf16[64,4096]{1,0:T(8,128)(2,1)S(1)}, u32[]{:S(2)}, u32[]{:S(2)}) %collective-permute-start.7) | collective-permute-done | bytes 524320 | tf_op jit(solution)/shard_map/ppermute | solution.py:74
  38.4 2.0 %collective-permute-start.8 = (bf16[4,128,512]{2,1,0:T(8,128)(2,1)S(1)}, bf16[4,128,512]{2,1,0:T(8,128)(2,1)S(1)}, u32[]{:S(2)}, u32[]{:S(2)}) collective-permute-start(bf16[4,128,512]{2,1,0:T(8,128)(2,1)S(1)} %collective-permute-done.4.refs_9_.refs_7_.refs_11_.refs_5_), channel_id=1, source_target_pairs={{0,2},{2,4},{4,6},{6,8},{8,10},{10,12},{12,14},{14,0},{1,3},{3,5},... | collective-permute-start | bytes 1572872 | tf_op jit(solution)/shard_map/ppermute | solution.py:74
  41.7 6.8 %collective-permute-done.8.refs_11_.refs_9_.refs_13_.refs_7_ = bf16[4,128,512]{2,1,0:T(8,128)(2,1)S(1)} collective-permute-done((bf16[4,128,512]{2,1,0:T(8,128)(2,1)S(1)}, bf16[4,128,512]{2,1,0:T(8,128)(2,1)S(1)}, u32[]{:S(2)}, u32[]{:S(2)}) %collective-permute-start.8) | collective-permute-done | bytes 524320 | tf_op jit(solution)/shard_map/ppermute | solution.py:74
  48.6 2.7 %collective-permute-done.9.refs_12_.refs_10_.refs_14_.refs_8_ = bf16[4,128,512]{2,1,0:T(8,128)(2,1)S(1)} collective-permute-done((bf16[4,128,512]{2,1,0:T(8,128)(2,1)S(1)}, bf16[4,128,512]{2,1,0:T(8,128)(2,1)S(1)}, u32[]{:S(2)}, u32[]{:S(2)}) %collective-permute-start.9) | collective-permute-done | bytes 524320 | tf_op jit(solution)/shard_map/ppermute | solution.py:74
  51.4 3.0 %collective-permute-start.12 = (bf16[4,128,512]{2,1,0:T(8,128)(2,1)S(1)}, bf16[4,128,512]{2,1,0:T(8,128)(2,1)S(1)}, u32[]{:S(2)}, u32[]{:S(2)}) collective-permute-start(bf16[4,128,512]{2,1,0:T(8,128)(2,1)S(1)} %collective-permute-done.8.refs_11_.refs_9_.refs_13_.refs_7_), channel_id=1, source_target_pairs={{0,2},{2,4},{4,6},{6,8},{8,10},{10,12},{12,14},{14,0},{1,3},{3,5},... | collective-permute-start | bytes 1572872 | tf_op jit(solution)/shard_map/ppermute | solution.py:74
  54.5 7.3 %collective-permute-done.12.refs_13_.refs_11_.refs_15_.refs_9_ = bf16[4,128,512]{2,1,0:T(8,128)(2,1)S(1)} collective-permute-done((bf16[4,128,512]{2,1,0:T(8,128)(2,1)S(1)}, bf16[4,128,512]{2,1,0:T(8,128)(2,1)S(1)}, u32[]{:S(2)}, u32[]{:S(2)}) %collective-permute-start.12) | collective-permute-done | bytes 524320 | tf_op jit(solution)/shard_map/ppermute | solution.py:74
  61.8 5.4 %collective-permute-done.13.refs_14_.refs_12_.refs_16_.refs_10_ = bf16[4,128,512]{2,1,0:T(8,128)(2,1)S(1)} collective-permute-done((bf16[4,128,512]{2,1,0:T(8,128)(2,1)S(1)}, bf16[4,128,512]{2,1,0:T(8,128)(2,1)S(1)}, u32[]{:S(2)}, u32[]{:S(2)}) %collective-permute-start.13) | collective-permute-done | bytes 524320 | tf_op jit(solution)/shard_map/ppermute | solution.py:74
  67.2 2.4 %collective-permute-start.17 = (bf16[2,128,512]{2,1,0:T(8,128)(2,1)S(1)}, bf16[2,128,512]{2,1,0:T(8,128)(2,1)S(1)}, u32[]{:S(2)}, u32[]{:S(2)}) collective-permute-start(bf16[2,128,512]{2,1,0:T(8,128)(2,1)S(1)} %slice.24), channel_id=1, source_target_pairs={{0,2},{2,4},{4,6},{6,8},{8,10},{10,12},{12,14},{14,0},{1,3},{3,5},... | collective-permute-start | bytes 786440 | tf_op jit(solution)/shard_map/ppermute | solution.py:74
  70.7 3.1 %near_product.1.refs_10_ = f32[512,512]{1,0:T(8,128)S(1)} custom-call(s32[4]{0:T(128)S(1)} %pad_add_fusion.first_ref.place_ref, bf16[64,4096]{1,0:T(8,128)(2,1)S(1)} %fusion.8.refs_0_, bf16[64,4096]{1,0:T(8,128)(2,1)S(1)} %copy-done.5, bf16[64,4096]{1,0:T(8,128)(2,1)} %collective-permute-done.11.refs_2_, ...), custom_call_target="tpu_custom_call" | custom-call | flops 1610612736 | bytes 8388608 | tf_op jit(solution)/shard_map/near_product/pallas_call | solution.py:137
  73.9 2.1 %collective-permute-done.18.refs_9_.refs_14_.refs_18_.refs_12_ = bf16[2,128,512]{2,1,0:T(8,128)(2,1)S(1)} collective-permute-done((bf16[2,128,512]{2,1,0:T(8,128)(2,1)S(1)}, bf16[2,128,512]{2,1,0:T(8,128)(2,1)S(1)}, u32[]{:S(2)}, u32[]{:S(2)}) %collective-permute-start.18) | collective-permute-done | bytes 262176 | tf_op jit(solution)/shard_map/ppermute | solution.py:74
  76.0 2.0 %first_product.1 = bf16[512,512]{1,0:T(8,128)(2,1)S(1)} custom-call(f32[8,4]{1,0:T(8,128)S(1)} %broadcast_select_fusion.mix_ref, s32[4]{0:T(128)S(1)} %pad_add_fusion.first_ref.place_ref, bf16[64,4096]{1,0:T(8,128)(2,1)S(1)} %fusion.8.refs_0_, bf16[64,4096]{1,0:T(8,128)(2,1)S(1)} %copy-done.5, bf16[64,4096]{1,0:T(8,128)(2,1)} %collective-permute-done.11.refs_2_, ...), custom_call_target="tpu_custom_call" | custom-call | flops 536870912 | bytes 4194304 | tf_op jit(solution)/shard_map/first_product/pallas_call | solution.py:175
  78.0 19.9 %all_to_all.5 = bf16[32,16,512]{2,1,0:T(8,128)(2,1)S(1)} all-to-all(bf16[32,16,512]{2,1,0:T(8,128)(2,1)S(1)} %bitcast.42), channel_id=1, replica_groups=mesh['hi'=2,'core'=2,'y'=4,'z'=8,'lo'=2] {'y','z'}, dimensions={0} | all-to-all | bytes 1048576 | tf_op jit(solution)/shard_map/all_to_all | solution.py:367
  98.1 3.7 %collective-permute-start.21 = (bf16[2,2,16,4096]{3,2,1,0:T(8,128)(2,1)S(1)}, bf16[2,2,16,4096]{3,2,1,0:T(8,128)(2,1)S(1)}, u32[]{:S(2)}, u32[]{:S(2)}) collective-permute-start(bf16[2,2,16,4096]{3,2,1,0:T(8,128)(2,1)S(1)} %bitcast.38), channel_id=1, source_target_pairs={{0,129},{1,0},{128,1},{129,128},{2,131},{3,2},{130,3},{131,130},{4... | collective-permute-start | bytes 1572872 | tf_op jit(solution)/shard_map/ppermute | solution.py:74
  101.9 7.1 %collective-permute-done.20.refs_2_.refs_6_ = bf16[2,2,16,4096]{3,2,1,0:T(8,128)(2,1)S(1)} collective-permute-done((bf16[2,2,16,4096]{3,2,1,0:T(8,128)(2,1)S(1)}, bf16[2,2,16,4096]{3,2,1,0:T(8,128)(2,1)S(1)}, u32[]{:S(2)}, u32[]{:S(2)}) %collective-permute-start.20) | collective-permute-done | bytes 524320 | tf_op jit(solution)/shard_map/ppermute | solution.py:74
  109.6 1.4 %collective-permute-start.22 = (bf16[1,2,16,4096]{3,2,1,0:T(8,128)(2,1)S(1)}, bf16[1,2,16,4096]{3,2,1,0:T(8,128)(2,1)S(1)}, u32[]{:S(2)}, u32[]{:S(2)}) collective-permute-start(bf16[1,2,16,4096]{3,2,1,0:T(8,128)(2,1)S(1)} %slice.30), channel_id=1, source_target_pairs={{0,1},{1,128},{128,129},{129,0},{2,3},{3,130},{130,131},{131,2},{4... | collective-permute-start | bytes 786440 | tf_op jit(solution)/shard_map/ppermute | solution.py:74
  111.0 1.9 %collective-permute-start.23 = (bf16[1,2,16,4096]{3,2,1,0:T(8,128)(2,1)S(1)}, bf16[1,2,16,4096]{3,2,1,0:T(8,128)(2,1)S(1)}, u32[]{:S(2)}, u32[]{:S(2)}) collective-permute-start(bf16[1,2,16,4096]{3,2,1,0:T(8,128)(2,1)S(1)} %slice.31), channel_id=1, source_target_pairs={{0,129},{1,0},{128,1},{129,128},{2,131},{3,2},{130,3},{131,130},{4... | collective-permute-start | bytes 786440 | tf_op jit(solution)/shard_map/ppermute | solution.py:74
  112.9 1.6 %sent_rows.2 = bf16[192,512]{1,0:T(8,128)(2,1)S(1)} custom-call(s32[4]{0:T(128)S(1)} %pad_add_fusion.first_ref.place_ref, bf16[2,2,16,4096]{3,2,1,0:T(8,128)(2,1)S(1)} %bitcast.40, bf16[2,2,16,4096]{3,2,1,0:T(8,128)(2,1)S(1)} %collective-permute-done.19.refs_1_, bf16[2,2,16,4096]{3,2,1,0:T(8,128)(2,1)S(1)} %collective-permute-done.20.refs_2_.refs_6_, ...), custom_call_target="tpu_custom_call" | custom-call | flops 805306368 | bytes 6291456 | tf_op jit(solution)/shard_map/sent_rows/pallas_call | solution.py:221
  114.5 5.0 %collective-permute-done.22.refs_2_.refs_0_ = bf16[1,2,16,4096]{3,2,1,0:T(8,128)(2,1)S(1)} collective-permute-done((bf16[1,2,16,4096]{3,2,1,0:T(8,128)(2,1)S(1)}, bf16[1,2,16,4096]{3,2,1,0:T(8,128)(2,1)S(1)}, u32[]{:S(2)}, u32[]{:S(2)}) %collective-permute-start.22) | collective-permute-done | bytes 262176 | tf_op jit(solution)/shard_map/ppermute | solution.py:74
  120.0 1.6 %collective-permute-start.28 = (bf16[192,512]{1,0:T(8,128)(2,1)S(1)}, bf16[192,512]{1,0:T(8,128)(2,1)S(1)}, u32[]{:S(2)}, u32[]{:S(2)}) collective-permute-start(bf16[192,512]{1,0:T(8,128)(2,1)S(1)} %sent_rows.2), channel_id=1, source_target_pairs={{0,1},{1,0},{2,3},{3,2},{4,5},{5,4},{6,7},{7,6},{8,9},{9,8},{10,11... | collective-permute-start | bytes 589832 | tf_op jit(solution)/shard_map/ppermute | solution.py:74
  121.7 1.4 %sent_rows.3 = bf16[64,512]{1,0:T(8,128)(2,1)S(1)} custom-call(s32[4]{0:T(128)S(1)} %pad_add_fusion.first_ref.place_ref, bf16[1,2,16,4096]{3,2,1,0:T(8,128)(2,1)S(1)} %collective-permute-done.22.refs_2_.refs_0_, bf16[1,2,16,4096]{3,2,1,0:T(8,128)(2,1)S(1)} %collective-permute-done.23.refs_3_.refs_1_, ...), custom_call_target="tpu_custom_call" | custom-call | flops 268435456 | bytes 6291456 | tf_op jit(solution)/shard_map/sent_rows/pallas_call | solution.py:221
  124.4 2.9 %kept_rows.1.kept_ref = f32[4,64,1024]{2,1,0:T(8,128)S(1)} custom-call(s32[4]{0:T(128)S(1)} %pad_add_fusion.first_ref.place_ref, s32[8]{0:T(128)S(1)} %get-tuple-element.84.slice_ref, bf16[2,2,16,4096]{3,2,1,0:T(8,128)(2,1)S(1)} %bitcast.41, bf16[2,2,16,4096]{3,2,1,0:T(8,128)(2,1)S(1)} %collective-permute-done.19.refs_1_, ...), custom_call_target="tpu_custom_call" | custom-call | flops 1073741824 | bytes 6291456 | tf_op jit(solution)/shard_map/kept_rows/pallas_call | solution.py:263
  128.3 2.2 %whitened_gradient.1 = f32[64,4,1024]{2,1,0:T(4,128)} custom-call(s32[4]{0:T(128)S(1)} %pad_add_fusion.first_ref.place_ref, s32[8]{0:T(128)S(1)} %pad_add_fusion.1.slice_ref, f32[4,64,1024]{2,1,0:T(8,128)S(1)} %kept_rows.1.kept_ref, bf16[192,512]{1,0:T(8,128)(2,1)S(1)} %collective-permute-done.28.early_ref, ...), custom_call_target="tpu_custom_call" | custom-call | tf_op jit(solution)/shard_map/whitened_gradient/pallas_call | solution.py:300
  (82 shorter events, 10.7 us)
Async XLA Ops:
  1.8 5.9 %collective-permute-start = (bf16[64,512]{1,0:T(8,128)(2,1)S(1)}, bf16[64,512]{1,0:T(8,128)(2,1)S(1)}, u32[]{:S(2)}, u32[]{:S(2)}) collective-permute-start(bf16[64,512]{1,0:T(8,128)(2,1)S(1)} %get-tuple-element.45), channel_id=1, source_target_pairs={{0,1},{1,0},{2,3},{3,2},{4,5},{5,4},{6,7},{7,6},{8,9},{9,8},{10,11... | collective-permute-start | bytes 196616 | tf_op jit(solution)/shard_map/ppermute | solution.py:74
  7.7 9.6 %collective-permute-start.1 = (bf16[128,512]{1,0:T(8,128)(2,1)S(1)}, bf16[128,512]{1,0:T(8,128)(2,1)S(1)}, u32[]{:S(2)}, u32[]{:S(2)}) collective-permute-start(bf16[128,512]{1,0:T(8,128)(2,1)S(1)} %maximum_select_fusion), channel_id=1, source_target_pairs={{0,16},{16,32},{32,48},{48,0},{1,17},{17,33},{33,49},{49,1},{2,18}... | collective-permute-start | bytes 393224 | tf_op jit(solution)/shard_map/ppermute | solution.py:74
  9.3 7.9 %collective-permute-start.2 = (bf16[128,512]{1,0:T(8,128)(2,1)S(1)}, bf16[128,512]{1,0:T(8,128)(2,1)S(1)}, u32[]{:S(2)}, u32[]{:S(2)}) collective-permute-start(bf16[128,512]{1,0:T(8,128)(2,1)S(1)} %maximum_select_fusion), channel_id=1, source_target_pairs={{0,48},{16,0},{32,16},{48,32},{1,49},{17,1},{33,17},{49,33},{2,50}... | collective-permute-start | bytes 393224 | tf_op jit(solution)/shard_map/ppermute | solution.py:74
  11.0 7.0 %collective-permute-start.3 = (bf16[128,512]{1,0:T(8,128)(2,1)S(1)}, bf16[128,512]{1,0:T(8,128)(2,1)S(1)}, u32[]{:S(2)}, u32[]{:S(2)}) collective-permute-start(bf16[128,512]{1,0:T(8,128)(2,1)S(1)} %maximum_select_fusion), channel_id=1, source_target_pairs={{0,32},{16,48},{32,0},{48,16},{1,33},{17,49},{33,1},{49,17},{2,34}... | collective-permute-start | bytes 393224 | tf_op jit(solution)/shard_map/ppermute | solution.py:74
  14.0 14.4 %collective-permute-start.6 = (bf16[64,4096]{1,0:T(8,128)(2,1)S(1)}, bf16[64,4096]{1,0:T(8,128)(2,1)S(1)}, u32[]{:S(2)}, u32[]{:S(2)}) collective-permute-start(bf16[64,4096]{1,0:T(8,128)(2,1)S(1)} %fusion.8.refs_0_), channel_id=1, source_target_pairs={{0,1},{1,128},{128,129},{129,0},{2,3},{3,130},{130,131},{131,2},{4... | collective-permute-start | bytes 1572872 | tf_op jit(solution)/shard_map/ppermute | solution.py:74
  14.6 23.8 %collective-permute-start.7 = (bf16[64,4096]{1,0:T(8,128)(2,1)S(1)}, bf16[64,4096]{1,0:T(8,128)(2,1)S(1)}, u32[]{:S(2)}, u32[]{:S(2)}) collective-permute-start(bf16[64,4096]{1,0:T(8,128)(2,1)S(1)} %fusion.8.refs_0_), channel_id=1, source_target_pairs={{0,129},{1,0},{128,1},{129,128},{2,131},{3,2},{130,3},{131,130},{4... | collective-permute-start | bytes 1572872 | tf_op jit(solution)/shard_map/ppermute | solution.py:74
  18.1 20.3 %collective-permute-start.4 = (bf16[4,128,512]{2,1,0:T(8,128)(2,1)S(1)}, bf16[4,128,512]{2,1,0:T(8,128)(2,1)S(1)}, u32[]{:S(2)}, u32[]{:S(2)}) collective-permute-start(bf16[4,128,512]{2,1,0:T(8,128)(2,1)S(1)} %pad_maximum_fusion.refs_8_.refs_6_.refs_10_.refs_4_), channel_id=1, source_target_pairs={{0,2},{2,4},{4,6},{6,8},{8,10},{10,12},{12,14},{14,0},{1,3},{3,5},... | collective-permute-start | bytes 1572872 | tf_op jit(solution)/shard_map/ppermute | solution.py:74
  20.1 18.3 %collective-permute-start.5 = (bf16[4,128,512]{2,1,0:T(8,128)(2,1)S(1)}, bf16[4,128,512]{2,1,0:T(8,128)(2,1)S(1)}, u32[]{:S(2)}, u32[]{:S(2)}) collective-permute-start(bf16[4,128,512]{2,1,0:T(8,128)(2,1)S(1)} %pad_maximum_fusion.refs_8_.refs_6_.refs_10_.refs_4_), channel_id=1, source_target_pairs={{0,14},{2,0},{4,2},{6,4},{8,6},{10,8},{12,10},{14,12},{1,15},{3,1}... | collective-permute-start | bytes 1572872 | tf_op jit(solution)/shard_map/ppermute | solution.py:74
  20.2 1.9 %collective-permute-start.10 = (bf16[64,4096]{1,0:T(8,128)(2,1)S(1)}, bf16[64,4096]{1,0:T(8,128)(2,1)S(1)}, u32[]{:S(2)}, u32[]{:S(2)}) collective-permute-start(bf16[64,4096]{1,0:T(8,128)(2,1)S(1)} %fusion.8.refs_0_), channel_id=1, source_target_pairs={{0,64},{64,0},{1,65},{65,1},{2,66},{66,2},{3,67},{67,3},{4,68},{68... | collective-permute-start | bytes 1572872 | tf_op jit(solution)/shard_map/ppermute | solution.py:74
  22.9 18.9 %collective-permute-start.11 = (bf16[64,4096]{1,0:T(8,128)(2,1)S(1)}, bf16[64,4096]{1,0:T(8,128)(2,1)}, u32[]{:S(2)}, u32[]{:S(2)}) collective-permute-start(bf16[64,4096]{1,0:T(8,128)(2,1)S(1)} %fusion.8.refs_0_), channel_id=1, source_target_pairs={{0,128},{1,129},{128,0},{129,1},{2,130},{3,131},{130,2},{131,3},{4... | collective-permute-start | bytes 1572872 | tf_op jit(solution)/shard_map/ppermute | solution.py:74
  38.4 10.2 %collective-permute-start.8 = (bf16[4,128,512]{2,1,0:T(8,128)(2,1)S(1)}, bf16[4,128,512]{2,1,0:T(8,128)(2,1)S(1)}, u32[]{:S(2)}, u32[]{:S(2)}) collective-permute-start(bf16[4,128,512]{2,1,0:T(8,128)(2,1)S(1)} %collective-permute-done.4.refs_9_.refs_7_.refs_11_.refs_5_), channel_id=1, source_target_pairs={{0,2},{2,4},{4,6},{6,8},{8,10},{10,12},{12,14},{14,0},{1,3},{3,5},... | collective-permute-start | bytes 1572872 | tf_op jit(solution)/shard_map/ppermute | solution.py:74
  40.4 11.0 %collective-permute-start.9 = (bf16[4,128,512]{2,1,0:T(8,128)(2,1)S(1)}, bf16[4,128,512]{2,1,0:T(8,128)(2,1)S(1)}, u32[]{:S(2)}, u32[]{:S(2)}) collective-permute-start(bf16[4,128,512]{2,1,0:T(8,128)(2,1)S(1)} %collective-permute-done.5.refs_10_.refs_8_.refs_12_.refs_6_), channel_id=1, source_target_pairs={{0,14},{2,0},{4,2},{6,4},{8,6},{10,8},{12,10},{14,12},{1,15},{3,1}... | collective-permute-start | bytes 1572872 | tf_op jit(solution)/shard_map/ppermute | solution.py:74
  41.2 13.2 %collective-permute-start.15 = (bf16[64,4096]{1,0:T(8,128)(2,1)}, bf16[64,4096]{1,0:T(8,128)(2,1)S(1)}, u32[]{:S(2)}, u32[]{:S(2)}) collective-permute-start(bf16[64,4096]{1,0:T(8,128)(2,1)} %copy-done), channel_id=1, source_target_pairs={{0,64},{64,0},{1,65},{65,1},{2,66},{66,2},{3,67},{67,3},{4,68},{68... | collective-permute-start | bytes 1572872 | tf_op jit(solution)/shard_map/ppermute | solution.py:74
  41.2 13.2 %collective-permute-start.16 = (bf16[64,4096]{1,0:T(8,128)(2,1)}, bf16[64,4096]{1,0:T(8,128)(2,1)S(1)}, u32[]{:S(2)}, u32[]{:S(2)}) collective-permute-start(bf16[64,4096]{1,0:T(8,128)(2,1)} %copy-done.2), channel_id=1, source_target_pairs={{0,64},{64,0},{1,65},{65,1},{2,66},{66,2},{3,67},{67,3},{4,68},{68... | collective-permute-start | bytes 1572872 | tf_op jit(solution)/shard_map/ppermute | solution.py:74
  51.4 18.3 %copy-start.1 = (bf16[64,4096]{1,0:T(8,128)(2,1)S(1)}, bf16[64,4096]{1,0:T(8,128)(2,1)}, u32[]{:S(2)}) copy-start(bf16[64,4096]{1,0:T(8,128)(2,1)} %copy-done) | copy-start | bytes 1572868
  51.4 18.3 %copy-start.3 = (bf16[64,4096]{1,0:T(8,128)(2,1)S(1)}, bf16[64,4096]{1,0:T(8,128)(2,1)}, u32[]{:S(2)}) copy-start(bf16[64,4096]{1,0:T(8,128)(2,1)} %copy-done.2) | copy-start | bytes 1572868
  51.4 10.4 %collective-permute-start.12 = (bf16[4,128,512]{2,1,0:T(8,128)(2,1)S(1)}, bf16[4,128,512]{2,1,0:T(8,128)(2,1)S(1)}, u32[]{:S(2)}, u32[]{:S(2)}) collective-permute-start(bf16[4,128,512]{2,1,0:T(8,128)(2,1)S(1)} %collective-permute-done.8.refs_11_.refs_9_.refs_13_.refs_7_), channel_id=1, source_target_pairs={{0,2},{2,4},{4,6},{6,8},{8,10},{10,12},{12,14},{14,0},{1,3},{3,5},... | collective-permute-start | bytes 1572872 | tf_op jit(solution)/shard_map/ppermute | solution.py:74
  54.4 12.7 %collective-permute-start.13 = (bf16[4,128,512]{2,1,0:T(8,128)(2,1)S(1)}, bf16[4,128,512]{2,1,0:T(8,128)(2,1)S(1)}, u32[]{:S(2)}, u32[]{:S(2)}) collective-permute-start(bf16[4,128,512]{2,1,0:T(8,128)(2,1)S(1)} %collective-permute-done.9.refs_12_.refs_10_.refs_14_.refs_8_), channel_id=1, source_target_pairs={{0,14},{2,0},{4,2},{6,4},{8,6},{10,8},{12,10},{14,12},{1,15},{3,1}... | collective-permute-start | bytes 1572872 | tf_op jit(solution)/shard_map/ppermute | solution.py:74
  54.4 12.7 %collective-permute-start.14 = (bf16[64,4096]{1,0:T(8,128)(2,1)}, bf16[64,4096]{1,0:T(8,128)(2,1)S(1)}, u32[]{:S(2)}, u32[]{:S(2)}) collective-permute-start(bf16[64,4096]{1,0:T(8,128)(2,1)} %collective-permute-done.11.refs_2_), channel_id=1, source_target_pairs={{0,64},{64,0},{1,65},{65,1},{2,66},{66,2},{3,67},{67,3},{4,68},{68... | collective-permute-start | bytes 1572872 | tf_op jit(solution)/shard_map/ppermute | solution.py:74
  67.2 6.7 %collective-permute-start.17 = (bf16[2,128,512]{2,1,0:T(8,128)(2,1)S(1)}, bf16[2,128,512]{2,1,0:T(8,128)(2,1)S(1)}, u32[]{:S(2)}, u32[]{:S(2)}) collective-permute-start(bf16[2,128,512]{2,1,0:T(8,128)(2,1)S(1)} %slice.24), channel_id=1, source_target_pairs={{0,2},{2,4},{4,6},{6,8},{8,10},{10,12},{12,14},{14,0},{1,3},{3,5},... | collective-permute-start | bytes 786440 | tf_op jit(solution)/shard_map/ppermute | solution.py:74
  69.6 6.4 %collective-permute-start.18 = (bf16[2,128,512]{2,1,0:T(8,128)(2,1)S(1)}, bf16[2,128,512]{2,1,0:T(8,128)(2,1)S(1)}, u32[]{:S(2)}, u32[]{:S(2)}) collective-permute-start(bf16[2,128,512]{2,1,0:T(8,128)(2,1)S(1)} %slice.25), channel_id=1, source_target_pairs={{0,14},{2,0},{4,2},{6,4},{8,6},{10,8},{12,10},{14,12},{1,15},{3,1}... | collective-permute-start | bytes 786440 | tf_op jit(solution)/shard_map/ppermute | solution.py:74
  98.0 10.9 %collective-permute-start.20 = (bf16[2,2,16,4096]{3,2,1,0:T(8,128)(2,1)S(1)}, bf16[2,2,16,4096]{3,2,1,0:T(8,128)(2,1)S(1)}, u32[]{:S(2)}, u32[]{:S(2)}) collective-permute-start(bf16[2,2,16,4096]{3,2,1,0:T(8,128)(2,1)S(1)} %bitcast.37), channel_id=1, source_target_pairs={{0,1},{1,128},{128,129},{129,0},{2,3},{3,130},{130,131},{131,2},{4... | collective-permute-start | bytes 1572872 | tf_op jit(solution)/shard_map/ppermute | solution.py:74
  98.1 10.8 %collective-permute-start.21 = (bf16[2,2,16,4096]{3,2,1,0:T(8,128)(2,1)S(1)}, bf16[2,2,16,4096]{3,2,1,0:T(8,128)(2,1)S(1)}, u32[]{:S(2)}, u32[]{:S(2)}) collective-permute-start(bf16[2,2,16,4096]{3,2,1,0:T(8,128)(2,1)S(1)} %bitcast.38), channel_id=1, source_target_pairs={{0,129},{1,0},{128,1},{129,128},{2,131},{3,2},{130,3},{131,130},{4... | collective-permute-start | bytes 1572872 | tf_op jit(solution)/shard_map/ppermute | solution.py:74
  101.9 7.1 %collective-permute-start.19 = (bf16[2,2,16,4096]{3,2,1,0:T(8,128)(2,1)S(1)}, bf16[2,2,16,4096]{3,2,1,0:T(8,128)(2,1)S(1)}, u32[]{:S(2)}, u32[]{:S(2)}) collective-permute-start(bf16[2,2,16,4096]{3,2,1,0:T(8,128)(2,1)S(1)} %bitcast.39), channel_id=1, source_target_pairs={{0,64},{64,0},{1,65},{65,1},{2,66},{66,2},{3,67},{67,3},{4,68},{68... | collective-permute-start | bytes 1572872 | tf_op jit(solution)/shard_map/ppermute | solution.py:74
  109.0 3.9 %collective-permute-start.24 = (bf16[2,2,16,4096]{3,2,1,0:T(8,128)(2,1)S(1)}, bf16[2,2,16,4096]{3,2,1,0:T(8,128)(2,1)S(1)}, u32[]{:S(2)}, u32[]{:S(2)}) collective-permute-start(bf16[2,2,16,4096]{3,2,1,0:T(8,128)(2,1)S(1)} %collective-permute-done.20.refs_2_.refs_6_), channel_id=1, source_target_pairs={{0,64},{64,0},{1,65},{65,1},{2,66},{66,2},{3,67},{67,3},{4,68},{68... | collective-permute-start | bytes 1572872 | tf_op jit(solution)/shard_map/ppermute | solution.py:74
  109.1 3.8 %collective-permute-start.25 = (bf16[2,2,16,4096]{3,2,1,0:T(8,128)(2,1)S(1)}, bf16[2,2,16,4096]{3,2,1,0:T(8,128)(2,1)S(1)}, u32[]{:S(2)}, u32[]{:S(2)}) collective-permute-start(bf16[2,2,16,4096]{3,2,1,0:T(8,128)(2,1)S(1)} %collective-permute-done.21.refs_4_.refs_8_), channel_id=1, source_target_pairs={{0,64},{64,0},{1,65},{65,1},{2,66},{66,2},{3,67},{67,3},{4,68},{68... | collective-permute-start | bytes 1572872 | tf_op jit(solution)/shard_map/ppermute | solution.py:74
  109.6 9.9 %collective-permute-start.22 = (bf16[1,2,16,4096]{3,2,1,0:T(8,128)(2,1)S(1)}, bf16[1,2,16,4096]{3,2,1,0:T(8,128)(2,1)S(1)}, u32[]{:S(2)}, u32[]{:S(2)}) collective-permute-start(bf16[1,2,16,4096]{3,2,1,0:T(8,128)(2,1)S(1)} %slice.30), channel_id=1, source_target_pairs={{0,1},{1,128},{128,129},{129,0},{2,3},{3,130},{130,131},{131,2},{4... | collective-permute-start | bytes 786440 | tf_op jit(solution)/shard_map/ppermute | solution.py:74
  111.0 8.5 %collective-permute-start.23 = (bf16[1,2,16,4096]{3,2,1,0:T(8,128)(2,1)S(1)}, bf16[1,2,16,4096]{3,2,1,0:T(8,128)(2,1)S(1)}, u32[]{:S(2)}, u32[]{:S(2)}) collective-permute-start(bf16[1,2,16,4096]{3,2,1,0:T(8,128)(2,1)S(1)} %slice.31), channel_id=1, source_target_pairs={{0,129},{1,0},{128,1},{129,128},{2,131},{3,2},{130,3},{131,130},{4... | collective-permute-start | bytes 786440 | tf_op jit(solution)/shard_map/ppermute | solution.py:74
  119.5 2.2 %collective-permute-start.26 = (bf16[1,2,16,4096]{3,2,1,0:T(8,128)(2,1)S(1)}, bf16[1,2,16,4096]{3,2,1,0:T(8,128)(2,1)S(1)}, u32[]{:S(2)}, u32[]{:S(2)}) collective-permute-start(bf16[1,2,16,4096]{3,2,1,0:T(8,128)(2,1)S(1)} %collective-permute-done.22.refs_2_.refs_0_), channel_id=1, source_target_pairs={{0,64},{64,0},{1,65},{65,1},{2,66},{66,2},{3,67},{67,3},{4,68},{68... | collective-permute-start | bytes 786440 | tf_op jit(solution)/shard_map/ppermute | solution.py:74
  119.5 2.2 %collective-permute-start.27 = (bf16[1,2,16,4096]{3,2,1,0:T(8,128)(2,1)S(1)}, bf16[1,2,16,4096]{3,2,1,0:T(8,128)(2,1)S(1)}, u32[]{:S(2)}, u32[]{:S(2)}) collective-permute-start(bf16[1,2,16,4096]{3,2,1,0:T(8,128)(2,1)S(1)} %collective-permute-done.23.refs_3_.refs_1_), channel_id=1, source_target_pairs={{0,64},{64,0},{1,65},{65,1},{2,66},{66,2},{3,67},{67,3},{4,68},{68... | collective-permute-start | bytes 786440 | tf_op jit(solution)/shard_map/ppermute | solution.py:74
  120.0 7.5 %collective-permute-start.28 = (bf16[192,512]{1,0:T(8,128)(2,1)S(1)}, bf16[192,512]{1,0:T(8,128)(2,1)S(1)}, u32[]{:S(2)}, u32[]{:S(2)}) collective-permute-start(bf16[192,512]{1,0:T(8,128)(2,1)S(1)} %sent_rows.2), channel_id=1, source_target_pairs={{0,1},{1,0},{2,3},{3,2},{4,5},{5,4},{6,7},{7,6},{8,9},{9,8},{10,11... | collective-permute-start | bytes 589832 | tf_op jit(solution)/shard_map/ppermute | solution.py:74
  123.1 5.2 %collective-permute-start.29 = (bf16[64,512]{1,0:T(8,128)(2,1)S(1)}, bf16[64,512]{1,0:T(8,128)(2,1)S(1)}, u32[]{:S(2)}, u32[]{:S(2)}) collective-permute-start(bf16[64,512]{1,0:T(8,128)(2,1)S(1)} %sent_rows.3), channel_id=1, source_target_pairs={{0,1},{1,0},{2,3},{3,2},{4,5},{5,4},{6,7},{7,6},{8,9},{9,8},{10,11... | collective-permute-start | bytes 196616 | tf_op jit(solution)/shard_map/ppermute | solution.py:74
  (7 other events, 23.4 us)

commit v10 on v8

--- a/solution.py
+++ b/solution.py
@@ -118,8 +118,19 @@
         acc_ref[...] += jnp.dot(field, basis, preferred_element_type=jnp.float32)
 
 
-NEAR = tuple(tuple((dz, dy) for dy in (0, 3, 1, 2)) for dz in (0, 7, 1, 6, 2, 5, 3))
-FAR = (((4, 0), (4, 3)), ((4, 1), (4, 2)))
+NEAR = (
+    *((((dz, 0), (dz, 1))) for dz in (0, 7, 1, 6, 2, 5, 3)),
+    tuple((dz, 2) for dz in (0, 7, 1, 6, 2)),
+    tuple((dz, 3) for dz in (0, 7, 1, 6, 2)),
+)
+FAR = (
+    ((5, 2), (3, 2)),
+    ((5, 3), (3, 3)),
+    ((4, 0),),
+    ((4, 1),),
+    ((4, 2),),
+    ((4, 3),),
+)
 
 
 def near_kernel(place_ref, *refs):
@@ -323,8 +334,8 @@
     mine = jnp.where(lo == 0, jnp.concatenate([kept, other]), jnp.concatenate([other, kept]))
     pseudo = moments(event_counts, latent_mean, latent_var).astype(jnp.bfloat16)[0]
     mine, pseudo = lax.optimization_barrier((mine, pseudo))
-    far, before, after = [shifted(pseudo, RING, step) for step in (2, 1, 3)]
-    block = jnp.stack([mine] + [shifted(mine, "y", step) for step in (1, 3, 2)])
+    block = jnp.stack([mine, shifted(mine, "y", 3)])
+    block, pseudo = lax.optimization_barrier((block, pseudo))
     own = with_core(pseudo)
 
     flips = jnp.array([0, 1, 2, 3], jnp.int32)
@@ -340,20 +351,28 @@
     sy = lax.dynamic_slice_in_dim(root.reshape(4, lax.axis_size(ROW), -1), row, 1, 1).reshape(-1, 1)
     sy = jnp.broadcast_to(sy, (sy.shape[0], 128))
 
-    right, left = shifted(block, "z", 1), shifted(block, "z", nz - 1)
-    pieces = [block, right, left]
-    right, left, before, after = lax.optimization_barrier((right, left, before, after))
-    before, after = with_core(before), with_core(after)
-    right, left = shifted(right, "z", 1), shifted(left, "z", nz - 1)
-    pieces += [right, left]
-    right, left, far, own, mix, sx, sy = lax.optimization_barrier(
-        (right, left, far, own, mix, sx, sy)
-    )
-    far = with_core(far)
-    right, left = shifted(right, "z", 1), shifted(left, "z", nz - 1)
-    pieces += [right, left]
-    right, left, far, before, after = lax.optimization_barrier((right, left, far, before, after))
-    last = [shifted(right[:2], "z", 1), shifted(left[2:], "z", nz - 1)]
+    def from_neighbours(blocks):
+        second = jnp.concatenate([b[-1:] for b in blocks])
+        first = jnp.concatenate([b[:1] for b in blocks])
+        return [shifted(second, "y", 3), shifted(first, "y", 1)]
+
+    def step(right, left):
+        return shifted(right, "z", 1), shifted(left, "z", nz - 1)
+
+    one = step(block, block)
+    one, own = lax.optimization_barrier((one, own))
+    two = step(*one)
+    before, after = shifted(own[0], RING, 1), shifted(own[0], RING, 3)
+    two, own, mix, sx, sy = lax.optimization_barrier((two, own, mix, sx, sy))
+    three = step(*two)
+    far = shifted(own[0], RING, 2)
+    beside_two = from_neighbours([block, *one, *two])
+    three, before, after = lax.optimization_barrier((three, before, after))
+    before, after, far = with_core(before), with_core(after), with_core(far)
+    ends = step(three[0][:1], three[1][1:])
+    pieces = [block, *one, *two, *three, *beside_two]
+    last = [*from_neighbours(three), *ends]
+    last += [shifted(ends[1], "y", 3), shifted(ends[0], "y", 1)]
 
     fields = (*own, *far, *before, *after)
     near = near_product(place, fields, pieces)

time: 136 us -> 138 us (1.015)
  waiting for transfers between devices: 59.6 us -> 47.9 us
  blocking collectives: 19.9 us -> 27.8 us
  starting transfers between devices: 34.7 us -> 40.3 us
    ppermute x30 -> x34, waiting for transfers between devices: 59.6 us -> 47.9 us  [shifted(): lax.ppermute(array, axis, [(k, (k + step) % size) for k in range(size)])]
    all_to_all x1, blocking collectives: 19.9 us -> 27.8 us  [local(): got = lax.all_to_all(sent, ('y', 'z'), 0, 0, tiled=True)]
    ppermute x30 -> x34, starting transfers between devices: 34.7 us -> 40.3 us  [shifted(): lax.ppermute(array, axis, [(k, (k + step) % size) for k in range(size)])]
  transfers between devices with their start and end apart: 30 -> 34, of which waited for: 17 -> 17; matrix products, arithmetic and copies ran while one was open for 4% -> 4% of each run, Pallas kernels for 7% -> 6%
where the time goes in v10:
time: 138 us
  waiting for transfers between devices  47.9 us (35%)
  starting transfers between devices  40.3 us (29%)
  blocking collectives  27.8 us (20%)
  Pallas kernels  13.7 us (10%)
  other arithmetic  4.67 us (3%)
  local copies, waits for them, and re-layouts  2.29 us (2%)
    ppermute x34, waiting for transfers between devices, shifted(): lax.ppermute(array, axis, [(k, (k + step) % size) for k in range(size)])  47.9 us
    ppermute x34, starting transfers between devices, shifted(): lax.ppermute(array, axis, [(k, (k + step) % size) for k in range(size)])  40.3 us
    all_to_all x1, blocking collectives, local(): got = lax.all_to_all(sent, ('y', 'z'), 0, 0, tiled=True)  27.8 us
    squeeze x1, other arithmetic, local(): moments(event_counts, latent_mean, latent_var).astype(jnp.bfloat16)[0]  4.3 us
    pallas_call x1, Pallas kernels, kept_rows(): pl.pallas_call(kept_kernel, out_shape=jax.ShapeDtypeStruct((times, rows,...  3.1 us
    pallas_call x2, Pallas kernels, sent_rows(): pl.pallas_call(sent_kernel, out_shape=jax.ShapeDtypeStruct((count, width)...  3.09 us
  transfers between devices with their start and end apart: 34, of which 17 were waited for; matrix products, arithmetic and copies ran while one was open for 4% of the time, Pallas kernels for 6%

profile of v10, /device:TPU:32, one launch (start us, length us, event | category | flops | bytes accessed | tf_op | source)
XLA Modules:
  0.0 137.6 jit_solution(14952979982078149661)
XLA Ops:
  1.8 1.6 %collective-permute-start = (bf16[64,512]{1,0:T(8,128)(2,1)S(1)}, bf16[64,512]{1,0:T(8,128)(2,1)S(1)}, u32[]{:S(2)}, u32[]{:S(2)}) collective-permute-start(bf16[64,512]{1,0:T(8,128)(2,1)S(1)} %get-tuple-element.38), channel_id=1, source_target_pairs={{0,1},{1,0},{2,3},{3,2},{4,5},{5,4},{6,7},{7,6},{8,9},{9,8},{10,11... | collective-permute-start | bytes 196616 | tf_op jit(solution)/shard_map/ppermute | solution.py:74
  4.1 4.3 %fusion.8.refs_0_ = bf16[64,4096]{1,0:T(8,128)(2,1)S(1)} fusion(s32[1,64,4096]{2,1,0:T(8,128)} %param.8, f32[1,64,4096]{2,1,0:T(8,128)} %param.10, f32[1,64,4096]{2,1,0:T(8,128)} %param.9), kind=kLoop, calls=%fused_computation.15 | loop fusion | flops 17563648 | bytes 3670016 | tf_op jit(solution)/shard_map/squeeze | solution.py:335
  8.6 3.1 %collective-permute-start.1 = (bf16[128,512]{1,0:T(8,128)(2,1)S(1)}, bf16[128,512]{1,0:T(8,128)(2,1)S(1)}, u32[]{:S(2)}, u32[]{:S(2)}) collective-permute-start(bf16[128,512]{1,0:T(8,128)(2,1)S(1)} %maximum_select_fusion), channel_id=1, source_target_pairs={{0,48},{16,0},{32,16},{48,32},{1,49},{17,1},{33,17},{49,33},{2,50}... | collective-permute-start | bytes 393224 | tf_op jit(solution)/shard_map/ppermute | solution.py:74
  11.7 2.5 %collective-permute-done.1 = bf16[128,512]{1,0:T(8,128)(2,1)S(1)} collective-permute-done((bf16[128,512]{1,0:T(8,128)(2,1)S(1)}, bf16[128,512]{1,0:T(8,128)(2,1)S(1)}, u32[]{:S(2)}, u32[]{:S(2)}) %collective-permute-start.1) | collective-permute-done | bytes 131104 | tf_op jit(solution)/shard_map/ppermute | solution.py:74
  15.0 2.0 %collective-permute-start.2 = (bf16[2,128,512]{2,1,0:T(8,128)(2,1)S(1)}, bf16[2,128,512]{2,1,0:T(8,128)(2,1)S(1)}, u32[]{:S(2)}, u32[]{:S(2)}) collective-permute-start(bf16[2,128,512]{2,1,0:T(8,128)(2,1)S(1)} %pad_maximum_fusion.refs_8_.refs_6_.refs_10_.refs_4_), channel_id=1, source_target_pairs={{0,2},{2,4},{4,6},{6,8},{8,10},{10,12},{12,14},{14,0},{1,3},{3,5},... | collective-permute-start | bytes 786440 | tf_op jit(solution)/shard_map/ppermute | solution.py:74
  17.4 6.3 %collective-permute-done.2.refs_9_.refs_7_.refs_11_.refs_5_ = bf16[2,128,512]{2,1,0:T(8,128)(2,1)S(1)} collective-permute-done((bf16[2,128,512]{2,1,0:T(8,128)(2,1)S(1)}, bf16[2,128,512]{2,1,0:T(8,128)(2,1)S(1)}, u32[]{:S(2)}, u32[]{:S(2)}) %collective-permute-start.2) | collective-permute-done | bytes 262176 | tf_op jit(solution)/shard_map/ppermute | solution.py:74
  23.7 1.8 %collective-permute-done.3.refs_10_.refs_8_.refs_12_.refs_6_ = bf16[2,128,512]{2,1,0:T(8,128)(2,1)S(1)} collective-permute-done((bf16[2,128,512]{2,1,0:T(8,128)(2,1)S(1)}, bf16[2,128,512]{2,1,0:T(8,128)(2,1)S(1)}, u32[]{:S(2)}, u32[]{:S(2)}) %collective-permute-start.3) | collective-permute-done | bytes 262176 | tf_op jit(solution)/shard_map/ppermute | solution.py:74
  26.1 2.7 %collective-permute-start.12 = (bf16[64,4096]{1,0:T(8,128)(2,1)S(1)}, bf16[64,4096]{1,0:T(8,128)(2,1)S(1)}, u32[]{:S(2)}, u32[]{:S(2)}) collective-permute-start(bf16[64,4096]{1,0:T(8,128)(2,1)S(1)} %fusion.8.refs_0_), channel_id=1, source_target_pairs={{0,129},{1,0},{128,1},{129,128},{2,131},{3,2},{130,3},{131,130},{4... | collective-permute-start | bytes 1572872 | tf_op jit(solution)/shard_map/ppermute | solution.py:74
  28.8 3.1 %collective-permute-start.5 = (bf16[2,128,512]{2,1,0:T(8,128)(2,1)S(1)}, bf16[2,128,512]{2,1,0:T(8,128)(2,1)S(1)}, u32[]{:S(2)}, u32[]{:S(2)}) collective-permute-start(bf16[2,128,512]{2,1,0:T(8,128)(2,1)S(1)} %collective-permute-done.2.refs_9_.refs_7_.refs_11_.refs_5_), channel_id=1, source_target_pairs={{0,2},{2,4},{4,6},{6,8},{8,10},{10,12},{12,14},{14,0},{1,3},{3,5},... | collective-permute-start | bytes 786440 | tf_op jit(solution)/shard_map/ppermute | solution.py:74
  32.0 5.0 %collective-permute-done.5.refs_11_.refs_9_.refs_13_.refs_7_ = bf16[2,128,512]{2,1,0:T(8,128)(2,1)S(1)} collective-permute-done((bf16[2,128,512]{2,1,0:T(8,128)(2,1)S(1)}, bf16[2,128,512]{2,1,0:T(8,128)(2,1)S(1)}, u32[]{:S(2)}, u32[]{:S(2)}) %collective-permute-start.5) | collective-permute-done | bytes 262176 | tf_op jit(solution)/shard_map/ppermute | solution.py:74
  37.0 2.9 %collective-permute-done.6.refs_12_.refs_10_.refs_14_.refs_8_ = bf16[2,128,512]{2,1,0:T(8,128)(2,1)S(1)} collective-permute-done((bf16[2,128,512]{2,1,0:T(8,128)(2,1)S(1)}, bf16[2,128,512]{2,1,0:T(8,128)(2,1)S(1)}, u32[]{:S(2)}, u32[]{:S(2)}) %collective-permute-start.6) | collective-permute-done | bytes 262176 | tf_op jit(solution)/shard_map/ppermute | solution.py:74
  40.1 1.9 %collective-permute-start.9 = (bf16[2,128,512]{2,1,0:T(8,128)(2,1)S(1)}, bf16[2,128,512]{2,1,0:T(8,128)(2,1)S(1)}, u32[]{:S(2)}, u32[]{:S(2)}) collective-permute-start(bf16[2,128,512]{2,1,0:T(8,128)(2,1)S(1)} %collective-permute-done.5.refs_11_.refs_9_.refs_13_.refs_7_), channel_id=1, source_target_pairs={{0,2},{2,4},{4,6},{6,8},{8,10},{10,12},{12,14},{14,0},{1,3},{3,5},... | collective-permute-start | bytes 786440 | tf_op jit(solution)/shard_map/ppermute | solution.py:74
  42.0 3.7 %collective-permute-start.21 = (bf16[5,128,512]{2,1,0:T(8,128)(2,1)S(1)}, bf16[5,128,512]{2,1,0:T(8,128)(2,1)S(1)}, u32[]{:S(2)}, u32[]{:S(2)}) collective-permute-start(bf16[5,128,512]{2,1,0:T(8,128)(2,1)S(1)} %get-tuple-element.72), channel_id=1, source_target_pairs={{0,48},{16,0},{32,16},{48,32},{1,49},{17,1},{33,17},{49,33},{2,50}... | collective-permute-start | bytes 1966088 | tf_op jit(solution)/shard_map/ppermute | solution.py:74
  47.4 1.5 %collective-permute-start.7 = (bf16[64,4096]{1,0:T(8,128)(2,1)S(1)}, bf16[64,4096]{1,0:T(8,128)(2,1)S(1)}, u32[]{:S(2)}, u32[]{:S(2)}) collective-permute-start(bf16[64,4096]{1,0:T(8,128)(2,1)S(1)} %fusion.8.refs_0_), channel_id=1, source_target_pairs={{0,128},{1,129},{128,0},{129,1},{2,130},{3,131},{130,2},{131,3},{4... | collective-permute-start | bytes 1572872 | tf_op jit(solution)/shard_map/ppermute | solution.py:74
  48.9 3.3 %collective-permute-start.18 = (bf16[1,128,512]{2,1,0:T(8,128)(2,1)S(1)}, bf16[1,128,512]{2,1,0:T(8,128)(2,1)S(1)}, u32[]{:S(2)}, u32[]{:S(2)}) collective-permute-start(bf16[1,128,512]{2,1,0:T(8,128)(2,1)S(1)} %get-tuple-element.84), channel_id=1, source_target_pairs={{0,14},{2,0},{4,2},{6,4},{8,6},{10,8},{12,10},{14,12},{1,15},{3,1}... | collective-permute-start | bytes 393224 | tf_op jit(solution)/shard_map/ppermute | solution.py:74
  52.3 2.4 %collective-permute-done.18.refs_11_.refs_18_.refs_22_.refs_16_ = bf16[1,128,512]{2,1,0:T(8,128)(2,1)S(1)} collective-permute-done((bf16[1,128,512]{2,1,0:T(8,128)(2,1)S(1)}, bf16[1,128,512]{2,1,0:T(8,128)(2,1)S(1)}, u32[]{:S(2)}, u32[]{:S(2)}) %collective-permute-start.18) | collective-permute-done | bytes 131104 | tf_op jit(solution)/shard_map/ppermute | solution.py:74
  54.8 2.5 %collective-permute-done.17.refs_10_.refs_17_.refs_21_.refs_15_ = bf16[1,128,512]{2,1,0:T(8,128)(2,1)S(1)} collective-permute-done((bf16[1,128,512]{2,1,0:T(8,128)(2,1)S(1)}, bf16[1,128,512]{2,1,0:T(8,128)(2,1)S(1)}, u32[]{:S(2)}, u32[]{:S(2)}) %collective-permute-start.17) | collective-permute-done | bytes 131104 | tf_op jit(solution)/shard_map/ppermute | solution.py:74
  57.3 2.7 %collective-permute-done.7.refs_2_ = bf16[64,4096]{1,0:T(8,128)(2,1)S(1)} collective-permute-done((bf16[64,4096]{1,0:T(8,128)(2,1)S(1)}, bf16[64,4096]{1,0:T(8,128)(2,1)S(1)}, u32[]{:S(2)}, u32[]{:S(2)}) %collective-permute-start.7) | collective-permute-done | bytes 524320 | tf_op jit(solution)/shard_map/ppermute | solution.py:74
  61.6 2.3 %collective-permute-start.15 = (bf16[2,128,512]{2,1,0:T(8,128)(2,1)S(1)}, bf16[2,128,512]{2,1,0:T(8,128)(2,1)S(1)}, u32[]{:S(2)}, u32[]{:S(2)}) collective-permute-start(bf16[2,128,512]{2,1,0:T(8,128)(2,1)S(1)} %pad_maximum_fusion.1), channel_id=1, source_target_pairs={{0,48},{16,0},{32,16},{48,32},{1,49},{17,1},{33,17},{49,33},{2,50}... | collective-permute-start | bytes 786440 | tf_op jit(solution)/shard_map/ppermute | solution.py:74
  63.9 1.9 %collective-permute-start.19 = (bf16[1,128,512]{2,1,0:T(8,128)(2,1)S(1)}, bf16[1,128,512]{2,1,0:T(8,128)(2,1)S(1)}, u32[]{:S(2)}, u32[]{:S(2)}) collective-permute-start(bf16[1,128,512]{2,1,0:T(8,128)(2,1)S(1)} %collective-permute-done.18.refs_11_.refs_18_.refs_22_.refs_16_), channel_id=1, source_target_pairs={{0,48},{16,0},{32,16},{48,32},{1,49},{17,1},{33,17},{49,33},{2,50}... | collective-permute-start | bytes 393224 | tf_op jit(solution)/shard_map/ppermute | solution.py:74
  65.9 2.5 %near_product.1.refs_14_ = f32[512,512]{1,0:T(8,128)S(1)} custom-call(s32[4]{0:T(128)S(1)} %pad_add_fusion.first_ref.place_ref, bf16[64,4096]{1,0:T(8,128)(2,1)S(1)} %fusion.8.refs_0_, bf16[64,4096]{1,0:T(8,128)(2,1)S(1)} %collective-permute-done.4.refs_1_, bf16[64,4096]{1,0:T(8,128)(2,1)S(1)} %collective-permute-done.7.refs_2_, ...), custom_call_target="tpu_custom_call" | custom-call | flops 1610612736 | bytes 8388608 | tf_op jit(solution)/shard_map/near_product/pallas_call | solution.py:148
  68.4 4.5 %collective-permute-done.19.refs_12_.refs_19_.refs_23_.refs_17_ = bf16[1,128,512]{2,1,0:T(8,128)(2,1)S(1)} collective-permute-done((bf16[1,128,512]{2,1,0:T(8,128)(2,1)S(1)}, bf16[1,128,512]{2,1,0:T(8,128)(2,1)S(1)}, u32[]{:S(2)}, u32[]{:S(2)}) %collective-permute-start.19) | collective-permute-done | bytes 131104 | tf_op jit(solution)/shard_map/ppermute | solution.py:74
  73.6 2.1 %first_product.1 = bf16[512,512]{1,0:T(8,128)(2,1)S(1)} custom-call(f32[8,4]{1,0:T(8,128)S(1)} %broadcast_select_fusion.mix_ref, s32[4]{0:T(128)S(1)} %pad_add_fusion.first_ref.place_ref, bf16[64,4096]{1,0:T(8,128)(2,1)S(1)} %fusion.8.refs_0_, bf16[64,4096]{1,0:T(8,128)(2,1)S(1)} %collective-permute-done.4.refs_1_, ...), custom_call_target="tpu_custom_call" | custom-call | flops 536870912 | bytes 4194304 | tf_op jit(solution)/shard_map/first_product/pallas_call | solution.py:186
  75.7 27.8 %all_to_all.5 = bf16[32,16,512]{2,1,0:T(8,128)(2,1)S(1)} all-to-all(bf16[32,16,512]{2,1,0:T(8,128)(2,1)S(1)} %bitcast.40), channel_id=1, replica_groups=mesh['hi'=2,'core'=2,'y'=4,'z'=8,'lo'=2] {'y','z'}, dimensions={0} | all-to-all | bytes 1048576 | tf_op jit(solution)/shard_map/all_to_all | solution.py:384
  103.7 3.2 %collective-permute-start.25 = (bf16[2,2,16,4096]{3,2,1,0:T(8,128)(2,1)S(1)}, bf16[2,2,16,4096]{3,2,1,0:T(8,128)(2,1)S(1)}, u32[]{:S(2)}, u32[]{:S(2)}) collective-permute-start(bf16[2,2,16,4096]{3,2,1,0:T(8,128)(2,1)S(1)} %bitcast.36), channel_id=1, source_target_pairs={{0,129},{1,0},{128,1},{129,128},{2,131},{3,2},{130,3},{131,130},{4... | collective-permute-start | bytes 1572872 | tf_op jit(solution)/shard_map/ppermute | solution.py:74
  106.9 9.2 %collective-permute-done.24.refs_2_.refs_6_ = bf16[2,2,16,4096]{3,2,1,0:T(8,128)(2,1)S(1)} collective-permute-done((bf16[2,2,16,4096]{3,2,1,0:T(8,128)(2,1)S(1)}, bf16[2,2,16,4096]{3,2,1,0:T(8,128)(2,1)S(1)}, u32[]{:S(2)}, u32[]{:S(2)}) %collective-permute-start.24) | collective-permute-done | bytes 524320 | tf_op jit(solution)/shard_map/ppermute | solution.py:74
  116.8 3.2 %collective-permute-start.27 = (bf16[1,2,16,4096]{3,2,1,0:T(8,128)(2,1)S(1)}, bf16[1,2,16,4096]{3,2,1,0:T(8,128)(2,1)S(1)}, u32[]{:S(2)}, u32[]{:S(2)}) collective-permute-start(bf16[1,2,16,4096]{3,2,1,0:T(8,128)(2,1)S(1)} %slice.81), channel_id=1, source_target_pairs={{0,129},{1,0},{128,1},{129,128},{2,131},{3,2},{130,3},{131,130},{4... | collective-permute-start | bytes 786440 | tf_op jit(solution)/shard_map/ppermute | solution.py:74
  120.1 1.7 %sent_rows.2 = bf16[192,512]{1,0:T(8,128)(2,1)S(1)} custom-call(s32[4]{0:T(128)S(1)} %pad_add_fusion.first_ref.place_ref, bf16[2,2,16,4096]{3,2,1,0:T(8,128)(2,1)S(1)} %bitcast.38, bf16[2,2,16,4096]{3,2,1,0:T(8,128)(2,1)S(1)} %collective-permute-done.23.refs_1_, bf16[2,2,16,4096]{3,2,1,0:T(8,128)(2,1)S(1)} %collective-permute-done.24.refs_2_.refs_6_, ...), custom_call_target="tpu_custom_call" | custom-call | flops 805306368 | bytes 6291456 | tf_op jit(solution)/shard_map/sent_rows/pallas_call | solution.py:232
  121.8 4.8 %collective-permute-done.26.refs_2_.refs_0_ = bf16[1,2,16,4096]{3,2,1,0:T(8,128)(2,1)S(1)} collective-permute-done((bf16[1,2,16,4096]{3,2,1,0:T(8,128)(2,1)S(1)}, bf16[1,2,16,4096]{3,2,1,0:T(8,128)(2,1)S(1)}, u32[]{:S(2)}, u32[]{:S(2)}) %collective-permute-start.26) | collective-permute-done | bytes 262176 | tf_op jit(solution)/shard_map/ppermute | solution.py:74
  128.5 1.4 %sent_rows.3 = bf16[64,512]{1,0:T(8,128)(2,1)S(1)} custom-call(s32[4]{0:T(128)S(1)} %pad_add_fusion.first_ref.place_ref, bf16[1,2,16,4096]{3,2,1,0:T(8,128)(2,1)S(1)} %collective-permute-done.26.refs_2_.refs_0_, bf16[1,2,16,4096]{3,2,1,0:T(8,128)(2,1)S(1)} %collective-permute-done.27.refs_3_.refs_1_, ...), custom_call_target="tpu_custom_call" | custom-call | flops 268435456 | bytes 6291456 | tf_op jit(solution)/shard_map/sent_rows/pallas_call | solution.py:232
  131.1 3.1 %kept_rows.1.kept_ref = f32[4,64,1024]{2,1,0:T(8,128)S(1)} custom-call(s32[4]{0:T(128)S(1)} %pad_add_fusion.first_ref.place_ref, s32[8]{0:T(128)S(1)} %get-tuple-element.70.slice_ref, bf16[2,2,16,4096]{3,2,1,0:T(8,128)(2,1)S(1)} %bitcast.39, bf16[2,2,16,4096]{3,2,1,0:T(8,128)(2,1)S(1)} %collective-permute-done.23.refs_1_, ...), custom_call_target="tpu_custom_call" | custom-call | flops 1073741824 | bytes 6291456 | tf_op jit(solution)/shard_map/kept_rows/pallas_call | solution.py:274
  135.4 2.2 %whitened_gradient.1 = f32[64,4,1024]{2,1,0:T(4,128)} custom-call(s32[4]{0:T(128)S(1)} %pad_add_fusion.first_ref.place_ref, s32[8]{0:T(128)S(1)} %pad_add_fusion.1.slice_ref, f32[4,64,1024]{2,1,0:T(8,128)S(1)} %kept_rows.1.kept_ref, bf16[192,512]{1,0:T(8,128)(2,1)S(1)} %collective-permute-done.32.early_ref, ...), custom_call_target="tpu_custom_call" | custom-call | tf_op jit(solution)/shard_map/whitened_gradient/pallas_call | solution.py:311
  (85 shorter events, 13.1 us)
Async XLA Ops:
  1.8 6.8 %collective-permute-start = (bf16[64,512]{1,0:T(8,128)(2,1)S(1)}, bf16[64,512]{1,0:T(8,128)(2,1)S(1)}, u32[]{:S(2)}, u32[]{:S(2)}) collective-permute-start(bf16[64,512]{1,0:T(8,128)(2,1)S(1)} %get-tuple-element.38), channel_id=1, source_target_pairs={{0,1},{1,0},{2,3},{3,2},{4,5},{5,4},{6,7},{7,6},{8,9},{9,8},{10,11... | collective-permute-start | bytes 196616 | tf_op jit(solution)/shard_map/ppermute | solution.py:74
  8.6 5.6 %collective-permute-start.1 = (bf16[128,512]{1,0:T(8,128)(2,1)S(1)}, bf16[128,512]{1,0:T(8,128)(2,1)S(1)}, u32[]{:S(2)}, u32[]{:S(2)}) collective-permute-start(bf16[128,512]{1,0:T(8,128)(2,1)S(1)} %maximum_select_fusion), channel_id=1, source_target_pairs={{0,48},{16,0},{32,16},{48,32},{1,49},{17,1},{33,17},{49,33},{2,50}... | collective-permute-start | bytes 393224 | tf_op jit(solution)/shard_map/ppermute | solution.py:74
  14.3 11.3 %collective-permute-start.4 = (bf16[64,4096]{1,0:T(8,128)(2,1)S(1)}, bf16[64,4096]{1,0:T(8,128)(2,1)S(1)}, u32[]{:S(2)}, u32[]{:S(2)}) collective-permute-start(bf16[64,4096]{1,0:T(8,128)(2,1)S(1)} %fusion.8.refs_0_), channel_id=1, source_target_pairs={{0,64},{64,0},{1,65},{65,1},{2,66},{66,2},{3,67},{67,3},{4,68},{68... | collective-permute-start | bytes 1572872 | tf_op jit(solution)/shard_map/ppermute | solution.py:74
  15.0 8.8 %collective-permute-start.2 = (bf16[2,128,512]{2,1,0:T(8,128)(2,1)S(1)}, bf16[2,128,512]{2,1,0:T(8,128)(2,1)S(1)}, u32[]{:S(2)}, u32[]{:S(2)}) collective-permute-start(bf16[2,128,512]{2,1,0:T(8,128)(2,1)S(1)} %pad_maximum_fusion.refs_8_.refs_6_.refs_10_.refs_4_), channel_id=1, source_target_pairs={{0,2},{2,4},{4,6},{6,8},{8,10},{10,12},{12,14},{14,0},{1,3},{3,5},... | collective-permute-start | bytes 786440 | tf_op jit(solution)/shard_map/ppermute | solution.py:74
  17.0 8.6 %collective-permute-start.3 = (bf16[2,128,512]{2,1,0:T(8,128)(2,1)S(1)}, bf16[2,128,512]{2,1,0:T(8,128)(2,1)S(1)}, u32[]{:S(2)}, u32[]{:S(2)}) collective-permute-start(bf16[2,128,512]{2,1,0:T(8,128)(2,1)S(1)} %pad_maximum_fusion.refs_8_.refs_6_.refs_10_.refs_4_), channel_id=1, source_target_pairs={{0,14},{2,0},{4,2},{6,4},{8,6},{10,8},{12,10},{14,12},{1,15},{3,1}... | collective-permute-start | bytes 786440 | tf_op jit(solution)/shard_map/ppermute | solution.py:74
  25.6 23.3 %collective-permute-start.11 = (bf16[64,4096]{1,0:T(8,128)(2,1)S(1)}, bf16[64,4096]{1,0:T(8,128)(2,1)S(1)}, u32[]{:S(2)}, u32[]{:S(2)}) collective-permute-start(bf16[64,4096]{1,0:T(8,128)(2,1)S(1)} %fusion.8.refs_0_), channel_id=1, source_target_pairs={{0,1},{1,128},{128,129},{129,0},{2,3},{3,130},{130,131},{131,2},{4... | collective-permute-start | bytes 1572872 | tf_op jit(solution)/shard_map/ppermute | solution.py:74
  26.1 22.8 %collective-permute-start.12 = (bf16[64,4096]{1,0:T(8,128)(2,1)S(1)}, bf16[64,4096]{1,0:T(8,128)(2,1)S(1)}, u32[]{:S(2)}, u32[]{:S(2)}) collective-permute-start(bf16[64,4096]{1,0:T(8,128)(2,1)S(1)} %fusion.8.refs_0_), channel_id=1, source_target_pairs={{0,129},{1,0},{128,1},{129,128},{2,131},{3,2},{130,3},{131,130},{4... | collective-permute-start | bytes 1572872 | tf_op jit(solution)/shard_map/ppermute | solution.py:74
  28.8 8.2 %collective-permute-start.5 = (bf16[2,128,512]{2,1,0:T(8,128)(2,1)S(1)}, bf16[2,128,512]{2,1,0:T(8,128)(2,1)S(1)}, u32[]{:S(2)}, u32[]{:S(2)}) collective-permute-start(bf16[2,128,512]{2,1,0:T(8,128)(2,1)S(1)} %collective-permute-done.2.refs_9_.refs_7_.refs_11_.refs_5_), channel_id=1, source_target_pairs={{0,2},{2,4},{4,6},{6,8},{8,10},{10,12},{12,14},{14,0},{1,3},{3,5},... | collective-permute-start | bytes 786440 | tf_op jit(solution)/shard_map/ppermute | solution.py:74
  31.9 8.0 %collective-permute-start.6 = (bf16[2,128,512]{2,1,0:T(8,128)(2,1)S(1)}, bf16[2,128,512]{2,1,0:T(8,128)(2,1)S(1)}, u32[]{:S(2)}, u32[]{:S(2)}) collective-permute-start(bf16[2,128,512]{2,1,0:T(8,128)(2,1)S(1)} %collective-permute-done.3.refs_10_.refs_8_.refs_12_.refs_6_), channel_id=1, source_target_pairs={{0,14},{2,0},{4,2},{6,4},{8,6},{10,8},{12,10},{14,12},{1,15},{3,1}... | collective-permute-start | bytes 786440 | tf_op jit(solution)/shard_map/ppermute | solution.py:74
  40.0 6.4 %collective-permute-start.10 = (bf16[2,128,512]{2,1,0:T(8,128)(2,1)S(1)}, bf16[2,128,512]{2,1,0:T(8,128)(2,1)S(1)}, u32[]{:S(2)}, u32[]{:S(2)}) collective-permute-start(bf16[2,128,512]{2,1,0:T(8,128)(2,1)S(1)} %collective-permute-done.6.refs_12_.refs_10_.refs_14_.refs_8_), channel_id=1, source_target_pairs={{0,14},{2,0},{4,2},{6,4},{8,6},{10,8},{12,10},{14,12},{1,15},{3,1}... | collective-permute-start | bytes 786440 | tf_op jit(solution)/shard_map/ppermute | solution.py:74
  40.1 7.3 %collective-permute-start.9 = (bf16[2,128,512]{2,1,0:T(8,128)(2,1)S(1)}, bf16[2,128,512]{2,1,0:T(8,128)(2,1)S(1)}, u32[]{:S(2)}, u32[]{:S(2)}) collective-permute-start(bf16[2,128,512]{2,1,0:T(8,128)(2,1)S(1)} %collective-permute-done.5.refs_11_.refs_9_.refs_13_.refs_7_), channel_id=1, source_target_pairs={{0,2},{2,4},{4,6},{6,8},{8,10},{10,12},{12,14},{14,0},{1,3},{3,5},... | collective-permute-start | bytes 786440 | tf_op jit(solution)/shard_map/ppermute | solution.py:74
  42.0 18.0 %collective-permute-start.21 = (bf16[5,128,512]{2,1,0:T(8,128)(2,1)S(1)}, bf16[5,128,512]{2,1,0:T(8,128)(2,1)S(1)}, u32[]{:S(2)}, u32[]{:S(2)}) collective-permute-start(bf16[5,128,512]{2,1,0:T(8,128)(2,1)S(1)} %get-tuple-element.72), channel_id=1, source_target_pairs={{0,48},{16,0},{32,16},{48,32},{1,49},{17,1},{33,17},{49,33},{2,50}... | collective-permute-start | bytes 1966088 | tf_op jit(solution)/shard_map/ppermute | solution.py:74
  46.3 15.3 %collective-permute-start.22 = (bf16[5,128,512]{2,1,0:T(8,128)(2,1)S(1)}, bf16[5,128,512]{2,1,0:T(8,128)(2,1)S(1)}, u32[]{:S(2)}, u32[]{:S(2)}) collective-permute-start(bf16[5,128,512]{2,1,0:T(8,128)(2,1)S(1)} %get-tuple-element.71), channel_id=1, source_target_pairs={{0,16},{16,32},{32,48},{48,0},{1,17},{17,33},{33,49},{49,1},{2,18}... | collective-permute-start | bytes 1966088 | tf_op jit(solution)/shard_map/ppermute | solution.py:74
  47.4 12.6 %collective-permute-start.7 = (bf16[64,4096]{1,0:T(8,128)(2,1)S(1)}, bf16[64,4096]{1,0:T(8,128)(2,1)S(1)}, u32[]{:S(2)}, u32[]{:S(2)}) collective-permute-start(bf16[64,4096]{1,0:T(8,128)(2,1)S(1)} %fusion.8.refs_0_), channel_id=1, source_target_pairs={{0,128},{1,129},{128,0},{129,1},{2,130},{3,131},{130,2},{131,3},{4... | collective-permute-start | bytes 1572872 | tf_op jit(solution)/shard_map/ppermute | solution.py:74
  48.9 5.8 %collective-permute-start.18 = (bf16[1,128,512]{2,1,0:T(8,128)(2,1)S(1)}, bf16[1,128,512]{2,1,0:T(8,128)(2,1)S(1)}, u32[]{:S(2)}, u32[]{:S(2)}) collective-permute-start(bf16[1,128,512]{2,1,0:T(8,128)(2,1)S(1)} %get-tuple-element.84), channel_id=1, source_target_pairs={{0,14},{2,0},{4,2},{6,4},{8,6},{10,8},{12,10},{14,12},{1,15},{3,1}... | collective-permute-start | bytes 393224 | tf_op jit(solution)/shard_map/ppermute | solution.py:74
  52.2 5.0 %collective-permute-start.17 = (bf16[1,128,512]{2,1,0:T(8,128)(2,1)S(1)}, bf16[1,128,512]{2,1,0:T(8,128)(2,1)S(1)}, u32[]{:S(2)}, u32[]{:S(2)}) collective-permute-start(bf16[1,128,512]{2,1,0:T(8,128)(2,1)S(1)} %get-tuple-element.81), channel_id=1, source_target_pairs={{0,2},{2,4},{4,6},{6,8},{8,10},{10,12},{12,14},{14,0},{1,3},{3,5},... | collective-permute-start | bytes 393224 | tf_op jit(solution)/shard_map/ppermute | solution.py:74
  54.8 9.2 %collective-permute-start.13 = (bf16[64,4096]{1,0:T(8,128)(2,1)S(1)}, bf16[64,4096]{1,0:T(8,128)(2,1)S(1)}, u32[]{:S(2)}, u32[]{:S(2)}) collective-permute-start(bf16[64,4096]{1,0:T(8,128)(2,1)S(1)} %collective-permute-done.11.refs_4_), channel_id=1, source_target_pairs={{0,64},{64,0},{1,65},{65,1},{2,66},{66,2},{3,67},{67,3},{4,68},{68... | collective-permute-start | bytes 1572872 | tf_op jit(solution)/shard_map/ppermute | solution.py:74
  57.3 8.5 %collective-permute-start.14 = (bf16[64,4096]{1,0:T(8,128)(2,1)S(1)}, bf16[64,4096]{1,0:T(8,128)(2,1)S(1)}, u32[]{:S(2)}, u32[]{:S(2)}) collective-permute-start(bf16[64,4096]{1,0:T(8,128)(2,1)S(1)} %collective-permute-done.12.refs_6_), channel_id=1, source_target_pairs={{0,64},{64,0},{1,65},{65,1},{2,66},{66,2},{3,67},{67,3},{4,68},{68... | collective-permute-start | bytes 1572872 | tf_op jit(solution)/shard_map/ppermute | solution.py:74
  60.0 6.0 %collective-permute-start.8 = (bf16[64,4096]{1,0:T(8,128)(2,1)S(1)}, bf16[64,4096]{1,0:T(8,128)(2,1)S(1)}, u32[]{:S(2)}, u32[]{:S(2)}) collective-permute-start(bf16[64,4096]{1,0:T(8,128)(2,1)S(1)} %collective-permute-done.7.refs_2_), channel_id=1, source_target_pairs={{0,64},{64,0},{1,65},{65,1},{2,66},{66,2},{3,67},{67,3},{4,68},{68... | collective-permute-start | bytes 1572872 | tf_op jit(solution)/shard_map/ppermute | solution.py:74
  60.1 13.5 %collective-permute-start.16 = (bf16[2,128,512]{2,1,0:T(8,128)(2,1)S(1)}, bf16[2,128,512]{2,1,0:T(8,128)(2,1)S(1)}, u32[]{:S(2)}, u32[]{:S(2)}) collective-permute-start(bf16[2,128,512]{2,1,0:T(8,128)(2,1)S(1)} %pad_maximum_fusion.2), channel_id=1, source_target_pairs={{0,16},{16,32},{32,48},{48,0},{1,17},{17,33},{33,49},{49,1},{2,18}... | collective-permute-start | bytes 786440 | tf_op jit(solution)/shard_map/ppermute | solution.py:74
  61.6 12.0 %collective-permute-start.15 = (bf16[2,128,512]{2,1,0:T(8,128)(2,1)S(1)}, bf16[2,128,512]{2,1,0:T(8,128)(2,1)S(1)}, u32[]{:S(2)}, u32[]{:S(2)}) collective-permute-start(bf16[2,128,512]{2,1,0:T(8,128)(2,1)S(1)} %pad_maximum_fusion.1), channel_id=1, source_target_pairs={{0,48},{16,0},{32,16},{48,32},{1,49},{17,1},{33,17},{49,33},{2,50}... | collective-permute-start | bytes 786440 | tf_op jit(solution)/shard_map/ppermute | solution.py:74
  63.9 9.0 %collective-permute-start.19 = (bf16[1,128,512]{2,1,0:T(8,128)(2,1)S(1)}, bf16[1,128,512]{2,1,0:T(8,128)(2,1)S(1)}, u32[]{:S(2)}, u32[]{:S(2)}) collective-permute-start(bf16[1,128,512]{2,1,0:T(8,128)(2,1)S(1)} %collective-permute-done.18.refs_11_.refs_18_.refs_22_.refs_16_), channel_id=1, source_target_pairs={{0,48},{16,0},{32,16},{48,32},{1,49},{17,1},{33,17},{49,33},{2,50}... | collective-permute-start | bytes 393224 | tf_op jit(solution)/shard_map/ppermute | solution.py:74
  65.8 7.7 %collective-permute-start.20 = (bf16[1,128,512]{2,1,0:T(8,128)(2,1)S(1)}, bf16[1,128,512]{2,1,0:T(8,128)(2,1)S(1)}, u32[]{:S(2)}, u32[]{:S(2)}) collective-permute-start(bf16[1,128,512]{2,1,0:T(8,128)(2,1)S(1)} %collective-permute-done.17.refs_10_.refs_17_.refs_21_.refs_15_), channel_id=1, source_target_pairs={{0,16},{16,32},{32,48},{48,0},{1,17},{17,33},{33,49},{49,1},{2,18}... | collective-permute-start | bytes 393224 | tf_op jit(solution)/shard_map/ppermute | solution.py:74
  103.6 12.6 %collective-permute-start.24 = (bf16[2,2,16,4096]{3,2,1,0:T(8,128)(2,1)S(1)}, bf16[2,2,16,4096]{3,2,1,0:T(8,128)(2,1)S(1)}, u32[]{:S(2)}, u32[]{:S(2)}) collective-permute-start(bf16[2,2,16,4096]{3,2,1,0:T(8,128)(2,1)S(1)} %bitcast.35), channel_id=1, source_target_pairs={{0,1},{1,128},{128,129},{129,0},{2,3},{3,130},{130,131},{131,2},{4... | collective-permute-start | bytes 1572872 | tf_op jit(solution)/shard_map/ppermute | solution.py:74
  103.7 12.5 %collective-permute-start.25 = (bf16[2,2,16,4096]{3,2,1,0:T(8,128)(2,1)S(1)}, bf16[2,2,16,4096]{3,2,1,0:T(8,128)(2,1)S(1)}, u32[]{:S(2)}, u32[]{:S(2)}) collective-permute-start(bf16[2,2,16,4096]{3,2,1,0:T(8,128)(2,1)S(1)} %bitcast.36), channel_id=1, source_target_pairs={{0,129},{1,0},{128,1},{129,128},{2,131},{3,2},{130,3},{131,130},{4... | collective-permute-start | bytes 1572872 | tf_op jit(solution)/shard_map/ppermute | solution.py:74
  106.9 9.3 %collective-permute-start.23 = (bf16[2,2,16,4096]{3,2,1,0:T(8,128)(2,1)S(1)}, bf16[2,2,16,4096]{3,2,1,0:T(8,128)(2,1)S(1)}, u32[]{:S(2)}, u32[]{:S(2)}) collective-permute-start(bf16[2,2,16,4096]{3,2,1,0:T(8,128)(2,1)S(1)} %bitcast.37), channel_id=1, source_target_pairs={{0,64},{64,0},{1,65},{65,1},{2,66},{66,2},{3,67},{67,3},{4,68},{68... | collective-permute-start | bytes 1572872 | tf_op jit(solution)/shard_map/ppermute | solution.py:74
  116.2 3.8 %collective-permute-start.28 = (bf16[2,2,16,4096]{3,2,1,0:T(8,128)(2,1)S(1)}, bf16[2,2,16,4096]{3,2,1,0:T(8,128)(2,1)S(1)}, u32[]{:S(2)}, u32[]{:S(2)}) collective-permute-start(bf16[2,2,16,4096]{3,2,1,0:T(8,128)(2,1)S(1)} %collective-permute-done.24.refs_2_.refs_6_), channel_id=1, source_target_pairs={{0,64},{64,0},{1,65},{65,1},{2,66},{66,2},{3,67},{67,3},{4,68},{68... | collective-permute-start | bytes 1572872 | tf_op jit(solution)/shard_map/ppermute | solution.py:74
  116.3 3.7 %collective-permute-start.29 = (bf16[2,2,16,4096]{3,2,1,0:T(8,128)(2,1)S(1)}, bf16[2,2,16,4096]{3,2,1,0:T(8,128)(2,1)S(1)}, u32[]{:S(2)}, u32[]{:S(2)}) collective-permute-start(bf16[2,2,16,4096]{3,2,1,0:T(8,128)(2,1)S(1)} %collective-permute-done.25.refs_4_.refs_8_), channel_id=1, source_target_pairs={{0,64},{64,0},{1,65},{65,1},{2,66},{66,2},{3,67},{67,3},{4,68},{68... | collective-permute-start | bytes 1572872 | tf_op jit(solution)/shard_map/ppermute | solution.py:74
  116.8 9.7 %collective-permute-start.26 = (bf16[1,2,16,4096]{3,2,1,0:T(8,128)(2,1)S(1)}, bf16[1,2,16,4096]{3,2,1,0:T(8,128)(2,1)S(1)}, u32[]{:S(2)}, u32[]{:S(2)}) collective-permute-start(bf16[1,2,16,4096]{3,2,1,0:T(8,128)(2,1)S(1)} %slice.80), channel_id=1, source_target_pairs={{0,1},{1,128},{128,129},{129,0},{2,3},{3,130},{130,131},{131,2},{4... | collective-permute-start | bytes 786440 | tf_op jit(solution)/shard_map/ppermute | solution.py:74
  116.8 9.7 %collective-permute-start.27 = (bf16[1,2,16,4096]{3,2,1,0:T(8,128)(2,1)S(1)}, bf16[1,2,16,4096]{3,2,1,0:T(8,128)(2,1)S(1)}, u32[]{:S(2)}, u32[]{:S(2)}) collective-permute-start(bf16[1,2,16,4096]{3,2,1,0:T(8,128)(2,1)S(1)} %slice.81), channel_id=1, source_target_pairs={{0,129},{1,0},{128,1},{129,128},{2,131},{3,2},{130,3},{131,130},{4... | collective-permute-start | bytes 786440 | tf_op jit(solution)/shard_map/ppermute | solution.py:74
  127.1 7.5 %collective-permute-start.32 = (bf16[192,512]{1,0:T(8,128)(2,1)S(1)}, bf16[192,512]{1,0:T(8,128)(2,1)S(1)}, u32[]{:S(2)}, u32[]{:S(2)}) collective-permute-start(bf16[192,512]{1,0:T(8,128)(2,1)S(1)} %sent_rows.2), channel_id=1, source_target_pairs={{0,1},{1,0},{2,3},{3,2},{4,5},{5,4},{6,7},{7,6},{8,9},{9,8},{10,11... | collective-permute-start | bytes 589832 | tf_op jit(solution)/shard_map/ppermute | solution.py:74
  129.9 5.5 %collective-permute-start.33 = (bf16[64,512]{1,0:T(8,128)(2,1)S(1)}, bf16[64,512]{1,0:T(8,128)(2,1)S(1)}, u32[]{:S(2)}, u32[]{:S(2)}) collective-permute-start(bf16[64,512]{1,0:T(8,128)(2,1)S(1)} %sent_rows.3), channel_id=1, source_target_pairs={{0,1},{1,0},{2,3},{3,2},{4,5},{5,4},{6,7},{7,6},{8,9},{9,8},{10,11... | collective-permute-start | bytes 196616 | tf_op jit(solution)/shard_map/ppermute | solution.py:74
  (5 other events, 9.5 us)

commit v11 on v9

--- a/solution.py
+++ b/solution.py
@@ -326,8 +326,7 @@
     before, after = shifted(pseudo, RING, 1), shifted(pseudo, RING, 3)
     block = jnp.stack([mine] + [shifted(mine, "y", step) for step in (1, 3, 2)])
     block, pseudo = lax.optimization_barrier((block, pseudo))
-    own = lax.optimization_barrier(with_core(pseudo))
-    far = shifted(own[0], RING, 2)
+    own = with_core(pseudo)
 
     flips = jnp.array([0, 1, 2, 3], jnp.int32)
     before_flip, after_flip = 2 * (1 - lo), 2 * lo
@@ -342,20 +341,22 @@
     sy = lax.dynamic_slice_in_dim(root.reshape(4, lax.axis_size(ROW), -1), row, 1, 1).reshape(-1, 1)
     sy = jnp.broadcast_to(sy, (sy.shape[0], 128))
 
-    right, left = shifted(block, "z", 1), shifted(block, "z", nz - 1)
-    pieces = [block, right, left]
-    right, left, before, after = lax.optimization_barrier((right, left, before, after))
+    def step(right, left):
+        return shifted(right, "z", 1), shifted(left, "z", nz - 1)
+
+    one = step(block, block)
+    one, own = lax.optimization_barrier((one, own))
+    two = step(*one)
+    far = shifted(own[0], RING, 2)
+    two, own, before, after, mix, sx, sy = lax.optimization_barrier(
+        (two, own, before, after, mix, sx, sy)
+    )
+    three = step(*two)
     before, after = with_core(before), with_core(after)
-    right, left = shifted(right, "z", 1), shifted(left, "z", nz - 1)
-    pieces += [right, left]
-    right, left, far, own, mix, sx, sy = lax.optimization_barrier(
-        (right, left, far, own, mix, sx, sy)
-    )
+    three, far, before, after = lax.optimization_barrier((three, far, before, after))
+    last = step(three[0][:2], three[1][2:])
     far = with_core(far)
-    right, left = shifted(right, "z", 1), shifted(left, "z", nz - 1)
-    pieces += [right, left]
-    right, left, far, before, after = lax.optimization_barrier((right, left, far, before, after))
-    last = [shifted(right[:2], "z", 1), shifted(left[2:], "z", nz - 1)]
+    pieces = [block, *one, *two, *three]
 
     fields = (*own, *far, *before, *after)
     near = near_product(place, fields, pieces)

time: 131 us -> 136 us (1.038)
  blocking collectives: 19.9 us -> 26.3 us
  starting transfers between devices: 34.2 us -> 32.6 us
    all_to_all x1, blocking collectives: 19.9 us -> 26.3 us  [local(): got = lax.all_to_all(sent, ('y', 'z'), 0, 0, tiled=True)]
    ppermute x30, starting transfers between devices: 34.2 us -> 32.6 us  [shifted(): lax.ppermute(array, axis, [(k, (k + step) % size) for k in range(size)])]
    unnamed x18 -> x10, local copies, waits for them, and re-layouts: 2.76 us -> 1.71 us
  transfers between devices with their start and end apart: 30 -> 30, of which waited for: 13 -> 14; matrix products, arithmetic and copies ran while one was open for 4% -> 4% of each run, Pallas kernels for 7% -> 7%
where the time goes in v11:
time: 136 us; the launch traced here: 135 us
  waiting for transfers between devices  53.7 us (39%)
  starting transfers between devices  32.6 us (24%)
  blocking collectives  26.3 us (19%)
  Pallas kernels  14.3 us (11%)
  other arithmetic  4.66 us (3%)
  local copies, waits for them, and re-layouts  2.99 us (2%)
    ppermute x30, waiting for transfers between devices, shifted(): lax.ppermute(array, axis, [(k, (k + step) % size) for k in range(size)])  53.7 us
    ppermute x30, starting transfers between devices, shifted(): lax.ppermute(array, axis, [(k, (k + step) % size) for k in range(size)])  32.6 us
    all_to_all x1, blocking collectives, local(): got = lax.all_to_all(sent, ('y', 'z'), 0, 0, tiled=True)  26.3 us
    squeeze x1, other arithmetic, local(): moments(event_counts, latent_mean, latent_var).astype(jnp.bfloat16)[0]  4.29 us
    pallas_call x1, Pallas kernels, near_product(): pl.pallas_call(near_kernel, out_shape=jax.ShapeDtypeStruct((rows, width),...  3.3 us
    pallas_call x2, Pallas kernels, sent_rows(): pl.pallas_call(sent_kernel, out_shape=jax.ShapeDtypeStruct((count, width)...  2.96 us
    pallas_call x1, Pallas kernels, kept_rows(): pl.pallas_call(kept_kernel, out_shape=jax.ShapeDtypeStruct((times, rows,...  2.9 us
  transfers between devices with their start and end apart: 30, of which 14 were waited for; matrix products, arithmetic and copies ran while one was open for 4% of the time, Pallas kernels for 7%

profile of v11, /device:TPU:32, one launch (start us, length us, event | category | flops | bytes accessed | tf_op | source)
XLA Modules:
  0.0 135.5 jit_solution(12079852755328513423)
XLA Ops:
  1.8 1.6 %collective-permute-start = (bf16[64,512]{1,0:T(8,128)(2,1)S(1)}, bf16[64,512]{1,0:T(8,128)(2,1)S(1)}, u32[]{:S(2)}, u32[]{:S(2)}) collective-permute-start(bf16[64,512]{1,0:T(8,128)(2,1)S(1)} %get-tuple-element.43), channel_id=1, source_target_pairs={{0,1},{1,0},{2,3},{3,2},{4,5},{5,4},{6,7},{7,6},{8,9},{9,8},{10,11... | collective-permute-start | bytes 196616 | tf_op jit(solution)/shard_map/ppermute | solution.py:74
  3.3 4.3 %fusion.8.refs_0_ = bf16[64,4096]{1,0:T(8,128)(2,1)S(1)} fusion(s32[1,64,4096]{2,1,0:T(8,128)} %param.8, f32[1,64,4096]{2,1,0:T(8,128)} %param.10, f32[1,64,4096]{2,1,0:T(8,128)} %param.9), kind=kLoop, calls=%fused_computation.16 | loop fusion | flops 17563648 | bytes 3670016 | tf_op jit(solution)/shard_map/squeeze | solution.py:324
  7.7 1.7 %collective-permute-start.1 = (bf16[128,512]{1,0:T(8,128)(2,1)S(1)}, bf16[128,512]{1,0:T(8,128)(2,1)S(1)}, u32[]{:S(2)}, u32[]{:S(2)}) collective-permute-start(bf16[128,512]{1,0:T(8,128)(2,1)S(1)} %maximum_select_fusion), channel_id=1, source_target_pairs={{0,16},{16,32},{32,48},{48,0},{1,17},{17,33},{33,49},{49,1},{2,18}... | collective-permute-start | bytes 393224 | tf_op jit(solution)/shard_map/ppermute | solution.py:74
  9.3 1.7 %collective-permute-start.2 = (bf16[128,512]{1,0:T(8,128)(2,1)S(1)}, bf16[128,512]{1,0:T(8,128)(2,1)S(1)}, u32[]{:S(2)}, u32[]{:S(2)}) collective-permute-start(bf16[128,512]{1,0:T(8,128)(2,1)S(1)} %maximum_select_fusion), channel_id=1, source_target_pairs={{0,48},{16,0},{32,16},{48,32},{1,49},{17,1},{33,17},{49,33},{2,50}... | collective-permute-start | bytes 393224 | tf_op jit(solution)/shard_map/ppermute | solution.py:74
  11.0 2.0 %collective-permute-start.3 = (bf16[128,512]{1,0:T(8,128)(2,1)S(1)}, bf16[128,512]{1,0:T(8,128)(2,1)S(1)}, u32[]{:S(2)}, u32[]{:S(2)}) collective-permute-start(bf16[128,512]{1,0:T(8,128)(2,1)S(1)} %maximum_select_fusion), channel_id=1, source_target_pairs={{0,32},{16,48},{32,0},{48,16},{1,33},{17,49},{33,1},{49,17},{2,34}... | collective-permute-start | bytes 393224 | tf_op jit(solution)/shard_map/ppermute | solution.py:74
  14.1 1.3 collective-permute-done.2
  15.4 2.6 %collective-permute-done.3 = bf16[128,512]{1,0:T(8,128)(2,1)S(1)} collective-permute-done((bf16[128,512]{1,0:T(8,128)(2,1)S(1)}, bf16[128,512]{1,0:T(8,128)(2,1)S(1)}, u32[]{:S(2)}, u32[]{:S(2)}) %collective-permute-start.3) | collective-permute-done | bytes 131104 | tf_op jit(solution)/shard_map/ppermute | solution.py:74
  18.1 2.0 %collective-permute-start.4 = (bf16[4,128,512]{2,1,0:T(8,128)(2,1)S(1)}, bf16[4,128,512]{2,1,0:T(8,128)(2,1)S(1)}, u32[]{:S(2)}, u32[]{:S(2)}) collective-permute-start(bf16[4,128,512]{2,1,0:T(8,128)(2,1)S(1)} %pad_maximum_fusion.refs_8_.refs_6_.refs_10_.refs_4_), channel_id=1, source_target_pairs={{0,2},{2,4},{4,6},{6,8},{8,10},{10,12},{12,14},{14,0},{1,3},{3,5},... | collective-permute-start | bytes 1572872 | tf_op jit(solution)/shard_map/ppermute | solution.py:74
  20.2 2.2 %collective-permute-start.10 = (bf16[64,4096]{1,0:T(8,128)(2,1)S(1)}, bf16[64,4096]{1,0:T(8,128)(2,1)}, u32[]{:S(2)}, u32[]{:S(2)}) collective-permute-start(bf16[64,4096]{1,0:T(8,128)(2,1)S(1)} %fusion.8.refs_0_), channel_id=1, source_target_pairs={{0,129},{1,0},{128,1},{129,128},{2,131},{3,2},{130,3},{131,130},{4... | collective-permute-start | bytes 1572872 | tf_op jit(solution)/shard_map/ppermute | solution.py:74
  22.4 8.7 %collective-permute-done.4.refs_9_.refs_7_.refs_11_.refs_5_ = bf16[4,128,512]{2,1,0:T(8,128)(2,1)S(1)} collective-permute-done((bf16[4,128,512]{2,1,0:T(8,128)(2,1)S(1)}, bf16[4,128,512]{2,1,0:T(8,128)(2,1)S(1)}, u32[]{:S(2)}, u32[]{:S(2)}) %collective-permute-start.4) | collective-permute-done | bytes 524320 | tf_op jit(solution)/shard_map/ppermute | solution.py:74
  31.1 1.8 %collective-permute-done.5.refs_10_.refs_8_.refs_12_.refs_6_ = bf16[4,128,512]{2,1,0:T(8,128)(2,1)S(1)} collective-permute-done((bf16[4,128,512]{2,1,0:T(8,128)(2,1)S(1)}, bf16[4,128,512]{2,1,0:T(8,128)(2,1)S(1)}, u32[]{:S(2)}, u32[]{:S(2)}) %collective-permute-start.5) | collective-permute-done | bytes 524320 | tf_op jit(solution)/shard_map/ppermute | solution.py:74
  33.7 3.1 %collective-permute-start.7 = (bf16[4,128,512]{2,1,0:T(8,128)(2,1)S(1)}, bf16[4,128,512]{2,1,0:T(8,128)(2,1)S(1)}, u32[]{:S(2)}, u32[]{:S(2)}) collective-permute-start(bf16[4,128,512]{2,1,0:T(8,128)(2,1)S(1)} %collective-permute-done.4.refs_9_.refs_7_.refs_11_.refs_5_), channel_id=1, source_target_pairs={{0,2},{2,4},{4,6},{6,8},{8,10},{10,12},{12,14},{14,0},{1,3},{3,5},... | collective-permute-start | bytes 1572872 | tf_op jit(solution)/shard_map/ppermute | solution.py:74
  37.6 2.7 %collective-permute-start.13 = (bf16[64,4096]{1,0:T(8,128)(2,1)S(1)}, bf16[64,4096]{1,0:T(8,128)(2,1)S(1)}, u32[]{:S(2)}, u32[]{:S(2)}) collective-permute-start(bf16[64,4096]{1,0:T(8,128)(2,1)S(1)} %fusion.8.refs_0_), channel_id=1, source_target_pairs={{0,128},{1,129},{128,0},{129,1},{2,130},{3,131},{130,2},{131,3},{4... | collective-permute-start | bytes 1572872 | tf_op jit(solution)/shard_map/ppermute | solution.py:74
  40.3 6.4 %collective-permute-done.7.refs_11_.refs_9_.refs_13_.refs_7_ = bf16[4,128,512]{2,1,0:T(8,128)(2,1)S(1)} collective-permute-done((bf16[4,128,512]{2,1,0:T(8,128)(2,1)S(1)}, bf16[4,128,512]{2,1,0:T(8,128)(2,1)S(1)}, u32[]{:S(2)}, u32[]{:S(2)}) %collective-permute-start.7) | collective-permute-done | bytes 524320 | tf_op jit(solution)/shard_map/ppermute | solution.py:74
  46.7 2.8 %collective-permute-done.8.refs_12_.refs_10_.refs_14_.refs_8_ = bf16[4,128,512]{2,1,0:T(8,128)(2,1)S(1)} collective-permute-done((bf16[4,128,512]{2,1,0:T(8,128)(2,1)S(1)}, bf16[4,128,512]{2,1,0:T(8,128)(2,1)S(1)}, u32[]{:S(2)}, u32[]{:S(2)}) %collective-permute-start.8) | collective-permute-done | bytes 524320 | tf_op jit(solution)/shard_map/ppermute | solution.py:74
  49.6 1.8 %collective-permute-start.11 = (bf16[4,128,512]{2,1,0:T(8,128)(2,1)S(1)}, bf16[4,128,512]{2,1,0:T(8,128)(2,1)S(1)}, u32[]{:S(2)}, u32[]{:S(2)}) collective-permute-start(bf16[4,128,512]{2,1,0:T(8,128)(2,1)S(1)} %collective-permute-done.7.refs_11_.refs_9_.refs_13_.refs_7_), channel_id=1, source_target_pairs={{0,2},{2,4},{4,6},{6,8},{8,10},{10,12},{12,14},{14,0},{1,3},{3,5},... | collective-permute-start | bytes 1572872 | tf_op jit(solution)/shard_map/ppermute | solution.py:74
  52.2 8.4 %collective-permute-done.11.refs_13_.refs_11_.refs_15_.refs_9_ = bf16[4,128,512]{2,1,0:T(8,128)(2,1)S(1)} collective-permute-done((bf16[4,128,512]{2,1,0:T(8,128)(2,1)S(1)}, bf16[4,128,512]{2,1,0:T(8,128)(2,1)S(1)}, u32[]{:S(2)}, u32[]{:S(2)}) %collective-permute-start.11) | collective-permute-done | bytes 524320 | tf_op jit(solution)/shard_map/ppermute | solution.py:74
  60.6 1.5 %collective-permute-done.12.refs_14_.refs_12_.refs_16_.refs_10_ = bf16[4,128,512]{2,1,0:T(8,128)(2,1)S(1)} collective-permute-done((bf16[4,128,512]{2,1,0:T(8,128)(2,1)S(1)}, bf16[4,128,512]{2,1,0:T(8,128)(2,1)S(1)}, u32[]{:S(2)}, u32[]{:S(2)}) %collective-permute-start.12) | collective-permute-done | bytes 524320 | tf_op jit(solution)/shard_map/ppermute | solution.py:74
  62.1 1.8 %collective-permute-start.17 = (bf16[2,128,512]{2,1,0:T(8,128)(2,1)S(1)}, bf16[2,128,512]{2,1,0:T(8,128)(2,1)S(1)}, u32[]{:S(2)}, u32[]{:S(2)}) collective-permute-start(bf16[2,128,512]{2,1,0:T(8,128)(2,1)S(1)} %slice.24), channel_id=1, source_target_pairs={{0,2},{2,4},{4,6},{6,8},{8,10},{10,12},{12,14},{14,0},{1,3},{3,5},... | collective-permute-start | bytes 786440 | tf_op jit(solution)/shard_map/ppermute | solution.py:74
  64.3 3.3 %near_product.1.refs_10_ = f32[512,512]{1,0:T(8,128)S(1)} custom-call(s32[4]{0:T(128)S(1)} %pad_add_fusion.first_ref.place_ref, bf16[64,4096]{1,0:T(8,128)(2,1)S(1)} %fusion.8.refs_0_, bf16[64,4096]{1,0:T(8,128)(2,1)S(1)} %copy-done.1, bf16[64,4096]{1,0:T(8,128)(2,1)S(1)} %collective-permute-done.13.refs_2_, ...), custom_call_target="tpu_custom_call" | custom-call | flops 1610612736 | bytes 8388608 | tf_op jit(solution)/shard_map/near_product/pallas_call | solution.py:137
  67.6 3.3 %collective-permute-done.17.refs_8_.refs_13_.refs_17_.refs_11_ = bf16[2,128,512]{2,1,0:T(8,128)(2,1)S(1)} collective-permute-done((bf16[2,128,512]{2,1,0:T(8,128)(2,1)S(1)}, bf16[2,128,512]{2,1,0:T(8,128)(2,1)S(1)}, u32[]{:S(2)}, u32[]{:S(2)}) %collective-permute-start.17) | collective-permute-done | bytes 262176 | tf_op jit(solution)/shard_map/ppermute | solution.py:74
  70.9 1.6 %collective-permute-done.18.refs_9_.refs_14_.refs_18_.refs_12_ = bf16[2,128,512]{2,1,0:T(8,128)(2,1)S(1)} collective-permute-done((bf16[2,128,512]{2,1,0:T(8,128)(2,1)S(1)}, bf16[2,128,512]{2,1,0:T(8,128)(2,1)S(1)}, u32[]{:S(2)}, u32[]{:S(2)}) %collective-permute-start.18) | collective-permute-done | bytes 262176 | tf_op jit(solution)/shard_map/ppermute | solution.py:74
  72.5 2.1 %first_product.1 = bf16[512,512]{1,0:T(8,128)(2,1)S(1)} custom-call(f32[8,4]{1,0:T(8,128)S(1)} %broadcast_select_fusion.mix_ref, s32[4]{0:T(128)S(1)} %pad_add_fusion.first_ref.place_ref, bf16[64,4096]{1,0:T(8,128)(2,1)S(1)} %fusion.8.refs_0_, bf16[64,4096]{1,0:T(8,128)(2,1)S(1)} %copy-done.1, bf16[64,4096]{1,0:T(8,128)(2,1)S(1)} %collective-permute-done.13.refs_2_, ...), custom_call_target="tpu_custom_call" | custom-call | flops 536870912 | bytes 4194304 | tf_op jit(solution)/shard_map/first_product/pallas_call | solution.py:175
  74.6 26.3 %all_to_all.5 = bf16[32,16,512]{2,1,0:T(8,128)(2,1)S(1)} all-to-all(bf16[32,16,512]{2,1,0:T(8,128)(2,1)S(1)} %bitcast.42), channel_id=1, replica_groups=mesh['hi'=2,'core'=2,'y'=4,'z'=8,'lo'=2] {'y','z'}, dimensions={0} | all-to-all | bytes 1048576 | tf_op jit(solution)/shard_map/all_to_all | solution.py:368
  101.2 3.7 %collective-permute-start.21 = (bf16[2,2,16,4096]{3,2,1,0:T(8,128)(2,1)S(1)}, bf16[2,2,16,4096]{3,2,1,0:T(8,128)(2,1)S(1)}, u32[]{:S(2)}, u32[]{:S(2)}) collective-permute-start(bf16[2,2,16,4096]{3,2,1,0:T(8,128)(2,1)S(1)} %bitcast.38), channel_id=1, source_target_pairs={{0,129},{1,0},{128,1},{129,128},{2,131},{3,2},{130,3},{131,130},{4... | collective-permute-start | bytes 1572872 | tf_op jit(solution)/shard_map/ppermute | solution.py:74
  104.9 9.3 %collective-permute-done.20.refs_2_.refs_6_ = bf16[2,2,16,4096]{3,2,1,0:T(8,128)(2,1)S(1)} collective-permute-done((bf16[2,2,16,4096]{3,2,1,0:T(8,128)(2,1)S(1)}, bf16[2,2,16,4096]{3,2,1,0:T(8,128)(2,1)S(1)}, u32[]{:S(2)}, u32[]{:S(2)}) %collective-permute-start.20) | collective-permute-done | bytes 524320 | tf_op jit(solution)/shard_map/ppermute | solution.py:74
  116.0 2.1 %collective-permute-start.23 = (bf16[1,2,16,4096]{3,2,1,0:T(8,128)(2,1)S(1)}, bf16[1,2,16,4096]{3,2,1,0:T(8,128)(2,1)S(1)}, u32[]{:S(2)}, u32[]{:S(2)}) collective-permute-start(bf16[1,2,16,4096]{3,2,1,0:T(8,128)(2,1)S(1)} %slice.31), channel_id=1, source_target_pairs={{0,129},{1,0},{128,1},{129,128},{2,131},{3,2},{130,3},{131,130},{4... | collective-permute-start | bytes 786440 | tf_op jit(solution)/shard_map/ppermute | solution.py:74
  118.1 1.6 %sent_rows.2 = bf16[192,512]{1,0:T(8,128)(2,1)S(1)} custom-call(s32[4]{0:T(128)S(1)} %pad_add_fusion.first_ref.place_ref, bf16[2,2,16,4096]{3,2,1,0:T(8,128)(2,1)S(1)} %bitcast.40, bf16[2,2,16,4096]{3,2,1,0:T(8,128)(2,1)S(1)} %collective-permute-done.19.refs_1_, bf16[2,2,16,4096]{3,2,1,0:T(8,128)(2,1)S(1)} %collective-permute-done.20.refs_2_.refs_6_, ...), custom_call_target="tpu_custom_call" | custom-call | flops 805306368 | bytes 6291456 | tf_op jit(solution)/shard_map/sent_rows/pallas_call | solution.py:221
  119.7 4.8 %collective-permute-done.22.refs_2_.refs_0_ = bf16[1,2,16,4096]{3,2,1,0:T(8,128)(2,1)S(1)} collective-permute-done((bf16[1,2,16,4096]{3,2,1,0:T(8,128)(2,1)S(1)}, bf16[1,2,16,4096]{3,2,1,0:T(8,128)(2,1)S(1)}, u32[]{:S(2)}, u32[]{:S(2)}) %collective-permute-start.22) | collective-permute-done | bytes 262176 | tf_op jit(solution)/shard_map/ppermute | solution.py:74
  126.4 1.4 %sent_rows.3 = bf16[64,512]{1,0:T(8,128)(2,1)S(1)} custom-call(s32[4]{0:T(128)S(1)} %pad_add_fusion.first_ref.place_ref, bf16[1,2,16,4096]{3,2,1,0:T(8,128)(2,1)S(1)} %collective-permute-done.22.refs_2_.refs_0_, bf16[1,2,16,4096]{3,2,1,0:T(8,128)(2,1)S(1)} %collective-permute-done.23.refs_3_.refs_1_, ...), custom_call_target="tpu_custom_call" | custom-call | flops 268435456 | bytes 6291456 | tf_op jit(solution)/shard_map/sent_rows/pallas_call | solution.py:221
  129.1 2.9 %kept_rows.1.kept_ref = f32[4,64,1024]{2,1,0:T(8,128)S(1)} custom-call(s32[4]{0:T(128)S(1)} %pad_add_fusion.first_ref.place_ref, s32[8]{0:T(128)S(1)} %get-tuple-element.80.slice_ref, bf16[2,2,16,4096]{3,2,1,0:T(8,128)(2,1)S(1)} %bitcast.41, bf16[2,2,16,4096]{3,2,1,0:T(8,128)(2,1)S(1)} %collective-permute-done.19.refs_1_, ...), custom_call_target="tpu_custom_call" | custom-call | flops 1073741824 | bytes 6291456 | tf_op jit(solution)/shard_map/kept_rows/pallas_call | solution.py:263
  133.3 2.2 %whitened_gradient.1 = f32[64,4,1024]{2,1,0:T(4,128)} custom-call(s32[4]{0:T(128)S(1)} %pad_add_fusion.first_ref.place_ref, s32[8]{0:T(128)S(1)} %pad_add_fusion.1.slice_ref, f32[4,64,1024]{2,1,0:T(8,128)S(1)} %kept_rows.1.kept_ref, bf16[192,512]{1,0:T(8,128)(2,1)S(1)} %collective-permute-done.28.early_ref, ...), custom_call_target="tpu_custom_call" | custom-call | tf_op jit(solution)/shard_map/whitened_gradient/pallas_call | solution.py:300
  (74 shorter events, 11.6 us)
Async XLA Ops:
  1.8 5.9 %collective-permute-start = (bf16[64,512]{1,0:T(8,128)(2,1)S(1)}, bf16[64,512]{1,0:T(8,128)(2,1)S(1)}, u32[]{:S(2)}, u32[]{:S(2)}) collective-permute-start(bf16[64,512]{1,0:T(8,128)(2,1)S(1)} %get-tuple-element.43), channel_id=1, source_target_pairs={{0,1},{1,0},{2,3},{3,2},{4,5},{5,4},{6,7},{7,6},{8,9},{9,8},{10,11... | collective-permute-start | bytes 196616 | tf_op jit(solution)/shard_map/ppermute | solution.py:74
  7.7 6.0 %copy-start.4 = (f32[4096]{0:T(1024)S(1)}, f32[4096]{0:T(1024)}, u32[]{:S(2)}) copy-start(f32[4096]{0:T(1024)} %param.12) | copy-start | bytes 49156
  7.7 6.4 %collective-permute-start.1 = (bf16[128,512]{1,0:T(8,128)(2,1)S(1)}, bf16[128,512]{1,0:T(8,128)(2,1)S(1)}, u32[]{:S(2)}, u32[]{:S(2)}) collective-permute-start(bf16[128,512]{1,0:T(8,128)(2,1)S(1)} %maximum_select_fusion), channel_id=1, source_target_pairs={{0,16},{16,32},{32,48},{48,0},{1,17},{17,33},{33,49},{49,1},{2,18}... | collective-permute-start | bytes 393224 | tf_op jit(solution)/shard_map/ppermute | solution.py:74
  9.3 6.0 %collective-permute-start.2 = (bf16[128,512]{1,0:T(8,128)(2,1)S(1)}, bf16[128,512]{1,0:T(8,128)(2,1)S(1)}, u32[]{:S(2)}, u32[]{:S(2)}) collective-permute-start(bf16[128,512]{1,0:T(8,128)(2,1)S(1)} %maximum_select_fusion), channel_id=1, source_target_pairs={{0,48},{16,0},{32,16},{48,32},{1,49},{17,1},{33,17},{49,33},{2,50}... | collective-permute-start | bytes 393224 | tf_op jit(solution)/shard_map/ppermute | solution.py:74
  11.0 7.0 %collective-permute-start.3 = (bf16[128,512]{1,0:T(8,128)(2,1)S(1)}, bf16[128,512]{1,0:T(8,128)(2,1)S(1)}, u32[]{:S(2)}, u32[]{:S(2)}) collective-permute-start(bf16[128,512]{1,0:T(8,128)(2,1)S(1)} %maximum_select_fusion), channel_id=1, source_target_pairs={{0,32},{16,48},{32,0},{48,16},{1,33},{17,49},{33,1},{49,17},{2,34}... | collective-permute-start | bytes 393224 | tf_op jit(solution)/shard_map/ppermute | solution.py:74
  18.1 13.0 %collective-permute-start.4 = (bf16[4,128,512]{2,1,0:T(8,128)(2,1)S(1)}, bf16[4,128,512]{2,1,0:T(8,128)(2,1)S(1)}, u32[]{:S(2)}, u32[]{:S(2)}) collective-permute-start(bf16[4,128,512]{2,1,0:T(8,128)(2,1)S(1)} %pad_maximum_fusion.refs_8_.refs_6_.refs_10_.refs_4_), channel_id=1, source_target_pairs={{0,2},{2,4},{4,6},{6,8},{8,10},{10,12},{12,14},{14,0},{1,3},{3,5},... | collective-permute-start | bytes 1572872 | tf_op jit(solution)/shard_map/ppermute | solution.py:74
  20.1 12.8 %collective-permute-start.5 = (bf16[4,128,512]{2,1,0:T(8,128)(2,1)S(1)}, bf16[4,128,512]{2,1,0:T(8,128)(2,1)S(1)}, u32[]{:S(2)}, u32[]{:S(2)}) collective-permute-start(bf16[4,128,512]{2,1,0:T(8,128)(2,1)S(1)} %pad_maximum_fusion.refs_8_.refs_6_.refs_10_.refs_4_), channel_id=1, source_target_pairs={{0,14},{2,0},{4,2},{6,4},{8,6},{10,8},{12,10},{14,12},{1,15},{3,1}... | collective-permute-start | bytes 1572872 | tf_op jit(solution)/shard_map/ppermute | solution.py:74
  20.2 12.7 %collective-permute-start.6 = (bf16[64,4096]{1,0:T(8,128)(2,1)S(1)}, bf16[64,4096]{1,0:T(8,128)(2,1)S(1)}, u32[]{:S(2)}, u32[]{:S(2)}) collective-permute-start(bf16[64,4096]{1,0:T(8,128)(2,1)S(1)} %fusion.8.refs_0_), channel_id=1, source_target_pairs={{0,64},{64,0},{1,65},{65,1},{2,66},{66,2},{3,67},{67,3},{4,68},{68... | collective-permute-start | bytes 1572872 | tf_op jit(solution)/shard_map/ppermute | solution.py:74
  20.2 20.1 %collective-permute-start.10 = (bf16[64,4096]{1,0:T(8,128)(2,1)S(1)}, bf16[64,4096]{1,0:T(8,128)(2,1)}, u32[]{:S(2)}, u32[]{:S(2)}) collective-permute-start(bf16[64,4096]{1,0:T(8,128)(2,1)S(1)} %fusion.8.refs_0_), channel_id=1, source_target_pairs={{0,129},{1,0},{128,1},{129,128},{2,131},{3,2},{130,3},{131,130},{4... | collective-permute-start | bytes 1572872 | tf_op jit(solution)/shard_map/ppermute | solution.py:74
  22.4 17.9 %collective-permute-start.9 = (bf16[64,4096]{1,0:T(8,128)(2,1)S(1)}, bf16[64,4096]{1,0:T(8,128)(2,1)}, u32[]{:S(2)}, u32[]{:S(2)}) collective-permute-start(bf16[64,4096]{1,0:T(8,128)(2,1)S(1)} %fusion.8.refs_0_), channel_id=1, source_target_pairs={{0,1},{1,128},{128,129},{129,0},{2,3},{3,130},{130,131},{131,2},{4... | collective-permute-start | bytes 1572872 | tf_op jit(solution)/shard_map/ppermute | solution.py:74
  33.7 13.1 %collective-permute-start.7 = (bf16[4,128,512]{2,1,0:T(8,128)(2,1)S(1)}, bf16[4,128,512]{2,1,0:T(8,128)(2,1)S(1)}, u32[]{:S(2)}, u32[]{:S(2)}) collective-permute-start(bf16[4,128,512]{2,1,0:T(8,128)(2,1)S(1)} %collective-permute-done.4.refs_9_.refs_7_.refs_11_.refs_5_), channel_id=1, source_target_pairs={{0,2},{2,4},{4,6},{6,8},{8,10},{10,12},{12,14},{14,0},{1,3},{3,5},... | collective-permute-start | bytes 1572872 | tf_op jit(solution)/shard_map/ppermute | solution.py:74
  36.8 12.8 %collective-permute-start.8 = (bf16[4,128,512]{2,1,0:T(8,128)(2,1)S(1)}, bf16[4,128,512]{2,1,0:T(8,128)(2,1)S(1)}, u32[]{:S(2)}, u32[]{:S(2)}) collective-permute-start(bf16[4,128,512]{2,1,0:T(8,128)(2,1)S(1)} %collective-permute-done.5.refs_10_.refs_8_.refs_12_.refs_6_), channel_id=1, source_target_pairs={{0,14},{2,0},{4,2},{6,4},{8,6},{10,8},{12,10},{14,12},{1,15},{3,1}... | collective-permute-start | bytes 1572872 | tf_op jit(solution)/shard_map/ppermute | solution.py:74
  37.6 14.6 %collective-permute-start.13 = (bf16[64,4096]{1,0:T(8,128)(2,1)S(1)}, bf16[64,4096]{1,0:T(8,128)(2,1)S(1)}, u32[]{:S(2)}, u32[]{:S(2)}) collective-permute-start(bf16[64,4096]{1,0:T(8,128)(2,1)S(1)} %fusion.8.refs_0_), channel_id=1, source_target_pairs={{0,128},{1,129},{128,0},{129,1},{2,130},{3,131},{130,2},{131,3},{4... | collective-permute-start | bytes 1572872 | tf_op jit(solution)/shard_map/ppermute | solution.py:74
  49.6 14.7 %copy-start.1 = (bf16[64,4096]{1,0:T(8,128)(2,1)S(1)}, bf16[64,4096]{1,0:T(8,128)(2,1)}, u32[]{:S(2)}) copy-start(bf16[64,4096]{1,0:T(8,128)(2,1)} %copy-done) | copy-start | bytes 1572868
  49.6 10.9 %collective-permute-start.11 = (bf16[4,128,512]{2,1,0:T(8,128)(2,1)S(1)}, bf16[4,128,512]{2,1,0:T(8,128)(2,1)S(1)}, u32[]{:S(2)}, u32[]{:S(2)}) collective-permute-start(bf16[4,128,512]{2,1,0:T(8,128)(2,1)S(1)} %collective-permute-done.7.refs_11_.refs_9_.refs_13_.refs_7_), channel_id=1, source_target_pairs={{0,2},{2,4},{4,6},{6,8},{8,10},{10,12},{12,14},{14,0},{1,3},{3,5},... | collective-permute-start | bytes 1572872 | tf_op jit(solution)/shard_map/ppermute | solution.py:74
  51.4 10.7 %collective-permute-start.12 = (bf16[4,128,512]{2,1,0:T(8,128)(2,1)S(1)}, bf16[4,128,512]{2,1,0:T(8,128)(2,1)S(1)}, u32[]{:S(2)}, u32[]{:S(2)}) collective-permute-start(bf16[4,128,512]{2,1,0:T(8,128)(2,1)S(1)} %collective-permute-done.8.refs_12_.refs_10_.refs_14_.refs_8_), channel_id=1, source_target_pairs={{0,14},{2,0},{4,2},{6,4},{8,6},{10,8},{12,10},{14,12},{1,15},{3,1}... | collective-permute-start | bytes 1572872 | tf_op jit(solution)/shard_map/ppermute | solution.py:74
  51.7 10.4 %collective-permute-start.14 = (bf16[64,4096]{1,0:T(8,128)(2,1)}, bf16[64,4096]{1,0:T(8,128)(2,1)S(1)}, u32[]{:S(2)}, u32[]{:S(2)}) collective-permute-start(bf16[64,4096]{1,0:T(8,128)(2,1)} %collective-permute-done.9.refs_4_), channel_id=1, source_target_pairs={{0,64},{64,0},{1,65},{65,1},{2,66},{66,2},{3,67},{67,3},{4,68},{68... | collective-permute-start | bytes 1572872 | tf_op jit(solution)/shard_map/ppermute | solution.py:74
  51.7 10.4 %collective-permute-start.15 = (bf16[64,4096]{1,0:T(8,128)(2,1)}, bf16[64,4096]{1,0:T(8,128)(2,1)S(1)}, u32[]{:S(2)}, u32[]{:S(2)}) collective-permute-start(bf16[64,4096]{1,0:T(8,128)(2,1)} %collective-permute-done.10.refs_6_), channel_id=1, source_target_pairs={{0,64},{64,0},{1,65},{65,1},{2,66},{66,2},{3,67},{67,3},{4,68},{68... | collective-permute-start | bytes 1572872 | tf_op jit(solution)/shard_map/ppermute | solution.py:74
  62.1 2.2 %collective-permute-start.16 = (bf16[64,4096]{1,0:T(8,128)(2,1)S(1)}, bf16[64,4096]{1,0:T(8,128)(2,1)S(1)}, u32[]{:S(2)}, u32[]{:S(2)}) collective-permute-start(bf16[64,4096]{1,0:T(8,128)(2,1)S(1)} %collective-permute-done.13.refs_2_), channel_id=1, source_target_pairs={{0,64},{64,0},{1,65},{65,1},{2,66},{66,2},{3,67},{67,3},{4,68},{68... | collective-permute-start | bytes 1572872 | tf_op jit(solution)/shard_map/ppermute | solution.py:74
  62.1 8.8 %collective-permute-start.17 = (bf16[2,128,512]{2,1,0:T(8,128)(2,1)S(1)}, bf16[2,128,512]{2,1,0:T(8,128)(2,1)S(1)}, u32[]{:S(2)}, u32[]{:S(2)}) collective-permute-start(bf16[2,128,512]{2,1,0:T(8,128)(2,1)S(1)} %slice.24), channel_id=1, source_target_pairs={{0,2},{2,4},{4,6},{6,8},{8,10},{10,12},{12,14},{14,0},{1,3},{3,5},... | collective-permute-start | bytes 786440 | tf_op jit(solution)/shard_map/ppermute | solution.py:74
  64.0 8.5 %collective-permute-start.18 = (bf16[2,128,512]{2,1,0:T(8,128)(2,1)S(1)}, bf16[2,128,512]{2,1,0:T(8,128)(2,1)S(1)}, u32[]{:S(2)}, u32[]{:S(2)}) collective-permute-start(bf16[2,128,512]{2,1,0:T(8,128)(2,1)S(1)} %slice.25), channel_id=1, source_target_pairs={{0,14},{2,0},{4,2},{6,4},{8,6},{10,8},{12,10},{14,12},{1,15},{3,1}... | collective-permute-start | bytes 786440 | tf_op jit(solution)/shard_map/ppermute | solution.py:74
  101.1 13.1 %collective-permute-start.20 = (bf16[2,2,16,4096]{3,2,1,0:T(8,128)(2,1)S(1)}, bf16[2,2,16,4096]{3,2,1,0:T(8,128)(2,1)S(1)}, u32[]{:S(2)}, u32[]{:S(2)}) collective-permute-start(bf16[2,2,16,4096]{3,2,1,0:T(8,128)(2,1)S(1)} %bitcast.37), channel_id=1, source_target_pairs={{0,1},{1,128},{128,129},{129,0},{2,3},{3,130},{130,131},{131,2},{4... | collective-permute-start | bytes 1572872 | tf_op jit(solution)/shard_map/ppermute | solution.py:74
  101.2 13.0 %collective-permute-start.21 = (bf16[2,2,16,4096]{3,2,1,0:T(8,128)(2,1)S(1)}, bf16[2,2,16,4096]{3,2,1,0:T(8,128)(2,1)S(1)}, u32[]{:S(2)}, u32[]{:S(2)}) collective-permute-start(bf16[2,2,16,4096]{3,2,1,0:T(8,128)(2,1)S(1)} %bitcast.38), channel_id=1, source_target_pairs={{0,129},{1,0},{128,1},{129,128},{2,131},{3,2},{130,3},{131,130},{4... | collective-permute-start | bytes 1572872 | tf_op jit(solution)/shard_map/ppermute | solution.py:74
  104.9 9.4 %collective-permute-start.19 = (bf16[2,2,16,4096]{3,2,1,0:T(8,128)(2,1)S(1)}, bf16[2,2,16,4096]{3,2,1,0:T(8,128)(2,1)S(1)}, u32[]{:S(2)}, u32[]{:S(2)}) collective-permute-start(bf16[2,2,16,4096]{3,2,1,0:T(8,128)(2,1)S(1)} %bitcast.39), channel_id=1, source_target_pairs={{0,64},{64,0},{1,65},{65,1},{2,66},{66,2},{3,67},{67,3},{4,68},{68... | collective-permute-start | bytes 1572872 | tf_op jit(solution)/shard_map/ppermute | solution.py:74
  114.3 3.8 %collective-permute-start.24 = (bf16[2,2,16,4096]{3,2,1,0:T(8,128)(2,1)S(1)}, bf16[2,2,16,4096]{3,2,1,0:T(8,128)(2,1)S(1)}, u32[]{:S(2)}, u32[]{:S(2)}) collective-permute-start(bf16[2,2,16,4096]{3,2,1,0:T(8,128)(2,1)S(1)} %collective-permute-done.20.refs_2_.refs_6_), channel_id=1, source_target_pairs={{0,64},{64,0},{1,65},{65,1},{2,66},{66,2},{3,67},{67,3},{4,68},{68... | collective-permute-start | bytes 1572872 | tf_op jit(solution)/shard_map/ppermute | solution.py:74
  114.4 3.7 %collective-permute-start.25 = (bf16[2,2,16,4096]{3,2,1,0:T(8,128)(2,1)S(1)}, bf16[2,2,16,4096]{3,2,1,0:T(8,128)(2,1)S(1)}, u32[]{:S(2)}, u32[]{:S(2)}) collective-permute-start(bf16[2,2,16,4096]{3,2,1,0:T(8,128)(2,1)S(1)} %collective-permute-done.21.refs_4_.refs_8_), channel_id=1, source_target_pairs={{0,64},{64,0},{1,65},{65,1},{2,66},{66,2},{3,67},{67,3},{4,68},{68... | collective-permute-start | bytes 1572872 | tf_op jit(solution)/shard_map/ppermute | solution.py:74
  114.9 9.6 %collective-permute-start.22 = (bf16[1,2,16,4096]{3,2,1,0:T(8,128)(2,1)S(1)}, bf16[1,2,16,4096]{3,2,1,0:T(8,128)(2,1)S(1)}, u32[]{:S(2)}, u32[]{:S(2)}) collective-permute-start(bf16[1,2,16,4096]{3,2,1,0:T(8,128)(2,1)S(1)} %slice.30), channel_id=1, source_target_pairs={{0,1},{1,128},{128,129},{129,0},{2,3},{3,130},{130,131},{131,2},{4... | collective-permute-start | bytes 786440 | tf_op jit(solution)/shard_map/ppermute | solution.py:74
  116.0 8.5 %collective-permute-start.23 = (bf16[1,2,16,4096]{3,2,1,0:T(8,128)(2,1)S(1)}, bf16[1,2,16,4096]{3,2,1,0:T(8,128)(2,1)S(1)}, u32[]{:S(2)}, u32[]{:S(2)}) collective-permute-start(bf16[1,2,16,4096]{3,2,1,0:T(8,128)(2,1)S(1)} %slice.31), channel_id=1, source_target_pairs={{0,129},{1,0},{128,1},{129,128},{2,131},{3,2},{130,3},{131,130},{4... | collective-permute-start | bytes 786440 | tf_op jit(solution)/shard_map/ppermute | solution.py:74
  124.4 2.0 %collective-permute-start.26 = (bf16[1,2,16,4096]{3,2,1,0:T(8,128)(2,1)S(1)}, bf16[1,2,16,4096]{3,2,1,0:T(8,128)(2,1)S(1)}, u32[]{:S(2)}, u32[]{:S(2)}) collective-permute-start(bf16[1,2,16,4096]{3,2,1,0:T(8,128)(2,1)S(1)} %collective-permute-done.22.refs_2_.refs_0_), channel_id=1, source_target_pairs={{0,64},{64,0},{1,65},{65,1},{2,66},{66,2},{3,67},{67,3},{4,68},{68... | collective-permute-start | bytes 786440 | tf_op jit(solution)/shard_map/ppermute | solution.py:74
  124.4 2.0 %collective-permute-start.27 = (bf16[1,2,16,4096]{3,2,1,0:T(8,128)(2,1)S(1)}, bf16[1,2,16,4096]{3,2,1,0:T(8,128)(2,1)S(1)}, u32[]{:S(2)}, u32[]{:S(2)}) collective-permute-start(bf16[1,2,16,4096]{3,2,1,0:T(8,128)(2,1)S(1)} %collective-permute-done.23.refs_3_.refs_1_), channel_id=1, source_target_pairs={{0,64},{64,0},{1,65},{65,1},{2,66},{66,2},{3,67},{67,3},{4,68},{68... | collective-permute-start | bytes 786440 | tf_op jit(solution)/shard_map/ppermute | solution.py:74
  125.0 7.5 %collective-permute-start.28 = (bf16[192,512]{1,0:T(8,128)(2,1)S(1)}, bf16[192,512]{1,0:T(8,128)(2,1)S(1)}, u32[]{:S(2)}, u32[]{:S(2)}) collective-permute-start(bf16[192,512]{1,0:T(8,128)(2,1)S(1)} %sent_rows.2), channel_id=1, source_target_pairs={{0,1},{1,0},{2,3},{3,2},{4,5},{5,4},{6,7},{7,6},{8,9},{9,8},{10,11... | collective-permute-start | bytes 589832 | tf_op jit(solution)/shard_map/ppermute | solution.py:74
  127.8 5.4 %collective-permute-start.29 = (bf16[64,512]{1,0:T(8,128)(2,1)S(1)}, bf16[64,512]{1,0:T(8,128)(2,1)S(1)}, u32[]{:S(2)}, u32[]{:S(2)}) collective-permute-start(bf16[64,512]{1,0:T(8,128)(2,1)S(1)} %sent_rows.3), channel_id=1, source_target_pairs={{0,1},{1,0},{2,3},{3,2},{4,5},{5,4},{6,7},{7,6},{8,9},{9,8},{10,11... | collective-permute-start | bytes 196616 | tf_op jit(solution)/shard_map/ppermute | solution.py:74
  (3 other events, 4.4 us)

commit v12 on v11

--- a/solution.py
+++ b/solution.py
@@ -345,14 +345,13 @@
         return shifted(right, "z", 1), shifted(left, "z", nz - 1)
 
     one = step(block, block)
-    one, own = lax.optimization_barrier((one, own))
+    one, own, before = lax.optimization_barrier((one, own, before))
     two = step(*one)
     far = shifted(own[0], RING, 2)
-    two, own, before, after, mix, sx, sy = lax.optimization_barrier(
-        (two, own, before, after, mix, sx, sy)
-    )
+    before = with_core(before)
+    two, after, mix, sx, sy = lax.optimization_barrier((two, after, mix, sx, sy))
     three = step(*two)
-    before, after = with_core(before), with_core(after)
+    after = with_core(after)
     three, far, before, after = lax.optimization_barrier((three, far, before, after))
     last = step(three[0][:2], three[1][2:])
     far = with_core(far)

time: 136 us -> 136 us (level)
  starting transfers between devices: 32.6 us -> 35.9 us
  blocking collectives: 26.3 us -> 23.2 us
    ppermute x30, starting transfers between devices: 32.6 us -> 35.9 us  [shifted(): lax.ppermute(array, axis, [(k, (k + step) % size) for k in range(size)])]
    all_to_all x1, blocking collectives: 26.3 us -> 23.2 us  [local(): got = lax.all_to_all(sent, ('y', 'z'), 0, 0, tiled=True)]
  transfers between devices with their start and end apart: 30 -> 30, of which waited for: 14 -> 15; matrix products, arithmetic and copies ran while one was open for 4% -> 4% of each run, Pallas kernels for 7% -> 7%
where the time goes in v12:
time: 136 us; the launch traced here: 135 us
  waiting for transfers between devices  53.6 us (39%)
  starting transfers between devices  35.9 us (26%)
  blocking collectives  23.2 us (17%)
  Pallas kernels  13.9 us (10%)
  other arithmetic  4.66 us (3%)
  local copies, waits for them, and re-layouts  2.99 us (2%)
    ppermute x30, waiting for transfers between devices, shifted(): lax.ppermute(array, axis, [(k, (k + step) % size) for k in range(size)])  53.6 us
    ppermute x30, starting transfers between devices, shifted(): lax.ppermute(array, axis, [(k, (k + step) % size) for k in range(size)])  35.9 us
    all_to_all x1, blocking collectives, local(): got = lax.all_to_all(sent, ('y', 'z'), 0, 0, tiled=True)  23.2 us
    squeeze x1, other arithmetic, local(): moments(event_counts, latent_mean, latent_var).astype(jnp.bfloat16)[0]  4.29 us
    pallas_call x1, Pallas kernels, near_product(): pl.pallas_call(near_kernel, out_shape=jax.ShapeDtypeStruct((rows, width),...  3.15 us
    pallas_call x2, Pallas kernels, sent_rows(): pl.pallas_call(sent_kernel, out_shape=jax.ShapeDtypeStruct((count, width)...  2.94 us
    pallas_call x1, Pallas kernels, kept_rows(): pl.pallas_call(kept_kernel, out_shape=jax.ShapeDtypeStruct((times, rows,...  2.87 us
  transfers between devices with their start and end apart: 30, of which 15 were waited for; matrix products, arithmetic and copies ran while one was open for 4% of the time, Pallas kernels for 7%

profile of v12, /device:TPU:32, one launch (start us, length us, event | category | flops | bytes accessed | tf_op | source)
XLA Modules:
  0.0 135.2 jit_solution(9509187772937455910)
XLA Ops:
  1.8 1.6 %collective-permute-start = (bf16[64,512]{1,0:T(8,128)(2,1)S(1)}, bf16[64,512]{1,0:T(8,128)(2,1)S(1)}, u32[]{:S(2)}, u32[]{:S(2)}) collective-permute-start(bf16[64,512]{1,0:T(8,128)(2,1)S(1)} %get-tuple-element.41), channel_id=1, source_target_pairs={{0,1},{1,0},{2,3},{3,2},{4,5},{5,4},{6,7},{7,6},{8,9},{9,8},{10,11... | collective-permute-start | bytes 196616 | tf_op jit(solution)/shard_map/ppermute | solution.py:74
  3.3 4.3 %fusion.8.refs_0_ = bf16[64,4096]{1,0:T(8,128)(2,1)S(1)} fusion(s32[1,64,4096]{2,1,0:T(8,128)} %param.8, f32[1,64,4096]{2,1,0:T(8,128)} %param.10, f32[1,64,4096]{2,1,0:T(8,128)} %param.9), kind=kLoop, calls=%fused_computation.16 | loop fusion | flops 17563648 | bytes 3670016 | tf_op jit(solution)/shard_map/squeeze | solution.py:324
  7.7 1.7 %collective-permute-start.1 = (bf16[128,512]{1,0:T(8,128)(2,1)S(1)}, bf16[128,512]{1,0:T(8,128)(2,1)S(1)}, u32[]{:S(2)}, u32[]{:S(2)}) collective-permute-start(bf16[128,512]{1,0:T(8,128)(2,1)S(1)} %maximum_select_fusion), channel_id=1, source_target_pairs={{0,16},{16,32},{32,48},{48,0},{1,17},{17,33},{33,49},{49,1},{2,18}... | collective-permute-start | bytes 393224 | tf_op jit(solution)/shard_map/ppermute | solution.py:74
  9.3 1.7 %collective-permute-start.2 = (bf16[128,512]{1,0:T(8,128)(2,1)S(1)}, bf16[128,512]{1,0:T(8,128)(2,1)S(1)}, u32[]{:S(2)}, u32[]{:S(2)}) collective-permute-start(bf16[128,512]{1,0:T(8,128)(2,1)S(1)} %maximum_select_fusion), channel_id=1, source_target_pairs={{0,48},{16,0},{32,16},{48,32},{1,49},{17,1},{33,17},{49,33},{2,50}... | collective-permute-start | bytes 393224 | tf_op jit(solution)/shard_map/ppermute | solution.py:74
  11.0 2.0 %collective-permute-start.3 = (bf16[128,512]{1,0:T(8,128)(2,1)S(1)}, bf16[128,512]{1,0:T(8,128)(2,1)S(1)}, u32[]{:S(2)}, u32[]{:S(2)}) collective-permute-start(bf16[128,512]{1,0:T(8,128)(2,1)S(1)} %maximum_select_fusion), channel_id=1, source_target_pairs={{0,32},{16,48},{32,0},{48,16},{1,33},{17,49},{33,1},{49,17},{2,34}... | collective-permute-start | bytes 393224 | tf_op jit(solution)/shard_map/ppermute | solution.py:74
  15.4 2.6 %collective-permute-done.3 = bf16[128,512]{1,0:T(8,128)(2,1)S(1)} collective-permute-done((bf16[128,512]{1,0:T(8,128)(2,1)S(1)}, bf16[128,512]{1,0:T(8,128)(2,1)S(1)}, u32[]{:S(2)}, u32[]{:S(2)}) %collective-permute-start.3) | collective-permute-done | bytes 131104 | tf_op jit(solution)/shard_map/ppermute | solution.py:74
  18.1 2.0 %collective-permute-start.4 = (bf16[4,128,512]{2,1,0:T(8,128)(2,1)S(1)}, bf16[4,128,512]{2,1,0:T(8,128)(2,1)S(1)}, u32[]{:S(2)}, u32[]{:S(2)}) collective-permute-start(bf16[4,128,512]{2,1,0:T(8,128)(2,1)S(1)} %pad_maximum_fusion.refs_8_.refs_6_.refs_10_.refs_4_), channel_id=1, source_target_pairs={{0,2},{2,4},{4,6},{6,8},{8,10},{10,12},{12,14},{14,0},{1,3},{3,5},... | collective-permute-start | bytes 1572872 | tf_op jit(solution)/shard_map/ppermute | solution.py:74
  20.2 2.2 %collective-permute-start.10 = (bf16[64,4096]{1,0:T(8,128)(2,1)S(1)}, bf16[64,4096]{1,0:T(8,128)(2,1)}, u32[]{:S(2)}, u32[]{:S(2)}) collective-permute-start(bf16[64,4096]{1,0:T(8,128)(2,1)S(1)} %fusion.8.refs_0_), channel_id=1, source_target_pairs={{0,129},{1,0},{128,1},{129,128},{2,131},{3,2},{130,3},{131,130},{4... | collective-permute-start | bytes 1572872 | tf_op jit(solution)/shard_map/ppermute | solution.py:74
  22.4 5.4 %collective-permute-done.7.refs_4_ = bf16[64,4096]{1,0:T(8,128)(2,1)S(1)} collective-permute-done((bf16[64,4096]{1,0:T(8,128)(2,1)S(1)}, bf16[64,4096]{1,0:T(8,128)(2,1)S(1)}, u32[]{:S(2)}, u32[]{:S(2)}) %collective-permute-start.7) | collective-permute-done | bytes 524320 | tf_op jit(solution)/shard_map/ppermute | solution.py:74
  27.8 3.3 %collective-permute-done.4.refs_9_.refs_7_.refs_11_.refs_5_ = bf16[4,128,512]{2,1,0:T(8,128)(2,1)S(1)} collective-permute-done((bf16[4,128,512]{2,1,0:T(8,128)(2,1)S(1)}, bf16[4,128,512]{2,1,0:T(8,128)(2,1)S(1)}, u32[]{:S(2)}, u32[]{:S(2)}) %collective-permute-start.4) | collective-permute-done | bytes 524320 | tf_op jit(solution)/shard_map/ppermute | solution.py:74
  31.1 1.8 %collective-permute-done.5.refs_10_.refs_8_.refs_12_.refs_6_ = bf16[4,128,512]{2,1,0:T(8,128)(2,1)S(1)} collective-permute-done((bf16[4,128,512]{2,1,0:T(8,128)(2,1)S(1)}, bf16[4,128,512]{2,1,0:T(8,128)(2,1)S(1)}, u32[]{:S(2)}, u32[]{:S(2)}) %collective-permute-start.5) | collective-permute-done | bytes 524320 | tf_op jit(solution)/shard_map/ppermute | solution.py:74
  33.7 3.1 %collective-permute-start.8 = (bf16[4,128,512]{2,1,0:T(8,128)(2,1)S(1)}, bf16[4,128,512]{2,1,0:T(8,128)(2,1)S(1)}, u32[]{:S(2)}, u32[]{:S(2)}) collective-permute-start(bf16[4,128,512]{2,1,0:T(8,128)(2,1)S(1)} %collective-permute-done.4.refs_9_.refs_7_.refs_11_.refs_5_), channel_id=1, source_target_pairs={{0,2},{2,4},{4,6},{6,8},{8,10},{10,12},{12,14},{14,0},{1,3},{3,5},... | collective-permute-start | bytes 1572872 | tf_op jit(solution)/shard_map/ppermute | solution.py:74
  37.6 2.7 %collective-permute-start.13 = (bf16[64,4096]{1,0:T(8,128)(2,1)S(1)}, bf16[64,4096]{1,0:T(8,128)(2,1)S(1)}, u32[]{:S(2)}, u32[]{:S(2)}) collective-permute-start(bf16[64,4096]{1,0:T(8,128)(2,1)S(1)} %fusion.8.refs_0_), channel_id=1, source_target_pairs={{0,128},{1,129},{128,0},{129,1},{2,130},{3,131},{130,2},{131,3},{4... | collective-permute-start | bytes 1572872 | tf_op jit(solution)/shard_map/ppermute | solution.py:74
  40.3 6.3 %collective-permute-done.8.refs_11_.refs_9_.refs_13_.refs_7_ = bf16[4,128,512]{2,1,0:T(8,128)(2,1)S(1)} collective-permute-done((bf16[4,128,512]{2,1,0:T(8,128)(2,1)S(1)}, bf16[4,128,512]{2,1,0:T(8,128)(2,1)S(1)}, u32[]{:S(2)}, u32[]{:S(2)}) %collective-permute-start.8) | collective-permute-done | bytes 524320 | tf_op jit(solution)/shard_map/ppermute | solution.py:74
  46.6 2.8 %collective-permute-done.9.refs_12_.refs_10_.refs_14_.refs_8_ = bf16[4,128,512]{2,1,0:T(8,128)(2,1)S(1)} collective-permute-done((bf16[4,128,512]{2,1,0:T(8,128)(2,1)S(1)}, bf16[4,128,512]{2,1,0:T(8,128)(2,1)S(1)}, u32[]{:S(2)}, u32[]{:S(2)}) %collective-permute-start.9) | collective-permute-done | bytes 524320 | tf_op jit(solution)/shard_map/ppermute | solution.py:74
  49.5 1.8 %collective-permute-start.11 = (bf16[4,128,512]{2,1,0:T(8,128)(2,1)S(1)}, bf16[4,128,512]{2,1,0:T(8,128)(2,1)S(1)}, u32[]{:S(2)}, u32[]{:S(2)}) collective-permute-start(bf16[4,128,512]{2,1,0:T(8,128)(2,1)S(1)} %collective-permute-done.8.refs_11_.refs_9_.refs_13_.refs_7_), channel_id=1, source_target_pairs={{0,2},{2,4},{4,6},{6,8},{8,10},{10,12},{12,14},{14,0},{1,3},{3,5},... | collective-permute-start | bytes 1572872 | tf_op jit(solution)/shard_map/ppermute | solution.py:74
  51.6 8.8 %collective-permute-done.11.refs_13_.refs_11_.refs_15_.refs_9_ = bf16[4,128,512]{2,1,0:T(8,128)(2,1)S(1)} collective-permute-done((bf16[4,128,512]{2,1,0:T(8,128)(2,1)S(1)}, bf16[4,128,512]{2,1,0:T(8,128)(2,1)S(1)}, u32[]{:S(2)}, u32[]{:S(2)}) %collective-permute-start.11) | collective-permute-done | bytes 524320 | tf_op jit(solution)/shard_map/ppermute | solution.py:74
  60.4 1.5 %collective-permute-done.12.refs_14_.refs_12_.refs_16_.refs_10_ = bf16[4,128,512]{2,1,0:T(8,128)(2,1)S(1)} collective-permute-done((bf16[4,128,512]{2,1,0:T(8,128)(2,1)S(1)}, bf16[4,128,512]{2,1,0:T(8,128)(2,1)S(1)}, u32[]{:S(2)}, u32[]{:S(2)}) %collective-permute-start.12) | collective-permute-done | bytes 524320 | tf_op jit(solution)/shard_map/ppermute | solution.py:74
  61.9 1.8 %collective-permute-start.17 = (bf16[2,128,512]{2,1,0:T(8,128)(2,1)S(1)}, bf16[2,128,512]{2,1,0:T(8,128)(2,1)S(1)}, u32[]{:S(2)}, u32[]{:S(2)}) collective-permute-start(bf16[2,128,512]{2,1,0:T(8,128)(2,1)S(1)} %slice.24), channel_id=1, source_target_pairs={{0,2},{2,4},{4,6},{6,8},{8,10},{10,12},{12,14},{14,0},{1,3},{3,5},... | collective-permute-start | bytes 786440 | tf_op jit(solution)/shard_map/ppermute | solution.py:74
  64.1 3.2 %near_product.1.refs_10_ = f32[512,512]{1,0:T(8,128)S(1)} custom-call(s32[4]{0:T(128)S(1)} %pad_add_fusion.first_ref.place_ref, bf16[64,4096]{1,0:T(8,128)(2,1)S(1)} %fusion.8.refs_0_, bf16[64,4096]{1,0:T(8,128)(2,1)S(1)} %copy-done.3, bf16[64,4096]{1,0:T(8,128)(2,1)S(1)} %collective-permute-done.13.refs_2_, ...), custom_call_target="tpu_custom_call" | custom-call | flops 1610612736 | bytes 8388608 | tf_op jit(solution)/shard_map/near_product/pallas_call | solution.py:137
  67.3 3.4 %collective-permute-done.17.refs_8_.refs_13_.refs_17_.refs_11_ = bf16[2,128,512]{2,1,0:T(8,128)(2,1)S(1)} collective-permute-done((bf16[2,128,512]{2,1,0:T(8,128)(2,1)S(1)}, bf16[2,128,512]{2,1,0:T(8,128)(2,1)S(1)}, u32[]{:S(2)}, u32[]{:S(2)}) %collective-permute-start.17) | collective-permute-done | bytes 262176 | tf_op jit(solution)/shard_map/ppermute | solution.py:74
  70.7 1.6 %collective-permute-done.18.refs_9_.refs_14_.refs_18_.refs_12_ = bf16[2,128,512]{2,1,0:T(8,128)(2,1)S(1)} collective-permute-done((bf16[2,128,512]{2,1,0:T(8,128)(2,1)S(1)}, bf16[2,128,512]{2,1,0:T(8,128)(2,1)S(1)}, u32[]{:S(2)}, u32[]{:S(2)}) %collective-permute-start.18) | collective-permute-done | bytes 262176 | tf_op jit(solution)/shard_map/ppermute | solution.py:74
  72.3 2.0 %first_product.1 = bf16[512,512]{1,0:T(8,128)(2,1)S(1)} custom-call(f32[8,4]{1,0:T(8,128)S(1)} %broadcast_select_fusion.mix_ref, s32[4]{0:T(128)S(1)} %pad_add_fusion.first_ref.place_ref, bf16[64,4096]{1,0:T(8,128)(2,1)S(1)} %fusion.8.refs_0_, bf16[64,4096]{1,0:T(8,128)(2,1)S(1)} %copy-done.3, bf16[64,4096]{1,0:T(8,128)(2,1)S(1)} %collective-permute-done.13.refs_2_, ...), custom_call_target="tpu_custom_call" | custom-call | flops 536870912 | bytes 4194304 | tf_op jit(solution)/shard_map/first_product/pallas_call | solution.py:175
  74.3 23.2 %all_to_all.5 = bf16[32,16,512]{2,1,0:T(8,128)(2,1)S(1)} all-to-all(bf16[32,16,512]{2,1,0:T(8,128)(2,1)S(1)} %bitcast.42), channel_id=1, replica_groups=mesh['hi'=2,'core'=2,'y'=4,'z'=8,'lo'=2] {'y','z'}, dimensions={0} | all-to-all | bytes 1048576 | tf_op jit(solution)/shard_map/all_to_all | solution.py:367
  98.2 6.5 %collective-permute-start.21 = (bf16[2,2,16,4096]{3,2,1,0:T(8,128)(2,1)S(1)}, bf16[2,2,16,4096]{3,2,1,0:T(8,128)(2,1)S(1)}, u32[]{:S(2)}, u32[]{:S(2)}) collective-permute-start(bf16[2,2,16,4096]{3,2,1,0:T(8,128)(2,1)S(1)} %bitcast.38), channel_id=1, source_target_pairs={{0,129},{1,0},{128,1},{129,128},{2,131},{3,2},{130,3},{131,130},{4... | collective-permute-start | bytes 1572872 | tf_op jit(solution)/shard_map/ppermute | solution.py:74
  104.7 9.3 %collective-permute-done.20.refs_2_.refs_6_ = bf16[2,2,16,4096]{3,2,1,0:T(8,128)(2,1)S(1)} collective-permute-done((bf16[2,2,16,4096]{3,2,1,0:T(8,128)(2,1)S(1)}, bf16[2,2,16,4096]{3,2,1,0:T(8,128)(2,1)S(1)}, u32[]{:S(2)}, u32[]{:S(2)}) %collective-permute-start.20) | collective-permute-done | bytes 524320 | tf_op jit(solution)/shard_map/ppermute | solution.py:74
  115.7 2.1 %collective-permute-start.23 = (bf16[1,2,16,4096]{3,2,1,0:T(8,128)(2,1)S(1)}, bf16[1,2,16,4096]{3,2,1,0:T(8,128)(2,1)S(1)}, u32[]{:S(2)}, u32[]{:S(2)}) collective-permute-start(bf16[1,2,16,4096]{3,2,1,0:T(8,128)(2,1)S(1)} %slice.31), channel_id=1, source_target_pairs={{0,129},{1,0},{128,1},{129,128},{2,131},{3,2},{130,3},{131,130},{4... | collective-permute-start | bytes 786440 | tf_op jit(solution)/shard_map/ppermute | solution.py:74
  117.9 1.6 %sent_rows.2 = bf16[192,512]{1,0:T(8,128)(2,1)S(1)} custom-call(s32[4]{0:T(128)S(1)} %pad_add_fusion.first_ref.place_ref, bf16[2,2,16,4096]{3,2,1,0:T(8,128)(2,1)S(1)} %bitcast.40, bf16[2,2,16,4096]{3,2,1,0:T(8,128)(2,1)S(1)} %collective-permute-done.19.refs_1_, bf16[2,2,16,4096]{3,2,1,0:T(8,128)(2,1)S(1)} %collective-permute-done.20.refs_2_.refs_6_, ...), custom_call_target="tpu_custom_call" | custom-call | flops 805306368 | bytes 6291456 | tf_op jit(solution)/shard_map/sent_rows/pallas_call | solution.py:221
  119.4 4.8 %collective-permute-done.22.refs_2_.refs_0_ = bf16[1,2,16,4096]{3,2,1,0:T(8,128)(2,1)S(1)} collective-permute-done((bf16[1,2,16,4096]{3,2,1,0:T(8,128)(2,1)S(1)}, bf16[1,2,16,4096]{3,2,1,0:T(8,128)(2,1)S(1)}, u32[]{:S(2)}, u32[]{:S(2)}) %collective-permute-start.22) | collective-permute-done | bytes 262176 | tf_op jit(solution)/shard_map/ppermute | solution.py:74
  126.2 1.4 %sent_rows.3 = bf16[64,512]{1,0:T(8,128)(2,1)S(1)} custom-call(s32[4]{0:T(128)S(1)} %pad_add_fusion.first_ref.place_ref, bf16[1,2,16,4096]{3,2,1,0:T(8,128)(2,1)S(1)} %collective-permute-done.22.refs_2_.refs_0_, bf16[1,2,16,4096]{3,2,1,0:T(8,128)(2,1)S(1)} %collective-permute-done.23.refs_3_.refs_1_, ...), custom_call_target="tpu_custom_call" | custom-call | flops 268435456 | bytes 6291456 | tf_op jit(solution)/shard_map/sent_rows/pallas_call | solution.py:221
  128.9 2.9 %kept_rows.1.kept_ref = f32[4,64,1024]{2,1,0:T(8,128)S(1)} custom-call(s32[4]{0:T(128)S(1)} %pad_add_fusion.first_ref.place_ref, s32[8]{0:T(128)S(1)} %get-tuple-element.76.slice_ref, bf16[2,2,16,4096]{3,2,1,0:T(8,128)(2,1)S(1)} %bitcast.41, bf16[2,2,16,4096]{3,2,1,0:T(8,128)(2,1)S(1)} %collective-permute-done.19.refs_1_, ...), custom_call_target="tpu_custom_call" | custom-call | flops 1073741824 | bytes 6291456 | tf_op jit(solution)/shard_map/kept_rows/pallas_call | solution.py:263
  133.0 2.2 %whitened_gradient.1 = f32[64,4,1024]{2,1,0:T(4,128)} custom-call(s32[4]{0:T(128)S(1)} %pad_add_fusion.first_ref.place_ref, s32[8]{0:T(128)S(1)} %pad_add_fusion.1.slice_ref, f32[4,64,1024]{2,1,0:T(8,128)S(1)} %kept_rows.1.kept_ref, bf16[192,512]{1,0:T(8,128)(2,1)S(1)} %collective-permute-done.28.early_ref, ...), custom_call_target="tpu_custom_call" | custom-call | tf_op jit(solution)/shard_map/whitened_gradient/pallas_call | solution.py:300
  (78 shorter events, 13.0 us)
Async XLA Ops:
  1.8 5.9 %collective-permute-start = (bf16[64,512]{1,0:T(8,128)(2,1)S(1)}, bf16[64,512]{1,0:T(8,128)(2,1)S(1)}, u32[]{:S(2)}, u32[]{:S(2)}) collective-permute-start(bf16[64,512]{1,0:T(8,128)(2,1)S(1)} %get-tuple-element.41), channel_id=1, source_target_pairs={{0,1},{1,0},{2,3},{3,2},{4,5},{5,4},{6,7},{7,6},{8,9},{9,8},{10,11... | collective-permute-start | bytes 196616 | tf_op jit(solution)/shard_map/ppermute | solution.py:74
  7.7 6.9 %collective-permute-start.1 = (bf16[128,512]{1,0:T(8,128)(2,1)S(1)}, bf16[128,512]{1,0:T(8,128)(2,1)S(1)}, u32[]{:S(2)}, u32[]{:S(2)}) collective-permute-start(bf16[128,512]{1,0:T(8,128)(2,1)S(1)} %maximum_select_fusion), channel_id=1, source_target_pairs={{0,16},{16,32},{32,48},{48,0},{1,17},{17,33},{33,49},{49,1},{2,18}... | collective-permute-start | bytes 393224 | tf_op jit(solution)/shard_map/ppermute | solution.py:74
  9.3 6.0 %collective-permute-start.2 = (bf16[128,512]{1,0:T(8,128)(2,1)S(1)}, bf16[128,512]{1,0:T(8,128)(2,1)S(1)}, u32[]{:S(2)}, u32[]{:S(2)}) collective-permute-start(bf16[128,512]{1,0:T(8,128)(2,1)S(1)} %maximum_select_fusion), channel_id=1, source_target_pairs={{0,48},{16,0},{32,16},{48,32},{1,49},{17,1},{33,17},{49,33},{2,50}... | collective-permute-start | bytes 393224 | tf_op jit(solution)/shard_map/ppermute | solution.py:74
  11.0 7.0 %collective-permute-start.3 = (bf16[128,512]{1,0:T(8,128)(2,1)S(1)}, bf16[128,512]{1,0:T(8,128)(2,1)S(1)}, u32[]{:S(2)}, u32[]{:S(2)}) collective-permute-start(bf16[128,512]{1,0:T(8,128)(2,1)S(1)} %maximum_select_fusion), channel_id=1, source_target_pairs={{0,32},{16,48},{32,0},{48,16},{1,33},{17,49},{33,1},{49,17},{2,34}... | collective-permute-start | bytes 393224 | tf_op jit(solution)/shard_map/ppermute | solution.py:74
  14.0 13.8 %collective-permute-start.7 = (bf16[64,4096]{1,0:T(8,128)(2,1)S(1)}, bf16[64,4096]{1,0:T(8,128)(2,1)S(1)}, u32[]{:S(2)}, u32[]{:S(2)}) collective-permute-start(bf16[64,4096]{1,0:T(8,128)(2,1)S(1)} %fusion.8.refs_0_), channel_id=1, source_target_pairs={{0,1},{1,128},{128,129},{129,0},{2,3},{3,130},{130,131},{131,2},{4... | collective-permute-start | bytes 1572872 | tf_op jit(solution)/shard_map/ppermute | solution.py:74
  18.1 13.0 %collective-permute-start.4 = (bf16[4,128,512]{2,1,0:T(8,128)(2,1)S(1)}, bf16[4,128,512]{2,1,0:T(8,128)(2,1)S(1)}, u32[]{:S(2)}, u32[]{:S(2)}) collective-permute-start(bf16[4,128,512]{2,1,0:T(8,128)(2,1)S(1)} %pad_maximum_fusion.refs_8_.refs_6_.refs_10_.refs_4_), channel_id=1, source_target_pairs={{0,2},{2,4},{4,6},{6,8},{8,10},{10,12},{12,14},{14,0},{1,3},{3,5},... | collective-permute-start | bytes 1572872 | tf_op jit(solution)/shard_map/ppermute | solution.py:74
  20.1 12.8 %collective-permute-start.5 = (bf16[4,128,512]{2,1,0:T(8,128)(2,1)S(1)}, bf16[4,128,512]{2,1,0:T(8,128)(2,1)S(1)}, u32[]{:S(2)}, u32[]{:S(2)}) collective-permute-start(bf16[4,128,512]{2,1,0:T(8,128)(2,1)S(1)} %pad_maximum_fusion.refs_8_.refs_6_.refs_10_.refs_4_), channel_id=1, source_target_pairs={{0,14},{2,0},{4,2},{6,4},{8,6},{10,8},{12,10},{14,12},{1,15},{3,1}... | collective-permute-start | bytes 1572872 | tf_op jit(solution)/shard_map/ppermute | solution.py:74
  20.2 12.7 %collective-permute-start.6 = (bf16[64,4096]{1,0:T(8,128)(2,1)S(1)}, bf16[64,4096]{1,0:T(8,128)(2,1)S(1)}, u32[]{:S(2)}, u32[]{:S(2)}) collective-permute-start(bf16[64,4096]{1,0:T(8,128)(2,1)S(1)} %fusion.8.refs_0_), channel_id=1, source_target_pairs={{0,64},{64,0},{1,65},{65,1},{2,66},{66,2},{3,67},{67,3},{4,68},{68... | collective-permute-start | bytes 1572872 | tf_op jit(solution)/shard_map/ppermute | solution.py:74
  20.2 20.1 %collective-permute-start.10 = (bf16[64,4096]{1,0:T(8,128)(2,1)S(1)}, bf16[64,4096]{1,0:T(8,128)(2,1)}, u32[]{:S(2)}, u32[]{:S(2)}) collective-permute-start(bf16[64,4096]{1,0:T(8,128)(2,1)S(1)} %fusion.8.refs_0_), channel_id=1, source_target_pairs={{0,129},{1,0},{128,1},{129,128},{2,131},{3,2},{130,3},{131,130},{4... | collective-permute-start | bytes 1572872 | tf_op jit(solution)/shard_map/ppermute | solution.py:74
  33.7 13.0 %collective-permute-start.8 = (bf16[4,128,512]{2,1,0:T(8,128)(2,1)S(1)}, bf16[4,128,512]{2,1,0:T(8,128)(2,1)S(1)}, u32[]{:S(2)}, u32[]{:S(2)}) collective-permute-start(bf16[4,128,512]{2,1,0:T(8,128)(2,1)S(1)} %collective-permute-done.4.refs_9_.refs_7_.refs_11_.refs_5_), channel_id=1, source_target_pairs={{0,2},{2,4},{4,6},{6,8},{8,10},{10,12},{12,14},{14,0},{1,3},{3,5},... | collective-permute-start | bytes 1572872 | tf_op jit(solution)/shard_map/ppermute | solution.py:74
  36.8 12.7 %collective-permute-start.9 = (bf16[4,128,512]{2,1,0:T(8,128)(2,1)S(1)}, bf16[4,128,512]{2,1,0:T(8,128)(2,1)S(1)}, u32[]{:S(2)}, u32[]{:S(2)}) collective-permute-start(bf16[4,128,512]{2,1,0:T(8,128)(2,1)S(1)} %collective-permute-done.5.refs_10_.refs_8_.refs_12_.refs_6_), channel_id=1, source_target_pairs={{0,14},{2,0},{4,2},{6,4},{8,6},{10,8},{12,10},{14,12},{1,15},{3,1}... | collective-permute-start | bytes 1572872 | tf_op jit(solution)/shard_map/ppermute | solution.py:74
  37.6 14.1 %collective-permute-start.13 = (bf16[64,4096]{1,0:T(8,128)(2,1)S(1)}, bf16[64,4096]{1,0:T(8,128)(2,1)S(1)}, u32[]{:S(2)}, u32[]{:S(2)}) collective-permute-start(bf16[64,4096]{1,0:T(8,128)(2,1)S(1)} %fusion.8.refs_0_), channel_id=1, source_target_pairs={{0,128},{1,129},{128,0},{129,1},{2,130},{3,131},{130,2},{131,3},{4... | collective-permute-start | bytes 1572872 | tf_op jit(solution)/shard_map/ppermute | solution.py:74
  40.3 11.3 %collective-permute-start.14 = (bf16[64,4096]{1,0:T(8,128)(2,1)}, bf16[64,4096]{1,0:T(8,128)(2,1)S(1)}, u32[]{:S(2)}, u32[]{:S(2)}) collective-permute-start(bf16[64,4096]{1,0:T(8,128)(2,1)} %copy-done), channel_id=1, source_target_pairs={{0,64},{64,0},{1,65},{65,1},{2,66},{66,2},{3,67},{67,3},{4,68},{68... | collective-permute-start | bytes 1572872 | tf_op jit(solution)/shard_map/ppermute | solution.py:74
  49.5 14.6 %copy-start.1 = (bf16[64,4096]{1,0:T(8,128)(2,1)S(1)}, bf16[64,4096]{1,0:T(8,128)(2,1)}, u32[]{:S(2)}) copy-start(bf16[64,4096]{1,0:T(8,128)(2,1)} %copy-done) | copy-start | bytes 1572868
  49.5 14.6 %copy-start.3 = (bf16[64,4096]{1,0:T(8,128)(2,1)S(1)}, bf16[64,4096]{1,0:T(8,128)(2,1)}, u32[]{:S(2)}) copy-start(bf16[64,4096]{1,0:T(8,128)(2,1)} %copy-done.2) | copy-start | bytes 1572868
  49.5 10.9 %collective-permute-start.11 = (bf16[4,128,512]{2,1,0:T(8,128)(2,1)S(1)}, bf16[4,128,512]{2,1,0:T(8,128)(2,1)S(1)}, u32[]{:S(2)}, u32[]{:S(2)}) collective-permute-start(bf16[4,128,512]{2,1,0:T(8,128)(2,1)S(1)} %collective-permute-done.8.refs_11_.refs_9_.refs_13_.refs_7_), channel_id=1, source_target_pairs={{0,2},{2,4},{4,6},{6,8},{8,10},{10,12},{12,14},{14,0},{1,3},{3,5},... | collective-permute-start | bytes 1572872 | tf_op jit(solution)/shard_map/ppermute | solution.py:74
  51.3 10.6 %collective-permute-start.12 = (bf16[4,128,512]{2,1,0:T(8,128)(2,1)S(1)}, bf16[4,128,512]{2,1,0:T(8,128)(2,1)S(1)}, u32[]{:S(2)}, u32[]{:S(2)}) collective-permute-start(bf16[4,128,512]{2,1,0:T(8,128)(2,1)S(1)} %collective-permute-done.9.refs_12_.refs_10_.refs_14_.refs_8_), channel_id=1, source_target_pairs={{0,14},{2,0},{4,2},{6,4},{8,6},{10,8},{12,10},{14,12},{1,15},{3,1}... | collective-permute-start | bytes 1572872 | tf_op jit(solution)/shard_map/ppermute | solution.py:74
  51.6 10.3 %collective-permute-start.15 = (bf16[64,4096]{1,0:T(8,128)(2,1)}, bf16[64,4096]{1,0:T(8,128)(2,1)S(1)}, u32[]{:S(2)}, u32[]{:S(2)}) collective-permute-start(bf16[64,4096]{1,0:T(8,128)(2,1)} %collective-permute-done.10.refs_6_), channel_id=1, source_target_pairs={{0,64},{64,0},{1,65},{65,1},{2,66},{66,2},{3,67},{67,3},{4,68},{68... | collective-permute-start | bytes 1572872 | tf_op jit(solution)/shard_map/ppermute | solution.py:74
  61.9 2.2 %collective-permute-start.16 = (bf16[64,4096]{1,0:T(8,128)(2,1)S(1)}, bf16[64,4096]{1,0:T(8,128)(2,1)S(1)}, u32[]{:S(2)}, u32[]{:S(2)}) collective-permute-start(bf16[64,4096]{1,0:T(8,128)(2,1)S(1)} %collective-permute-done.13.refs_2_), channel_id=1, source_target_pairs={{0,64},{64,0},{1,65},{65,1},{2,66},{66,2},{3,67},{67,3},{4,68},{68... | collective-permute-start | bytes 1572872 | tf_op jit(solution)/shard_map/ppermute | solution.py:74
  61.9 8.8 %collective-permute-start.17 = (bf16[2,128,512]{2,1,0:T(8,128)(2,1)S(1)}, bf16[2,128,512]{2,1,0:T(8,128)(2,1)S(1)}, u32[]{:S(2)}, u32[]{:S(2)}) collective-permute-start(bf16[2,128,512]{2,1,0:T(8,128)(2,1)S(1)} %slice.24), channel_id=1, source_target_pairs={{0,2},{2,4},{4,6},{6,8},{8,10},{10,12},{12,14},{14,0},{1,3},{3,5},... | collective-permute-start | bytes 786440 | tf_op jit(solution)/shard_map/ppermute | solution.py:74
  63.8 8.6 %collective-permute-start.18 = (bf16[2,128,512]{2,1,0:T(8,128)(2,1)S(1)}, bf16[2,128,512]{2,1,0:T(8,128)(2,1)S(1)}, u32[]{:S(2)}, u32[]{:S(2)}) collective-permute-start(bf16[2,128,512]{2,1,0:T(8,128)(2,1)S(1)} %slice.25), channel_id=1, source_target_pairs={{0,14},{2,0},{4,2},{6,4},{8,6},{10,8},{12,10},{14,12},{1,15},{3,1}... | collective-permute-start | bytes 786440 | tf_op jit(solution)/shard_map/ppermute | solution.py:74
  97.6 16.4 %collective-permute-start.20 = (bf16[2,2,16,4096]{3,2,1,0:T(8,128)(2,1)S(1)}, bf16[2,2,16,4096]{3,2,1,0:T(8,128)(2,1)S(1)}, u32[]{:S(2)}, u32[]{:S(2)}) collective-permute-start(bf16[2,2,16,4096]{3,2,1,0:T(8,128)(2,1)S(1)} %bitcast.37), channel_id=1, source_target_pairs={{0,1},{1,128},{128,129},{129,0},{2,3},{3,130},{130,131},{131,2},{4... | collective-permute-start | bytes 1572872 | tf_op jit(solution)/shard_map/ppermute | solution.py:74
  98.2 15.8 %collective-permute-start.21 = (bf16[2,2,16,4096]{3,2,1,0:T(8,128)(2,1)S(1)}, bf16[2,2,16,4096]{3,2,1,0:T(8,128)(2,1)S(1)}, u32[]{:S(2)}, u32[]{:S(2)}) collective-permute-start(bf16[2,2,16,4096]{3,2,1,0:T(8,128)(2,1)S(1)} %bitcast.38), channel_id=1, source_target_pairs={{0,129},{1,0},{128,1},{129,128},{2,131},{3,2},{130,3},{131,130},{4... | collective-permute-start | bytes 1572872 | tf_op jit(solution)/shard_map/ppermute | solution.py:74
  104.7 9.3 %collective-permute-start.19 = (bf16[2,2,16,4096]{3,2,1,0:T(8,128)(2,1)S(1)}, bf16[2,2,16,4096]{3,2,1,0:T(8,128)(2,1)S(1)}, u32[]{:S(2)}, u32[]{:S(2)}) collective-permute-start(bf16[2,2,16,4096]{3,2,1,0:T(8,128)(2,1)S(1)} %bitcast.39), channel_id=1, source_target_pairs={{0,64},{64,0},{1,65},{65,1},{2,66},{66,2},{3,67},{67,3},{4,68},{68... | collective-permute-start | bytes 1572872 | tf_op jit(solution)/shard_map/ppermute | solution.py:74
  114.0 3.8 %collective-permute-start.24 = (bf16[2,2,16,4096]{3,2,1,0:T(8,128)(2,1)S(1)}, bf16[2,2,16,4096]{3,2,1,0:T(8,128)(2,1)S(1)}, u32[]{:S(2)}, u32[]{:S(2)}) collective-permute-start(bf16[2,2,16,4096]{3,2,1,0:T(8,128)(2,1)S(1)} %collective-permute-done.20.refs_2_.refs_6_), channel_id=1, source_target_pairs={{0,64},{64,0},{1,65},{65,1},{2,66},{66,2},{3,67},{67,3},{4,68},{68... | collective-permute-start | bytes 1572872 | tf_op jit(solution)/shard_map/ppermute | solution.py:74
  114.1 3.7 %collective-permute-start.25 = (bf16[2,2,16,4096]{3,2,1,0:T(8,128)(2,1)S(1)}, bf16[2,2,16,4096]{3,2,1,0:T(8,128)(2,1)S(1)}, u32[]{:S(2)}, u32[]{:S(2)}) collective-permute-start(bf16[2,2,16,4096]{3,2,1,0:T(8,128)(2,1)S(1)} %collective-permute-done.21.refs_4_.refs_8_), channel_id=1, source_target_pairs={{0,64},{64,0},{1,65},{65,1},{2,66},{66,2},{3,67},{67,3},{4,68},{68... | collective-permute-start | bytes 1572872 | tf_op jit(solution)/shard_map/ppermute | solution.py:74
  114.6 9.6 %collective-permute-start.22 = (bf16[1,2,16,4096]{3,2,1,0:T(8,128)(2,1)S(1)}, bf16[1,2,16,4096]{3,2,1,0:T(8,128)(2,1)S(1)}, u32[]{:S(2)}, u32[]{:S(2)}) collective-permute-start(bf16[1,2,16,4096]{3,2,1,0:T(8,128)(2,1)S(1)} %slice.30), channel_id=1, source_target_pairs={{0,1},{1,128},{128,129},{129,0},{2,3},{3,130},{130,131},{131,2},{4... | collective-permute-start | bytes 786440 | tf_op jit(solution)/shard_map/ppermute | solution.py:74
  115.7 8.5 %collective-permute-start.23 = (bf16[1,2,16,4096]{3,2,1,0:T(8,128)(2,1)S(1)}, bf16[1,2,16,4096]{3,2,1,0:T(8,128)(2,1)S(1)}, u32[]{:S(2)}, u32[]{:S(2)}) collective-permute-start(bf16[1,2,16,4096]{3,2,1,0:T(8,128)(2,1)S(1)} %slice.31), channel_id=1, source_target_pairs={{0,129},{1,0},{128,1},{129,128},{2,131},{3,2},{130,3},{131,130},{4... | collective-permute-start | bytes 786440 | tf_op jit(solution)/shard_map/ppermute | solution.py:74
  124.2 2.0 %collective-permute-start.26 = (bf16[1,2,16,4096]{3,2,1,0:T(8,128)(2,1)S(1)}, bf16[1,2,16,4096]{3,2,1,0:T(8,128)(2,1)S(1)}, u32[]{:S(2)}, u32[]{:S(2)}) collective-permute-start(bf16[1,2,16,4096]{3,2,1,0:T(8,128)(2,1)S(1)} %collective-permute-done.22.refs_2_.refs_0_), channel_id=1, source_target_pairs={{0,64},{64,0},{1,65},{65,1},{2,66},{66,2},{3,67},{67,3},{4,68},{68... | collective-permute-start | bytes 786440 | tf_op jit(solution)/shard_map/ppermute | solution.py:74
  124.2 2.0 %collective-permute-start.27 = (bf16[1,2,16,4096]{3,2,1,0:T(8,128)(2,1)S(1)}, bf16[1,2,16,4096]{3,2,1,0:T(8,128)(2,1)S(1)}, u32[]{:S(2)}, u32[]{:S(2)}) collective-permute-start(bf16[1,2,16,4096]{3,2,1,0:T(8,128)(2,1)S(1)} %collective-permute-done.23.refs_3_.refs_1_), channel_id=1, source_target_pairs={{0,64},{64,0},{1,65},{65,1},{2,66},{66,2},{3,67},{67,3},{4,68},{68... | collective-permute-start | bytes 786440 | tf_op jit(solution)/shard_map/ppermute | solution.py:74
  124.8 7.5 %collective-permute-start.28 = (bf16[192,512]{1,0:T(8,128)(2,1)S(1)}, bf16[192,512]{1,0:T(8,128)(2,1)S(1)}, u32[]{:S(2)}, u32[]{:S(2)}) collective-permute-start(bf16[192,512]{1,0:T(8,128)(2,1)S(1)} %sent_rows.2), channel_id=1, source_target_pairs={{0,1},{1,0},{2,3},{3,2},{4,5},{5,4},{6,7},{7,6},{8,9},{9,8},{10,11... | collective-permute-start | bytes 589832 | tf_op jit(solution)/shard_map/ppermute | solution.py:74
  127.6 5.5 %collective-permute-start.29 = (bf16[64,512]{1,0:T(8,128)(2,1)S(1)}, bf16[64,512]{1,0:T(8,128)(2,1)S(1)}, u32[]{:S(2)}, u32[]{:S(2)}) collective-permute-start(bf16[64,512]{1,0:T(8,128)(2,1)S(1)} %sent_rows.3), channel_id=1, source_target_pairs={{0,1},{1,0},{2,3},{3,2},{4,5},{5,4},{6,7},{7,6},{8,9},{9,8},{10,11... | collective-permute-start | bytes 196616 | tf_op jit(solution)/shard_map/ppermute | solution.py:74
  (5 other events, 15.5 us)

commit v13 on v9

--- a/solution.py
+++ b/solution.py
@@ -74,29 +74,27 @@
     return lax.ppermute(array, axis, [(k, (k + step) % size) for k in range(size)])
 
 
-def split_kernel(first_ref, basis_ref, kept_ref, sent_ref):
+def split_kernel(place_ref, basis_ref, kept_ref):
     source = lax.broadcasted_iota(jnp.int32, (256, 128), 0)
     target = lax.broadcasted_iota(jnp.int32, (256, 128), 1)
-    for half, ref in ((first_ref[0], kept_ref), (1 - first_ref[0], sent_ref)):
-        match = source == (target // 8) * 16 + half * 8 + lax.rem(target, 8)
-        chosen = match.astype(jnp.float32).astype(jnp.bfloat16)
-        for block in range(basis_ref.shape[1] // 256):
-            moved = jnp.dot(
-                basis_ref[:, block * 256 : block * 256 + 256],
-                chosen,
-                preferred_element_type=jnp.float32,
-            )
-            ref[:, block * 128 : block * 128 + 128] = moved.astype(jnp.bfloat16)
+    match = source == (target // 8) * 16 + place_ref[0] * 8 + lax.rem(target, 8)
+    chosen = match.astype(jnp.float32).astype(jnp.bfloat16)
+    for block in range(basis_ref.shape[1] // 256):
+        moved = jnp.dot(
+            basis_ref[:, block * 256 : block * 256 + 256],
+            chosen,
+            preferred_element_type=jnp.float32,
+        )
+        kept_ref[:, block * 128 : block * 128 + 128] = moved.astype(jnp.bfloat16)
 
 
 def split_columns(place, basis):
     rows, columns = basis.shape
-    half = jax.ShapeDtypeStruct((rows, columns // 2), basis.dtype)
     return pl.pallas_call(
         split_kernel,
-        out_shape=(half, half),
+        out_shape=jax.ShapeDtypeStruct((rows, columns // 2), basis.dtype),
         in_specs=[SMEM, VMEM],
-        out_specs=(VMEM, VMEM),
+        out_specs=VMEM,
         compiler_params=pltpu.CompilerParams(vmem_limit_bytes=GRANT),
         name="split_columns",
     )(place, basis)
@@ -318,9 +316,13 @@
     ny, nz = lax.axis_size("y"), lax.axis_size("z")
     place = jnp.stack([lo, time, y, z]).astype(jnp.int32)
 
-    kept, sent = split_columns(place, eigen_basis)
-    other = shifted(sent, "lo", 1)
-    mine = jnp.where(lo == 0, jnp.concatenate([kept, other]), jnp.concatenate([other, kept]))
+    other = shifted(eigen_basis, "lo", 1)
+    pair = jnp.where(
+        lo == 0,
+        jnp.concatenate([eigen_basis, other]),
+        jnp.concatenate([other, eigen_basis]),
+    )
+    mine = split_columns(place, pair)
     pseudo = moments(event_counts, latent_mean, latent_var).astype(jnp.bfloat16)[0]
     mine, pseudo = lax.optimization_barrier((mine, pseudo))
     before, after = shifted(pseudo, RING, 1), shifted(pseudo, RING, 3)

time: 131 us -> 130 us (level)
  waiting for transfers between devices: 52.8 us -> 48.6 us
  starting transfers between devices: 34.2 us -> 36.9 us
  blocking collectives: 19.9 us -> 21.4 us
    ppermute x30, waiting for transfers between devices: 52.8 us -> 48.6 us  [shifted(): lax.ppermute(array, axis, [(k, (k + step) % size) for k in range(size)])]
    ppermute x30, starting transfers between devices: 34.2 us -> 36.9 us  [shifted(): lax.ppermute(array, axis, [(k, (k + step) % size) for k in range(size)])]
    all_to_all x1, blocking collectives: 19.9 us -> 21.4 us  [local(): got = lax.all_to_all(sent, ('y', 'z'), 0, 0, tiled=True)]
  transfers between devices with their start and end apart: 30 -> 30, of which waited for: 13 -> 12; matrix products, arithmetic and copies ran while one was open for 4% -> 5% of each run, Pallas kernels for 7% -> 7%
where the time goes in v13:
time: 130 us
  waiting for transfers between devices  48.6 us (37%)
  starting transfers between devices  36.9 us (28%)
  blocking collectives  21.4 us (16%)
  Pallas kernels  13.9 us (11%)
  other arithmetic  4.72 us (4%)
  local copies, waits for them, and re-layouts  3.13 us (2%)
    ppermute x30, waiting for transfers between devices, shifted(): lax.ppermute(array, axis, [(k, (k + step) % size) for k in range(size)])  48.6 us
    ppermute x30, starting transfers between devices, shifted(): lax.ppermute(array, axis, [(k, (k + step) % size) for k in range(size)])  36.9 us
    all_to_all x1, blocking collectives, local(): got = lax.all_to_all(sent, ('y', 'z'), 0, 0, tiled=True)  21.4 us
    squeeze x1, other arithmetic, local(): moments(event_counts, latent_mean, latent_var).astype(jnp.bfloat16)[0]  4.33 us
    pallas_call x1, Pallas kernels, near_product(): pl.pallas_call(near_kernel, out_shape=jax.ShapeDtypeStruct((rows, width),...  3.14 us
    pallas_call x2, Pallas kernels, sent_rows(): pl.pallas_call(sent_kernel, out_shape=jax.ShapeDtypeStruct((count, width)...  2.94 us
    pallas_call x1, Pallas kernels, kept_rows(): pl.pallas_call(kept_kernel, out_shape=jax.ShapeDtypeStruct((times, rows,...  2.87 us
  transfers between devices with their start and end apart: 30, of which 12 were waited for; matrix products, arithmetic and copies ran while one was open for 5% of the time, Pallas kernels for 7%

profile of v13, /device:TPU:32, one launch (start us, length us, event | category | flops | bytes accessed | tf_op | source)
XLA Modules:
  0.0 129.5 jit_solution(13862509343668797631)
XLA Ops:
  0.0 1.5 %collective-permute-start = (bf16[64,1024]{1,0:T(8,128)(2,1)}, bf16[64,1024]{1,0:T(8,128)(2,1)S(1)}, u32[]{:S(2)}, u32[]{:S(2)}) collective-permute-start(bf16[64,1024]{1,0:T(8,128)(2,1)} %param.11), channel_id=1, source_target_pairs={{0,1},{1,0},{2,3},{3,2},{4,5},{5,4},{6,7},{7,6},{8,9},{9,8},{10,11... | collective-permute-start | bytes 393224 | tf_op jit(solution)/shard_map/ppermute | solution.py:74
  1.5 4.3 %fusion.8.refs_0_ = bf16[64,4096]{1,0:T(8,128)(2,1)S(1)} fusion(s32[1,64,4096]{2,1,0:T(8,128)} %param.8, f32[1,64,4096]{2,1,0:T(8,128)} %param.10, f32[1,64,4096]{2,1,0:T(8,128)} %param.9), kind=kLoop, calls=%fused_computation.16 | loop fusion | flops 17563648 | bytes 3670016 | tf_op jit(solution)/shard_map/squeeze | solution.py:326
  6.8 1.7 %collective-permute-start.1 = (bf16[128,512]{1,0:T(8,128)(2,1)S(1)}, bf16[128,512]{1,0:T(8,128)(2,1)S(1)}, u32[]{:S(2)}, u32[]{:S(2)}) collective-permute-start(bf16[128,512]{1,0:T(8,128)(2,1)S(1)} %split_columns.1), channel_id=1, source_target_pairs={{0,16},{16,32},{32,48},{48,0},{1,17},{17,33},{33,49},{49,1},{2,18}... | collective-permute-start | bytes 393224 | tf_op jit(solution)/shard_map/ppermute | solution.py:74
  8.4 1.7 %collective-permute-start.2 = (bf16[128,512]{1,0:T(8,128)(2,1)S(1)}, bf16[128,512]{1,0:T(8,128)(2,1)S(1)}, u32[]{:S(2)}, u32[]{:S(2)}) collective-permute-start(bf16[128,512]{1,0:T(8,128)(2,1)S(1)} %split_columns.1), channel_id=1, source_target_pairs={{0,48},{16,0},{32,16},{48,32},{1,49},{17,1},{33,17},{49,33},{2,50}... | collective-permute-start | bytes 393224 | tf_op jit(solution)/shard_map/ppermute | solution.py:74
  10.1 2.0 %collective-permute-start.3 = (bf16[128,512]{1,0:T(8,128)(2,1)S(1)}, bf16[128,512]{1,0:T(8,128)(2,1)S(1)}, u32[]{:S(2)}, u32[]{:S(2)}) collective-permute-start(bf16[128,512]{1,0:T(8,128)(2,1)S(1)} %split_columns.1), channel_id=1, source_target_pairs={{0,32},{16,48},{32,0},{48,16},{1,33},{17,49},{33,1},{49,17},{2,34}... | collective-permute-start | bytes 393224 | tf_op jit(solution)/shard_map/ppermute | solution.py:74
  14.1 2.2 %collective-permute-start.7 = (bf16[64,4096]{1,0:T(8,128)(2,1)S(1)}, bf16[64,4096]{1,0:T(8,128)(2,1)S(1)}, u32[]{:S(2)}, u32[]{:S(2)}) collective-permute-start(bf16[64,4096]{1,0:T(8,128)(2,1)S(1)} %fusion.8.refs_0_), channel_id=1, source_target_pairs={{0,129},{1,0},{128,1},{129,128},{2,131},{3,2},{130,3},{131,130},{4... | collective-permute-start | bytes 1572872 | tf_op jit(solution)/shard_map/ppermute | solution.py:74
  17.1 2.0 %collective-permute-start.4 = (bf16[4,128,512]{2,1,0:T(8,128)(2,1)S(1)}, bf16[4,128,512]{2,1,0:T(8,128)(2,1)S(1)}, u32[]{:S(2)}, u32[]{:S(2)}) collective-permute-start(bf16[4,128,512]{2,1,0:T(8,128)(2,1)S(1)} %pad_maximum_fusion.refs_8_.refs_6_.refs_10_.refs_4_), channel_id=1, source_target_pairs={{0,2},{2,4},{4,6},{6,8},{8,10},{10,12},{12,14},{14,0},{1,3},{3,5},... | collective-permute-start | bytes 1572872 | tf_op jit(solution)/shard_map/ppermute | solution.py:74
  19.3 1.9 %collective-permute-done.10.refs_1_ = bf16[64,4096]{1,0:T(8,128)(2,1)S(1)} collective-permute-done((bf16[64,4096]{1,0:T(8,128)(2,1)S(1)}, bf16[64,4096]{1,0:T(8,128)(2,1)S(1)}, u32[]{:S(2)}, u32[]{:S(2)}) %collective-permute-start.10) | collective-permute-done | bytes 524320 | tf_op jit(solution)/shard_map/ppermute | solution.py:74
  21.9 2.7 %collective-permute-start.11 = (bf16[64,4096]{1,0:T(8,128)(2,1)S(1)}, bf16[64,4096]{1,0:T(8,128)(2,1)}, u32[]{:S(2)}, u32[]{:S(2)}) collective-permute-start(bf16[64,4096]{1,0:T(8,128)(2,1)S(1)} %fusion.8.refs_0_), channel_id=1, source_target_pairs={{0,128},{1,129},{128,0},{129,1},{2,130},{3,131},{130,2},{131,3},{4... | collective-permute-start | bytes 1572872 | tf_op jit(solution)/shard_map/ppermute | solution.py:74
  24.7 2.8 %collective-permute-done.6.refs_4_ = bf16[64,4096]{1,0:T(8,128)(2,1)S(1)} collective-permute-done((bf16[64,4096]{1,0:T(8,128)(2,1)S(1)}, bf16[64,4096]{1,0:T(8,128)(2,1)S(1)}, u32[]{:S(2)}, u32[]{:S(2)}) %collective-permute-start.6) | collective-permute-done | bytes 524320 | tf_op jit(solution)/shard_map/ppermute | solution.py:74
  27.5 9.9 %collective-permute-done.7.refs_6_ = bf16[64,4096]{1,0:T(8,128)(2,1)S(1)} collective-permute-done((bf16[64,4096]{1,0:T(8,128)(2,1)S(1)}, bf16[64,4096]{1,0:T(8,128)(2,1)S(1)}, u32[]{:S(2)}, u32[]{:S(2)}) %collective-permute-start.7) | collective-permute-done | bytes 524320 | tf_op jit(solution)/shard_map/ppermute | solution.py:74
  37.4 2.0 %collective-permute-start.8 = (bf16[4,128,512]{2,1,0:T(8,128)(2,1)S(1)}, bf16[4,128,512]{2,1,0:T(8,128)(2,1)S(1)}, u32[]{:S(2)}, u32[]{:S(2)}) collective-permute-start(bf16[4,128,512]{2,1,0:T(8,128)(2,1)S(1)} %collective-permute-done.4.refs_9_.refs_7_.refs_11_.refs_5_), channel_id=1, source_target_pairs={{0,2},{2,4},{4,6},{6,8},{8,10},{10,12},{12,14},{14,0},{1,3},{3,5},... | collective-permute-start | bytes 1572872 | tf_op jit(solution)/shard_map/ppermute | solution.py:74
  40.8 6.6 %collective-permute-done.8.refs_11_.refs_9_.refs_13_.refs_7_ = bf16[4,128,512]{2,1,0:T(8,128)(2,1)S(1)} collective-permute-done((bf16[4,128,512]{2,1,0:T(8,128)(2,1)S(1)}, bf16[4,128,512]{2,1,0:T(8,128)(2,1)S(1)}, u32[]{:S(2)}, u32[]{:S(2)}) %collective-permute-start.8) | collective-permute-done | bytes 524320 | tf_op jit(solution)/shard_map/ppermute | solution.py:74
  47.4 2.8 %collective-permute-done.9.refs_12_.refs_10_.refs_14_.refs_8_ = bf16[4,128,512]{2,1,0:T(8,128)(2,1)S(1)} collective-permute-done((bf16[4,128,512]{2,1,0:T(8,128)(2,1)S(1)}, bf16[4,128,512]{2,1,0:T(8,128)(2,1)S(1)}, u32[]{:S(2)}, u32[]{:S(2)}) %collective-permute-start.9) | collective-permute-done | bytes 524320 | tf_op jit(solution)/shard_map/ppermute | solution.py:74
  50.5 2.6 %collective-permute-start.13 = (bf16[4,128,512]{2,1,0:T(8,128)(2,1)S(1)}, bf16[4,128,512]{2,1,0:T(8,128)(2,1)S(1)}, u32[]{:S(2)}, u32[]{:S(2)}) collective-permute-start(bf16[4,128,512]{2,1,0:T(8,128)(2,1)S(1)} %collective-permute-done.9.refs_12_.refs_10_.refs_14_.refs_8_), channel_id=1, source_target_pairs={{0,14},{2,0},{4,2},{6,4},{8,6},{10,8},{12,10},{14,12},{1,15},{3,1}... | collective-permute-start | bytes 1572872 | tf_op jit(solution)/shard_map/ppermute | solution.py:74
  53.1 7.2 %collective-permute-done.12.refs_13_.refs_11_.refs_15_.refs_9_ = bf16[4,128,512]{2,1,0:T(8,128)(2,1)S(1)} collective-permute-done((bf16[4,128,512]{2,1,0:T(8,128)(2,1)S(1)}, bf16[4,128,512]{2,1,0:T(8,128)(2,1)S(1)}, u32[]{:S(2)}, u32[]{:S(2)}) %collective-permute-start.12) | collective-permute-done | bytes 524320 | tf_op jit(solution)/shard_map/ppermute | solution.py:74
  60.3 5.3 %collective-permute-start.17 = (bf16[2,128,512]{2,1,0:T(8,128)(2,1)S(1)}, bf16[2,128,512]{2,1,0:T(8,128)(2,1)S(1)}, u32[]{:S(2)}, u32[]{:S(2)}) collective-permute-start(bf16[2,128,512]{2,1,0:T(8,128)(2,1)S(1)} %slice.24), channel_id=1, source_target_pairs={{0,2},{2,4},{4,6},{6,8},{8,10},{10,12},{12,14},{14,0},{1,3},{3,5},... | collective-permute-start | bytes 786440 | tf_op jit(solution)/shard_map/ppermute | solution.py:74
  66.8 3.1 %near_product.1.refs_10_ = f32[512,512]{1,0:T(8,128)S(1)} custom-call(s32[4]{0:T(128)S(1)} %pad_add_fusion.place_ref, bf16[64,4096]{1,0:T(8,128)(2,1)S(1)} %fusion.8.refs_0_, bf16[64,4096]{1,0:T(8,128)(2,1)S(1)} %copy-done.5, bf16[64,4096]{1,0:T(8,128)(2,1)} %collective-permute-done.11.refs_2_, bf16[64,4096]{1,0:T(8,128)(2,1)S(1)} %collective-permute-done.14.refs_3_, ...), custom_call_target="tpu_custom_call" | custom-call | flops 1610612736 | bytes 8388608 | tf_op jit(solution)/shard_map/near_product/pallas_call | solution.py:135
  70.0 3.6 %collective-permute-done.18.refs_9_.refs_14_.refs_18_.refs_12_ = bf16[2,128,512]{2,1,0:T(8,128)(2,1)S(1)} collective-permute-done((bf16[2,128,512]{2,1,0:T(8,128)(2,1)S(1)}, bf16[2,128,512]{2,1,0:T(8,128)(2,1)S(1)}, u32[]{:S(2)}, u32[]{:S(2)}) %collective-permute-start.18) | collective-permute-done | bytes 262176 | tf_op jit(solution)/shard_map/ppermute | solution.py:74
  73.6 2.0 %first_product.1 = bf16[512,512]{1,0:T(8,128)(2,1)S(1)} custom-call(f32[8,4]{1,0:T(8,128)S(1)} %broadcast_select_fusion.mix_ref, s32[4]{0:T(128)S(1)} %pad_add_fusion.place_ref, bf16[64,4096]{1,0:T(8,128)(2,1)S(1)} %fusion.8.refs_0_, bf16[64,4096]{1,0:T(8,128)(2,1)S(1)} %copy-done.5, bf16[64,4096]{1,0:T(8,128)(2,1)} %collective-permute-done.11.refs_2_, ...), custom_call_target="tpu_custom_call" | custom-call | flops 536870912 | bytes 4194304 | tf_op jit(solution)/shard_map/first_product/pallas_call | solution.py:173
  75.6 21.4 %all_to_all.5 = bf16[32,16,512]{2,1,0:T(8,128)(2,1)S(1)} all-to-all(bf16[32,16,512]{2,1,0:T(8,128)(2,1)S(1)} %bitcast.42), channel_id=1, replica_groups=mesh['hi'=2,'core'=2,'y'=4,'z'=8,'lo'=2] {'y','z'}, dimensions={0} | all-to-all | bytes 1048576 | tf_op jit(solution)/shard_map/all_to_all | solution.py:369
  97.2 3.7 %collective-permute-start.21 = (bf16[2,2,16,4096]{3,2,1,0:T(8,128)(2,1)S(1)}, bf16[2,2,16,4096]{3,2,1,0:T(8,128)(2,1)S(1)}, u32[]{:S(2)}, u32[]{:S(2)}) collective-permute-start(bf16[2,2,16,4096]{3,2,1,0:T(8,128)(2,1)S(1)} %bitcast.38), channel_id=1, source_target_pairs={{0,129},{1,0},{128,1},{129,128},{2,131},{3,2},{130,3},{131,130},{4... | collective-permute-start | bytes 1572872 | tf_op jit(solution)/shard_map/ppermute | solution.py:74
  100.9 7.1 %collective-permute-done.20.refs_2_.refs_6_ = bf16[2,2,16,4096]{3,2,1,0:T(8,128)(2,1)S(1)} collective-permute-done((bf16[2,2,16,4096]{3,2,1,0:T(8,128)(2,1)S(1)}, bf16[2,2,16,4096]{3,2,1,0:T(8,128)(2,1)S(1)}, u32[]{:S(2)}, u32[]{:S(2)}) %collective-permute-start.20) | collective-permute-done | bytes 524320 | tf_op jit(solution)/shard_map/ppermute | solution.py:74
  108.7 1.4 %collective-permute-start.22 = (bf16[1,2,16,4096]{3,2,1,0:T(8,128)(2,1)S(1)}, bf16[1,2,16,4096]{3,2,1,0:T(8,128)(2,1)S(1)}, u32[]{:S(2)}, u32[]{:S(2)}) collective-permute-start(bf16[1,2,16,4096]{3,2,1,0:T(8,128)(2,1)S(1)} %slice.30), channel_id=1, source_target_pairs={{0,1},{1,128},{128,129},{129,0},{2,3},{3,130},{130,131},{131,2},{4... | collective-permute-start | bytes 786440 | tf_op jit(solution)/shard_map/ppermute | solution.py:74
  110.0 1.9 %collective-permute-start.23 = (bf16[1,2,16,4096]{3,2,1,0:T(8,128)(2,1)S(1)}, bf16[1,2,16,4096]{3,2,1,0:T(8,128)(2,1)S(1)}, u32[]{:S(2)}, u32[]{:S(2)}) collective-permute-start(bf16[1,2,16,4096]{3,2,1,0:T(8,128)(2,1)S(1)} %slice.31), channel_id=1, source_target_pairs={{0,129},{1,0},{128,1},{129,128},{2,131},{3,2},{130,3},{131,130},{4... | collective-permute-start | bytes 786440 | tf_op jit(solution)/shard_map/ppermute | solution.py:74
  112.0 1.6 %sent_rows.2 = bf16[192,512]{1,0:T(8,128)(2,1)S(1)} custom-call(s32[4]{0:T(128)S(1)} %pad_add_fusion.place_ref, bf16[2,2,16,4096]{3,2,1,0:T(8,128)(2,1)S(1)} %bitcast.40, bf16[2,2,16,4096]{3,2,1,0:T(8,128)(2,1)S(1)} %collective-permute-done.19.refs_1_, bf16[2,2,16,4096]{3,2,1,0:T(8,128)(2,1)S(1)} %collective-permute-done.20.refs_2_.refs_6_, ...), custom_call_target="tpu_custom_call" | custom-call | flops 805306368 | bytes 6291456 | tf_op jit(solution)/shard_map/sent_rows/pallas_call | solution.py:219
  113.5 5.0 %collective-permute-done.22.refs_2_.refs_0_ = bf16[1,2,16,4096]{3,2,1,0:T(8,128)(2,1)S(1)} collective-permute-done((bf16[1,2,16,4096]{3,2,1,0:T(8,128)(2,1)S(1)}, bf16[1,2,16,4096]{3,2,1,0:T(8,128)(2,1)S(1)}, u32[]{:S(2)}, u32[]{:S(2)}) %collective-permute-start.22) | collective-permute-done | bytes 262176 | tf_op jit(solution)/shard_map/ppermute | solution.py:74
  119.1 1.6 %collective-permute-start.28 = (bf16[192,512]{1,0:T(8,128)(2,1)S(1)}, bf16[192,512]{1,0:T(8,128)(2,1)S(1)}, u32[]{:S(2)}, u32[]{:S(2)}) collective-permute-start(bf16[192,512]{1,0:T(8,128)(2,1)S(1)} %sent_rows.2), channel_id=1, source_target_pairs={{0,1},{1,0},{2,3},{3,2},{4,5},{5,4},{6,7},{7,6},{8,9},{9,8},{10,11... | collective-permute-start | bytes 589832 | tf_op jit(solution)/shard_map/ppermute | solution.py:74
  120.8 1.4 %sent_rows.3 = bf16[64,512]{1,0:T(8,128)(2,1)S(1)} custom-call(s32[4]{0:T(128)S(1)} %pad_add_fusion.place_ref, bf16[1,2,16,4096]{3,2,1,0:T(8,128)(2,1)S(1)} %collective-permute-done.22.refs_2_.refs_0_, bf16[1,2,16,4096]{3,2,1,0:T(8,128)(2,1)S(1)} %collective-permute-done.23.refs_3_.refs_1_, ...), custom_call_target="tpu_custom_call" | custom-call | flops 268435456 | bytes 6291456 | tf_op jit(solution)/shard_map/sent_rows/pallas_call | solution.py:219
  122.2 1.3 %collective-permute-start.29 = (bf16[64,512]{1,0:T(8,128)(2,1)S(1)}, bf16[64,512]{1,0:T(8,128)(2,1)S(1)}, u32[]{:S(2)}, u32[]{:S(2)}) collective-permute-start(bf16[64,512]{1,0:T(8,128)(2,1)S(1)} %sent_rows.3), channel_id=1, source_target_pairs={{0,1},{1,0},{2,3},{3,2},{4,5},{5,4},{6,7},{7,6},{8,9},{9,8},{10,11... | collective-permute-start | bytes 196616 | tf_op jit(solution)/shard_map/ppermute | solution.py:74
  123.5 2.9 %kept_rows.1.kept_ref = f32[4,64,1024]{2,1,0:T(8,128)S(1)} custom-call(s32[4]{0:T(128)S(1)} %pad_add_fusion.place_ref, s32[8]{0:T(128)S(1)} %get-tuple-element.80.slice_ref, bf16[2,2,16,4096]{3,2,1,0:T(8,128)(2,1)S(1)} %bitcast.41, bf16[2,2,16,4096]{3,2,1,0:T(8,128)(2,1)S(1)} %collective-permute-done.19.refs_1_, ...), custom_call_target="tpu_custom_call" | custom-call | flops 1073741824 | bytes 6291456 | tf_op jit(solution)/shard_map/kept_rows/pallas_call | solution.py:261
  127.3 2.2 %whitened_gradient.1 = f32[64,4,1024]{2,1,0:T(4,128)} custom-call(s32[4]{0:T(128)S(1)} %pad_add_fusion.place_ref, s32[8]{0:T(128)S(1)} %pad_add_fusion.1.slice_ref, f32[4,64,1024]{2,1,0:T(8,128)S(1)} %kept_rows.1.kept_ref, bf16[192,512]{1,0:T(8,128)(2,1)S(1)} %collective-permute-done.28.early_ref, bf16[64,512]{1,0:T(8,128)(2,1)S(1)} %collective-permute-done.29.late_ref, ...), custom_call_target="tpu_custom_call" | custom-call | tf_op jit(solution)/shard_map/whitened_gradient/pallas_call | solution.py:298
  (82 shorter events, 9.3 us)
Async XLA Ops:
  0.0 5.9 %collective-permute-start = (bf16[64,1024]{1,0:T(8,128)(2,1)}, bf16[64,1024]{1,0:T(8,128)(2,1)S(1)}, u32[]{:S(2)}, u32[]{:S(2)}) collective-permute-start(bf16[64,1024]{1,0:T(8,128)(2,1)} %param.11), channel_id=1, source_target_pairs={{0,1},{1,0},{2,3},{3,2},{4,5},{5,4},{6,7},{7,6},{8,9},{9,8},{10,11... | collective-permute-start | bytes 393224 | tf_op jit(solution)/shard_map/ppermute | solution.py:74
  6.8 9.6 %collective-permute-start.1 = (bf16[128,512]{1,0:T(8,128)(2,1)S(1)}, bf16[128,512]{1,0:T(8,128)(2,1)S(1)}, u32[]{:S(2)}, u32[]{:S(2)}) collective-permute-start(bf16[128,512]{1,0:T(8,128)(2,1)S(1)} %split_columns.1), channel_id=1, source_target_pairs={{0,16},{16,32},{32,48},{48,0},{1,17},{17,33},{33,49},{49,1},{2,18}... | collective-permute-start | bytes 393224 | tf_op jit(solution)/shard_map/ppermute | solution.py:74
  8.4 7.9 %collective-permute-start.2 = (bf16[128,512]{1,0:T(8,128)(2,1)S(1)}, bf16[128,512]{1,0:T(8,128)(2,1)S(1)}, u32[]{:S(2)}, u32[]{:S(2)}) collective-permute-start(bf16[128,512]{1,0:T(8,128)(2,1)S(1)} %split_columns.1), channel_id=1, source_target_pairs={{0,48},{16,0},{32,16},{48,32},{1,49},{17,1},{33,17},{49,33},{2,50}... | collective-permute-start | bytes 393224 | tf_op jit(solution)/shard_map/ppermute | solution.py:74
  10.1 7.0 %collective-permute-start.3 = (bf16[128,512]{1,0:T(8,128)(2,1)S(1)}, bf16[128,512]{1,0:T(8,128)(2,1)S(1)}, u32[]{:S(2)}, u32[]{:S(2)}) collective-permute-start(bf16[128,512]{1,0:T(8,128)(2,1)S(1)} %split_columns.1), channel_id=1, source_target_pairs={{0,32},{16,48},{32,0},{48,16},{1,33},{17,49},{33,1},{49,17},{2,34}... | collective-permute-start | bytes 393224 | tf_op jit(solution)/shard_map/ppermute | solution.py:74
  13.1 14.4 %collective-permute-start.6 = (bf16[64,4096]{1,0:T(8,128)(2,1)S(1)}, bf16[64,4096]{1,0:T(8,128)(2,1)S(1)}, u32[]{:S(2)}, u32[]{:S(2)}) collective-permute-start(bf16[64,4096]{1,0:T(8,128)(2,1)S(1)} %fusion.8.refs_0_), channel_id=1, source_target_pairs={{0,1},{1,128},{128,129},{129,0},{2,3},{3,130},{130,131},{131,2},{4... | collective-permute-start | bytes 1572872 | tf_op jit(solution)/shard_map/ppermute | solution.py:74
  14.1 23.3 %collective-permute-start.7 = (bf16[64,4096]{1,0:T(8,128)(2,1)S(1)}, bf16[64,4096]{1,0:T(8,128)(2,1)S(1)}, u32[]{:S(2)}, u32[]{:S(2)}) collective-permute-start(bf16[64,4096]{1,0:T(8,128)(2,1)S(1)} %fusion.8.refs_0_), channel_id=1, source_target_pairs={{0,129},{1,0},{128,1},{129,128},{2,131},{3,2},{130,3},{131,130},{4... | collective-permute-start | bytes 1572872 | tf_op jit(solution)/shard_map/ppermute | solution.py:74
  17.1 20.3 %collective-permute-start.4 = (bf16[4,128,512]{2,1,0:T(8,128)(2,1)S(1)}, bf16[4,128,512]{2,1,0:T(8,128)(2,1)S(1)}, u32[]{:S(2)}, u32[]{:S(2)}) collective-permute-start(bf16[4,128,512]{2,1,0:T(8,128)(2,1)S(1)} %pad_maximum_fusion.refs_8_.refs_6_.refs_10_.refs_4_), channel_id=1, source_target_pairs={{0,2},{2,4},{4,6},{6,8},{8,10},{10,12},{12,14},{14,0},{1,3},{3,5},... | collective-permute-start | bytes 1572872 | tf_op jit(solution)/shard_map/ppermute | solution.py:74
  19.1 18.3 %collective-permute-start.5 = (bf16[4,128,512]{2,1,0:T(8,128)(2,1)S(1)}, bf16[4,128,512]{2,1,0:T(8,128)(2,1)S(1)}, u32[]{:S(2)}, u32[]{:S(2)}) collective-permute-start(bf16[4,128,512]{2,1,0:T(8,128)(2,1)S(1)} %pad_maximum_fusion.refs_8_.refs_6_.refs_10_.refs_4_), channel_id=1, source_target_pairs={{0,14},{2,0},{4,2},{6,4},{8,6},{10,8},{12,10},{14,12},{1,15},{3,1}... | collective-permute-start | bytes 1572872 | tf_op jit(solution)/shard_map/ppermute | solution.py:74
  19.2 1.9 %collective-permute-start.10 = (bf16[64,4096]{1,0:T(8,128)(2,1)S(1)}, bf16[64,4096]{1,0:T(8,128)(2,1)S(1)}, u32[]{:S(2)}, u32[]{:S(2)}) collective-permute-start(bf16[64,4096]{1,0:T(8,128)(2,1)S(1)} %fusion.8.refs_0_), channel_id=1, source_target_pairs={{0,64},{64,0},{1,65},{65,1},{2,66},{66,2},{3,67},{67,3},{4,68},{68... | collective-permute-start | bytes 1572872 | tf_op jit(solution)/shard_map/ppermute | solution.py:74
  21.9 18.9 %collective-permute-start.11 = (bf16[64,4096]{1,0:T(8,128)(2,1)S(1)}, bf16[64,4096]{1,0:T(8,128)(2,1)}, u32[]{:S(2)}, u32[]{:S(2)}) collective-permute-start(bf16[64,4096]{1,0:T(8,128)(2,1)S(1)} %fusion.8.refs_0_), channel_id=1, source_target_pairs={{0,128},{1,129},{128,0},{129,1},{2,130},{3,131},{130,2},{131,3},{4... | collective-permute-start | bytes 1572872 | tf_op jit(solution)/shard_map/ppermute | solution.py:74
  37.4 10.0 %collective-permute-start.8 = (bf16[4,128,512]{2,1,0:T(8,128)(2,1)S(1)}, bf16[4,128,512]{2,1,0:T(8,128)(2,1)S(1)}, u32[]{:S(2)}, u32[]{:S(2)}) collective-permute-start(bf16[4,128,512]{2,1,0:T(8,128)(2,1)S(1)} %collective-permute-done.4.refs_9_.refs_7_.refs_11_.refs_5_), channel_id=1, source_target_pairs={{0,2},{2,4},{4,6},{6,8},{8,10},{10,12},{12,14},{14,0},{1,3},{3,5},... | collective-permute-start | bytes 1572872 | tf_op jit(solution)/shard_map/ppermute | solution.py:74
  39.4 10.8 %collective-permute-start.9 = (bf16[4,128,512]{2,1,0:T(8,128)(2,1)S(1)}, bf16[4,128,512]{2,1,0:T(8,128)(2,1)S(1)}, u32[]{:S(2)}, u32[]{:S(2)}) collective-permute-start(bf16[4,128,512]{2,1,0:T(8,128)(2,1)S(1)} %collective-permute-done.5.refs_10_.refs_8_.refs_12_.refs_6_), channel_id=1, source_target_pairs={{0,14},{2,0},{4,2},{6,4},{8,6},{10,8},{12,10},{14,12},{1,15},{3,1}... | collective-permute-start | bytes 1572872 | tf_op jit(solution)/shard_map/ppermute | solution.py:74
  40.3 12.9 %collective-permute-start.15 = (bf16[64,4096]{1,0:T(8,128)(2,1)}, bf16[64,4096]{1,0:T(8,128)(2,1)S(1)}, u32[]{:S(2)}, u32[]{:S(2)}) collective-permute-start(bf16[64,4096]{1,0:T(8,128)(2,1)} %copy-done), channel_id=1, source_target_pairs={{0,64},{64,0},{1,65},{65,1},{2,66},{66,2},{3,67},{67,3},{4,68},{68... | collective-permute-start | bytes 1572872 | tf_op jit(solution)/shard_map/ppermute | solution.py:74
  40.3 12.8 %collective-permute-start.16 = (bf16[64,4096]{1,0:T(8,128)(2,1)}, bf16[64,4096]{1,0:T(8,128)(2,1)S(1)}, u32[]{:S(2)}, u32[]{:S(2)}) collective-permute-start(bf16[64,4096]{1,0:T(8,128)(2,1)} %copy-done.2), channel_id=1, source_target_pairs={{0,64},{64,0},{1,65},{65,1},{2,66},{66,2},{3,67},{67,3},{4,68},{68... | collective-permute-start | bytes 1572872 | tf_op jit(solution)/shard_map/ppermute | solution.py:74
  50.3 15.5 %copy-start.1 = (bf16[64,4096]{1,0:T(8,128)(2,1)S(1)}, bf16[64,4096]{1,0:T(8,128)(2,1)}, u32[]{:S(2)}) copy-start(bf16[64,4096]{1,0:T(8,128)(2,1)} %copy-done) | copy-start | bytes 1572868
  50.3 15.5 %copy-start.3 = (bf16[64,4096]{1,0:T(8,128)(2,1)S(1)}, bf16[64,4096]{1,0:T(8,128)(2,1)}, u32[]{:S(2)}) copy-start(bf16[64,4096]{1,0:T(8,128)(2,1)} %copy-done.2) | copy-start | bytes 1572868
  50.3 10.0 %collective-permute-start.12 = (bf16[4,128,512]{2,1,0:T(8,128)(2,1)S(1)}, bf16[4,128,512]{2,1,0:T(8,128)(2,1)S(1)}, u32[]{:S(2)}, u32[]{:S(2)}) collective-permute-start(bf16[4,128,512]{2,1,0:T(8,128)(2,1)S(1)} %collective-permute-done.8.refs_11_.refs_9_.refs_13_.refs_7_), channel_id=1, source_target_pairs={{0,2},{2,4},{4,6},{6,8},{8,10},{10,12},{12,14},{14,0},{1,3},{3,5},... | collective-permute-start | bytes 1572872 | tf_op jit(solution)/shard_map/ppermute | solution.py:74
  50.5 9.8 %collective-permute-start.13 = (bf16[4,128,512]{2,1,0:T(8,128)(2,1)S(1)}, bf16[4,128,512]{2,1,0:T(8,128)(2,1)S(1)}, u32[]{:S(2)}, u32[]{:S(2)}) collective-permute-start(bf16[4,128,512]{2,1,0:T(8,128)(2,1)S(1)} %collective-permute-done.9.refs_12_.refs_10_.refs_14_.refs_8_), channel_id=1, source_target_pairs={{0,14},{2,0},{4,2},{6,4},{8,6},{10,8},{12,10},{14,12},{1,15},{3,1}... | collective-permute-start | bytes 1572872 | tf_op jit(solution)/shard_map/ppermute | solution.py:74
  53.1 7.2 %collective-permute-start.14 = (bf16[64,4096]{1,0:T(8,128)(2,1)}, bf16[64,4096]{1,0:T(8,128)(2,1)S(1)}, u32[]{:S(2)}, u32[]{:S(2)}) collective-permute-start(bf16[64,4096]{1,0:T(8,128)(2,1)} %collective-permute-done.11.refs_2_), channel_id=1, source_target_pairs={{0,64},{64,0},{1,65},{65,1},{2,66},{66,2},{3,67},{67,3},{4,68},{68... | collective-permute-start | bytes 1572872 | tf_op jit(solution)/shard_map/ppermute | solution.py:74
  60.3 9.7 %collective-permute-start.17 = (bf16[2,128,512]{2,1,0:T(8,128)(2,1)S(1)}, bf16[2,128,512]{2,1,0:T(8,128)(2,1)S(1)}, u32[]{:S(2)}, u32[]{:S(2)}) collective-permute-start(bf16[2,128,512]{2,1,0:T(8,128)(2,1)S(1)} %slice.24), channel_id=1, source_target_pairs={{0,2},{2,4},{4,6},{6,8},{8,10},{10,12},{12,14},{14,0},{1,3},{3,5},... | collective-permute-start | bytes 786440 | tf_op jit(solution)/shard_map/ppermute | solution.py:74
  65.7 7.9 %collective-permute-start.18 = (bf16[2,128,512]{2,1,0:T(8,128)(2,1)S(1)}, bf16[2,128,512]{2,1,0:T(8,128)(2,1)S(1)}, u32[]{:S(2)}, u32[]{:S(2)}) collective-permute-start(bf16[2,128,512]{2,1,0:T(8,128)(2,1)S(1)} %slice.25), channel_id=1, source_target_pairs={{0,14},{2,0},{4,2},{6,4},{8,6},{10,8},{12,10},{14,12},{1,15},{3,1}... | collective-permute-start | bytes 786440 | tf_op jit(solution)/shard_map/ppermute | solution.py:74
  97.1 10.9 %collective-permute-start.20 = (bf16[2,2,16,4096]{3,2,1,0:T(8,128)(2,1)S(1)}, bf16[2,2,16,4096]{3,2,1,0:T(8,128)(2,1)S(1)}, u32[]{:S(2)}, u32[]{:S(2)}) collective-permute-start(bf16[2,2,16,4096]{3,2,1,0:T(8,128)(2,1)S(1)} %bitcast.37), channel_id=1, source_target_pairs={{0,1},{1,128},{128,129},{129,0},{2,3},{3,130},{130,131},{131,2},{4... | collective-permute-start | bytes 1572872 | tf_op jit(solution)/shard_map/ppermute | solution.py:74
  97.2 10.8 %collective-permute-start.21 = (bf16[2,2,16,4096]{3,2,1,0:T(8,128)(2,1)S(1)}, bf16[2,2,16,4096]{3,2,1,0:T(8,128)(2,1)S(1)}, u32[]{:S(2)}, u32[]{:S(2)}) collective-permute-start(bf16[2,2,16,4096]{3,2,1,0:T(8,128)(2,1)S(1)} %bitcast.38), channel_id=1, source_target_pairs={{0,129},{1,0},{128,1},{129,128},{2,131},{3,2},{130,3},{131,130},{4... | collective-permute-start | bytes 1572872 | tf_op jit(solution)/shard_map/ppermute | solution.py:74
  100.9 7.1 %collective-permute-start.19 = (bf16[2,2,16,4096]{3,2,1,0:T(8,128)(2,1)S(1)}, bf16[2,2,16,4096]{3,2,1,0:T(8,128)(2,1)S(1)}, u32[]{:S(2)}, u32[]{:S(2)}) collective-permute-start(bf16[2,2,16,4096]{3,2,1,0:T(8,128)(2,1)S(1)} %bitcast.39), channel_id=1, source_target_pairs={{0,64},{64,0},{1,65},{65,1},{2,66},{66,2},{3,67},{67,3},{4,68},{68... | collective-permute-start | bytes 1572872 | tf_op jit(solution)/shard_map/ppermute | solution.py:74
  108.1 3.9 %collective-permute-start.24 = (bf16[2,2,16,4096]{3,2,1,0:T(8,128)(2,1)S(1)}, bf16[2,2,16,4096]{3,2,1,0:T(8,128)(2,1)S(1)}, u32[]{:S(2)}, u32[]{:S(2)}) collective-permute-start(bf16[2,2,16,4096]{3,2,1,0:T(8,128)(2,1)S(1)} %collective-permute-done.20.refs_2_.refs_6_), channel_id=1, source_target_pairs={{0,64},{64,0},{1,65},{65,1},{2,66},{66,2},{3,67},{67,3},{4,68},{68... | collective-permute-start | bytes 1572872 | tf_op jit(solution)/shard_map/ppermute | solution.py:74
  108.2 3.8 %collective-permute-start.25 = (bf16[2,2,16,4096]{3,2,1,0:T(8,128)(2,1)S(1)}, bf16[2,2,16,4096]{3,2,1,0:T(8,128)(2,1)S(1)}, u32[]{:S(2)}, u32[]{:S(2)}) collective-permute-start(bf16[2,2,16,4096]{3,2,1,0:T(8,128)(2,1)S(1)} %collective-permute-done.21.refs_4_.refs_8_), channel_id=1, source_target_pairs={{0,64},{64,0},{1,65},{65,1},{2,66},{66,2},{3,67},{67,3},{4,68},{68... | collective-permute-start | bytes 1572872 | tf_op jit(solution)/shard_map/ppermute | solution.py:74
  108.7 9.9 %collective-permute-start.22 = (bf16[1,2,16,4096]{3,2,1,0:T(8,128)(2,1)S(1)}, bf16[1,2,16,4096]{3,2,1,0:T(8,128)(2,1)S(1)}, u32[]{:S(2)}, u32[]{:S(2)}) collective-permute-start(bf16[1,2,16,4096]{3,2,1,0:T(8,128)(2,1)S(1)} %slice.30), channel_id=1, source_target_pairs={{0,1},{1,128},{128,129},{129,0},{2,3},{3,130},{130,131},{131,2},{4... | collective-permute-start | bytes 786440 | tf_op jit(solution)/shard_map/ppermute | solution.py:74
  110.0 8.5 %collective-permute-start.23 = (bf16[1,2,16,4096]{3,2,1,0:T(8,128)(2,1)S(1)}, bf16[1,2,16,4096]{3,2,1,0:T(8,128)(2,1)S(1)}, u32[]{:S(2)}, u32[]{:S(2)}) collective-permute-start(bf16[1,2,16,4096]{3,2,1,0:T(8,128)(2,1)S(1)} %slice.31), channel_id=1, source_target_pairs={{0,129},{1,0},{128,1},{129,128},{2,131},{3,2},{130,3},{131,130},{4... | collective-permute-start | bytes 786440 | tf_op jit(solution)/shard_map/ppermute | solution.py:74
  118.5 2.2 %collective-permute-start.26 = (bf16[1,2,16,4096]{3,2,1,0:T(8,128)(2,1)S(1)}, bf16[1,2,16,4096]{3,2,1,0:T(8,128)(2,1)S(1)}, u32[]{:S(2)}, u32[]{:S(2)}) collective-permute-start(bf16[1,2,16,4096]{3,2,1,0:T(8,128)(2,1)S(1)} %collective-permute-done.22.refs_2_.refs_0_), channel_id=1, source_target_pairs={{0,64},{64,0},{1,65},{65,1},{2,66},{66,2},{3,67},{67,3},{4,68},{68... | collective-permute-start | bytes 786440 | tf_op jit(solution)/shard_map/ppermute | solution.py:74
  118.5 2.2 %collective-permute-start.27 = (bf16[1,2,16,4096]{3,2,1,0:T(8,128)(2,1)S(1)}, bf16[1,2,16,4096]{3,2,1,0:T(8,128)(2,1)S(1)}, u32[]{:S(2)}, u32[]{:S(2)}) collective-permute-start(bf16[1,2,16,4096]{3,2,1,0:T(8,128)(2,1)S(1)} %collective-permute-done.23.refs_3_.refs_1_), channel_id=1, source_target_pairs={{0,64},{64,0},{1,65},{65,1},{2,66},{66,2},{3,67},{67,3},{4,68},{68... | collective-permute-start | bytes 786440 | tf_op jit(solution)/shard_map/ppermute | solution.py:74
  119.1 7.5 %collective-permute-start.28 = (bf16[192,512]{1,0:T(8,128)(2,1)S(1)}, bf16[192,512]{1,0:T(8,128)(2,1)S(1)}, u32[]{:S(2)}, u32[]{:S(2)}) collective-permute-start(bf16[192,512]{1,0:T(8,128)(2,1)S(1)} %sent_rows.2), channel_id=1, source_target_pairs={{0,1},{1,0},{2,3},{3,2},{4,5},{5,4},{6,7},{7,6},{8,9},{9,8},{10,11... | collective-permute-start | bytes 589832 | tf_op jit(solution)/shard_map/ppermute | solution.py:74
  122.2 5.2 %collective-permute-start.29 = (bf16[64,512]{1,0:T(8,128)(2,1)S(1)}, bf16[64,512]{1,0:T(8,128)(2,1)S(1)}, u32[]{:S(2)}, u32[]{:S(2)}) collective-permute-start(bf16[64,512]{1,0:T(8,128)(2,1)S(1)} %sent_rows.3), channel_id=1, source_target_pairs={{0,1},{1,0},{2,3},{3,2},{4,5},{5,4},{6,7},{7,6},{8,9},{9,8},{10,11... | collective-permute-start | bytes 196616 | tf_op jit(solution)/shard_map/ppermute | solution.py:74
  (7 other events, 27.0 us)

commit v14 on v13

--- a/solution.py
+++ b/solution.py
@@ -377,9 +377,9 @@
     before, after = with_core(before), with_core(after)
     early = sent_rows(place, (*own, *before, *after), pieces)
     far, early = lax.optimization_barrier((far, early))
-    got_early = shifted(early, "lo", 1)
     far = (*far, *(shifted(half, "core", 1) for half in far))
-    got_late = shifted(sent_rows(place, far, pieces), "lo", 1)
+    late, early = lax.optimization_barrier((sent_rows(place, far, pieces), early))
+    got_late, got_early = shifted(late, "lo", 1), shifted(early, "lo", 1)
     white = whitened.reshape(-1, *whitened.shape[3:])
     kept = kept_rows(place, slices, (*own, *far, *before, *after), pieces, sx, sy, white)
     gradient = whitened_gradient(place, swapped, kept, got_early, got_late, sx, sy)

time: 130 us -> 133 us (1.023)
  waiting for transfers between devices: 48.6 us -> 52.3 us
    ppermute x30, waiting for transfers between devices: 48.6 us -> 52.3 us  [shifted(): lax.ppermute(array, axis, [(k, (k + step) % size) for k in range(size)])]
  transfers between devices with their start and end apart: 30 -> 30, of which waited for: 12 -> 13; matrix products, arithmetic and copies ran while one was open for 5% -> 4% of each run, Pallas kernels for 7% -> 6%
where the time goes in v14:
time: 133 us; the launch traced here: 132 us
  waiting for transfers between devices  52.3 us (39%)
  starting transfers between devices  36.1 us (27%)
  blocking collectives  21.4 us (16%)
  Pallas kernels  13.9 us (10%)
  other arithmetic  4.72 us (4%)
  local copies, waits for them, and re-layouts  3.13 us (2%)
    ppermute x30, waiting for transfers between devices, shifted(): lax.ppermute(array, axis, [(k, (k + step) % size) for k in range(size)])  52.3 us
    ppermute x30, starting transfers between devices, shifted(): lax.ppermute(array, axis, [(k, (k + step) % size) for k in range(size)])  36.1 us
    all_to_all x1, blocking collectives, local(): got = lax.all_to_all(sent, ('y', 'z'), 0, 0, tiled=True)  21.4 us
    squeeze x1, other arithmetic, local(): moments(event_counts, latent_mean, latent_var).astype(jnp.bfloat16)[0]  4.33 us
    pallas_call x1, Pallas kernels, near_product(): pl.pallas_call(near_kernel, out_shape=jax.ShapeDtypeStruct((rows, width),...  3.14 us
    pallas_call x2, Pallas kernels, sent_rows(): pl.pallas_call(sent_kernel, out_shape=jax.ShapeDtypeStruct((count, width)...  2.94 us
    pallas_call x1, Pallas kernels, kept_rows(): pl.pallas_call(kept_kernel, out_shape=jax.ShapeDtypeStruct((times, rows,...  2.87 us
  transfers between devices with their start and end apart: 30, of which 13 were waited for; matrix products, arithmetic and copies ran while one was open for 4% of the time, Pallas kernels for 6%

profile of v14, /device:TPU:32, one launch (start us, length us, event | category | flops | bytes accessed | tf_op | source)
XLA Modules:
  0.0 132.5 jit_solution(15693033450443316726)
XLA Ops:
  0.0 1.5 %collective-permute-start = (bf16[64,1024]{1,0:T(8,128)(2,1)}, bf16[64,1024]{1,0:T(8,128)(2,1)S(1)}, u32[]{:S(2)}, u32[]{:S(2)}) collective-permute-start(bf16[64,1024]{1,0:T(8,128)(2,1)} %param.11), channel_id=1, source_target_pairs={{0,1},{1,0},{2,3},{3,2},{4,5},{5,4},{6,7},{7,6},{8,9},{9,8},{10,11... | collective-permute-start | bytes 393224 | tf_op jit(solution)/shard_map/ppermute | solution.py:74
  1.5 4.3 %fusion.8.refs_0_ = bf16[64,4096]{1,0:T(8,128)(2,1)S(1)} fusion(s32[1,64,4096]{2,1,0:T(8,128)} %param.8, f32[1,64,4096]{2,1,0:T(8,128)} %param.10, f32[1,64,4096]{2,1,0:T(8,128)} %param.9), kind=kLoop, calls=%fused_computation.16 | loop fusion | flops 17563648 | bytes 3670016 | tf_op jit(solution)/shard_map/squeeze | solution.py:326
  6.8 1.7 %collective-permute-start.1 = (bf16[128,512]{1,0:T(8,128)(2,1)S(1)}, bf16[128,512]{1,0:T(8,128)(2,1)S(1)}, u32[]{:S(2)}, u32[]{:S(2)}) collective-permute-start(bf16[128,512]{1,0:T(8,128)(2,1)S(1)} %split_columns.1), channel_id=1, source_target_pairs={{0,16},{16,32},{32,48},{48,0},{1,17},{17,33},{33,49},{49,1},{2,18}... | collective-permute-start | bytes 393224 | tf_op jit(solution)/shard_map/ppermute | solution.py:74
  8.4 1.7 %collective-permute-start.2 = (bf16[128,512]{1,0:T(8,128)(2,1)S(1)}, bf16[128,512]{1,0:T(8,128)(2,1)S(1)}, u32[]{:S(2)}, u32[]{:S(2)}) collective-permute-start(bf16[128,512]{1,0:T(8,128)(2,1)S(1)} %split_columns.1), channel_id=1, source_target_pairs={{0,48},{16,0},{32,16},{48,32},{1,49},{17,1},{33,17},{49,33},{2,50}... | collective-permute-start | bytes 393224 | tf_op jit(solution)/shard_map/ppermute | solution.py:74
  10.1 2.0 %collective-permute-start.3 = (bf16[128,512]{1,0:T(8,128)(2,1)S(1)}, bf16[128,512]{1,0:T(8,128)(2,1)S(1)}, u32[]{:S(2)}, u32[]{:S(2)}) collective-permute-start(bf16[128,512]{1,0:T(8,128)(2,1)S(1)} %split_columns.1), channel_id=1, source_target_pairs={{0,32},{16,48},{32,0},{48,16},{1,33},{17,49},{33,1},{49,17},{2,34}... | collective-permute-start | bytes 393224 | tf_op jit(solution)/shard_map/ppermute | solution.py:74
  14.1 2.2 %collective-permute-start.7 = (bf16[64,4096]{1,0:T(8,128)(2,1)S(1)}, bf16[64,4096]{1,0:T(8,128)(2,1)S(1)}, u32[]{:S(2)}, u32[]{:S(2)}) collective-permute-start(bf16[64,4096]{1,0:T(8,128)(2,1)S(1)} %fusion.8.refs_0_), channel_id=1, source_target_pairs={{0,129},{1,0},{128,1},{129,128},{2,131},{3,2},{130,3},{131,130},{4... | collective-permute-start | bytes 1572872 | tf_op jit(solution)/shard_map/ppermute | solution.py:74
  17.1 2.0 %collective-permute-start.4 = (bf16[4,128,512]{2,1,0:T(8,128)(2,1)S(1)}, bf16[4,128,512]{2,1,0:T(8,128)(2,1)S(1)}, u32[]{:S(2)}, u32[]{:S(2)}) collective-permute-start(bf16[4,128,512]{2,1,0:T(8,128)(2,1)S(1)} %pad_maximum_fusion.refs_8_.refs_6_.refs_10_.refs_4_), channel_id=1, source_target_pairs={{0,2},{2,4},{4,6},{6,8},{8,10},{10,12},{12,14},{14,0},{1,3},{3,5},... | collective-permute-start | bytes 1572872 | tf_op jit(solution)/shard_map/ppermute | solution.py:74
  19.3 1.9 %collective-permute-done.10.refs_1_ = bf16[64,4096]{1,0:T(8,128)(2,1)S(1)} collective-permute-done((bf16[64,4096]{1,0:T(8,128)(2,1)S(1)}, bf16[64,4096]{1,0:T(8,128)(2,1)S(1)}, u32[]{:S(2)}, u32[]{:S(2)}) %collective-permute-start.10) | collective-permute-done | bytes 524320 | tf_op jit(solution)/shard_map/ppermute | solution.py:74
  21.9 2.7 %collective-permute-start.11 = (bf16[64,4096]{1,0:T(8,128)(2,1)S(1)}, bf16[64,4096]{1,0:T(8,128)(2,1)}, u32[]{:S(2)}, u32[]{:S(2)}) collective-permute-start(bf16[64,4096]{1,0:T(8,128)(2,1)S(1)} %fusion.8.refs_0_), channel_id=1, source_target_pairs={{0,128},{1,129},{128,0},{129,1},{2,130},{3,131},{130,2},{131,3},{4... | collective-permute-start | bytes 1572872 | tf_op jit(solution)/shard_map/ppermute | solution.py:74
  24.7 2.8 %collective-permute-done.6.refs_4_ = bf16[64,4096]{1,0:T(8,128)(2,1)S(1)} collective-permute-done((bf16[64,4096]{1,0:T(8,128)(2,1)S(1)}, bf16[64,4096]{1,0:T(8,128)(2,1)S(1)}, u32[]{:S(2)}, u32[]{:S(2)}) %collective-permute-start.6) | collective-permute-done | bytes 524320 | tf_op jit(solution)/shard_map/ppermute | solution.py:74
  27.5 9.9 %collective-permute-done.7.refs_6_ = bf16[64,4096]{1,0:T(8,128)(2,1)S(1)} collective-permute-done((bf16[64,4096]{1,0:T(8,128)(2,1)S(1)}, bf16[64,4096]{1,0:T(8,128)(2,1)S(1)}, u32[]{:S(2)}, u32[]{:S(2)}) %collective-permute-start.7) | collective-permute-done | bytes 524320 | tf_op jit(solution)/shard_map/ppermute | solution.py:74
  37.4 2.0 %collective-permute-start.8 = (bf16[4,128,512]{2,1,0:T(8,128)(2,1)S(1)}, bf16[4,128,512]{2,1,0:T(8,128)(2,1)S(1)}, u32[]{:S(2)}, u32[]{:S(2)}) collective-permute-start(bf16[4,128,512]{2,1,0:T(8,128)(2,1)S(1)} %collective-permute-done.4.refs_9_.refs_7_.refs_11_.refs_5_), channel_id=1, source_target_pairs={{0,2},{2,4},{4,6},{6,8},{8,10},{10,12},{12,14},{14,0},{1,3},{3,5},... | collective-permute-start | bytes 1572872 | tf_op jit(solution)/shard_map/ppermute | solution.py:74
  40.8 6.6 %collective-permute-done.8.refs_11_.refs_9_.refs_13_.refs_7_ = bf16[4,128,512]{2,1,0:T(8,128)(2,1)S(1)} collective-permute-done((bf16[4,128,512]{2,1,0:T(8,128)(2,1)S(1)}, bf16[4,128,512]{2,1,0:T(8,128)(2,1)S(1)}, u32[]{:S(2)}, u32[]{:S(2)}) %collective-permute-start.8) | collective-permute-done | bytes 524320 | tf_op jit(solution)/shard_map/ppermute | solution.py:74
  47.4 2.8 %collective-permute-done.9.refs_12_.refs_10_.refs_14_.refs_8_ = bf16[4,128,512]{2,1,0:T(8,128)(2,1)S(1)} collective-permute-done((bf16[4,128,512]{2,1,0:T(8,128)(2,1)S(1)}, bf16[4,128,512]{2,1,0:T(8,128)(2,1)S(1)}, u32[]{:S(2)}, u32[]{:S(2)}) %collective-permute-start.9) | collective-permute-done | bytes 524320 | tf_op jit(solution)/shard_map/ppermute | solution.py:74
  50.5 2.6 %collective-permute-start.13 = (bf16[4,128,512]{2,1,0:T(8,128)(2,1)S(1)}, bf16[4,128,512]{2,1,0:T(8,128)(2,1)S(1)}, u32[]{:S(2)}, u32[]{:S(2)}) collective-permute-start(bf16[4,128,512]{2,1,0:T(8,128)(2,1)S(1)} %collective-permute-done.9.refs_12_.refs_10_.refs_14_.refs_8_), channel_id=1, source_target_pairs={{0,14},{2,0},{4,2},{6,4},{8,6},{10,8},{12,10},{14,12},{1,15},{3,1}... | collective-permute-start | bytes 1572872 | tf_op jit(solution)/shard_map/ppermute | solution.py:74
  53.1 7.2 %collective-permute-done.12.refs_13_.refs_11_.refs_15_.refs_9_ = bf16[4,128,512]{2,1,0:T(8,128)(2,1)S(1)} collective-permute-done((bf16[4,128,512]{2,1,0:T(8,128)(2,1)S(1)}, bf16[4,128,512]{2,1,0:T(8,128)(2,1)S(1)}, u32[]{:S(2)}, u32[]{:S(2)}) %collective-permute-start.12) | collective-permute-done | bytes 524320 | tf_op jit(solution)/shard_map/ppermute | solution.py:74
  60.3 5.3 %collective-permute-start.17 = (bf16[2,128,512]{2,1,0:T(8,128)(2,1)S(1)}, bf16[2,128,512]{2,1,0:T(8,128)(2,1)S(1)}, u32[]{:S(2)}, u32[]{:S(2)}) collective-permute-start(bf16[2,128,512]{2,1,0:T(8,128)(2,1)S(1)} %slice.24), channel_id=1, source_target_pairs={{0,2},{2,4},{4,6},{6,8},{8,10},{10,12},{12,14},{14,0},{1,3},{3,5},... | collective-permute-start | bytes 786440 | tf_op jit(solution)/shard_map/ppermute | solution.py:74
  66.8 3.1 %near_product.1.refs_10_ = f32[512,512]{1,0:T(8,128)S(1)} custom-call(s32[4]{0:T(128)S(1)} %pad_add_fusion.place_ref, bf16[64,4096]{1,0:T(8,128)(2,1)S(1)} %fusion.8.refs_0_, bf16[64,4096]{1,0:T(8,128)(2,1)S(1)} %copy-done.5, bf16[64,4096]{1,0:T(8,128)(2,1)} %collective-permute-done.11.refs_2_, bf16[64,4096]{1,0:T(8,128)(2,1)S(1)} %collective-permute-done.14.refs_3_, ...), custom_call_target="tpu_custom_call" | custom-call | flops 1610612736 | bytes 8388608 | tf_op jit(solution)/shard_map/near_product/pallas_call | solution.py:135
  70.0 3.6 %collective-permute-done.18.refs_9_.refs_14_.refs_18_.refs_12_ = bf16[2,128,512]{2,1,0:T(8,128)(2,1)S(1)} collective-permute-done((bf16[2,128,512]{2,1,0:T(8,128)(2,1)S(1)}, bf16[2,128,512]{2,1,0:T(8,128)(2,1)S(1)}, u32[]{:S(2)}, u32[]{:S(2)}) %collective-permute-start.18) | collective-permute-done | bytes 262176 | tf_op jit(solution)/shard_map/ppermute | solution.py:74
  73.6 2.0 %first_product.1 = bf16[512,512]{1,0:T(8,128)(2,1)S(1)} custom-call(f32[8,4]{1,0:T(8,128)S(1)} %broadcast_select_fusion.mix_ref, s32[4]{0:T(128)S(1)} %pad_add_fusion.place_ref, bf16[64,4096]{1,0:T(8,128)(2,1)S(1)} %fusion.8.refs_0_, bf16[64,4096]{1,0:T(8,128)(2,1)S(1)} %copy-done.5, bf16[64,4096]{1,0:T(8,128)(2,1)} %collective-permute-done.11.refs_2_, ...), custom_call_target="tpu_custom_call" | custom-call | flops 536870912 | bytes 4194304 | tf_op jit(solution)/shard_map/first_product/pallas_call | solution.py:173
  75.6 21.4 %all_to_all.5 = bf16[32,16,512]{2,1,0:T(8,128)(2,1)S(1)} all-to-all(bf16[32,16,512]{2,1,0:T(8,128)(2,1)S(1)} %bitcast.42), channel_id=1, replica_groups=mesh['hi'=2,'core'=2,'y'=4,'z'=8,'lo'=2] {'y','z'}, dimensions={0} | all-to-all | bytes 1048576 | tf_op jit(solution)/shard_map/all_to_all | solution.py:369
  97.2 3.7 %collective-permute-start.21 = (bf16[2,2,16,4096]{3,2,1,0:T(8,128)(2,1)S(1)}, bf16[2,2,16,4096]{3,2,1,0:T(8,128)(2,1)S(1)}, u32[]{:S(2)}, u32[]{:S(2)}) collective-permute-start(bf16[2,2,16,4096]{3,2,1,0:T(8,128)(2,1)S(1)} %bitcast.38), channel_id=1, source_target_pairs={{0,129},{1,0},{128,1},{129,128},{2,131},{3,2},{130,3},{131,130},{4... | collective-permute-start | bytes 1572872 | tf_op jit(solution)/shard_map/ppermute | solution.py:74
  100.9 7.1 %collective-permute-done.20.refs_2_.refs_6_ = bf16[2,2,16,4096]{3,2,1,0:T(8,128)(2,1)S(1)} collective-permute-done((bf16[2,2,16,4096]{3,2,1,0:T(8,128)(2,1)S(1)}, bf16[2,2,16,4096]{3,2,1,0:T(8,128)(2,1)S(1)}, u32[]{:S(2)}, u32[]{:S(2)}) %collective-permute-start.20) | collective-permute-done | bytes 524320 | tf_op jit(solution)/shard_map/ppermute | solution.py:74
  108.7 1.4 %collective-permute-start.22 = (bf16[1,2,16,4096]{3,2,1,0:T(8,128)(2,1)S(1)}, bf16[1,2,16,4096]{3,2,1,0:T(8,128)(2,1)S(1)}, u32[]{:S(2)}, u32[]{:S(2)}) collective-permute-start(bf16[1,2,16,4096]{3,2,1,0:T(8,128)(2,1)S(1)} %slice.30), channel_id=1, source_target_pairs={{0,1},{1,128},{128,129},{129,0},{2,3},{3,130},{130,131},{131,2},{4... | collective-permute-start | bytes 786440 | tf_op jit(solution)/shard_map/ppermute | solution.py:74
  110.0 1.9 %collective-permute-start.23 = (bf16[1,2,16,4096]{3,2,1,0:T(8,128)(2,1)S(1)}, bf16[1,2,16,4096]{3,2,1,0:T(8,128)(2,1)S(1)}, u32[]{:S(2)}, u32[]{:S(2)}) collective-permute-start(bf16[1,2,16,4096]{3,2,1,0:T(8,128)(2,1)S(1)} %slice.31), channel_id=1, source_target_pairs={{0,129},{1,0},{128,1},{129,128},{2,131},{3,2},{130,3},{131,130},{4... | collective-permute-start | bytes 786440 | tf_op jit(solution)/shard_map/ppermute | solution.py:74
  112.0 1.6 %sent_rows.2 = bf16[192,512]{1,0:T(8,128)(2,1)S(1)} custom-call(s32[4]{0:T(128)S(1)} %pad_add_fusion.place_ref, bf16[2,2,16,4096]{3,2,1,0:T(8,128)(2,1)S(1)} %bitcast.40, bf16[2,2,16,4096]{3,2,1,0:T(8,128)(2,1)S(1)} %collective-permute-done.19.refs_1_, bf16[2,2,16,4096]{3,2,1,0:T(8,128)(2,1)S(1)} %collective-permute-done.20.refs_2_.refs_6_, ...), custom_call_target="tpu_custom_call" | custom-call | flops 805306368 | bytes 6291456 | tf_op jit(solution)/shard_map/sent_rows/pallas_call | solution.py:219
  113.5 5.0 %collective-permute-done.22.refs_2_.refs_0_ = bf16[1,2,16,4096]{3,2,1,0:T(8,128)(2,1)S(1)} collective-permute-done((bf16[1,2,16,4096]{3,2,1,0:T(8,128)(2,1)S(1)}, bf16[1,2,16,4096]{3,2,1,0:T(8,128)(2,1)S(1)}, u32[]{:S(2)}, u32[]{:S(2)}) %collective-permute-start.22) | collective-permute-done | bytes 262176 | tf_op jit(solution)/shard_map/ppermute | solution.py:74
  120.4 1.4 %sent_rows.3 = bf16[64,512]{1,0:T(8,128)(2,1)S(1)} custom-call(s32[4]{0:T(128)S(1)} %pad_add_fusion.place_ref, bf16[1,2,16,4096]{3,2,1,0:T(8,128)(2,1)S(1)} %collective-permute-done.22.refs_2_.refs_0_, bf16[1,2,16,4096]{3,2,1,0:T(8,128)(2,1)S(1)} %collective-permute-done.23.refs_3_.refs_1_, ...), custom_call_target="tpu_custom_call" | custom-call | flops 268435456 | bytes 6291456 | tf_op jit(solution)/shard_map/sent_rows/pallas_call | solution.py:219
  121.8 1.7 %collective-permute-start.28 = (bf16[192,512]{1,0:T(8,128)(2,1)S(1)}, bf16[192,512]{1,0:T(8,128)(2,1)S(1)}, u32[]{:S(2)}, u32[]{:S(2)}) collective-permute-start(bf16[192,512]{1,0:T(8,128)(2,1)S(1)} %sent_rows.2), channel_id=1, source_target_pairs={{0,1},{1,0},{2,3},{3,2},{4,5},{5,4},{6,7},{7,6},{8,9},{9,8},{10,11... | collective-permute-start | bytes 589832 | tf_op jit(solution)/shard_map/ppermute | solution.py:74
  124.0 2.9 %kept_rows.1.kept_ref = f32[4,64,1024]{2,1,0:T(8,128)S(1)} custom-call(s32[4]{0:T(128)S(1)} %pad_add_fusion.place_ref, s32[8]{0:T(128)S(1)} %get-tuple-element.84.slice_ref, bf16[2,2,16,4096]{3,2,1,0:T(8,128)(2,1)S(1)} %bitcast.41, bf16[2,2,16,4096]{3,2,1,0:T(8,128)(2,1)S(1)} %collective-permute-done.19.refs_1_, ...), custom_call_target="tpu_custom_call" | custom-call | flops 1073741824 | bytes 6291456 | tf_op jit(solution)/shard_map/kept_rows/pallas_call | solution.py:261
  126.9 3.3 %collective-permute-done.29.late_ref = bf16[64,512]{1,0:T(8,128)(2,1)S(1)} collective-permute-done((bf16[64,512]{1,0:T(8,128)(2,1)S(1)}, bf16[64,512]{1,0:T(8,128)(2,1)S(1)}, u32[]{:S(2)}, u32[]{:S(2)}) %collective-permute-start.29) | collective-permute-done | bytes 65568 | tf_op jit(solution)/shard_map/ppermute | solution.py:74
  130.3 2.2 %whitened_gradient.1 = f32[64,4,1024]{2,1,0:T(4,128)} custom-call(s32[4]{0:T(128)S(1)} %pad_add_fusion.place_ref, s32[8]{0:T(128)S(1)} %pad_add_fusion.1.slice_ref, f32[4,64,1024]{2,1,0:T(8,128)S(1)} %kept_rows.1.kept_ref, bf16[192,512]{1,0:T(8,128)(2,1)S(1)} %collective-permute-done.28.early_ref, bf16[64,512]{1,0:T(8,128)(2,1)S(1)} %collective-permute-done.29.late_ref, ...), custom_call_target="tpu_custom_call" | custom-call | tf_op jit(solution)/shard_map/whitened_gradient/pallas_call | solution.py:298
  (82 shorter events, 10.1 us)
Async XLA Ops:
  0.0 5.9 %collective-permute-start = (bf16[64,1024]{1,0:T(8,128)(2,1)}, bf16[64,1024]{1,0:T(8,128)(2,1)S(1)}, u32[]{:S(2)}, u32[]{:S(2)}) collective-permute-start(bf16[64,1024]{1,0:T(8,128)(2,1)} %param.11), channel_id=1, source_target_pairs={{0,1},{1,0},{2,3},{3,2},{4,5},{5,4},{6,7},{7,6},{8,9},{9,8},{10,11... | collective-permute-start | bytes 393224 | tf_op jit(solution)/shard_map/ppermute | solution.py:74
  6.8 9.6 %collective-permute-start.1 = (bf16[128,512]{1,0:T(8,128)(2,1)S(1)}, bf16[128,512]{1,0:T(8,128)(2,1)S(1)}, u32[]{:S(2)}, u32[]{:S(2)}) collective-permute-start(bf16[128,512]{1,0:T(8,128)(2,1)S(1)} %split_columns.1), channel_id=1, source_target_pairs={{0,16},{16,32},{32,48},{48,0},{1,17},{17,33},{33,49},{49,1},{2,18}... | collective-permute-start | bytes 393224 | tf_op jit(solution)/shard_map/ppermute | solution.py:74
  8.4 7.9 %collective-permute-start.2 = (bf16[128,512]{1,0:T(8,128)(2,1)S(1)}, bf16[128,512]{1,0:T(8,128)(2,1)S(1)}, u32[]{:S(2)}, u32[]{:S(2)}) collective-permute-start(bf16[128,512]{1,0:T(8,128)(2,1)S(1)} %split_columns.1), channel_id=1, source_target_pairs={{0,48},{16,0},{32,16},{48,32},{1,49},{17,1},{33,17},{49,33},{2,50}... | collective-permute-start | bytes 393224 | tf_op jit(solution)/shard_map/ppermute | solution.py:74
  10.1 7.0 %collective-permute-start.3 = (bf16[128,512]{1,0:T(8,128)(2,1)S(1)}, bf16[128,512]{1,0:T(8,128)(2,1)S(1)}, u32[]{:S(2)}, u32[]{:S(2)}) collective-permute-start(bf16[128,512]{1,0:T(8,128)(2,1)S(1)} %split_columns.1), channel_id=1, source_target_pairs={{0,32},{16,48},{32,0},{48,16},{1,33},{17,49},{33,1},{49,17},{2,34}... | collective-permute-start | bytes 393224 | tf_op jit(solution)/shard_map/ppermute | solution.py:74
  13.1 14.4 %collective-permute-start.6 = (bf16[64,4096]{1,0:T(8,128)(2,1)S(1)}, bf16[64,4096]{1,0:T(8,128)(2,1)S(1)}, u32[]{:S(2)}, u32[]{:S(2)}) collective-permute-start(bf16[64,4096]{1,0:T(8,128)(2,1)S(1)} %fusion.8.refs_0_), channel_id=1, source_target_pairs={{0,1},{1,128},{128,129},{129,0},{2,3},{3,130},{130,131},{131,2},{4... | collective-permute-start | bytes 1572872 | tf_op jit(solution)/shard_map/ppermute | solution.py:74
  14.1 23.3 %collective-permute-start.7 = (bf16[64,4096]{1,0:T(8,128)(2,1)S(1)}, bf16[64,4096]{1,0:T(8,128)(2,1)S(1)}, u32[]{:S(2)}, u32[]{:S(2)}) collective-permute-start(bf16[64,4096]{1,0:T(8,128)(2,1)S(1)} %fusion.8.refs_0_), channel_id=1, source_target_pairs={{0,129},{1,0},{128,1},{129,128},{2,131},{3,2},{130,3},{131,130},{4... | collective-permute-start | bytes 1572872 | tf_op jit(solution)/shard_map/ppermute | solution.py:74
  17.1 20.3 %collective-permute-start.4 = (bf16[4,128,512]{2,1,0:T(8,128)(2,1)S(1)}, bf16[4,128,512]{2,1,0:T(8,128)(2,1)S(1)}, u32[]{:S(2)}, u32[]{:S(2)}) collective-permute-start(bf16[4,128,512]{2,1,0:T(8,128)(2,1)S(1)} %pad_maximum_fusion.refs_8_.refs_6_.refs_10_.refs_4_), channel_id=1, source_target_pairs={{0,2},{2,4},{4,6},{6,8},{8,10},{10,12},{12,14},{14,0},{1,3},{3,5},... | collective-permute-start | bytes 1572872 | tf_op jit(solution)/shard_map/ppermute | solution.py:74
  19.1 18.3 %collective-permute-start.5 = (bf16[4,128,512]{2,1,0:T(8,128)(2,1)S(1)}, bf16[4,128,512]{2,1,0:T(8,128)(2,1)S(1)}, u32[]{:S(2)}, u32[]{:S(2)}) collective-permute-start(bf16[4,128,512]{2,1,0:T(8,128)(2,1)S(1)} %pad_maximum_fusion.refs_8_.refs_6_.refs_10_.refs_4_), channel_id=1, source_target_pairs={{0,14},{2,0},{4,2},{6,4},{8,6},{10,8},{12,10},{14,12},{1,15},{3,1}... | collective-permute-start | bytes 1572872 | tf_op jit(solution)/shard_map/ppermute | solution.py:74
  19.2 1.9 %collective-permute-start.10 = (bf16[64,4096]{1,0:T(8,128)(2,1)S(1)}, bf16[64,4096]{1,0:T(8,128)(2,1)S(1)}, u32[]{:S(2)}, u32[]{:S(2)}) collective-permute-start(bf16[64,4096]{1,0:T(8,128)(2,1)S(1)} %fusion.8.refs_0_), channel_id=1, source_target_pairs={{0,64},{64,0},{1,65},{65,1},{2,66},{66,2},{3,67},{67,3},{4,68},{68... | collective-permute-start | bytes 1572872 | tf_op jit(solution)/shard_map/ppermute | solution.py:74
  21.9 18.9 %collective-permute-start.11 = (bf16[64,4096]{1,0:T(8,128)(2,1)S(1)}, bf16[64,4096]{1,0:T(8,128)(2,1)}, u32[]{:S(2)}, u32[]{:S(2)}) collective-permute-start(bf16[64,4096]{1,0:T(8,128)(2,1)S(1)} %fusion.8.refs_0_), channel_id=1, source_target_pairs={{0,128},{1,129},{128,0},{129,1},{2,130},{3,131},{130,2},{131,3},{4... | collective-permute-start | bytes 1572872 | tf_op jit(solution)/shard_map/ppermute | solution.py:74
  37.4 10.0 %collective-permute-start.8 = (bf16[4,128,512]{2,1,0:T(8,128)(2,1)S(1)}, bf16[4,128,512]{2,1,0:T(8,128)(2,1)S(1)}, u32[]{:S(2)}, u32[]{:S(2)}) collective-permute-start(bf16[4,128,512]{2,1,0:T(8,128)(2,1)S(1)} %collective-permute-done.4.refs_9_.refs_7_.refs_11_.refs_5_), channel_id=1, source_target_pairs={{0,2},{2,4},{4,6},{6,8},{8,10},{10,12},{12,14},{14,0},{1,3},{3,5},... | collective-permute-start | bytes 1572872 | tf_op jit(solution)/shard_map/ppermute | solution.py:74
  39.4 10.8 %collective-permute-start.9 = (bf16[4,128,512]{2,1,0:T(8,128)(2,1)S(1)}, bf16[4,128,512]{2,1,0:T(8,128)(2,1)S(1)}, u32[]{:S(2)}, u32[]{:S(2)}) collective-permute-start(bf16[4,128,512]{2,1,0:T(8,128)(2,1)S(1)} %collective-permute-done.5.refs_10_.refs_8_.refs_12_.refs_6_), channel_id=1, source_target_pairs={{0,14},{2,0},{4,2},{6,4},{8,6},{10,8},{12,10},{14,12},{1,15},{3,1}... | collective-permute-start | bytes 1572872 | tf_op jit(solution)/shard_map/ppermute | solution.py:74
  40.3 12.9 %collective-permute-start.15 = (bf16[64,4096]{1,0:T(8,128)(2,1)}, bf16[64,4096]{1,0:T(8,128)(2,1)S(1)}, u32[]{:S(2)}, u32[]{:S(2)}) collective-permute-start(bf16[64,4096]{1,0:T(8,128)(2,1)} %copy-done), channel_id=1, source_target_pairs={{0,64},{64,0},{1,65},{65,1},{2,66},{66,2},{3,67},{67,3},{4,68},{68... | collective-permute-start | bytes 1572872 | tf_op jit(solution)/shard_map/ppermute | solution.py:74
  40.3 12.8 %collective-permute-start.16 = (bf16[64,4096]{1,0:T(8,128)(2,1)}, bf16[64,4096]{1,0:T(8,128)(2,1)S(1)}, u32[]{:S(2)}, u32[]{:S(2)}) collective-permute-start(bf16[64,4096]{1,0:T(8,128)(2,1)} %copy-done.2), channel_id=1, source_target_pairs={{0,64},{64,0},{1,65},{65,1},{2,66},{66,2},{3,67},{67,3},{4,68},{68... | collective-permute-start | bytes 1572872 | tf_op jit(solution)/shard_map/ppermute | solution.py:74
  50.3 15.5 %copy-start.1 = (bf16[64,4096]{1,0:T(8,128)(2,1)S(1)}, bf16[64,4096]{1,0:T(8,128)(2,1)}, u32[]{:S(2)}) copy-start(bf16[64,4096]{1,0:T(8,128)(2,1)} %copy-done) | copy-start | bytes 1572868
  50.3 15.5 %copy-start.3 = (bf16[64,4096]{1,0:T(8,128)(2,1)S(1)}, bf16[64,4096]{1,0:T(8,128)(2,1)}, u32[]{:S(2)}) copy-start(bf16[64,4096]{1,0:T(8,128)(2,1)} %copy-done.2) | copy-start | bytes 1572868
  50.3 10.0 %collective-permute-start.12 = (bf16[4,128,512]{2,1,0:T(8,128)(2,1)S(1)}, bf16[4,128,512]{2,1,0:T(8,128)(2,1)S(1)}, u32[]{:S(2)}, u32[]{:S(2)}) collective-permute-start(bf16[4,128,512]{2,1,0:T(8,128)(2,1)S(1)} %collective-permute-done.8.refs_11_.refs_9_.refs_13_.refs_7_), channel_id=1, source_target_pairs={{0,2},{2,4},{4,6},{6,8},{8,10},{10,12},{12,14},{14,0},{1,3},{3,5},... | collective-permute-start | bytes 1572872 | tf_op jit(solution)/shard_map/ppermute | solution.py:74
  50.5 9.8 %collective-permute-start.13 = (bf16[4,128,512]{2,1,0:T(8,128)(2,1)S(1)}, bf16[4,128,512]{2,1,0:T(8,128)(2,1)S(1)}, u32[]{:S(2)}, u32[]{:S(2)}) collective-permute-start(bf16[4,128,512]{2,1,0:T(8,128)(2,1)S(1)} %collective-permute-done.9.refs_12_.refs_10_.refs_14_.refs_8_), channel_id=1, source_target_pairs={{0,14},{2,0},{4,2},{6,4},{8,6},{10,8},{12,10},{14,12},{1,15},{3,1}... | collective-permute-start | bytes 1572872 | tf_op jit(solution)/shard_map/ppermute | solution.py:74
  53.1 7.2 %collective-permute-start.14 = (bf16[64,4096]{1,0:T(8,128)(2,1)}, bf16[64,4096]{1,0:T(8,128)(2,1)S(1)}, u32[]{:S(2)}, u32[]{:S(2)}) collective-permute-start(bf16[64,4096]{1,0:T(8,128)(2,1)} %collective-permute-done.11.refs_2_), channel_id=1, source_target_pairs={{0,64},{64,0},{1,65},{65,1},{2,66},{66,2},{3,67},{67,3},{4,68},{68... | collective-permute-start | bytes 1572872 | tf_op jit(solution)/shard_map/ppermute | solution.py:74
  60.3 9.7 %collective-permute-start.17 = (bf16[2,128,512]{2,1,0:T(8,128)(2,1)S(1)}, bf16[2,128,512]{2,1,0:T(8,128)(2,1)S(1)}, u32[]{:S(2)}, u32[]{:S(2)}) collective-permute-start(bf16[2,128,512]{2,1,0:T(8,128)(2,1)S(1)} %slice.24), channel_id=1, source_target_pairs={{0,2},{2,4},{4,6},{6,8},{8,10},{10,12},{12,14},{14,0},{1,3},{3,5},... | collective-permute-start | bytes 786440 | tf_op jit(solution)/shard_map/ppermute | solution.py:74
  65.7 7.9 %collective-permute-start.18 = (bf16[2,128,512]{2,1,0:T(8,128)(2,1)S(1)}, bf16[2,128,512]{2,1,0:T(8,128)(2,1)S(1)}, u32[]{:S(2)}, u32[]{:S(2)}) collective-permute-start(bf16[2,128,512]{2,1,0:T(8,128)(2,1)S(1)} %slice.25), channel_id=1, source_target_pairs={{0,14},{2,0},{4,2},{6,4},{8,6},{10,8},{12,10},{14,12},{1,15},{3,1}... | collective-permute-start | bytes 786440 | tf_op jit(solution)/shard_map/ppermute | solution.py:74
  97.1 10.9 %collective-permute-start.20 = (bf16[2,2,16,4096]{3,2,1,0:T(8,128)(2,1)S(1)}, bf16[2,2,16,4096]{3,2,1,0:T(8,128)(2,1)S(1)}, u32[]{:S(2)}, u32[]{:S(2)}) collective-permute-start(bf16[2,2,16,4096]{3,2,1,0:T(8,128)(2,1)S(1)} %bitcast.37), channel_id=1, source_target_pairs={{0,1},{1,128},{128,129},{129,0},{2,3},{3,130},{130,131},{131,2},{4... | collective-permute-start | bytes 1572872 | tf_op jit(solution)/shard_map/ppermute | solution.py:74
  97.2 10.8 %collective-permute-start.21 = (bf16[2,2,16,4096]{3,2,1,0:T(8,128)(2,1)S(1)}, bf16[2,2,16,4096]{3,2,1,0:T(8,128)(2,1)S(1)}, u32[]{:S(2)}, u32[]{:S(2)}) collective-permute-start(bf16[2,2,16,4096]{3,2,1,0:T(8,128)(2,1)S(1)} %bitcast.38), channel_id=1, source_target_pairs={{0,129},{1,0},{128,1},{129,128},{2,131},{3,2},{130,3},{131,130},{4... | collective-permute-start | bytes 1572872 | tf_op jit(solution)/shard_map/ppermute | solution.py:74
  100.9 7.1 %collective-permute-start.19 = (bf16[2,2,16,4096]{3,2,1,0:T(8,128)(2,1)S(1)}, bf16[2,2,16,4096]{3,2,1,0:T(8,128)(2,1)S(1)}, u32[]{:S(2)}, u32[]{:S(2)}) collective-permute-start(bf16[2,2,16,4096]{3,2,1,0:T(8,128)(2,1)S(1)} %bitcast.39), channel_id=1, source_target_pairs={{0,64},{64,0},{1,65},{65,1},{2,66},{66,2},{3,67},{67,3},{4,68},{68... | collective-permute-start | bytes 1572872 | tf_op jit(solution)/shard_map/ppermute | solution.py:74
  108.1 3.9 %collective-permute-start.24 = (bf16[2,2,16,4096]{3,2,1,0:T(8,128)(2,1)S(1)}, bf16[2,2,16,4096]{3,2,1,0:T(8,128)(2,1)S(1)}, u32[]{:S(2)}, u32[]{:S(2)}) collective-permute-start(bf16[2,2,16,4096]{3,2,1,0:T(8,128)(2,1)S(1)} %collective-permute-done.20.refs_2_.refs_6_), channel_id=1, source_target_pairs={{0,64},{64,0},{1,65},{65,1},{2,66},{66,2},{3,67},{67,3},{4,68},{68... | collective-permute-start | bytes 1572872 | tf_op jit(solution)/shard_map/ppermute | solution.py:74
  108.2 3.8 %collective-permute-start.25 = (bf16[2,2,16,4096]{3,2,1,0:T(8,128)(2,1)S(1)}, bf16[2,2,16,4096]{3,2,1,0:T(8,128)(2,1)S(1)}, u32[]{:S(2)}, u32[]{:S(2)}) collective-permute-start(bf16[2,2,16,4096]{3,2,1,0:T(8,128)(2,1)S(1)} %collective-permute-done.21.refs_4_.refs_8_), channel_id=1, source_target_pairs={{0,64},{64,0},{1,65},{65,1},{2,66},{66,2},{3,67},{67,3},{4,68},{68... | collective-permute-start | bytes 1572872 | tf_op jit(solution)/shard_map/ppermute | solution.py:74
  108.7 9.9 %collective-permute-start.22 = (bf16[1,2,16,4096]{3,2,1,0:T(8,128)(2,1)S(1)}, bf16[1,2,16,4096]{3,2,1,0:T(8,128)(2,1)S(1)}, u32[]{:S(2)}, u32[]{:S(2)}) collective-permute-start(bf16[1,2,16,4096]{3,2,1,0:T(8,128)(2,1)S(1)} %slice.30), channel_id=1, source_target_pairs={{0,1},{1,128},{128,129},{129,0},{2,3},{3,130},{130,131},{131,2},{4... | collective-permute-start | bytes 786440 | tf_op jit(solution)/shard_map/ppermute | solution.py:74
  110.0 8.5 %collective-permute-start.23 = (bf16[1,2,16,4096]{3,2,1,0:T(8,128)(2,1)S(1)}, bf16[1,2,16,4096]{3,2,1,0:T(8,128)(2,1)S(1)}, u32[]{:S(2)}, u32[]{:S(2)}) collective-permute-start(bf16[1,2,16,4096]{3,2,1,0:T(8,128)(2,1)S(1)} %slice.31), channel_id=1, source_target_pairs={{0,129},{1,0},{128,1},{129,128},{2,131},{3,2},{130,3},{131,130},{4... | collective-permute-start | bytes 786440 | tf_op jit(solution)/shard_map/ppermute | solution.py:74
  118.5 1.5 %collective-permute-start.26 = (bf16[1,2,16,4096]{3,2,1,0:T(8,128)(2,1)S(1)}, bf16[1,2,16,4096]{3,2,1,0:T(8,128)(2,1)S(1)}, u32[]{:S(2)}, u32[]{:S(2)}) collective-permute-start(bf16[1,2,16,4096]{3,2,1,0:T(8,128)(2,1)S(1)} %collective-permute-done.22.refs_2_.refs_0_), channel_id=1, source_target_pairs={{0,64},{64,0},{1,65},{65,1},{2,66},{66,2},{3,67},{67,3},{4,68},{68... | collective-permute-start | bytes 786440 | tf_op jit(solution)/shard_map/ppermute | solution.py:74
  118.5 1.9 %collective-permute-start.27 = (bf16[1,2,16,4096]{3,2,1,0:T(8,128)(2,1)S(1)}, bf16[1,2,16,4096]{3,2,1,0:T(8,128)(2,1)S(1)}, u32[]{:S(2)}, u32[]{:S(2)}) collective-permute-start(bf16[1,2,16,4096]{3,2,1,0:T(8,128)(2,1)S(1)} %collective-permute-done.23.refs_3_.refs_1_), channel_id=1, source_target_pairs={{0,64},{64,0},{1,65},{65,1},{2,66},{66,2},{3,67},{67,3},{4,68},{68... | collective-permute-start | bytes 786440 | tf_op jit(solution)/shard_map/ppermute | solution.py:74
  121.8 8.4 %collective-permute-start.28 = (bf16[192,512]{1,0:T(8,128)(2,1)S(1)}, bf16[192,512]{1,0:T(8,128)(2,1)S(1)}, u32[]{:S(2)}, u32[]{:S(2)}) collective-permute-start(bf16[192,512]{1,0:T(8,128)(2,1)S(1)} %sent_rows.2), channel_id=1, source_target_pairs={{0,1},{1,0},{2,3},{3,2},{4,5},{5,4},{6,7},{7,6},{8,9},{9,8},{10,11... | collective-permute-start | bytes 589832 | tf_op jit(solution)/shard_map/ppermute | solution.py:74
  123.6 6.7 %collective-permute-start.29 = (bf16[64,512]{1,0:T(8,128)(2,1)S(1)}, bf16[64,512]{1,0:T(8,128)(2,1)S(1)}, u32[]{:S(2)}, u32[]{:S(2)}) collective-permute-start(bf16[64,512]{1,0:T(8,128)(2,1)S(1)} %sent_rows.3), channel_id=1, source_target_pairs={{0,1},{1,0},{2,3},{3,2},{4,5},{5,4},{6,7},{7,6},{8,9},{9,8},{10,11... | collective-permute-start | bytes 196616 | tf_op jit(solution)/shard_map/ppermute | solution.py:74
  (7 other events, 29.2 us)
